TPU v7x, 32 devices: a whole 2x2x4 slice. The times are simulated.
32 devices in a mesh: section: 2 (over x), seq: 4 (over y, core), dp: 4 (over z).
Axes of the slice: x: 2, y: 2, z: 4, core: 2. Of those that a mesh axis runs over, the one named last changes fastest.
Arguments:
- boundary: bfloat16 [2, 8, 1024, 1024], P('section', 'dp', 'seq'), may hold values from -6 to 6
- positions: int32 [8, 1024], P('dp', 'seq'), may hold values from 0 to 1023, as said below
- decay_exp: int32 [2, 8], P('section'), may hold values from 8 to 32
- mixer_in: bfloat16 [2, 1024, 4096], P('section'), may hold values from -0.1875 to 0.1875
- mixer_out: bfloat16 [2, 1024, 1024], P('section'), may hold values from -0.1875 to 0.1875
- channel_in: bfloat16 [2, 1024, 5632], P('section'), may hold values from -0.1875 to 0.1875
- channel_out: bfloat16 [2, 2816, 1024], P('section'), may hold values from -0.109375 to 0.109375
Outputs:
- boundary_out: bfloat16 [2, 8, 1024, 1024], P('section', 'dp', 'seq')
- grad_mixer_in: float32 [2, 1024, 4096], P('section', 'seq')
- grad_mixer_out: float32 [2, 1024, 1024], P('section', 'seq')
- grad_channel_in: float32 [2, 1024, 5632], P('section', 'seq')
- grad_channel_out: float32 [2, 2816, 1024], P('section', 'seq')
Inputs may be any that keep to these rules, and one draw needn't show every extreme that they name: `positions`: each sequence is cut into documents, the first token of every sequence starting one, and the first sequence is one whole document; a position counts the tokens since its document's start.
All inputs are finite; a program needn't handle non-finite values.
Results may differ from a plain program's by a relative error of at most 0.028.
Values may be sent and summed in bfloat16 or wider, within the bound.
No kernel may reach another device: no remote copies, remote signals or barrier semaphores. Data moves between devices by JAX's collectives and lax.ppermute only.
A program may use at most 256 MiB of HBM per device.

v0:
```python
import math

import jax
import jax.numpy as jnp
from jax import lax
from jax.sharding import PartitionSpec as P

HEADS = 8
BLK = 256


epsilon = 1e-06
theta_base = 10000.0


def entering(part, axis, combine, identity):
    place = lax.axis_index(axis)
    gathered = jax.tree.map(lambda a: lax.all_gather(a, axis), part)
    state = jax.tree.map(lambda a, e: jnp.zeros_like(a) + jnp.asarray(e, a.dtype), part, identity)

    def one(lap, state):
        return combine(
            state, jax.tree.map(lambda a: lax.dynamic_index_in_dim(a, lap, 0, False), gathered)
        )

    return lax.fori_loop(0, place, one, state)


def entering_2(array, axis, join, neutral):
    count = lax.axis_size(axis)
    place = lax.axis_index(axis)
    ahead = count - 1 - place
    gathered = jax.tree.map(
        lambda a, kind: lax.all_gather(a.astype(kind), axis),
        array,
        jax.tree.map(lambda a: jnp.bfloat16 if a.dtype == jnp.float32 else a.dtype, array),
    )
    state = jax.tree.map(lambda a, e: jnp.zeros_like(a) + jnp.asarray(e, a.dtype), array, neutral)

    def one(lap, state):
        source = count - 1 - lap
        return join(
            state,
            jax.tree.map(
                lambda a, own: lax.dynamic_index_in_dim(a, source, 0, False).astype(own.dtype),
                gathered,
                array,
            ),
        )

    return lax.fori_loop(0, ahead, one, state)


def from_behind(block, axis, distance):
    devices = range(lax.axis_size(axis))
    route = [(i - distance, i) for i in devices if i - distance in devices]
    return lax.ppermute(block, axis, route)


def simple_norm(source):
    factor = lax.rsqrt(jnp.mean(source * source, axis=-1, keepdims=True) + epsilon)
    return (source * factor, factor)


def norm_back(cotangent, normed, factor):
    return factor * (cotangent - normed * jnp.mean(cotangent * normed, axis=-1, keepdims=True))


def angle_tables(position_row, half_size):
    frequency = jnp.exp(
        jnp.arange(half_size, dtype=jnp.float32) * (-math.log(theta_base) / half_size)
    )
    angles = position_row.astype(jnp.float32)[:, None] * frequency[None, :]
    cosine = jnp.cos(angles)[:, None, :]
    sine_rows = jnp.sin(angles)[:, None, :]
    return (
        jnp.concatenate([cosine, cosine], axis=-1),
        jnp.concatenate([-sine_rows, sine_rows], axis=-1),
    )


def rotate(source, cosine, sine_rows):
    half_size = source.shape[-1] // 2
    return source * cosine + jnp.roll(source, half_size, axis=-1) * sine_rows


def unrotate(cotangent, cosine, sine_rows):
    half_size = cotangent.shape[-1] // 2
    return cotangent * cosine + jnp.roll(cotangent * sine_rows, half_size, axis=-1)


def swish_slope(source):
    sigma = jax.nn.sigmoid(source)
    return sigma * (1.0 + source * (1.0 - sigma))


def decay_tables(slopes, block_rows):
    offsets = jnp.arange(block_rows, dtype=jnp.float32)
    distance = offsets[:, None] - offsets[None, :]
    decay_mask = jnp.where(
        distance[None] >= 0.0,
        jnp.exp(-slopes[:, None, None] * jnp.maximum(distance, 0.0)[None]),
        0.0,
    )
    query_decay = jnp.exp(-slopes[None, :] * offsets[:, None])
    key_decay = jnp.exp(-slopes[None, :] * (block_rows - offsets)[:, None])
    block_decay = jnp.exp(-slopes * block_rows)
    return (decay_mask, query_decay, key_decay, block_decay)


def link_states(earlier, later):
    return (earlier[0] * later[0], later[0] * earlier[1] + later[1])


def attend_forward(queries, key_rows, values, slopes, state_in):
    length, head_count, head_size = queries.shape
    blocks = length // BLK
    decay_mask, query_decay, key_decay, block_decay = decay_tables(slopes, BLK)
    query_blk = queries.reshape(blocks, BLK, head_count, head_size)
    key_blk = key_rows.reshape(blocks, BLK, head_count, head_size)
    value_blk = values.reshape(blocks, BLK, head_count, head_size)
    scores = jnp.einsum("bihe,bjhe->bhij", query_blk, key_blk, preferred_element_type=jnp.float32)
    weights = (decay_mask[None] * scores).astype(jnp.bfloat16)
    inner_term = jnp.einsum(
        "bhij,bjhe->bihe", weights, value_blk, preferred_element_type=jnp.float32
    )
    keyed_rows = (key_blk.astype(jnp.float32) * key_decay[None, :, :, None]).astype(jnp.bfloat16)
    block_states = jnp.einsum(
        "bjhe,bjhf->bhef", keyed_rows, value_blk, preferred_element_type=jnp.float32
    )
    running = [jnp.zeros((head_count, head_size, head_size), jnp.float32)]
    running.append(block_decay[:, None, None] * running[-1] + block_states[0])
    device_decay = jnp.exp(-slopes * length)[:, None, None]
    state_in = entering(
        (device_decay, running[blocks]),
        "seq",
        link_states,
        (jnp.ones_like(device_decay), jnp.zeros_like(running[blocks])),
    )[1]
    starts = jnp.stack([jnp.exp(-slopes * 0)[:, None, None] * state_in + running[0]])
    carried = jnp.einsum(
        "bihe,bhef->bihf",
        query_blk,
        starts.astype(jnp.bfloat16),
        preferred_element_type=jnp.float32,
    )
    attended = inner_term + query_decay[None, :, :, None] * carried
    return (attended.reshape(length, head_count * head_size), starts, state_in)


def attend_backward(cotangent, queries, key_rows, values, starts, slopes):
    length, head_count, head_size = queries.shape
    blocks = length // BLK
    decay_mask, query_decay, key_decay, block_decay = decay_tables(slopes, BLK)
    query_blk = queries.reshape(blocks, BLK, head_count, head_size)
    key_blk = key_rows.reshape(blocks, BLK, head_count, head_size)
    value_blk = values.reshape(blocks, BLK, head_count, head_size)
    grad_blk = cotangent.reshape(blocks, BLK, head_count, head_size)
    scores = jnp.einsum("bihe,bjhe->bhij", query_blk, key_blk, preferred_element_type=jnp.float32)
    weights = (decay_mask[None] * scores).astype(jnp.bfloat16)
    grad_weights = jnp.einsum(
        "bihe,bjhe->bhij", grad_blk, value_blk, preferred_element_type=jnp.float32
    )
    grad_scores = (decay_mask[None] * grad_weights).astype(jnp.bfloat16)
    scaled = (query_decay[None, :, :, None] * grad_blk.astype(jnp.float32)).astype(jnp.bfloat16)
    state_terms = jnp.einsum(
        "bihe,bihf->bhef", query_blk, scaled, preferred_element_type=jnp.float32
    )
    running = [jnp.zeros((head_count, head_size, head_size), jnp.float32)] * (blocks + 1)
    for number in reversed(range(blocks)):
        running[number] = block_decay[:, None, None] * running[number + 1] + state_terms[number]
    device_decay = jnp.exp(-slopes * length)[:, None, None]
    state_end = entering_2(
        (device_decay, running[0]),
        "seq",
        link_states,
        (jnp.ones_like(device_decay), jnp.zeros_like(running[0])),
    )[1]
    state_after = jnp.stack(
        [
            jnp.exp(-slopes * (BLK * (blocks - number - 1)))[:, None, None] * state_end
            + running[number + 1]
            for number in range(blocks)
        ]
    ).astype(jnp.bfloat16)
    keyed_rows = (key_blk.astype(jnp.float32) * key_decay[None, :, :, None]).astype(jnp.bfloat16)
    grad_values = jnp.einsum(
        "bhij,bihe->bjhe", weights, grad_blk, preferred_element_type=jnp.float32
    )
    grad_values = grad_values + jnp.einsum(
        "bjhe,bhef->bjhf", keyed_rows, state_after, preferred_element_type=jnp.float32
    )
    grad_queries = jnp.einsum(
        "bhij,bjhe->bihe", grad_scores, key_blk, preferred_element_type=jnp.float32
    )
    grad_queries = grad_queries + jnp.einsum(
        "bihf,bhef->bihe", scaled, starts.astype(jnp.bfloat16), preferred_element_type=jnp.float32
    )
    grad_keys = jnp.einsum(
        "bhij,bihe->bjhe", grad_scores, query_blk, preferred_element_type=jnp.float32
    )
    grad_keys = grad_keys + key_decay[None, :, :, None] * jnp.einsum(
        "bjhf,bhef->bjhe", value_blk, state_after, preferred_element_type=jnp.float32
    )
    row_shape = (length, head_count, head_size)
    return (
        grad_queries.reshape(row_shape),
        grad_keys.reshape(row_shape),
        grad_values.reshape(row_shape),
    )


def layer_forward(
    inputs, cosine, sine_rows, slopes, first_in, first_out, second_in, second_out, state_in
):
    row_count, model_width = inputs.shape
    head_size = model_width // HEADS
    normed, factor = simple_norm(inputs)
    projected = jnp.dot(normed.astype(jnp.bfloat16), first_in, preferred_element_type=jnp.float32)
    queries = rotate(
        jax.nn.silu(projected[:, :model_width]).reshape(row_count, HEADS, head_size),
        cosine,
        sine_rows,
    ).astype(jnp.bfloat16)
    key_rows = rotate(
        jax.nn.silu(projected[:, model_width : 2 * model_width]).reshape(
            row_count, HEADS, head_size
        ),
        cosine,
        sine_rows,
    ).astype(jnp.bfloat16)
    values = (
        projected[:, 2 * model_width : 3 * model_width]
        .reshape(row_count, HEADS, head_size)
        .astype(jnp.bfloat16)
    )
    attended, starts, state_in = attend_forward(queries, key_rows, values, slopes, state_in)
    mixed_rows, mixed_factor = simple_norm(attended)
    gated_rows = (mixed_rows * projected[:, 3 * model_width :]).astype(jnp.bfloat16)
    middle = inputs + jnp.dot(gated_rows, first_out, preferred_element_type=jnp.float32)
    second, second_factor = simple_norm(middle)
    gate_up = jnp.dot(second.astype(jnp.bfloat16), second_in, preferred_element_type=jnp.float32)
    hidden = second_out.shape[0]
    product = (gate_up[:, :hidden] * gate_up[:, hidden:]).astype(jnp.bfloat16)
    outputs = middle + jnp.dot(product, second_out, preferred_element_type=jnp.float32)
    record = dict(
        normed=normed,
        factor=factor,
        projected=projected,
        queries=queries,
        keys=key_rows,
        values=values,
        starts=starts,
        mixed=mixed_rows,
        mixed_factor=mixed_factor,
        gated=gated_rows,
        second=second,
        second_factor=second_factor,
        gate_up=gate_up,
        product=product,
        cosine=cosine,
        sine=sine_rows,
        state_in=state_in,
    )
    return (outputs, record)


def layer_backward(grad_out, record, slopes, first_in, first_out, second_in, second_out):
    row_count, model_width = record["mixed"].shape
    head_size = model_width // HEADS
    hidden = second_out.shape[0]
    low_grad = grad_out.astype(jnp.bfloat16)
    grad_down = jnp.einsum(
        "tf,td->fd", record["product"], low_grad, preferred_element_type=jnp.float32
    )
    grad_product = jnp.einsum("td,fd->tf", low_grad, second_out, preferred_element_type=jnp.float32)
    gate_up = record["gate_up"]
    grad_gate_up = jnp.concatenate(
        [grad_product * gate_up[:, hidden:], grad_product * gate_up[:, :hidden]], axis=-1
    ).astype(jnp.bfloat16)
    grad_unit_in = jnp.einsum(
        "td,tf->df",
        record["second"].astype(jnp.bfloat16),
        grad_gate_up,
        preferred_element_type=jnp.float32,
    )
    grad_second = jnp.einsum(
        "tf,df->td", grad_gate_up, second_in, preferred_element_type=jnp.float32
    )
    grad_middle = grad_out + norm_back(grad_second, record["second"], record["second_factor"])
    middle_low = grad_middle.astype(jnp.bfloat16)
    grad_layer_out = jnp.einsum(
        "td,te->de", record["gated"], middle_low, preferred_element_type=jnp.float32
    )
    grad_gated = jnp.einsum("te,de->td", middle_low, first_out, preferred_element_type=jnp.float32)
    projected = record["projected"]
    grad_gate = grad_gated * record["mixed"]
    grad_attended = norm_back(
        grad_gated * projected[:, 3 * model_width :], record["mixed"], record["mixed_factor"]
    ).astype(jnp.bfloat16)
    grad_queries, grad_keys, grad_values = attend_backward(
        grad_attended.reshape(row_count, HEADS, head_size),
        record["queries"],
        record["keys"],
        record["values"],
        record["starts"],
        slopes,
    )
    grad_qp = unrotate(grad_queries, record["cosine"], record["sine"]).reshape(
        row_count, model_width
    ) * swish_slope(projected[:, :model_width])
    grad_kp = unrotate(grad_keys, record["cosine"], record["sine"]).reshape(
        row_count, model_width
    ) * swish_slope(projected[:, model_width : 2 * model_width])
    grad_projected = jnp.concatenate(
        [grad_qp, grad_kp, grad_values.reshape(row_count, model_width), grad_gate], axis=-1
    ).astype(jnp.bfloat16)
    grad_layer_in = jnp.einsum(
        "td,tf->df",
        record["normed"].astype(jnp.bfloat16),
        grad_projected,
        preferred_element_type=jnp.float32,
    )
    grad_first = jnp.einsum(
        "tf,df->td", grad_projected, first_in, preferred_element_type=jnp.float32
    )
    grad_inputs = grad_middle + norm_back(grad_first, record["normed"], record["factor"])
    return (grad_inputs, (grad_layer_in, grad_layer_out, grad_unit_in, grad_down))


def per_device(boundary, positions, decay_exp, mixer_in, mixer_out, channel_in, channel_out):
    is_first = lax.axis_index("section") == 0
    own_rows = boundary[0]
    micro_count = own_rows.shape[0]
    row_count = own_rows.shape[1]
    model_width = own_rows.shape[2]
    slopes = jnp.exp2(-0.5 * decay_exp[0].astype(jnp.float32))
    layer_in, layer_out, unit_in, unit_out = (
        mixer_in[0],
        mixer_out[0],
        channel_in[0],
        channel_out[0],
    )
    half_size = model_width // HEADS // 2
    received = jnp.zeros((row_count, model_width), jnp.bfloat16)
    records = []
    outputs = []
    for moment in range(micro_count + 1):
        own_batch = min(moment, micro_count - 1)
        prior_batch = max(moment - 1, 0)
        inputs = jnp.where(
            is_first, own_rows[own_batch].astype(jnp.float32), received.astype(jnp.float32)
        )
        pick_index = jnp.where(is_first, own_batch, prior_batch)
        cosine, sine_rows = angle_tables(
            lax.dynamic_index_in_dim(positions, pick_index, 0, keepdims=False), half_size
        )
        result, record = layer_forward(
            inputs, cosine, sine_rows, slopes, layer_in, layer_out, unit_in, unit_out, None
        )
        records.append(record)
        outputs.append(result)
        if moment < micro_count:
            received = from_behind(result.astype(jnp.bfloat16), "section", 1)
    stacked = jax.tree.map(lambda *members: jnp.stack(members), *records)
    gradients = tuple(
        (
            jnp.zeros(member.shape, jnp.float32)
            for member in (layer_in, layer_out, unit_in, unit_out)
        )
    )
    returned = jnp.zeros((row_count, model_width), jnp.bfloat16)
    back_out = []
    for moment in range(micro_count + 1):
        upstream = own_rows[min(moment, micro_count - 1)].astype(jnp.float32) * (
            1.0 if moment < micro_count else 0.0
        )
        grad_out = jnp.where(is_first, returned.astype(jnp.float32), upstream)
        pick_index = jnp.where(is_first, max(moment - 1, 0), min(moment + 1, micro_count))
        record = jax.tree.map(
            lambda member: lax.dynamic_index_in_dim(member, pick_index, 0, keepdims=False), stacked
        )
        grad_inputs, summands = layer_backward(
            grad_out, record, slopes, layer_in, layer_out, unit_in, unit_out
        )
        gradients = tuple(
            (running_total + addend for running_total, addend in zip(gradients, summands))
        )
        back_out.append(grad_inputs)
        if moment < micro_count:
            returned = from_behind(grad_inputs.astype(jnp.bfloat16), "section", -1)
    joined = jnp.where(is_first, jnp.stack(back_out[1:]), jnp.stack(outputs[1:])).astype(
        jnp.bfloat16
    )[None]
    summands = tuple((member[None] for member in gradients))
    shares = (
        lax.psum_scatter(
            summands[0].astype(jnp.bfloat16), "seq", scatter_dimension=1, tiled=True
        ).astype(jnp.float32),
        lax.psum_scatter(
            summands[1].astype(jnp.bfloat16), "seq", scatter_dimension=1, tiled=True
        ).astype(jnp.float32),
        lax.psum_scatter(
            summands[2].astype(jnp.bfloat16), "seq", scatter_dimension=1, tiled=True
        ).astype(jnp.float32),
        lax.psum_scatter(
            summands[3].astype(jnp.bfloat16), "seq", scatter_dimension=1, tiled=True
        ).astype(jnp.float32),
    )
    summed = (
        lax.psum(shares[0].astype(jnp.bfloat16), "dp").astype(jnp.float32),
        lax.psum(shares[1].astype(jnp.bfloat16), "dp").astype(jnp.float32),
        lax.psum(shares[2].astype(jnp.bfloat16), "dp").astype(jnp.float32),
        lax.psum(shares[3].astype(jnp.bfloat16), "dp").astype(jnp.float32),
    )
    return (joined, summed[0], summed[1], summed[2], summed[3])


def solution(mesh):
    in_specs = (
        P("section", "dp", "seq", None),
        P("dp", "seq"),
        P("section", None),
        P("section", None, None),
        P("section", None, None),
        P("section", None, None),
        P("section", None, None),
    )
    out_specs = (
        P("section", "dp", "seq", None),
        P("section", "seq", None),
        P("section", "seq", None),
        P("section", "seq", None),
        P("section", "seq", None),
    )
    return jax.shard_map(
        per_device, mesh=mesh, in_specs=in_specs, out_specs=out_specs, check_vma=False
    )
```

profile of v0, /device:TPU:0, one launch (start us, length us, event | category | flops | bytes accessed | tf_op | source)
XLA Modules:
  0.0 1073.9 jit_solution(8539952508167467212)
XLA Ops:
  46.0 15.3 %all-gather.17.cloned.1.call-done = f32[32,128,128]{2,1,0:T(8,128)} async-done(((f32[8,128,128]{2,1,0:T(8,128)}), f32[32,128,128]{2,1,0:T(8,128)}) %all-gather.17.cloned.1.call-update) | async-done | bytes 2097168 | tf_op jit(solution)/shard_map/all_gather | solution.py:18
  70.9 7.1 fusion.11
  88.7 7.4 collective-permute-done
  118.7 8.3 all-gather.9
  222.4 11.2 %pad_maximum_fusion.1 = f32[3,256,4096]{2,1,0:T(8,128)} fusion(f32[1,256,4096]{2,1,0:T(8,128)} %bitcast.912, f32[1,256,4096]{2,1,0:T(8,128)} %bitcast.911, f32[1,256,4096]{2,1,0:T(8,128)} %bitcast.910), kind=kLoop, calls=%fused_computation.15 | loop fusion | flops 6291456 | bytes 25165824 | tf_op jit(solution)/shard_map/stack | solution.py:365
  233.6 9.8 dynamic-slice_bitcast_fusion.6
  256.1 9.3 fusion.7
  271.5 6.9 pad_maximum_fusion
  278.4 6.2 dynamic-slice_bitcast_fusion.3
  292.4 8.9 fusion.219
  321.2 21.0 %all-gather.23.cloned.1.call-done = bf16[32,128,128]{2,1,0:T(8,128)(2,1)} async-done(((bf16[8,128,128]{2,1,0:T(8,128)(2,1)}), bf16[32,128,128]{2,1,0:T(8,128)(2,1)}) %all-gather.23.cloned.1.call-update) | async-done | bytes 1048592 | tf_op jit(solution)/shard_map/all_gather | solution.py:34
  343.0 7.9 while.81
  383.6 6.3 fusion.209
  391.7 11.8 %collective-permute-done.2 = bf16[256,1024]{1,0:T(8,128)(2,1)S(1)} collective-permute-done((bf16[256,1024]{1,0:T(8,128)(2,1)S(1)}, bf16[256,1024]{1,0:T(8,128)(2,1)S(1)}, u32[]{:S(2)}, u32[]{:S(2)}) %collective-permute-start.2) | collective-permute-done | bytes 524320 | tf_op jit(solution)/shard_map/ppermute | solution.py:57
  406.9 9.4 fusion.205
  430.7 9.0 all-gather.25.cloned.1.call-done
  440.6 8.2 while.82
  481.5 6.3 fusion.196
  489.9 11.5 %collective-permute-done.3 = bf16[256,1024]{1,0:T(8,128)(2,1)S(1)} collective-permute-done((bf16[256,1024]{1,0:T(8,128)(2,1)S(1)}, bf16[256,1024]{1,0:T(8,128)(2,1)S(1)}, u32[]{:S(2)}, u32[]{:S(2)}) %collective-permute-start.3) | collective-permute-done | bytes 524320 | tf_op jit(solution)/shard_map/ppermute | solution.py:57
  504.9 9.4 fusion.192
  544.6 6.2 fusion.65
  550.9 11.5 %fusion.38 = bf16[1,2816,1024]{2,1,0:T(8,128)(2,1)} fusion(f32[2816,1024]{1,0:T(8,128)} %fusion.67, f32[2816,1024]{1,0:T(8,128)} %fusion.65, bf16[3,256,2816]{2,1,0:T(8,128)(2,1)S(1)} %pad_maximum_fusion.2, s32[]{:T(128)S(6)} %select_n.208, bf16[256,1024]{1,0:T(8,128)(2,1)S(1)} %copy-done.55, pred[]{:T(512)S(6)} %eq.3, ...), kind=kOutput, calls=%fused_computation.58 | convolution fusion | flops 1486356480 | bytes 31326212 | tf_op jit(solution)/shard_map/tf,td->fd/dot_general | solution.py:273
  563.6 9.8 fusion.258
  573.5 11.7 %fusion.260 = f32[1024,4096]{1,0:T(8,128)} fusion(f32[3,256,1024]{2,1,0:T(8,128)} %pad_maximum_fusion.5, s32[]{:T(128)S(6)} %select_n.206, bf16[256,1024]{1,0:T(8,128)(2,1)S(1)} %copy-done.106, bf16[256,1024]{1,0:T(8,128)(2,1)S(1)} %copy-done.92, bf16[256,1024]{1,0:T(8,128)(2,1)S(1)} %copy-done.88, bf16[256,1024]{1,0:T(8,128)(2,1)S(1)} %copy-done.86), kind=kOutput, calls=%fused_computation.422 | convolution fusion | flops 2155872256 | bytes 19398660 | tf_op jit(solution)/shard_map/td,tf->df/dot_general | solution.py:318
  623.7 16.8 %fusion.25 = bf16[1,1024,4096]{2,1,0:T(8,128)(2,1)} fusion(f32[1024,4096]{1,0:T(8,128)} %fusion.258, f32[1024,4096]{1,0:T(8,128)} %fusion.260, f32[3,256,1024]{2,1,0:T(8,128)} %pad_maximum_fusion.5, s32[]{:T(128)S(6)} %select_n.208, bf16[256,1024]{1,0:T(8,128)(2,1)} %get-tuple-element.600, bf16[256,1024]{1,0:T(8,128)(2,1)} %copy.449, ...), kind=kOutput, calls=%fused_computation.42 | convolution fusion | flops 2168455168 | bytes 44564484 | tf_op jit(solution)/shard_map/td,tf->df/dot_general | solution.py:318
  641.9 16.1 %fusion.62 = f32[1024,5632]{1,0:T(8,128)} fusion(bf16[256,2816]{1,0:T(8,128)(2,1)} %copy-done.49, bf16[256,2816]{1,0:T(8,128)(2,1)S(1)} %copy-done.48, f32[3,256,1024]{2,1,0:T(8,128)} %copy-done.14, s32[]{:T(128)S(6)} %select_n.203), kind=kOutput, calls=%fused_computation.116 | convolution fusion | flops 2958557184 | bytes 26476548 | tf_op jit(solution)/shard_map/td,tf->df/dot_general | solution.py:281
  658.0 11.2 %fusion.61 = f32[1024,5632]{1,0:T(8,128)} fusion(bf16[256,2816]{1,0:T(8,128)(2,1)S(1)} %copy-done.51, bf16[256,2816]{1,0:T(8,128)(2,1)S(1)} %copy-done.50, f32[3,256,1024]{2,1,0:T(8,128)} %copy-done.14, s32[]{:T(128)S(6)} %select_n.206), kind=kOutput, calls=%fused_computation.115 | convolution fusion | flops 2958557184 | bytes 26476548 | tf_op jit(solution)/shard_map/td,tf->df/dot_general | solution.py:281
  669.3 21.6 %fusion = bf16[1,1024,5632]{2,1,0:T(8,128)(2,1)} fusion(f32[1024,5632]{1,0:T(8,128)} %fusion.62, f32[1024,5632]{1,0:T(8,128)} %fusion.61, bf16[256,2816]{1,0:T(8,128)(2,1)} %get-tuple-element.588, bf16[256,2816]{1,0:T(8,128)(2,1)S(1)} %copy-done.53, f32[3,256,1024]{2,1,0:T(8,128)} %copy-done.14, s32[]{:T(128)S(6)} %select_n.208), kind=kOutput, calls=%fused_computation.16 | convolution fusion | flops 2975858688 | bytes 61079556 | tf_op jit(solution)/shard_map/td,tf->df/dot_general | solution.py:281
  691.0 20.7 %reduce-scatter.5.cloned.1.call-done = bf16[1,256,4096]{2,1,0:T(8,128)(2,1)} async-done(((bf16[1,1024,4096]{2,1,0:T(8,128)(2,1)}), bf16[1,256,4096]{2,1,0:T(8,128)(2,1)}) %reduce-scatter.5.cloned.1.call-update) | async-done | bytes 2097168 | tf_op jit(solution)/shard_map/reduce_scatter | solution.py:397
  711.7 94.8 %reduce-scatter.9.cloned.1.call-done = bf16[1,256,5632]{2,1,0:T(8,128)(2,1)} async-done(((bf16[1,1024,5632]{2,1,0:T(8,128)(2,1)}), bf16[1,256,5632]{2,1,0:T(8,128)(2,1)}) %reduce-scatter.9.cloned.1.call-update) | async-done | bytes 2883600 | tf_op jit(solution)/shard_map/reduce_scatter | solution.py:403
  814.0 7.1 fusion.182
  824.4 230.2 %all-reduce.3.cloned.1.call-done = (bf16[1,256,4096]{2,1,0:T(8,128)(2,1)}, bf16[1,256,1024]{2,1,0:T(8,128)(2,1)}, bf16[1,256,5632]{2,1,0:T(8,128)(2,1)}, bf16[1,704,1024]{2,1,0:T(8,128)(2,1)}) async-done(((bf16[1,256,4096]{2,1,0:T(8,128)(2,1)}, bf16[1,256,1024]{2,1,0:T(8,128)(2,1)}, bf16[1,256,5632]{2,1,0:T(8,128)(2,1)}, bf16[1,704,1024]{2,1,0:T(8,128)(2,1)}), (bf16[1,256,4096]{2,1,0:T(8,128)(2,1)}, ...) | async-done | bytes 6946832 | tf_op jit(solution)/shard_map/psum | solution.py:411
  (692 shorter events, 429.5 us)
Async XLA Ops:
  7.2 62.8 %copy-start = (bf16[1,1024,1024]{2,1,0:T(8,128)(2,1)S(1)}, bf16[1,1024,1024]{2,1,0:T(8,128)(2,1)}, u32[]{:S(2)}) copy-start(bf16[1,1024,1024]{2,1,0:T(8,128)(2,1)} %param.23) | copy-start | bytes 6291460
  7.2 54.1 %all-gather.17.cloned.1.call-start = ((), (), s32[]{:S(2)}) async-start(), calls=%async_computation.8 | async-start | bytes 2621440 | tf_op jit(solution)/shard_map/all_gather | solution.py:18
  35.8 113.1 %all-gather.19.cloned.1.call-start = ((), (), s32[]{:S(2)}) async-start(), calls=%async_computation.9 | async-start | bytes 2621440 | tf_op jit(solution)/shard_map/all_gather | solution.py:18
  42.5 18.7 %copy-start.153 = (pred[256,256]{1,0:T(8,128)(4,1)}, pred[256,256]{1,0:T(8,128)(4,1)S(1)}, u32[]{:S(2)}) copy-start(pred[256,256]{1,0:T(8,128)(4,1)S(1)} %fusion.399) | copy-start | bytes 196612
  42.6 18.7 %copy-start.148 = (f32[256,256]{1,0:T(8,128)}, f32[256,256]{1,0:T(8,128)S(1)}, u32[]{:S(2)}) copy-start(f32[256,256]{1,0:T(8,128)S(1)} %fusion.398) | copy-start | bytes 786436
  80.7 15.3 %collective-permute-start = (bf16[256,1024]{1,0:T(8,128)(2,1)}, bf16[256,1024]{1,0:T(8,128)(2,1)}, u32[]{:S(2)}, u32[]{:S(2)}) collective-permute-start(bf16[256,1024]{1,0:T(8,128)(2,1)} %fusion.120), channel_id=1, source_target_pairs={{0,16},{1,17},{2,18},{3,19},{4,20},{5,21},{6,22},{7,23},{8,24},{9,... | collective-permute-start | bytes 1572872 | tf_op jit(solution)/shard_map/ppermute | solution.py:57
  87.0 28.5 %copy-start.130 = (f32[256,128]{0,1:T(8,128)}, f32[256,128]{0,1:T(8,128)S(1)}, u32[]{:S(2)}) copy-start(f32[256,128]{0,1:T(8,128)S(1)} %copy.310) | copy-start | bytes 393220
  118.7 124.7 %all-gather.21.cloned.1.call-start = ((), (), s32[]{:S(2)}) async-start(), calls=%async_computation.10 | async-start | bytes 2621440 | tf_op jit(solution)/shard_map/all_gather | solution.py:18
  169.4 15.6 %collective-permute-start.1 = (bf16[256,1024]{1,0:T(8,128)(2,1)}, bf16[256,1024]{1,0:T(8,128)(2,1)}, u32[]{:S(2)}, u32[]{:S(2)}) collective-permute-start(bf16[256,1024]{1,0:T(8,128)(2,1)} %fusion.111), channel_id=1, source_target_pairs={{0,16},{1,17},{2,18},{3,19},{4,20},{5,21},{6,22},{7,23},{8,24},{9,... | collective-permute-start | bytes 1572872 | tf_op jit(solution)/shard_map/ppermute | solution.py:57
  187.6 26.4 %copy-start.174 = (f32[256]{0:T(256)}, f32[256]{0:T(256)S(1)}, u32[]{:S(2)}) copy-start(f32[256]{0:T(256)S(1)} %add_rsqrt_fusion.2) | copy-start | bytes 3076
  208.9 133.3 %all-gather.23.cloned.1.call-start = ((), (), s32[]{:S(2)}) async-start(), calls=%async_computation.11 | async-start | bytes 1310720 | tf_op jit(solution)/shard_map/all_gather | solution.py:34
  310.5 129.2 %all-gather.25.cloned.1.call-start = ((), (), s32[]{:S(2)}) async-start(), calls=%async_computation.12 | async-start | bytes 1310720 | tf_op jit(solution)/shard_map/all_gather | solution.py:34
  383.5 20.0 %slice-start.4 = ((s8[5767168]{0:T(1024)(128)(4,1)}), s8[4194304]{0:T(1024)(128)(4,1)S(1)}, s32[]{:S(2)}) async-start(s8[5767168]{0:T(1024)(128)(4,1)} %bitcast.885), calls=%async_computation.19 | async-start | bytes 8388608
  383.5 20.0 %slice-start.10 = ((s8[5767168]{0:T(1024)(128)(4,1)}), s8[4194304]{0:T(1024)(128)(4,1)S(1)}, s32[]{:S(2)}) async-start(s8[5767168]{0:T(1024)(128)(4,1)} %bitcast.915), calls=%async_computation.25 | async-start | bytes 8388608
  383.5 19.9 %slice-start.5 = ((s8[5767168]{0:T(1024)(128)(4,1)}), s8[1572864]{0:T(1024)(128)(4,1)S(1)}, s32[]{:S(2)}) async-start(s8[5767168]{0:T(1024)(128)(4,1)} %bitcast.885), calls=%async_computation.20 | async-start | bytes 3145728
  383.5 19.9 %slice-start.11 = ((s8[5767168]{0:T(1024)(128)(4,1)}), s8[1572864]{0:T(1024)(128)(4,1)S(1)}, s32[]{:S(2)}) async-start(s8[5767168]{0:T(1024)(128)(4,1)} %bitcast.915), calls=%async_computation.26 | async-start | bytes 3145728
  390.2 13.3 %collective-permute-start.2 = (bf16[256,1024]{1,0:T(8,128)(2,1)S(1)}, bf16[256,1024]{1,0:T(8,128)(2,1)S(1)}, u32[]{:S(2)}, u32[]{:S(2)}) collective-permute-start(bf16[256,1024]{1,0:T(8,128)(2,1)S(1)} %fusion.213), channel_id=1, source_target_pairs={{16,0},{17,1},{18,2},{19,3},{20,4},{21,5},{22,6},{23,7},{24,8},{25... | collective-permute-start | bytes 1572872 | tf_op jit(solution)/shard_map/ppermute | solution.py:57
  423.8 167.0 %all-gather.27.cloned.1.call-start = ((), (), s32[]{:S(2)}) async-start(), calls=%async_computation.13 | async-start | bytes 1310720 | tf_op jit(solution)/shard_map/all_gather | solution.py:34
  481.4 20.0 %slice-start.6 = ((s8[5767168]{0:T(1024)(128)(4,1)}), s8[4194304]{0:T(1024)(128)(4,1)S(1)}, s32[]{:S(2)}) async-start(s8[5767168]{0:T(1024)(128)(4,1)} %bitcast.887), calls=%async_computation.21 | async-start | bytes 8388608
  481.4 20.0 %slice-start.8 = ((s8[5767168]{0:T(1024)(128)(4,1)}), s8[4194304]{0:T(1024)(128)(4,1)S(1)}, s32[]{:S(2)}) async-start(s8[5767168]{0:T(1024)(128)(4,1)} %bitcast.913), calls=%async_computation.23 | async-start | bytes 8388608
  481.5 19.9 %slice-start.7 = ((s8[5767168]{0:T(1024)(128)(4,1)}), s8[1572864]{0:T(1024)(128)(4,1)S(1)}, s32[]{:S(2)}) async-start(s8[5767168]{0:T(1024)(128)(4,1)} %bitcast.887), calls=%async_computation.22 | async-start | bytes 3145728
  481.5 19.9 %slice-start.9 = ((s8[5767168]{0:T(1024)(128)(4,1)}), s8[1572864]{0:T(1024)(128)(4,1)S(1)}, s32[]{:S(2)}) async-start(s8[5767168]{0:T(1024)(128)(4,1)} %bitcast.913), calls=%async_computation.24 | async-start | bytes 3145728
  488.1 13.3 %collective-permute-start.3 = (bf16[256,1024]{1,0:T(8,128)(2,1)S(1)}, bf16[256,1024]{1,0:T(8,128)(2,1)S(1)}, u32[]{:S(2)}, u32[]{:S(2)}) collective-permute-start(bf16[256,1024]{1,0:T(8,128)(2,1)S(1)} %fusion.199), channel_id=1, source_target_pairs={{16,0},{17,1},{18,2},{19,3},{20,4},{21,5},{22,6},{23,7},{24,8},{25... | collective-permute-start | bytes 1572872 | tf_op jit(solution)/shard_map/ppermute | solution.py:57
  521.8 169.2 %reduce-scatter.7.cloned.1.call-start = ((), (), s32[]{:S(2)}) async-start(), calls=%async_computation.5 | async-start | bytes 2621440 | tf_op jit(solution)/shard_map/reduce_scatter | solution.py:400
  531.8 159.2 %reduce-scatter.11.cloned.1.call-start = ((), (), s32[]{:S(2)}) async-start(), calls=%async_computation.7 | async-start | bytes 7208960 | tf_op jit(solution)/shard_map/reduce_scatter | solution.py:406
  562.4 149.4 %reduce-scatter.5.cloned.1.call-start = ((), (), s32[]{:S(2)}) async-start(), calls=%async_computation.4 | async-start | bytes 10485760 | tf_op jit(solution)/shard_map/reduce_scatter | solution.py:397
  623.7 16.9 %copy-start.75 = (bf16[256,1024]{1,0:T(8,128)(2,1)}, bf16[256,1024]{1,0:T(8,128)(2,1)S(1)}, u32[]{:S(2)}) copy-start(bf16[256,1024]{1,0:T(8,128)(2,1)S(1)} %get-tuple-element.593) | copy-start | bytes 1572868
  623.7 16.9 %copy-start.77 = (bf16[256,1024]{1,0:T(8,128)(2,1)}, bf16[256,1024]{1,0:T(8,128)(2,1)S(1)}, u32[]{:S(2)}) copy-start(bf16[256,1024]{1,0:T(8,128)(2,1)S(1)} %get-tuple-element.594) | copy-start | bytes 1572868
  640.6 166.0 %reduce-scatter.9.cloned.1.call-start = ((), (), s32[]{:S(2)}) async-start(), calls=%async_computation.6 | async-start | bytes 14417920 | tf_op jit(solution)/shard_map/reduce_scatter | solution.py:403
  641.9 16.1 %copy-start.50 = (bf16[256,2816]{1,0:T(8,128)(2,1)S(1)}, bf16[256,2816]{1,0:T(8,128)(2,1)}, u32[]{:S(2)}) copy-start(bf16[256,2816]{1,0:T(8,128)(2,1)} %get-tuple-element.589) | copy-start | bytes 4325380
  641.9 16.1 %copy-start.51 = (bf16[256,2816]{1,0:T(8,128)(2,1)S(1)}, bf16[256,2816]{1,0:T(8,128)(2,1)}, u32[]{:S(2)}) copy-start(bf16[256,2816]{1,0:T(8,128)(2,1)} %get-tuple-element.590) | copy-start | bytes 4325380
  690.9 363.6 %all-reduce.3.cloned.1.call-start = ((), (), s32[]{:S(2)}) async-start(), calls=%async_computation.14 | async-start | bytes 13893632 | tf_op jit(solution)/shard_map/psum | solution.py:411
  (190 other events, 922.7 us)
Sparse Core Ops, SparseCore 0:
  35.9 25.2 all-gather.16
  118.8 27.0 all-gather.18
  209.0 29.7 all-gather.20
  310.7 31.4 all-gather.22
  423.9 15.8 all-gather.24
  521.9 15.8 all-gather.26
  540.8 31.4 reduce-scatter.6
  575.0 54.8 reduce-scatter.10
  640.7 70.9 reduce-scatter.4
  714.4 92.1 reduce-scatter.8
  809.4 245.0 all-reduce.2
where the time goes:
time: 1090 us; the launch traced here: 1070 us
  waiting for transfers between devices  426 us (39%)
  matrix products  316 us (29%)
  other arithmetic  147 us (13%)
  local copies, waits for them, and re-layouts  139 us (13%)
  between operations  16.6 us (2%)
  blocking collectives  14.3 us (1%)
  starting transfers between devices  14.1 us (1%)
    psum x1, waiting for transfers between devices, per_device(): lax.psum(shares[0].astype(jnp.bfloat16), 'dp').astype(jnp.float32)  230 us
    reduce_scatter x1, waiting for transfers between devices, per_device(): lax.psum_scatter(summands[2].astype(jnp.bfloat16), 'seq', scatter_dimensi...  94.8 us
    another operation x27, other arithmetic, per_device(): stacked = jax.tree.map(lambda *members: jnp.stack(members), *records)  52.6 us
    dot_general x3, matrix products, layer_backward(): jnp.einsum('td,tf->df', record['second'].astype(jnp.bfloat16), grad_gate_...  49 us
    dot_general x3, matrix products, layer_backward(): jnp.einsum('td,tf->df', record['normed'].astype(jnp.bfloat16), grad_proje...  38.4 us
    ppermute x4, waiting for transfers between devices, from_behind(): return lax.ppermute(block, axis, route)  34.7 us
    all_gather x3, waiting for transfers between devices, entering_2(): lax.all_gather(a.astype(kind), axis)  30 us
    unnamed x422, local copies, waits for them, and re-layouts  28.6 us
  transfers between devices with their start and end apart: 15, of which 10 were waited for; matrix products, arithmetic and copies ran while one was open for 25% of the time, Pallas kernels for 0%

commit v1 on v0

v1 whole, which is shorter than its diff:
```python
import functools
import math

import jax
import jax.numpy as jnp
from jax import lax
from jax.experimental import pallas as pl
from jax.experimental.pallas import tpu as pltpu
from jax.sharding import PartitionSpec as P

HEADS = 8
BLK = 256
LANES = 128
VMEM_BYTES = 56 * 1024 * 1024

epsilon = 1e-06
theta_base = 10000.0
f32 = jnp.float32
bf16 = jnp.bfloat16


def nn(a, b):
    return jnp.dot(a, b, preferred_element_type=f32)


def nt(a, b):
    return lax.dot_general(a, b, (((1,), (1,)), ((), ())), preferred_element_type=f32)


def tn(a, b):
    return lax.dot_general(a, b, (((0,), (0,)), ((), ())), preferred_element_type=f32)


def sigmoid(v):
    return 1.0 / (1.0 + jnp.exp(-v))


def norm_factor(v, width):
    return lax.rsqrt(jnp.sum(v * v, axis=-1, keepdims=True) * (1.0 / width) + epsilon)


def norm_back(cotangent, normed, factor, width):
    mean = jnp.sum(cotangent * normed, axis=-1, keepdims=True) * (1.0 / width)
    return factor * (cotangent - normed * mean)


def row_index(rows, columns):
    return lax.broadcasted_iota(jnp.int32, (rows, columns), 0).astype(f32)


def decay_mask(slope, rows):
    row = lax.broadcasted_iota(jnp.int32, (rows, rows), 0)
    column = lax.broadcasted_iota(jnp.int32, (rows, rows), 1)
    distance = jnp.maximum(row - column, 0).astype(f32)
    return jnp.where(row >= column, jnp.exp(distance * (-slope)), 0.0)


def head(number):
    return slice(number * LANES, (number + 1) * LANES)


def half_turn(v):
    return pltpu.roll(v, LANES // 2, 1)


def whole(shape):
    return pl.BlockSpec(shape, lambda j: (0,) * len(shape))


def params():
    return pltpu.CompilerParams(vmem_limit_bytes=VMEM_BYTES)


SMEM = pl.BlockSpec(memory_space=pltpu.SMEM)
ANY = pl.BlockSpec(memory_space=pl.ANY)


def project_body(slope, x, cosine, sine, w, h1, r1, pre, qk, state, keys, steps):
    j = pl.program_id(0)
    rows, width = x.shape
    columns = w.shape[1]
    heads = columns // LANES
    quarter = steps // 4

    @pl.when(j == 0)
    def _():
        v = x[...].astype(f32)
        factor = norm_factor(v, width)
        h1[...] = (v * factor).astype(bf16)
        r1[...] = jnp.broadcast_to(factor, r1.shape)

    p = nn(h1[...], w[...])
    pre[...] = p.astype(bf16)

    @pl.when(j < 2 * quarter)
    def _():
        for n in range(heads):
            v = p[:, head(n)]
            v = v * sigmoid(v)
            qk[:, head(n)] = (v * cosine[...] + half_turn(v) * sine[...]).astype(bf16)

    for part in range(quarter):

        @pl.when(j == quarter + part)
        def _():
            keys[:, part * columns : (part + 1) * columns] = qk[...]

        @pl.when(j == 2 * quarter + part)
        def _():
            values = p.astype(bf16)
            ahead = rows - row_index(rows, LANES)
            for n in range(heads):
                number = part * heads + n
                decay = jnp.exp(ahead * (-slope[number]))
                keyed = (keys[:, head(number)].astype(f32) * decay).astype(bf16)
                state[number] = tn(keyed, values[:, head(n)]).astype(bf16)


def project(slopes, x, cosine, sine, w):
    rows, width = x.shape
    total = w.shape[1]
    steps = 8
    columns = total // steps
    heads = width // LANES
    body = functools.partial(project_body, steps=steps)
    return pl.pallas_call(
        body,
        grid=(steps,),
        in_specs=[
            SMEM,
            whole((rows, width)),
            whole((rows, LANES)),
            whole((rows, LANES)),
            pl.BlockSpec((width, columns), lambda j: (0, j)),
        ],
        out_specs=[
            whole((rows, width)),
            whole((rows, LANES)),
            pl.BlockSpec((rows, columns), lambda j: (0, j)),
            pl.BlockSpec((rows, columns), lambda j: (0, jnp.minimum(j, steps // 2 - 1))),
            whole((heads, LANES, LANES)),
        ],
        out_shape=[
            jax.ShapeDtypeStruct((rows, width), bf16),
            jax.ShapeDtypeStruct((rows, LANES), f32),
            jax.ShapeDtypeStruct((rows, total), bf16),
            jax.ShapeDtypeStruct((rows, total // 2), bf16),
            jax.ShapeDtypeStruct((heads, LANES, LANES), bf16),
        ],
        scratch_shapes=[pltpu.VMEM((rows, width), bf16)],
        compiler_params=params(),
        cost_estimate=pl.CostEstimate(
            flops=2 * rows * width * total, bytes_accessed=2 * width * total, transcendentals=0
        ),
        name="project",
    )(slopes, x, cosine, sine, w)


def finish_body(
    slope, far, near, x, q, k, v, u, far_state, near_state, wo, wg, wu, wd,
    mixed, gated, ra, h2, r2, low, g, up, product, y, attended, total, steps,
):
    j = pl.program_id(0)
    rows, width = x.shape

    @pl.when(j == 0)
    def _():
        ahead = row_index(rows, LANES)
        for n in range(HEADS):
            state = far[n] * far_state[n].astype(f32) + near[n] * near_state[n].astype(f32)
            low[n] = state.astype(bf16)
            query = q[:, head(n)]
            weights = (decay_mask(slope[n], rows) * nt(query, k[:, head(n)])).astype(bf16)
            inner = nn(weights, v[:, head(n)])
            carried = nn(query, low[n])
            attended[:, head(n)] = inner + jnp.exp(ahead * (-slope[n])) * carried
        rows_out = attended[...]
        factor = norm_factor(rows_out, width)
        ra[...] = jnp.broadcast_to(factor, ra.shape)
        normed = rows_out * factor
        mixed[...] = normed.astype(bf16)
        gated[...] = (normed * u[...].astype(f32)).astype(bf16)
        middle = x[...].astype(f32) + nn(gated[...], wo[...])
        total[...] = middle
        factor = norm_factor(middle, width)
        r2[...] = jnp.broadcast_to(factor, r2.shape)
        h2[...] = (middle * factor).astype(bf16)

    gate = nn(h2[...], wg[...])
    rise = nn(h2[...], wu[...])
    g[...] = gate.astype(bf16)
    up[...] = rise.astype(bf16)
    product[...] = (gate * rise).astype(bf16)
    total[...] += nn(product[...], wd[...])

    @pl.when(j == steps - 1)
    def _():
        y[...] = total[...].astype(bf16)


def finish(slopes, far, near, x, qk, pre, far_state, near_state, wo, wi, wd):
    rows, width = x.shape
    hidden = wd.shape[0]
    columns = 256
    steps = hidden // columns
    states = (HEADS, LANES, LANES)
    wide = whole((rows, width))
    thin = whole((rows, LANES))
    side = lambda number: pl.BlockSpec((rows, width), lambda j: (0, number))
    column = pl.BlockSpec((rows, columns), lambda j: (0, j))
    body = functools.partial(finish_body, steps=steps)
    act = jax.ShapeDtypeStruct((rows, width), bf16)
    factor = jax.ShapeDtypeStruct((rows, LANES), f32)
    unit = jax.ShapeDtypeStruct((rows, hidden), bf16)
    return pl.pallas_call(
        body,
        grid=(steps,),
        in_specs=[
            SMEM, SMEM, SMEM, wide, side(0), side(1), side(2), side(3),
            whole(states), whole(states), whole((width, width)),
            pl.BlockSpec((width, columns), lambda j: (0, j)),
            pl.BlockSpec((width, columns), lambda j: (0, j + steps)),
            pl.BlockSpec((columns, width), lambda j: (j, 0)),
        ],
        out_specs=[wide, wide, thin, wide, thin, whole(states), column, column, column, wide],
        out_shape=[
            act, act, factor, act, factor,
            jax.ShapeDtypeStruct(states, bf16), unit, unit, unit, act,
        ],
        scratch_shapes=[pltpu.VMEM((rows, width), f32), pltpu.VMEM((rows, width), f32)],
        compiler_params=params(),
        cost_estimate=pl.CostEstimate(
            flops=2 * rows * width * (width + 3 * hidden),
            bytes_accessed=2 * width * (width + 3 * hidden),
            transcendentals=0,
        ),
        name="finish",
    )(slopes, far, near, x, qk, qk, pre, pre, far_state, near_state, wo, wi, wi, wd)


def back_channel_body(
    slope, dy, wd, wg, wu, g, up, h2, r2, wo, mixed, ra, u, q, k, v, low, qp, cosine, sine,
    dg, dup, dmid, dm, dq, du, dk, dv, state, total, datt, steps,
):
    j = pl.program_id(0)
    rows, width = dy.shape
    product = nt(dy[...], wd[...])
    dg[...] = (product * up[...].astype(f32)).astype(bf16)
    dup[...] = (product * g[...].astype(f32)).astype(bf16)
    step = nt(dg[...], wg[...]) + nt(dup[...], wu[...])

    @pl.when(j == 0)
    def _():
        total[...] = step

    @pl.when(j > 0)
    def _():
        total[...] += step

    @pl.when(j == steps - 1)
    def _():
        middle = dy[...].astype(f32) + norm_back(
            total[...], h2[...].astype(f32), r2[:, 0:1], width
        )
        dmid[...] = middle
        dm[...] = middle.astype(bf16)
        dgated = nt(dm[...], wo[...])
        normed = mixed[...].astype(f32)
        du[...] = (dgated * normed).astype(bf16)
        datt[...] = norm_back(dgated * u[...].astype(f32), normed, ra[:, 0:1], width).astype(bf16)
        ahead = row_index(rows, LANES)
        for n in range(HEADS):
            query, key, value, cot = q[:, head(n)], k[:, head(n)], v[:, head(n)], datt[:, head(n)]
            mask = decay_mask(slope[n], rows)
            weights = (mask * nt(query, key)).astype(bf16)
            scores = (mask * nt(cot, value)).astype(bf16)
            scaled = (jnp.exp(ahead * (-slope[n])) * cot.astype(f32)).astype(bf16)
            state[n] = tn(query, scaled).astype(bf16)
            dquery = nn(scores, key) + nt(scaled, low[n])
            back = dquery * cosine[...] + half_turn(dquery * sine[...])
            p = qp[:, head(n)].astype(f32)
            s = sigmoid(p)
            dq[:, head(n)] = (back * (s * (1.0 + p * (1.0 - s)))).astype(bf16)
            dk[:, head(n)] = tn(scores, query)
            dv[:, head(n)] = tn(weights, cot)


def back_channel(slopes, dy, r, cosine, sine, wo, wi, wd):
    rows, width = dy.shape
    hidden = wd.shape[0]
    columns = 256
    steps = hidden // columns
    states = (HEADS, LANES, LANES)
    wide = whole((rows, width))
    thin = whole((rows, LANES))
    side = lambda number: pl.BlockSpec((rows, width), lambda j: (0, number))
    column = pl.BlockSpec((rows, columns), lambda j: (0, j))
    act = jax.ShapeDtypeStruct((rows, width), bf16)
    full = jax.ShapeDtypeStruct((rows, width), f32)
    unit = jax.ShapeDtypeStruct((rows, hidden), bf16)
    return pl.pallas_call(
        functools.partial(back_channel_body, steps=steps),
        grid=(steps,),
        in_specs=[
            SMEM, wide,
            pl.BlockSpec((columns, width), lambda j: (j, 0)),
            pl.BlockSpec((width, columns), lambda j: (0, j)),
            pl.BlockSpec((width, columns), lambda j: (0, j + steps)),
            column, column, wide, thin, whole((width, width)), wide, thin,
            side(3), side(0), side(1), side(2), whole(states), side(0), thin, thin,
        ],
        out_specs=[column, column, wide, wide, wide, wide, wide, wide, whole(states)],
        out_shape=[unit, unit, full, act, act, act, full, full, jax.ShapeDtypeStruct(states, bf16)],
        scratch_shapes=[pltpu.VMEM((rows, width), f32), pltpu.VMEM((rows, width), bf16)],
        compiler_params=params(),
        cost_estimate=pl.CostEstimate(
            flops=2 * rows * width * (width + 3 * hidden),
            bytes_accessed=2 * width * (width + 3 * hidden),
            transcendentals=0,
        ),
        name="back_channel",
    )(
        slopes, dy, wd, wi, wi, r["g"], r["up"], r["h2"], r["r2"], wo, r["mixed"], r["ra"],
        r["pre"], r["qk"], r["qk"], r["pre"], r["low"], r["pre"], cosine, sine,
    )


def back_mixer_body(
    slope, far, near, dq, du, dk, dv, k, v, kp, far_state, near_state, cosine, sine, h1, r1, dmid, w,
    dkp, dvp, dx, parts, total, steps,
):
    j = pl.program_id(0)
    rows, width = dq.shape
    columns = w.shape[1]

    @pl.when(j == 0)
    def _():
        ahead = rows - row_index(rows, LANES)
        for n in range(HEADS):
            state = far[n] * far_state[n].astype(f32) + near[n] * near_state[n].astype(f32)
            state = state.astype(bf16)
            decay = jnp.exp(ahead * (-slope[n]))
            keyed = (k[:, head(n)].astype(f32) * decay).astype(bf16)
            dkey = dk[:, head(n)] + decay * nt(v[:, head(n)], state)
            back = dkey * cosine[...] + half_turn(dkey * sine[...])
            p = kp[:, head(n)].astype(f32)
            s = sigmoid(p)
            dkp[:, head(n)] = (back * (s * (1.0 + p * (1.0 - s)))).astype(bf16)
            dvp[:, head(n)] = (dv[:, head(n)] + nn(keyed, state)).astype(bf16)
        for number, part in enumerate((dq, dkp, dvp, du)):
            for piece in range(width // columns):
                parts[number * (width // columns) + piece] = part[
                    :, piece * columns : (piece + 1) * columns
                ]
        total[...] = jnp.zeros_like(total)

    total[...] += nt(parts[j], w[...])

    @pl.when(j == steps - 1)
    def _():
        dx[...] = (
            dmid[...] + norm_back(total[...], h1[...].astype(f32), r1[:, 0:1], width)
        ).astype(bf16)


def back_mixer(slopes, far, near, dq, du, dk, dv, r, far_state, near_state, cosine, sine, dmid, w):
    rows, width = dq.shape
    steps = 8
    columns = w.shape[1] // steps
    states = (HEADS, LANES, LANES)
    wide = whole((rows, width))
    thin = whole((rows, LANES))
    side = lambda number: pl.BlockSpec((rows, width), lambda j: (0, number))
    act = jax.ShapeDtypeStruct((rows, width), bf16)
    return pl.pallas_call(
        functools.partial(back_mixer_body, steps=steps),
        grid=(steps,),
        in_specs=[
            SMEM, SMEM, SMEM, wide, wide, wide, wide, side(1), side(2), side(1),
            whole(states), whole(states), thin, thin, wide, thin, wide,
            pl.BlockSpec((width, columns), lambda j: (0, j)),
        ],
        out_specs=[wide, wide, wide],
        out_shape=[act, act, act],
        scratch_shapes=[pltpu.VMEM((steps, rows, columns), bf16), pltpu.VMEM((rows, width), f32)],
        compiler_params=params(),
        cost_estimate=pl.CostEstimate(
            flops=2 * rows * width * w.shape[1],
            bytes_accessed=2 * width * w.shape[1],
            transcendentals=0,
        ),
        name="back_mixer",
    )(
        slopes, far, near, dq, du, dk, dv, r["qk"], r["pre"], r["pre"], far_state, near_state,
        cosine, sine, r["h1"], r["r1"], dmid, w,
    )


def weight_body(*refs, batch, sides, groups, wide):
    place = refs[0]
    lefts = refs[1 : 1 + 2 * batch]
    rights = refs[1 + 2 * batch : 1 + 2 * batch + 2 * batch * sides]
    outs = refs[1 + 2 * batch + 2 * batch * sides : -7]
    x, xt, ys, stage, xsem, ysem, osem = refs[-7:]
    rows = lefts[0].shape[0]
    columns = x.shape[1]
    quarter = columns // 4
    span = ys.shape[2]

    def copies(section):
        found = []
        for b in range(batch):
            found.append(
                pltpu.make_async_copy(
                    lefts[section * batch + b], x.at[pl.ds(b * rows, rows)], xsem.at[b]
                )
            )
        for s in range(sides):
            for b in range(batch):
                source = rights[(section * sides + s) * batch + b]
                found.append(
                    pltpu.make_async_copy(source, ys.at[s, pl.ds(b * rows, rows)], ysem.at[s, b])
                )
        return found

    for section in range(2):

        @pl.when(place[4] == section)
        def _():
            for copy in copies(section):
                copy.start()

    first = copies(0)
    for copy in first[:batch]:
        copy.wait()
    for piece in range(columns // LANES):
        xt[piece * LANES : (piece + 1) * LANES, :] = x[:, piece * LANES : (piece + 1) * LANES].T

    pending = []
    for number, (out, (s, start, blocks)) in enumerate(zip(outs, groups)):
        if all(s != done for done, _, _ in groups[:number]):
            for copy in first[batch + s * batch : batch + (s + 1) * batch]:
                copy.wait()
        for role in range(4):
            left = xt[pl.ds(pl.multiple_of(place[role] * quarter, 16), quarter), :]
            slot = number * 4 + role
            for block in range(0, blocks, wide):
                size = min(wide, blocks - block)
                at = (start + block) * LANES
                tile = nn(left, ys[s, :, at : at + size * LANES]).astype(bf16)
                for n in range(size):
                    stage[slot, block + n] = tile[:, head(n)]
            copy = pltpu.make_async_copy(
                stage.at[slot, pl.ds(0, blocks)], out.at[pl.ds(role * blocks, blocks)], osem.at[slot]
            )
            copy.start()
            pending.append(copy)
    for copy in pending:
        copy.wait()


def weight_gradient(place, lefts, rights, groups):
    batch = len(lefts[0])
    sides = len(rights[0])
    rows, columns = lefts[0][0].shape
    span = rights[0][0][0].shape[1]
    quarter = columns // 4
    most = max(blocks for _, _, blocks in groups)
    flat_left = [a for section in lefts for a in section]
    flat_right = [a for section in rights for side in section for a in side]
    return pl.pallas_call(
        functools.partial(weight_body, batch=batch, sides=sides, groups=groups, wide=4),
        in_specs=[SMEM] + [ANY] * (len(flat_left) + len(flat_right)),
        out_specs=[ANY] * len(groups),
        out_shape=[
            jax.ShapeDtypeStruct((4 * blocks, quarter, LANES), bf16) for _, _, blocks in groups
        ],
        scratch_shapes=[
            pltpu.VMEM((batch * rows, columns), bf16),
            pltpu.VMEM((columns, batch * rows), bf16),
            pltpu.VMEM((sides, batch * rows, span), bf16),
            pltpu.VMEM((4 * len(groups), most, quarter, LANES), bf16),
            pltpu.SemaphoreType.DMA((batch,)),
            pltpu.SemaphoreType.DMA((sides, batch)),
            pltpu.SemaphoreType.DMA((4 * len(groups),)),
        ],
        compiler_params=params(),
        cost_estimate=pl.CostEstimate(
            flops=2 * batch * rows * columns * sides * span,
            bytes_accessed=2 * columns * sides * span,
            transcendentals=0,
        ),
        name="weight_gradient",
    )(place, *flat_left, *flat_right)


def settle_body(edge, outer, inner, *rest):
    out = rest[-1]

    @pl.when(edge[0] == 1)
    def _():
        for n in range(outer.shape[0]):
            out[:, head(n)] = outer[n].astype(f32)

    @pl.when(edge[0] == 0)
    def _():
        for n in range(inner.shape[0]):
            out[:, head(n)] = inner[n].astype(f32)


def settle(edge, outer, inner, total, held, number):
    blocks, quarter, _ = outer.shape
    more = [] if held is None else [held]
    return pl.pallas_call(
        settle_body,
        grid=(1,),
        in_specs=[SMEM, whole(outer.shape), whole(inner.shape)] + [ANY] * len(more),
        out_specs=pl.BlockSpec((quarter, blocks * LANES), lambda j: (0, number)),
        out_shape=jax.ShapeDtypeStruct((quarter, total), f32),
        input_output_aliases={3: 0} if more else {},
        compiler_params=params(),
        name="settle",
    )(edge, outer, inner, *more)


def add(a, b):
    return (a.astype(f32) + b.astype(f32)).astype(bf16)


def mixed_states(own, slopes, forward):
    count = lax.axis_size("seq")
    place = lax.axis_index("seq")
    decay = jnp.exp(-slopes * BLK)
    if count != 4:
        gathered = lax.all_gather(own, "seq")
        distance = place - 1 - jnp.arange(count) if forward else jnp.arange(count) - place - 1
        factors = jnp.where(
            distance[:, None] >= 0,
            jnp.exp(-slopes[None, :] * (BLK * jnp.maximum(distance, 0)[:, None]).astype(f32)),
            0.0,
        )
        state = jnp.sum(factors[:, :, None, None] * gathered.astype(f32), axis=0).astype(bf16)
        return state, state, jnp.ones_like(slopes), jnp.zeros_like(slopes)
    late = (place % 2 == 1) if forward else (place % 2 == 0)
    near_state = lax.ppermute(own, "seq", [(0, 1), (1, 0), (2, 3), (3, 2)])
    here, there = own.astype(f32), near_state.astype(f32)
    factor = decay[:, None, None]
    joined = jnp.where(late, factor * there + here, factor * here + there).astype(bf16)
    route = [(0, 2), (1, 3)] if forward else [(2, 0), (3, 1)]
    far_state = lax.ppermute(joined, "seq", route)
    far = jnp.where(late, decay, jnp.ones_like(decay))
    near = jnp.where(late, jnp.ones_like(decay), jnp.zeros_like(decay))
    return far_state, near_state, far, near


def sum_quarters(chunks):
    sums = []
    previous = None
    for chunk in chunks:
        blocks = chunk.shape[0] // 4
        given, kept = chunk[: 2 * blocks], chunk[2 * blocks :]
        taken = lax.ppermute(given, "seq", [(0, 1), (1, 0), (2, 3), (3, 2)])
        far = add(kept[:blocks], taken[:blocks])
        own = add(kept[blocks:], taken[blocks:])
        if previous is not None:
            far, _ = lax.optimization_barrier((far, previous))
        previous = lax.ppermute(far, "seq", [(0, 2), (2, 0), (1, 3), (3, 1)])
        sums.append(add(own, previous))
    return sums


def sum_line(parts):
    place = lax.axis_index("dp")
    edge = (place == 0) | (place == 3)
    count = len(parts)
    partial = [None] * count
    across = [None] * count
    out = []
    for step in range(count + 2):
        part = parts[step] if step < count else None
        done = None
        if step >= 2:
            done = partial[step - 2].astype(f32) + across[step - 2].astype(f32)
        if 1 <= step <= count:
            across[step - 1] = lax.ppermute(partial[step - 1], "dp", [(1, 2), (2, 1)])
        if part is not None and done is not None and part.shape == done.shape:
            sent = jnp.where(edge, part.astype(f32), done).astype(bf16)
            got = lax.ppermute(sent, "dp", [(0, 1), (1, 0), (2, 3), (3, 2)])
            out.append((got, sent))
            partial[step] = add(part, got)
            continue
        if part is not None:
            partial[step] = add(part, lax.ppermute(part, "dp", [(0, 1), (3, 2)]))
        if done is not None:
            done = done.astype(bf16)
            out.append((lax.ppermute(done, "dp", [(1, 0), (2, 3)]), done))
    return out


def sum_any(chunk, place):
    part = lax.psum_scatter(chunk, "seq", scatter_dimension=0, tiled=True)
    part = lax.psum(part, "dp")
    return part


def angle_tables(position_row, half_size):
    frequency = jnp.exp(
        jnp.arange(half_size, dtype=jnp.float32) * (-math.log(theta_base) / half_size)
    )
    angles = position_row.astype(jnp.float32)[..., None] * frequency
    cosine = jnp.cos(angles)
    sine_rows = jnp.sin(angles)
    return (
        jnp.concatenate([cosine, cosine], axis=-1),
        jnp.concatenate([-sine_rows, sine_rows], axis=-1),
    )


def first_half(x, slopes, cosine, sine, w):
    h1, r1, pre, qk, state = project(slopes, x, cosine, sine, w)
    return dict(x=x, h1=h1, r1=r1, pre=pre, qk=qk), mixed_states(state, slopes, True)


def second_half(record, states, slopes, wo, wi, wd):
    far_state, near_state, far, near = states
    mixed, gated, ra, h2, r2, low, g, up, product, y = finish(
        slopes, far, near, record["x"], record["qk"], record["pre"], far_state, near_state,
        wo, wi, wd,
    )
    record.update(
        mixed=mixed, gated=gated, ra=ra, h2=h2, r2=r2, low=low, g=g, up=up, product=product
    )
    return y


def back_first(dy, record, slopes, cosine, sine, wo, wi, wd):
    dg, dup, dmid, dm, dq, du, dk, dv, state = back_channel(
        slopes, dy, record, cosine, sine, wo, wi, wd
    )
    record.update(dy=dy, dg=dg, dup=dup, dmid=dmid, dm=dm, dq=dq, du=du, dk=dk, dv=dv)
    return mixed_states(state, slopes, False)


def back_second(record, states, slopes, cosine, sine, w):
    far_state, near_state, far, near = states
    dkp, dvp, dx = back_mixer(
        slopes, far, near, record["dq"], record["du"], record["dk"], record["dv"], record,
        far_state, near_state, cosine, sine, record["dmid"], w,
    )
    record.update(dkp=dkp, dvp=dvp)
    return dx


def per_device(boundary, positions, decay_exp, mixer_in, mixer_out, channel_in, channel_out):
    section = lax.axis_index("section")
    is_first = section == 0
    own = boundary[0]
    batch, rows, width = own.shape
    assert rows == BLK
    slopes = jnp.exp2(-0.5 * decay_exp[0].astype(jnp.float32))
    w, wo, wi, wd = mixer_in[0], mixer_out[0], channel_in[0], channel_out[0]
    hidden = wd.shape[0]
    half_size = width // HEADS // 2
    cosine, sine = angle_tables(positions, half_size)
    every = range(batch)

    early, states = [None] * batch, [None] * batch
    for b in every:
        early[b], states[b] = first_half(own[b], slopes, cosine[b], sine[b], w)
    arrived = []
    for b in every:
        y = second_half(early[b], states[b], slopes, wo, wi, wd)
        arrived.append(lax.ppermute(y, "section", [(0, 1)]))
    late = [None] * batch
    for b in every:
        late[b], states[b] = first_half(arrived[b], slopes, cosine[b], sine[b], w)
    outputs, later = [None] * batch, [None] * batch
    for b in every:
        outputs[b] = second_half(late[b], states[b], slopes, wo, wi, wd)
        later[b] = back_first(own[b], late[b], slopes, cosine[b], sine[b], wo, wi, wd)
    returned = []
    for b in every:
        dx = back_second(late[b], later[b], slopes, cosine[b], sine[b], w)
        returned.append(lax.ppermute(dx, "section", [(1, 0)]))
    for b in every:
        later[b] = back_first(returned[b], early[b], slopes, cosine[b], sine[b], wo, wi, wd)

    place = lax.axis_index("seq")
    core, y_place = place % 2, place // 2
    roles = [
        2 * (1 - y_place) + 1 - core,
        2 * y_place + 1 - core,
        2 * (1 - y_place) + core,
        2 * y_place + core,
        section,
    ]
    usual = lax.axis_size("seq") == 4 and lax.axis_size("dp") == 4
    if not usual:
        roles = [0, 1, 2, 3, section]
    roles = jnp.stack([jnp.asarray(r, jnp.int32) for r in roles])

    def operands(*names):
        return [[[r[name] for r in records] for name in names] for records in (early, late)]

    def left(name):
        return [side[0] for side in operands(name)]

    def gradient(name, names, groups):
        return weight_gradient(roles, left(name), operands(*names), groups)

    chunks = []
    chunks += gradient("product", ("dy",), [(0, 0, 4), (0, 4, 4)])
    half = hidden // LANES // 2
    chunks += gradient(
        "h2", ("dg", "dup"), [(0, 0, half), (0, half, half), (1, 0, half), (1, half, half)]
    )
    dx = [back_second(early[b], later[b], slopes, cosine[b], sine[b], w) for b in every]
    eight = width // LANES
    chunks += gradient("gated", ("dm",), [(0, 0, eight)])
    chunks += gradient(
        "h1", ("dq", "dkp", "dvp", "du"), [(s, 0, eight) for s in range(4)]
    )
    joined = jnp.where(is_first, jnp.stack(dx), jnp.stack(outputs))[None]

    spans = [(3, width), (3, width)] + [(2, 2 * hidden)] * 4 + [(1, width)] + [(0, 4 * width)] * 4
    order = [0, 1, 0, 1, 2, 3, 0, 0, 1, 2, 3]
    edge = (lax.axis_index("dp") == 0) | (lax.axis_index("dp") == 3)
    if usual:
        shaped = [c.reshape(c.shape[0] * c.shape[1] // 256, 256, LANES) for c in chunks]
        pairs = sum_line(sum_quarters(shaped))
        flag = edge.astype(jnp.int32)[None]
        held = [None] * 4
        for (index, total), number, (outer, inner), chunk in zip(spans, order, pairs, chunks):
            shape = (chunk.shape[0] // 4,) + chunk.shape[1:]
            held[index] = settle(
                flag, outer.reshape(shape), inner.reshape(shape), total, held[index], number
            )
        return (joined, *(h[None] for h in held))
    found = [[], [], [], []]
    for (index, total), chunk in zip(spans, chunks):
        blocks, quarter = chunk.shape[0] // 4, chunk.shape[1]
        rows_first = chunk.reshape(4, blocks, quarter, LANES).transpose(0, 2, 1, 3)
        found[index].append(rows_first.reshape(4 * quarter, blocks * LANES))
    summed = []
    for pieces in found:
        part = lax.psum_scatter(
            jnp.concatenate(pieces, axis=1), "seq", scatter_dimension=0, tiled=True
        )
        summed.append(lax.psum(part, "dp").astype(f32)[None])
    return (joined, *summed)


def solution(mesh):
    in_specs = (
        P("section", "dp", "seq", None),
        P("dp", "seq"),
        P("section", None),
        P("section", None, None),
        P("section", None, None),
        P("section", None, None),
        P("section", None, None),
    )
    out_specs = (
        P("section", "dp", "seq", None),
        P("section", "seq", None),
        P("section", "seq", None),
        P("section", "seq", None),
        P("section", "seq", None),
    )
    return jax.shard_map(
        per_device, mesh=mesh, in_specs=in_specs, out_specs=out_specs, check_vma=False
    )
```

time: 1090 us -> 688 us (0.63)
  Pallas kernels: 0 us -> 327 us
  matrix products: 316 us -> 0 us
  waiting for transfers between devices: 426 us -> 142 us
  starting transfers between devices: 14.1 us -> 129 us
  other arithmetic: 147 us -> 40 us
  local copies, waits for them, and re-layouts: 139 us -> 34.1 us
  between operations: 16.6 us -> 2.11 us
  blocking collectives: 14.3 us -> 0 us
    pallas_call x0 -> x31, Pallas kernels: none -> 327 us  [the longest x4 98 us: back_channel(): pl.pallas_call(functools.partial(back_channel_body, steps=steps), grid=(s...]
    dot_general x69 -> x0, matrix products: 316 us -> none  [the longest x3 49 us: layer_backward(): jnp.einsum('td,tf->df', record['second'].astype(jnp.bfloat16), grad_gate_...]
    psum x1 -> x0, waiting for transfers between devices: 230 us -> none  [per_device(): lax.psum(shares[0].astype(jnp.bfloat16), 'dp').astype(jnp.float32)]
    ppermute x4 -> x68, starting transfers between devices: 13 us -> 129 us  [the longest x7 53.6 us: sum_line(): got = lax.ppermute(sent, 'dp', [(0, 1), (1, 0), (2, 3), (3, 2)])]
    reduce_scatter x4 -> x0, waiting for transfers between devices: 116 us -> none  [the longest x1 94.8 us: per_device(): lax.psum_scatter(summands[2].astype(jnp.bfloat16), 'seq', scatter_dimensi...]
    ppermute x4 -> x68, waiting for transfers between devices: 34.7 us -> 142 us  [the longest x4 40.9 us: sum_line(): partial[step] = add(part, lax.ppermute(part, 'dp', [(0, 1), (3, 2)]))]
    another operation x31 -> x0, other arithmetic: 64.9 us -> none  [the longest x27 52.6 us: per_device(): stacked = jax.tree.map(lambda *members: jnp.stack(members), *records)]
    all_gather x6 -> x0, waiting for transfers between devices: 45.3 us -> none  [the longest x3 30 us: entering_2(): lax.all_gather(a.astype(kind), axis)]
  transfers between devices with their start and end apart: 15 -> 68, of which waited for: 10 -> 23; matrix products, arithmetic and copies ran while one was open for 25% -> 8% of each run, Pallas kernels for 0% -> 44%
where the time goes in v1:
time: 688 us; the launch traced here: 675 us
  Pallas kernels  327 us (48%)
  waiting for transfers between devices  142 us (21%)
  starting transfers between devices  129 us (19%)
  other arithmetic  40 us (6%)
  local copies, waits for them, and re-layouts  34.1 us (5%)
    pallas_call x4, Pallas kernels, back_channel(): pl.pallas_call(functools.partial(back_channel_body, steps=steps), grid=(s...  98 us
    pallas_call x4, Pallas kernels, finish(): pl.pallas_call(body, grid=(steps,), in_specs=[SMEM, SMEM, SMEM, wide, sid...  75.4 us
    ppermute x7, starting transfers between devices, sum_line(): got = lax.ppermute(sent, 'dp', [(0, 1), (1, 0), (2, 3), (3, 2)])  53.6 us
    pallas_call x4, Pallas kernels, back_mixer(): pl.pallas_call(functools.partial(back_mixer_body, steps=steps), grid=(ste...  51.4 us
    pallas_call x4, Pallas kernels, project(): pl.pallas_call(body, grid=(steps,), in_specs=[SMEM, whole((rows, width)),...  42.1 us
    ppermute x4, waiting for transfers between devices, sum_line(): partial[step] = add(part, lax.ppermute(part, 'dp', [(0, 1), (3, 2)]))  40.9 us
    pallas_call x4, Pallas kernels, weight_gradient(): pl.pallas_call(functools.partial(weight_body, batch=batch, sides=sides, g...  33.6 us
    ppermute x7, waiting for transfers between devices, sum_line(): got = lax.ppermute(sent, 'dp', [(0, 1), (1, 0), (2, 3), (3, 2)])  29.4 us
  transfers between devices with their start and end apart: 68, of which 23 were waited for; matrix products, arithmetic and copies ran while one was open for 8% of the time, Pallas kernels for 44%

profile of v1, /device:TPU:0, one launch (start us, length us, event | category | flops | bytes accessed | tf_op | source)
XLA Modules:
  0.0 674.7 jit_solution(4067951670673847068)
XLA Ops:
  6.9 10.5 %project.4 = (bf16[256,1024]{1,0:T(8,128)(2,1)}, f32[256,128]{1,0:T(8,128)}, bf16[256,4096]{1,0:T(8,128)(2,1)}, bf16[256,2048]{1,0:T(8,128)(2,1)}, bf16[8,128,128]{2,1,0:T(8,128)(2,1)}) custom-call(f32[8]{0:T(128)} %exponential_bitcast_fusion.slope, bf16[256,1024]{1,0:T(8,128)(2,1)} %get-tuple-element.267.x.dy.refs_7_, ...), custom_call_target="tpu_custom_call" | custom-call | flops 2147483648 | bytes 8388608 | tf_op jit(solution)/shard_map/project/pallas_call | solution.py:126
  32.0 18.8 %finish.4 = (bf16[256,1024]{1,0:T(8,128)(2,1)}, bf16[256,1024]{1,0:T(8,128)(2,1)}, f32[256,128]{1,0:T(8,128)}, bf16[256,1024]{1,0:T(8,128)(2,1)}, f32[256,128]{1...) custom-call(f32[8]{0:T(128)} %exponential_bitcast_fusion.slope, ...), custom_call_target="tpu_custom_call" | custom-call | flops 4966055936 | bytes 19398656 | tf_op jit(solution)/shard_map/finish/pallas_call | solution.py:215
  54.2 10.5 %project.6 = (bf16[256,1024]{1,0:T(8,128)(2,1)}, f32[256,128]{1,0:T(8,128)}, bf16[256,4096]{1,0:T(8,128)(2,1)}, bf16[256,2048]{1,0:T(8,128)(2,1)}, bf16[8,128,128]{2,1,0:T(8,128)(2,1)}) custom-call(f32[8]{0:T(128)} %exponential_bitcast_fusion.slope, bf16[256,1024]{1,0:T(8,128)(2,1)} %get-tuple-element.268.x.dy.refs_8_, ...), custom_call_target="tpu_custom_call" | custom-call | flops 2147483648 | bytes 8388608 | tf_op jit(solution)/shard_map/project/pallas_call | solution.py:126
  65.9 10.5 %project.5 = (bf16[256,1024]{1,0:T(8,128)(2,1)}, f32[256,128]{1,0:T(8,128)}, bf16[256,4096]{1,0:T(8,128)(2,1)}, bf16[256,2048]{1,0:T(8,128)(2,1)}, bf16[8,128,128]{2,1,0:T(8,128)(2,1)}) custom-call(f32[8]{0:T(128)} %exponential_bitcast_fusion.slope, bf16[256,1024]{1,0:T(8,128)(2,1)} %copy-done.24, f32[256,128]{1,0:T(8,128)} %get-tuple-element.283.cosine, ...), custom_call_target="tpu_custom_call" | custom-call | flops 2147483648 | bytes 8388608 | tf_op jit(solution)/shard_map/project/pallas_call | solution.py:126
  91.5 18.9 %finish.6 = (bf16[256,1024]{1,0:T(8,128)(2,1)}, bf16[256,1024]{1,0:T(8,128)(2,1)}, f32[256,128]{1,0:T(8,128)}, bf16[256,1024]{1,0:T(8,128)(2,1)}, f32[256,128]{1...) custom-call(f32[8]{0:T(128)} %exponential_bitcast_fusion.slope, ...), custom_call_target="tpu_custom_call" | custom-call | flops 4966055936 | bytes 19398656 | tf_op jit(solution)/shard_map/finish/pallas_call | solution.py:215
  115.6 18.8 %finish.5 = (bf16[256,1024]{1,0:T(8,128)(2,1)}, bf16[256,1024]{1,0:T(8,128)(2,1)}, f32[256,128]{1,0:T(8,128)}, bf16[256,1024]{1,0:T(8,128)(2,1)}, f32[256,128]{1...) custom-call(f32[8]{0:T(128)} %exponential_bitcast_fusion.slope, ...), custom_call_target="tpu_custom_call" | custom-call | flops 4966055936 | bytes 19398656 | tf_op jit(solution)/shard_map/finish/pallas_call | solution.py:215
  134.4 24.5 %back_channel.4 = (bf16[256,2816]{1,0:T(8,128)(2,1)}, bf16[256,2816]{1,0:T(8,128)(2,1)}, f32[256,1024]{1,0:T(8,128)}, bf16[256,1024]{1,0:T(8,128)(2,1)}, bf16[25...) custom-call(f32[8]{0:T(128)} %exponential_bitcast_fusion.slope, ...), custom_call_target="tpu_custom_call" | custom-call | flops 4966055936 | bytes 19398656 | tf_op jit(solution)/shard_map/back_channel/pallas_call | solution.py:301
  159.8 10.5 %project.7 = (bf16[256,1024]{1,0:T(8,128)(2,1)}, f32[256,128]{1,0:T(8,128)}, bf16[256,4096]{1,0:T(8,128)(2,1)}, bf16[256,2048]{1,0:T(8,128)(2,1)}, bf16[8,128,128]{2,1,0:T(8,128)(2,1)}) custom-call(f32[8]{0:T(128)} %exponential_bitcast_fusion.slope, bf16[256,1024]{1,0:T(8,128)(2,1)} %copy-done.23, f32[256,128]{1,0:T(8,128)} %get-tuple-element.282.cosine, ...), custom_call_target="tpu_custom_call" | custom-call | flops 2147483648 | bytes 8388608 | tf_op jit(solution)/shard_map/project/pallas_call | solution.py:126
  184.9 18.9 %finish.7 = (bf16[256,1024]{1,0:T(8,128)(2,1)}, bf16[256,1024]{1,0:T(8,128)(2,1)}, f32[256,128]{1,0:T(8,128)}, bf16[256,1024]{1,0:T(8,128)(2,1)}, f32[256,128]{1...) custom-call(f32[8]{0:T(128)} %exponential_bitcast_fusion.slope, ...), custom_call_target="tpu_custom_call" | custom-call | flops 4966055936 | bytes 19398656 | tf_op jit(solution)/shard_map/finish/pallas_call | solution.py:215
  203.8 24.4 %back_channel.6 = (bf16[256,2816]{1,0:T(8,128)(2,1)}, bf16[256,2816]{1,0:T(8,128)(2,1)}, f32[256,1024]{1,0:T(8,128)}, bf16[256,1024]{1,0:T(8,128)(2,1)}, bf16[25...) custom-call(f32[8]{0:T(128)} %exponential_bitcast_fusion.slope, ...), custom_call_target="tpu_custom_call" | custom-call | flops 4966055936 | bytes 19398656 | tf_op jit(solution)/shard_map/back_channel/pallas_call | solution.py:301
  229.6 12.8 %back_mixer.4 = (bf16[256,1024]{1,0:T(8,128)(2,1)}, bf16[256,1024]{1,0:T(8,128)(2,1)}, bf16[256,1024]{1,0:T(8,128)(2,1)}) custom-call(f32[8]{0:T(128)} %exponential_bitcast_fusion.slope, f32[8]{0:T(128)} %broadcast_select_fusion.1.far, f32[8]{0:T(128)} %select_n.169.near, bf16[256,1024]{1,0:T(8,128)(2,1)} %get-tuple-element.147.dq.refs_13_, ...), custom_call_target="tpu_custom_call" | custom-call | flops 2147483648 | bytes 8388608 | tf_op jit(solution)/shard_map/back_mixer/pallas_call | solution.py:375
  245.3 9.4 %collective-permute-done.16.far_state = bf16[8,128,128]{2,1,0:T(8,128)(2,1)S(1)} collective-permute-done((bf16[8,128,128]{2,1,0:T(8,128)(2,1)S(1)}, bf16[8,128,128]{2,1,0:T(8,128)(2,1)S(1)}, u32[]{:S(2)}, u32[]{:S(2)}) %collective-permute-start.16) | collective-permute-done | bytes 262176 | tf_op jit(solution)/shard_map/ppermute | solution.py:550
  255.4 12.7 %back_mixer.6 = (bf16[256,1024]{1,0:T(8,128)(2,1)}, bf16[256,1024]{1,0:T(8,128)(2,1)}, bf16[256,1024]{1,0:T(8,128)(2,1)}) custom-call(f32[8]{0:T(128)} %exponential_bitcast_fusion.slope, f32[8]{0:T(128)} %broadcast_select_fusion.1.far, f32[8]{0:T(128)} %select_n.169.near, bf16[256,1024]{1,0:T(8,128)(2,1)} %get-tuple-element.186.dq.refs_14_, ...), custom_call_target="tpu_custom_call" | custom-call | flops 2147483648 | bytes 8388608 | tf_op jit(solution)/shard_map/back_mixer/pallas_call | solution.py:375
  271.0 24.4 %back_channel.5 = (bf16[256,2816]{1,0:T(8,128)(2,1)}, bf16[256,2816]{1,0:T(8,128)(2,1)}, f32[256,1024]{1,0:T(8,128)}, bf16[256,1024]{1,0:T(8,128)(2,1)}, bf16[25...) custom-call(f32[8]{0:T(128)} %exponential_bitcast_fusion.slope, ...), custom_call_target="tpu_custom_call" | custom-call | flops 4966055936 | bytes 19398656 | tf_op jit(solution)/shard_map/back_channel/pallas_call | solution.py:301
  296.3 7.5 %weight_gradient.7 = (bf16[16,704,128]{2,1,0:T(8,128)(2,1)}, bf16[16,704,128]{2,1,0:T(8,128)(2,1)}) custom-call(s32[5]{0:T(128)} %stack.47.refs_0_, bf16[256,2816]{1,0:T(8,128)(2,1)} %get-tuple-element.245.refs_1_, bf16[256,2816]{1,0:T(8,128)(2,1)} %get-tuple-element.246.refs_2_, bf16[256,2816]{1,0:T(8,128)(2,1)} %get-tuple-element.247.refs_3_, ...), custom_call_target="tpu_custom_call" | custom-call | flops 2952790016 | bytes 5767168 | tf_op jit(solution)/shard_map/weight_gradient/pallas_call | solution.py:471
  308.4 24.7 %back_channel.7 = (bf16[256,2816]{1,0:T(8,128)(2,1)}, bf16[256,2816]{1,0:T(8,128)(2,1)}, f32[256,1024]{1,0:T(8,128)}, bf16[256,1024]{1,0:T(8,128)(2,1)}, bf16[25...) custom-call(f32[8]{0:T(128)} %exponential_bitcast_fusion.slope, ...), custom_call_target="tpu_custom_call" | custom-call | flops 4966055936 | bytes 19398656 | tf_op jit(solution)/shard_map/back_channel/pallas_call | solution.py:301
  334.6 11.8 %weight_gradient.6 = (bf16[44,256,128]{2,1,0:T(8,128)(2,1)}, bf16[44,256,128]{2,1,0:T(8,128)(2,1)}, bf16[44,256,128]{2,1,0:T(8,128)(2,1)}, bf16[44,256,128]{2,1,0:T(8,128)(2,1)}) custom-call(s32[5]{0:T(128)} %stack.47.refs_0_, bf16[256,1024]{1,0:T(8,128)(2,1)} %get-tuple-element.158.h2.refs_1_, bf16[256,1024]{1,0:T(8,128)(2,1)} %get-tuple-element.197.h2.refs_2_, ...), custom_call_target="tpu_custom_call" | custom-call | flops 5905580032 | bytes 11534336 | tf_op jit(solution)/shard_map/weight_gradient/pallas_call | solution.py:471
  374.2 13.2 %back_mixer.5 = (bf16[256,1024]{1,0:T(8,128)(2,1)}, bf16[256,1024]{1,0:T(8,128)(2,1)}, bf16[256,1024]{1,0:T(8,128)(2,1)}) custom-call(f32[8]{0:T(128)} %exponential_bitcast_fusion.slope, f32[8]{0:T(128)} %broadcast_select_fusion.1.far, f32[8]{0:T(128)} %select_n.169.near, bf16[256,1024]{1,0:T(8,128)(2,1)} %get-tuple-element.163.dq.refs_5_, ...), custom_call_target="tpu_custom_call" | custom-call | flops 2147483648 | bytes 8388608 | tf_op jit(solution)/shard_map/back_mixer/pallas_call | solution.py:375
  387.9 12.7 %back_mixer.7 = (bf16[256,1024]{1,0:T(8,128)(2,1)}, bf16[256,1024]{1,0:T(8,128)(2,1)}, bf16[256,1024]{1,0:T(8,128)(2,1)}) custom-call(f32[8]{0:T(128)} %exponential_bitcast_fusion.slope, f32[8]{0:T(128)} %broadcast_select_fusion.1.far, f32[8]{0:T(128)} %select_n.169.near, bf16[256,1024]{1,0:T(8,128)(2,1)} %get-tuple-element.202.dq.refs_6_, ...), custom_call_target="tpu_custom_call" | custom-call | flops 2147483648 | bytes 8388608 | tf_op jit(solution)/shard_map/back_mixer/pallas_call | solution.py:375
  403.1 9.6 %weight_gradient.4 = (bf16[32,256,128]{2,1,0:T(8,128)(2,1)}, bf16[32,256,128]{2,1,0:T(8,128)(2,1)}, bf16[32,256,128]{2,1,0:T(8,128)(2,1)}, bf16[32,256,128]{2,1,0:T(8,128)(2,1)}) custom-call(s32[5]{0:T(128)} %stack.47.refs_0_, bf16[256,1024]{1,0:T(8,128)(2,1)} %get-tuple-element.168.h1.refs_1_, bf16[256,1024]{1,0:T(8,128)(2,1)} %get-tuple-element.207.h1.refs_2_, ...), custom_call_target="tpu_custom_call" | custom-call | flops 4294967296 | bytes 8388608 | tf_op jit(solution)/shard_map/weight_gradient/pallas_call | solution.py:471
  431.3 8.0 %collective-permute-done.33 = bf16[11,256,128]{2,1,0:T(8,128)(2,1)S(1)} collective-permute-done((bf16[11,256,128]{2,1,0:T(8,128)(2,1)S(1)}, bf16[11,256,128]{2,1,0:T(8,128)(2,1)S(1)}, u32[]{:S(2)}, u32[]{:S(2)}) %collective-permute-start.33) | collective-permute-done | bytes 720928 | tf_op jit(solution)/shard_map/ppermute | solution.py:567
  443.8 13.8 %collective-permute-done.54 = bf16[11,256,128]{2,1,0:T(8,128)(2,1)S(1)} collective-permute-done((bf16[11,256,128]{2,1,0:T(8,128)(2,1)S(1)}, bf16[11,256,128]{2,1,0:T(8,128)(2,1)S(1)}, u32[]{:S(2)}, u32[]{:S(2)}) %collective-permute-start.54) | collective-permute-done | bytes 720928 | tf_op jit(solution)/shard_map/ppermute | solution.py:593
  462.7 14.0 %collective-permute-done.35 = bf16[11,256,128]{2,1,0:T(8,128)(2,1)S(1)} collective-permute-done((bf16[11,256,128]{2,1,0:T(8,128)(2,1)S(1)}, bf16[11,256,128]{2,1,0:T(8,128)(2,1)S(1)}, u32[]{:S(2)}, u32[]{:S(2)}) %collective-permute-start.35) | collective-permute-done | bytes 720928 | tf_op jit(solution)/shard_map/ppermute | solution.py:567
  485.9 11.5 %collective-permute-start.56 = (bf16[11,256,128]{2,1,0:T(8,128)(2,1)S(1)}, bf16[11,256,128]{2,1,0:T(8,128)(2,1)S(1)}, u32[]{:S(2)}, u32[]{:S(2)}) collective-permute-start(bf16[11,256,128]{2,1,0:T(8,128)(2,1)S(1)} %fusion.2), channel_id=1, source_target_pairs={{0,1},{1,0},{2,3},{3,2},{4,5},{5,4},{6,7},{7,6},{8,9},{9,8},{10,11... | collective-permute-start | bytes 2162696 | tf_op jit(solution)/shard_map/ppermute | solution.py:588
  503.1 10.8 %collective-permute-done.56 = bf16[11,256,128]{2,1,0:T(8,128)(2,1)S(1)} collective-permute-done((bf16[11,256,128]{2,1,0:T(8,128)(2,1)S(1)}, bf16[11,256,128]{2,1,0:T(8,128)(2,1)S(1)}, u32[]{:S(2)}, u32[]{:S(2)}) %collective-permute-start.56) | collective-permute-done | bytes 720928 | tf_op jit(solution)/shard_map/ppermute | solution.py:588
  527.6 7.7 %collective-permute-start.65 = (bf16[11,256,128]{2,1,0:T(8,128)(2,1)S(1)}, bf16[11,256,128]{2,1,0:T(8,128)(2,1)S(1)}, u32[]{:S(2)}, u32[]{:S(2)}) collective-permute-start(bf16[11,256,128]{2,1,0:T(8,128)(2,1)S(1)} %fusion.4.inner), channel_id=1, source_target_pairs={{0,1},{1,0},{2,3},{3,2},{4,5},{5,4},{6,7},{7,6},{8,9},{9,8},{10,11... | collective-permute-start | bytes 2162696 | tf_op jit(solution)/shard_map/ppermute | solution.py:588
  539.5 8.9 %collective-permute-start.58 = (bf16[11,256,128]{2,1,0:T(8,128)(2,1)S(1)}, bf16[11,256,128]{2,1,0:T(8,128)(2,1)S(1)}, u32[]{:S(2)}, u32[]{:S(2)}) collective-permute-start(bf16[11,256,128]{2,1,0:T(8,128)(2,1)S(1)} %fusion.inner), channel_id=1, source_target_pairs={{0,1},{1,0},{2,3},{3,2},{4,5},{5,4},{6,7},{7,6},{8,9},{9,8},{10,11... | collective-permute-start | bytes 2162696 | tf_op jit(solution)/shard_map/ppermute | solution.py:588
  557.8 22.4 %collective-permute-done.49 = bf16[8,256,128]{2,1,0:T(8,128)(2,1)S(1)} collective-permute-done((bf16[8,256,128]{2,1,0:T(8,128)(2,1)S(1)}, bf16[8,256,128]{2,1,0:T(8,128)(2,1)S(1)}, u32[]{:S(2)}, u32[]{:S(2)}) %collective-permute-start.49) | collective-permute-done | bytes 524320 | tf_op jit(solution)/shard_map/ppermute | solution.py:593
  581.6 7.1 %collective-permute-done.44.outer = bf16[8,256,128]{2,1,0:T(8,128)(2,1)S(1)} collective-permute-done((bf16[8,256,128]{2,1,0:T(8,128)(2,1)S(1)}, bf16[8,256,128]{2,1,0:T(8,128)(2,1)S(1)}, u32[]{:S(2)}, u32[]{:S(2)}) %collective-permute-start.44) | collective-permute-done | bytes 524320 | tf_op jit(solution)/shard_map/ppermute | solution.py:588
  591.6 7.0 %collective-permute-start.51 = (bf16[8,256,128]{2,1,0:T(8,128)(2,1)S(1)}, bf16[8,256,128]{2,1,0:T(8,128)(2,1)S(1)}, u32[]{:S(2)}, u32[]{:S(2)}) collective-permute-start(bf16[8,256,128]{2,1,0:T(8,128)(2,1)S(1)} %fusion.16.inner), channel_id=1, source_target_pairs={{0,1},{1,0},{2,3},{3,2},{4,5},{5,4},{6,7},{7,6},{8,9},{9,8},{10,11... | collective-permute-start | bytes 1572872 | tf_op jit(solution)/shard_map/ppermute | solution.py:588
  599.0 9.6 %collective-permute-start.46 = (bf16[8,256,128]{2,1,0:T(8,128)(2,1)S(1)}, bf16[8,256,128]{2,1,0:T(8,128)(2,1)S(1)}, u32[]{:S(2)}, u32[]{:S(2)}) collective-permute-start(bf16[8,256,128]{2,1,0:T(8,128)(2,1)S(1)} %fusion.12.inner), channel_id=1, source_target_pairs={{0,1},{1,0},{2,3},{3,2},{4,5},{5,4},{6,7},{7,6},{8,9},{9,8},{10,11... | collective-permute-start | bytes 1572872 | tf_op jit(solution)/shard_map/ppermute | solution.py:588
  612.4 10.2 %collective-permute-done.46.outer = bf16[8,256,128]{2,1,0:T(8,128)(2,1)S(1)} collective-permute-done((bf16[8,256,128]{2,1,0:T(8,128)(2,1)S(1)}, bf16[8,256,128]{2,1,0:T(8,128)(2,1)S(1)}, u32[]{:S(2)}, u32[]{:S(2)}) %collective-permute-start.46) | collective-permute-done | bytes 524320 | tf_op jit(solution)/shard_map/ppermute | solution.py:588
  (314 shorter events, 236.2 us)
Async XLA Ops:
  84.1 30.8 %collective-permute-start.4 = (bf16[8,128,128]{2,1,0:T(8,128)(2,1)S(1)}, bf16[8,128,128]{2,1,0:T(8,128)(2,1)S(1)}, u32[]{:S(2)}, u32[]{:S(2)}) collective-permute-start(bf16[8,128,128]{2,1,0:T(8,128)(2,1)S(1)} %get-tuple-element.280), channel_id=1, source_target_pairs={{0,8},{4,12},{1,9},{5,13},{2,10},{6,14},{3,11},{7,15},{16,24},{20,... | collective-permute-start | bytes 786440 | tf_op jit(solution)/shard_map/ppermute | solution.py:550
  110.3 48.7 %collective-permute-start.12 = (bf16[256,1024]{1,0:T(8,128)(2,1)}, bf16[256,1024]{1,0:T(8,128)(2,1)S(1)}, u32[]{:S(2)}, u32[]{:S(2)}) collective-permute-start(bf16[256,1024]{1,0:T(8,128)(2,1)} %get-tuple-element.175), channel_id=1, source_target_pairs={{0,16},{1,17},{2,18},{3,19},{4,20},{5,21},{6,22},{7,23},{8,24},{9,... | collective-permute-start | bytes 1572872 | tf_op jit(solution)/shard_map/ppermute | solution.py:673
  178.1 50.8 %collective-permute-start.6 = (bf16[8,128,128]{2,1,0:T(8,128)(2,1)S(1)}, bf16[8,128,128]{2,1,0:T(8,128)(2,1)S(1)}, u32[]{:S(2)}, u32[]{:S(2)}) collective-permute-start(bf16[8,128,128]{2,1,0:T(8,128)(2,1)S(1)} %get-tuple-element.278), channel_id=1, source_target_pairs={{8,0},{12,4},{9,1},{13,5},{10,2},{14,6},{11,3},{15,7},{24,16},{28,... | collective-permute-start | bytes 786440 | tf_op jit(solution)/shard_map/ppermute | solution.py:550
  242.4 27.8 %collective-permute-start.7 = (bf16[256,1024]{1,0:T(8,128)(2,1)}, bf16[256,1024]{1,0:T(8,128)(2,1)S(1)}, u32[]{:S(2)}, u32[]{:S(2)}) collective-permute-start(bf16[256,1024]{1,0:T(8,128)(2,1)} %get-tuple-element.155), channel_id=1, source_target_pairs={{16,0},{17,1},{18,2},{19,3},{20,4},{21,5},{22,6},{23,7},{24,8},{25... | collective-permute-start | bytes 1572872 | tf_op jit(solution)/shard_map/ppermute | solution.py:684
  268.1 27.5 %collective-permute-start.17 = (bf16[256,1024]{1,0:T(8,128)(2,1)}, bf16[256,1024]{1,0:T(8,128)(2,1)S(1)}, u32[]{:S(2)}, u32[]{:S(2)}) collective-permute-start(bf16[256,1024]{1,0:T(8,128)(2,1)} %get-tuple-element.194), channel_id=1, source_target_pairs={{16,0},{17,1},{18,2},{19,3},{20,4},{21,5},{22,6},{23,7},{24,8},{25... | collective-permute-start | bytes 1572872 | tf_op jit(solution)/shard_map/ppermute | solution.py:684
  295.4 54.7 %collective-permute-start.8 = (bf16[8,128,128]{2,1,0:T(8,128)(2,1)}, bf16[8,128,128]{2,1,0:T(8,128)(2,1)S(1)}, u32[]{:S(2)}, u32[]{:S(2)}) collective-permute-start(bf16[8,128,128]{2,1,0:T(8,128)(2,1)} %get-tuple-element.167), channel_id=1, source_target_pairs={{0,4},{4,0},{8,12},{12,8},{1,5},{5,1},{9,13},{13,9},{2,6},{6,2},{1... | collective-permute-start | bytes 786440 | tf_op jit(solution)/shard_map/ppermute | solution.py:545
  307.8 47.2 %collective-permute-start.30 = (bf16[22,256,128]{2,1,0:T(8,128)(2,1)}, bf16[22,256,128]{2,1,0:T(8,128)(2,1)}, u32[]{:S(2)}, u32[]{:S(2)}) collective-permute-start(bf16[22,256,128]{2,1,0:T(8,128)(2,1)} %bitcast.24), channel_id=1, source_target_pairs={{0,4},{4,0},{8,12},{12,8},{1,5},{5,1},{9,13},{13,9},{2,6},{6,2},{1... | collective-permute-start | bytes 4325384 | tf_op jit(solution)/shard_map/ppermute | solution.py:562
  308.3 92.3 %collective-permute-start.29 = (bf16[22,256,128]{2,1,0:T(8,128)(2,1)}, bf16[22,256,128]{2,1,0:T(8,128)(2,1)}, u32[]{:S(2)}, u32[]{:S(2)}) collective-permute-start(bf16[22,256,128]{2,1,0:T(8,128)(2,1)} %bitcast.22), channel_id=1, source_target_pairs={{0,4},{4,0},{8,12},{12,8},{1,5},{5,1},{9,13},{13,9},{2,6},{6,2},{1... | collective-permute-start | bytes 4325384 | tf_op jit(solution)/shard_map/ppermute | solution.py:562
  349.1 70.1 %collective-permute-start.28 = (bf16[22,256,128]{2,1,0:T(8,128)(2,1)}, bf16[22,256,128]{2,1,0:T(8,128)(2,1)S(1)}, u32[]{:S(2)}, u32[]{:S(2)}) collective-permute-start(bf16[22,256,128]{2,1,0:T(8,128)(2,1)} %slice.285), channel_id=1, source_target_pairs={{0,4},{4,0},{8,12},{12,8},{1,5},{5,1},{9,13},{13,9},{2,6},{6,2},{1... | collective-permute-start | bytes 4325384 | tf_op jit(solution)/shard_map/ppermute | solution.py:562
  353.7 33.7 %collective-permute-start.19 = (bf16[8,128,128]{2,1,0:T(8,128)(2,1)}, bf16[8,128,128]{2,1,0:T(8,128)(2,1)}, u32[]{:S(2)}, u32[]{:S(2)}) collective-permute-start(bf16[8,128,128]{2,1,0:T(8,128)(2,1)} %get-tuple-element.277), channel_id=1, source_target_pairs={{8,0},{12,4},{9,1},{13,5},{10,2},{14,6},{11,3},{15,7},{24,16},{28,... | collective-permute-start | bytes 786440 | tf_op jit(solution)/shard_map/ppermute | solution.py:550
  357.2 45.7 %collective-permute-start.31 = (bf16[11,256,128]{2,1,0:T(8,128)(2,1)}, bf16[11,256,128]{2,1,0:T(8,128)(2,1)}, u32[]{:S(2)}, u32[]{:S(2)}) collective-permute-start(bf16[11,256,128]{2,1,0:T(8,128)(2,1)} %fusion.10), channel_id=1, source_target_pairs={{0,8},{8,0},{4,12},{12,4},{1,9},{9,1},{5,13},{13,5},{2,10},{10,2},... | collective-permute-start | bytes 2162696 | tf_op jit(solution)/shard_map/ppermute | solution.py:567
  374.2 43.4 %collective-permute-start.24 = (bf16[16,256,128]{2,1,0:T(8,128)(2,1)}, bf16[16,256,128]{2,1,0:T(8,128)(2,1)}, u32[]{:S(2)}, u32[]{:S(2)}) collective-permute-start(bf16[16,256,128]{2,1,0:T(8,128)(2,1)} %slice.325), channel_id=1, source_target_pairs={{0,4},{4,0},{8,12},{12,8},{1,5},{5,1},{9,13},{13,9},{2,6},{6,2},{1... | collective-permute-start | bytes 3145736 | tf_op jit(solution)/shard_map/ppermute | solution.py:562
  387.4 41.3 %collective-permute-start.27 = (bf16[22,256,128]{2,1,0:T(8,128)(2,1)}, bf16[22,256,128]{2,1,0:T(8,128)(2,1)}, u32[]{:S(2)}, u32[]{:S(2)}) collective-permute-start(bf16[22,256,128]{2,1,0:T(8,128)(2,1)} %slice.282), channel_id=1, source_target_pairs={{0,4},{4,0},{8,12},{12,8},{1,5},{5,1},{9,13},{13,9},{2,6},{6,2},{1... | collective-permute-start | bytes 4325384 | tf_op jit(solution)/shard_map/ppermute | solution.py:562
  400.6 38.7 %collective-permute-start.26 = (bf16[22,256,128]{2,1,0:T(8,128)(2,1)}, bf16[22,256,128]{2,1,0:T(8,128)(2,1)}, u32[]{:S(2)}, u32[]{:S(2)}) collective-permute-start(bf16[22,256,128]{2,1,0:T(8,128)(2,1)} %slice.279), channel_id=1, source_target_pairs={{0,4},{4,0},{8,12},{12,8},{1,5},{5,1},{9,13},{13,9},{2,6},{6,2},{1... | collective-permute-start | bytes 4325384 | tf_op jit(solution)/shard_map/ppermute | solution.py:562
  417.6 41.9 %collective-permute-start.25 = (bf16[22,256,128]{2,1,0:T(8,128)(2,1)}, bf16[22,256,128]{2,1,0:T(8,128)(2,1)S(1)}, u32[]{:S(2)}, u32[]{:S(2)}) collective-permute-start(bf16[22,256,128]{2,1,0:T(8,128)(2,1)} %slice.276), channel_id=1, source_target_pairs={{0,4},{4,0},{8,12},{12,8},{1,5},{5,1},{9,13},{13,9},{2,6},{6,2},{1... | collective-permute-start | bytes 4325384 | tf_op jit(solution)/shard_map/ppermute | solution.py:562
  428.7 28.9 %collective-permute-start.54 = (bf16[11,256,128]{2,1,0:T(8,128)(2,1)S(1)}, bf16[11,256,128]{2,1,0:T(8,128)(2,1)S(1)}, u32[]{:S(2)}, u32[]{:S(2)}) collective-permute-start(bf16[11,256,128]{2,1,0:T(8,128)(2,1)S(1)} %add_convert_fusion.9), channel_id=1, source_target_pairs={{0,1},{3,2},{4,5},{7,6},{8,9},{11,10},{12,13},{15,14},{16,17},{19,... | collective-permute-start | bytes 2162696 | tf_op jit(solution)/shard_map/ppermute | solution.py:593
  443.6 42.2 %collective-permute-start.21 = (bf16[16,256,128]{2,1,0:T(8,128)(2,1)S(1)}, bf16[16,256,128]{2,1,0:T(8,128)(2,1)S(1)}, u32[]{:S(2)}, u32[]{:S(2)}) collective-permute-start(bf16[16,256,128]{2,1,0:T(8,128)(2,1)S(1)} %slice.264), channel_id=1, source_target_pairs={{0,4},{4,0},{8,12},{12,8},{1,5},{5,1},{9,13},{13,9},{2,6},{6,2},{1... | collective-permute-start | bytes 3145736 | tf_op jit(solution)/shard_map/ppermute | solution.py:562
  461.4 36.1 %collective-permute-start.23 = (bf16[16,256,128]{2,1,0:T(8,128)(2,1)S(1)}, bf16[16,256,128]{2,1,0:T(8,128)(2,1)S(1)}, u32[]{:S(2)}, u32[]{:S(2)}) collective-permute-start(bf16[16,256,128]{2,1,0:T(8,128)(2,1)S(1)} %slice.270), channel_id=1, source_target_pairs={{0,4},{4,0},{8,12},{12,8},{1,5},{5,1},{9,13},{13,9},{2,6},{6,2},{1... | collective-permute-start | bytes 3145736 | tf_op jit(solution)/shard_map/ppermute | solution.py:562
  461.6 64.1 %collective-permute-start.20 = (bf16[16,256,128]{2,1,0:T(8,128)(2,1)S(1)}, bf16[16,256,128]{2,1,0:T(8,128)(2,1)S(1)}, u32[]{:S(2)}, u32[]{:S(2)}) collective-permute-start(bf16[16,256,128]{2,1,0:T(8,128)(2,1)S(1)} %slice.259), channel_id=1, source_target_pairs={{0,4},{4,0},{8,12},{12,8},{1,5},{5,1},{9,13},{13,9},{2,6},{6,2},{1... | collective-permute-start | bytes 3145736 | tf_op jit(solution)/shard_map/ppermute | solution.py:562
  476.7 24.8 %collective-permute-start.63 = (bf16[11,256,128]{2,1,0:T(8,128)(2,1)S(1)}, bf16[11,256,128]{2,1,0:T(8,128)(2,1)S(1)}, u32[]{:S(2)}, u32[]{:S(2)}) collective-permute-start(bf16[11,256,128]{2,1,0:T(8,128)(2,1)S(1)} %fusion.6), channel_id=1, source_target_pairs={{0,1},{1,0},{2,3},{3,2},{4,5},{5,4},{6,7},{7,6},{8,9},{9,8},{10,11... | collective-permute-start | bytes 2162696 | tf_op jit(solution)/shard_map/ppermute | solution.py:588
  485.9 28.0 %collective-permute-start.56 = (bf16[11,256,128]{2,1,0:T(8,128)(2,1)S(1)}, bf16[11,256,128]{2,1,0:T(8,128)(2,1)S(1)}, u32[]{:S(2)}, u32[]{:S(2)}) collective-permute-start(bf16[11,256,128]{2,1,0:T(8,128)(2,1)S(1)} %fusion.2), channel_id=1, source_target_pairs={{0,1},{1,0},{2,3},{3,2},{4,5},{5,4},{6,7},{7,6},{8,9},{9,8},{10,11... | collective-permute-start | bytes 2162696 | tf_op jit(solution)/shard_map/ppermute | solution.py:588
  527.6 27.7 %collective-permute-start.65 = (bf16[11,256,128]{2,1,0:T(8,128)(2,1)S(1)}, bf16[11,256,128]{2,1,0:T(8,128)(2,1)S(1)}, u32[]{:S(2)}, u32[]{:S(2)}) collective-permute-start(bf16[11,256,128]{2,1,0:T(8,128)(2,1)S(1)} %fusion.4.inner), channel_id=1, source_target_pairs={{0,1},{1,0},{2,3},{3,2},{4,5},{5,4},{6,7},{7,6},{8,9},{9,8},{10,11... | collective-permute-start | bytes 2162696 | tf_op jit(solution)/shard_map/ppermute | solution.py:588
  539.5 50.2 %collective-permute-start.58 = (bf16[11,256,128]{2,1,0:T(8,128)(2,1)S(1)}, bf16[11,256,128]{2,1,0:T(8,128)(2,1)S(1)}, u32[]{:S(2)}, u32[]{:S(2)}) collective-permute-start(bf16[11,256,128]{2,1,0:T(8,128)(2,1)S(1)} %fusion.inner), channel_id=1, source_target_pairs={{0,1},{1,0},{2,3},{3,2},{4,5},{5,4},{6,7},{7,6},{8,9},{9,8},{10,11... | collective-permute-start | bytes 2162696 | tf_op jit(solution)/shard_map/ppermute | solution.py:588
  548.6 31.6 %collective-permute-start.49 = (bf16[8,256,128]{2,1,0:T(8,128)(2,1)S(1)}, bf16[8,256,128]{2,1,0:T(8,128)(2,1)S(1)}, u32[]{:S(2)}, u32[]{:S(2)}) collective-permute-start(bf16[8,256,128]{2,1,0:T(8,128)(2,1)S(1)} %add_convert_fusion.20), channel_id=1, source_target_pairs={{0,1},{3,2},{4,5},{7,6},{8,9},{11,10},{12,13},{15,14},{16,17},{19,... | collective-permute-start | bytes 1572872 | tf_op jit(solution)/shard_map/ppermute | solution.py:593
  550.6 30.5 %collective-permute-start.40 = (bf16[8,256,128]{2,1,0:T(8,128)(2,1)S(1)}, bf16[8,256,128]{2,1,0:T(8,128)(2,1)S(1)}, u32[]{:S(2)}, u32[]{:S(2)}) collective-permute-start(bf16[8,256,128]{2,1,0:T(8,128)(2,1)S(1)} %add_convert_fusion.34), channel_id=1, source_target_pairs={{0,8},{8,0},{4,12},{12,4},{1,9},{9,1},{5,13},{13,5},{2,10},{10,2},... | collective-permute-start | bytes 1572872 | tf_op jit(solution)/shard_map/ppermute | solution.py:567
  552.3 36.3 %collective-permute-start.44 = (bf16[8,256,128]{2,1,0:T(8,128)(2,1)S(1)}, bf16[8,256,128]{2,1,0:T(8,128)(2,1)S(1)}, u32[]{:S(2)}, u32[]{:S(2)}) collective-permute-start(bf16[8,256,128]{2,1,0:T(8,128)(2,1)S(1)} %fusion.14.inner), channel_id=1, source_target_pairs={{0,1},{1,0},{2,3},{3,2},{4,5},{5,4},{6,7},{7,6},{8,9},{9,8},{10,11... | collective-permute-start | bytes 1572872 | tf_op jit(solution)/shard_map/ppermute | solution.py:588
  557.1 51.6 %collective-permute-start.66 = (bf16[11,256,128]{2,1,0:T(8,128)(2,1)S(1)}, bf16[11,256,128]{2,1,0:T(8,128)(2,1)S(1)}, u32[]{:S(2)}, u32[]{:S(2)}) collective-permute-start(bf16[11,256,128]{2,1,0:T(8,128)(2,1)S(1)} %fusion.5), channel_id=1, source_target_pairs={{1,2},{2,1},{5,6},{6,5},{9,10},{10,9},{13,14},{14,13},{17,18},{18,... | collective-permute-start | bytes 2162696 | tf_op jit(solution)/shard_map/ppermute | solution.py:585
  590.5 33.1 %collective-permute-start.59 = (bf16[11,256,128]{2,1,0:T(8,128)(2,1)S(1)}, bf16[11,256,128]{2,1,0:T(8,128)(2,1)S(1)}, u32[]{:S(2)}, u32[]{:S(2)}) collective-permute-start(bf16[11,256,128]{2,1,0:T(8,128)(2,1)S(1)} %fusion.1), channel_id=1, source_target_pairs={{1,2},{2,1},{5,6},{6,5},{9,10},{10,9},{13,14},{14,13},{17,18},{18,... | collective-permute-start | bytes 2162696 | tf_op jit(solution)/shard_map/ppermute | solution.py:585
  608.8 32.2 %collective-permute-start.67 = (bf16[11,256,128]{2,1,0:T(8,128)(2,1)S(1)}, bf16[11,256,128]{2,1,0:T(8,128)(2,1)S(1)}, u32[]{:S(2)}, u32[]{:S(2)}) collective-permute-start(bf16[11,256,128]{2,1,0:T(8,128)(2,1)S(1)} %add_convert_fusion.inner), channel_id=1, source_target_pairs={{1,0},{2,3},{5,4},{6,7},{9,8},{10,11},{13,12},{14,15},{17,16},{18,... | collective-permute-start | bytes 2162696 | tf_op jit(solution)/shard_map/ppermute | solution.py:596
  623.8 29.8 %collective-permute-start.60 = (bf16[11,256,128]{2,1,0:T(8,128)(2,1)S(1)}, bf16[11,256,128]{2,1,0:T(8,128)(2,1)}, u32[]{:S(2)}, u32[]{:S(2)}) collective-permute-start(bf16[11,256,128]{2,1,0:T(8,128)(2,1)S(1)} %add_convert_fusion.7.inner), channel_id=1, source_target_pairs={{1,0},{2,3},{5,4},{6,7},{9,8},{10,11},{13,12},{14,15},{17,16},{18,... | collective-permute-start | bytes 2162696 | tf_op jit(solution)/shard_map/ppermute | solution.py:596
  625.3 39.5 %collective-permute-start.53 = (bf16[8,256,128]{2,1,0:T(8,128)(2,1)S(1)}, bf16[8,256,128]{2,1,0:T(8,128)(2,1)}, u32[]{:S(2)}, u32[]{:S(2)}) collective-permute-start(bf16[8,256,128]{2,1,0:T(8,128)(2,1)S(1)} %add_convert_fusion.18.inner), channel_id=1, source_target_pairs={{1,0},{2,3},{5,4},{6,7},{9,8},{10,11},{13,12},{14,15},{17,16},{18,... | collective-permute-start | bytes 1572872 | tf_op jit(solution)/shard_map/ppermute | solution.py:596
  626.8 45.4 %collective-permute-start.48 = (bf16[8,256,128]{2,1,0:T(8,128)(2,1)S(1)}, bf16[8,256,128]{2,1,0:T(8,128)(2,1)}, u32[]{:S(2)}, u32[]{:S(2)}) collective-permute-start(bf16[8,256,128]{2,1,0:T(8,128)(2,1)S(1)} %add_convert_fusion.24.inner), channel_id=1, source_target_pairs={{1,0},{2,3},{5,4},{6,7},{9,8},{10,11},{13,12},{14,15},{17,16},{18,... | collective-permute-start | bytes 1572872 | tf_op jit(solution)/shard_map/ppermute | solution.py:596
  (92 other events, 954.0 us)

commit v2 on v1

v2 whole, which is shorter than its diff:
```python
import functools
import math

import jax
import jax.numpy as jnp
from jax import lax
from jax.experimental import pallas as pl
from jax.experimental.pallas import tpu as pltpu
from jax.sharding import PartitionSpec as P

HEADS = 8
BLK = 256
LANES = 128
STEPS = 8

epsilon = 1e-06
theta_base = 10000.0
f32 = jnp.float32
bf16 = jnp.bfloat16


def nn(a, b):
    return jnp.dot(a, b, preferred_element_type=f32)


def nt(a, b):
    return lax.dot_general(a, b, (((1,), (1,)), ((), ())), preferred_element_type=f32)


def tn(a, b):
    return lax.dot_general(a, b, (((0,), (0,)), ((), ())), preferred_element_type=f32)


def sigmoid(v):
    return 1.0 / (1.0 + jnp.exp(-v))


def norm_factor(v, width):
    return lax.rsqrt(jnp.sum(v * v, axis=-1, keepdims=True) * (1.0 / width) + epsilon)


def norm_back(cotangent, normed, factor, width):
    mean = jnp.sum(cotangent * normed, axis=-1, keepdims=True) * (1.0 / width)
    return factor * (cotangent - normed * mean)


def row_index(rows, columns):
    return lax.broadcasted_iota(jnp.int32, (rows, columns), 0).astype(f32)


def decay_mask(slope, rows):
    row = lax.broadcasted_iota(jnp.int32, (rows, rows), 0)
    column = lax.broadcasted_iota(jnp.int32, (rows, rows), 1)
    distance = jnp.maximum(row - column, 0).astype(f32)
    return jnp.where(row >= column, jnp.exp(distance * (-slope)), 0.0)


def head(number):
    return slice(number * LANES, (number + 1) * LANES)


def half_turn(v):
    return pltpu.roll(v, LANES // 2, 1)


def whole(shape):
    return pl.BlockSpec(shape, lambda j: (0,) * len(shape))


def hbm(shape, kind):
    return pltpu.HBM(tuple(shape), kind)


def far_away(*arrays):
    return [pltpu.with_memory_space_constraint(a, pltpu.HBM) for a in arrays]


def close_by(*arrays):
    return [pltpu.with_memory_space_constraint(a, pltpu.VMEM) for a in arrays]


def params(megabytes):
    return pltpu.CompilerParams(vmem_limit_bytes=megabytes * 1024 * 1024)


SMEM = pl.BlockSpec(memory_space=pltpu.SMEM)
ANY = pl.BlockSpec(memory_space=pltpu.HBM)
VMEM = pl.BlockSpec(memory_space=pltpu.VMEM)


def tables(position, rows):
    lane = lax.broadcasted_iota(jnp.int32, (rows, LANES), 1)
    half = LANES // 2
    feature = jnp.where(lane < half, lane, lane - half).astype(f32)
    frequency = jnp.exp(feature * (-math.log(theta_base) / half))
    angle = position * frequency
    return jnp.cos(angle), jnp.where(lane < half, -jnp.sin(angle), jnp.sin(angle))


def project_body(slope, x, cosine, sine, w, h1, r1, pre, qk, state,
                 xv, cv, sv, hv, rv, prev, qkv, stv, isem, osem):
    rows, width = x.shape
    steps = STEPS
    columns = w.shape[1] // steps
    heads = columns // LANES
    first = [
        pltpu.make_async_copy(source, target, isem.at[n])
        for n, (source, target) in enumerate(((x, xv), (cosine, cv), (sine, sv)))
    ]
    for copy in first:
        copy.start()

    first[0].wait()
    v = xv[...].astype(f32)
    factor = norm_factor(v, width)
    hv[...] = (v * factor).astype(bf16)
    rv[...] = jnp.broadcast_to(factor, rv.shape)
    first[1].wait()
    first[2].wait()
    outs = [pltpu.make_async_copy(hv, h1, osem.at[0]), pltpu.make_async_copy(rv, r1, osem.at[1])]
    for copy in outs:
        copy.start()

    def pre_out(j):
        at = pl.ds(pl.multiple_of(j * columns, LANES), columns)
        return pltpu.make_async_copy(prev.at[:, at], pre.at[:, at], osem.at[3 + j])

    def step(j, carry):
        at = pl.multiple_of(j * columns, LANES)
        p = nn(hv[...], w[:, pl.ds(at, columns)])
        prev[:, pl.ds(at, columns)] = p.astype(bf16)
        pre_out(j).start()

        @pl.when(j < steps // 2)
        def _():
            for n in range(heads):
                v = p[:, head(n)]
                v = v * sigmoid(v)
                turned = v * cv[...] + half_turn(v) * sv[...]
                qkv[:, pl.ds(at + n * LANES, LANES)] = turned.astype(bf16)

        @pl.when((j >= steps // 2) & (j < 3 * steps // 4))
        def _():
            values = p.astype(bf16)
            ahead = rows - row_index(rows, LANES)
            for n in range(heads):
                number = (j - steps // 2) * heads + n
                decay = jnp.exp(ahead * (-slope[number]))
                key = qkv[:, pl.ds(at - width + n * LANES, LANES)]
                keyed = (key.astype(f32) * decay).astype(bf16)
                stv[number] = tn(keyed, values[:, head(n)]).astype(bf16)

        return carry

    lax.fori_loop(0, steps, step, 0)
    last = [pltpu.make_async_copy(qkv, qk, osem.at[2]), pltpu.make_async_copy(stv, state, osem.at[11])]
    for copy in last:
        copy.start()
    for copy in outs + last:
        copy.wait()
    for j in range(steps):
        pre_out(j).wait()


def project(slopes, x, cosine, sine, w):
    rows, width = x.shape
    total = w.shape[1]
    states = (HEADS, LANES, LANES)
    return pl.pallas_call(
        project_body,
        in_specs=[SMEM] + [ANY] * 3 + [VMEM],
        out_specs=[ANY] * 5,
        out_shape=[
            hbm((rows, width), bf16),
            hbm((rows, LANES), f32),
            hbm((rows, total), bf16),
            hbm((rows, total // 2), bf16),
            hbm(states, bf16),
        ],
        scratch_shapes=[
            pltpu.VMEM((rows, width), bf16),
            pltpu.VMEM((rows, LANES), f32),
            pltpu.VMEM((rows, LANES), f32),
            pltpu.VMEM((rows, width), bf16),
            pltpu.VMEM((rows, LANES), f32),
            pltpu.VMEM((rows, total), bf16),
            pltpu.VMEM((rows, total // 2), bf16),
            pltpu.VMEM(states, bf16),
            pltpu.SemaphoreType.DMA((3,)),
            pltpu.SemaphoreType.DMA((12,)),
        ],
        compiler_params=params(8),
        cost_estimate=pl.CostEstimate(
            flops=2 * rows * width * total, bytes_accessed=2 * width * total, transcendentals=0
        ),
        name="project",
    )(slopes, *far_away(x, cosine, sine), *close_by(w))


def moves(pairs, sem, start=0):
    return [
        pltpu.make_async_copy(source, target, sem.at[start + n])
        for n, (source, target) in enumerate(pairs)
    ]


def entering_state(factors, states, number):
    state = factors[0, number] * states[number].astype(f32)
    state += factors[1, number] * states[HEADS + number].astype(f32)
    return state.astype(bf16)


def finish_body(
    slope, factors, x, qk, pre, far, near, wo, wi, wd,
    mixed, gated, ra, h2, r2, low, g, up, product, y,
    xv, qkv, vuv, statev, mixedv, gatedv, rav, h2v, r2v, lowv, gv, upv, productv, yv,
    attended, total, held, isem, osem, csem,
):
    rows, width = x.shape
    hidden = wd.shape[0]
    columns = held.shape[1]
    steps = hidden // columns
    ins = moves(
        (
            (qk, qkv), (pre.at[:, pl.ds(2 * width, 2 * width)], vuv),
            (far, statev.at[pl.ds(0, HEADS)]), (near, statev.at[pl.ds(HEADS, HEADS)]), (x, xv),
        ),
        isem,
    )
    for copy in ins:
        copy.start()
    for copy in ins[:4]:
        copy.wait()
    ahead = row_index(rows, LANES)

    def pair(i, carry):
        for m in range(4):
            n = i * 4 + m
            at = pl.multiple_of(n * LANES, LANES)
            lane = pl.ds(at, LANES)
            state = entering_state(factors, statev, n)
            lowv[n] = state
            query = qkv[:, lane]
            key = qkv[:, pl.ds(at + width, LANES)]
            weights = (decay_mask(slope[n], rows) * nt(query, key)).astype(bf16)
            inner = nn(weights, vuv[:, lane])
            carried = nn(query, state)
            attended[:, lane] = inner + jnp.exp(ahead * (-slope[n])) * carried
        return carry

    lax.fori_loop(0, HEADS // 4, pair, 0)
    rows_out = attended[...]
    factor = norm_factor(rows_out, width)
    rav[...] = jnp.broadcast_to(factor, rav.shape)
    normed = rows_out * factor
    mixedv[...] = normed.astype(bf16)
    gatedv[...] = (normed * vuv[:, width:].astype(f32)).astype(bf16)
    outs = moves(((mixedv, mixed), (gatedv, gated), (rav, ra), (lowv, low)), osem)
    for copy in outs:
        copy.start()
    ins[4].wait()
    middle = xv[...].astype(f32) + nn(gatedv[...], wo[...])
    total[...] = middle
    factor = norm_factor(middle, width)
    r2v[...] = jnp.broadcast_to(factor, r2v.shape)
    h2v[...] = (middle * factor).astype(bf16)
    more = moves(((h2v, h2), (r2v, r2)), osem, 4)
    for copy in more:
        copy.start()
    held[...] = jnp.zeros_like(held)

    def chunk_out(i):
        at = pl.ds(pl.multiple_of(i * columns, LANES), columns)
        return [
            pltpu.make_async_copy(source.at[:, at], target.at[:, at], csem.at[n, i])
            for n, (source, target) in enumerate(((gv, g), (upv, up), (productv, product)))
        ]

    def step(i, carry):
        start = pl.multiple_of(i * columns, LANES)
        before = pl.multiple_of(jnp.maximum(i - 1, 0) * columns, LANES)
        at = pl.ds(start, columns)
        total[...] += nn(held[...], wd[pl.ds(before, columns), :])
        gate = nn(h2v[...], wi[:, at])
        rise = nn(h2v[...], wi[:, pl.ds(start + hidden, columns)])
        both = (gate * rise).astype(bf16)
        gv[:, at] = gate.astype(bf16)
        upv[:, at] = rise.astype(bf16)
        productv[:, at] = both
        held[...] = both
        for copy in chunk_out(i):
            copy.start()
        return carry

    lax.fori_loop(0, steps, step, 0)
    yv[...] = (total[...] + nn(held[...], wd[hidden - columns :, :])).astype(bf16)
    last = moves(((yv, y),), osem, 6)
    for copy in last:
        copy.start()
    for copy in outs + more + last:
        copy.wait()

    def drain(i, carry):
        for copy in chunk_out(i):
            copy.wait()
        return carry

    lax.fori_loop(0, steps, drain, 0)


def finish(slopes, factors, x, qk, pre, entering, wo, wi, wd):
    rows, width = x.shape
    hidden = wd.shape[0]
    columns = 256
    steps = hidden // columns
    states = (HEADS, LANES, LANES)
    act = hbm((rows, width), bf16)
    factor = hbm((rows, LANES), f32)
    unit = hbm((rows, hidden), bf16)
    outs = [
        act, act, factor, act, factor, hbm(states, bf16), unit, unit, unit, act,
    ]
    return pl.pallas_call(
        finish_body,
        in_specs=[SMEM] * 2 + [ANY] * 5 + [VMEM] * 3,
        out_specs=[ANY] * len(outs),
        out_shape=outs,
        scratch_shapes=[
            pltpu.VMEM((rows, width), bf16),
            pltpu.VMEM((rows, 2 * width), bf16),
            pltpu.VMEM((rows, 2 * width), bf16),
            pltpu.VMEM((2 * HEADS, LANES, LANES), bf16),
        ]
        + [pltpu.VMEM(o.shape, o.dtype) for o in outs]
        + [
            pltpu.VMEM((rows, width), f32),
            pltpu.VMEM((rows, width), f32),
            pltpu.VMEM((rows, columns), bf16),
            pltpu.SemaphoreType.DMA((5,)),
            pltpu.SemaphoreType.DMA((7,)),
            pltpu.SemaphoreType.DMA((3, steps)),
        ],
        compiler_params=params(18),
        cost_estimate=pl.CostEstimate(
            flops=2 * rows * width * (width + 3 * hidden),
            bytes_accessed=2 * width * (width + 3 * hidden),
            transcendentals=0,
        ),
        name="finish",
    )(slopes, factors, *far_away(x, qk, pre, *entering), *close_by(wo, wi, wd))


def back_channel_body(
    slope, dy, wo, wi, wd, g, up, h2, r2, mixed, ra, qk, pre, low, cosine, sine,
    dg, dup, dmid, dm, dq, du, dk, dv, state,
    dyv, gv, upv, h2v, r2v, mixedv, rav, qkv, qpv, vuv, lowv, cv, sv,
    dgv, dupv, dmidv, dmv, dqv, duv, dkv, dvv, statev,
    total, datt, heldg, heldu, isem, osem, csem,
):
    rows, width = dy.shape
    hidden = wd.shape[0]
    columns = heldg.shape[1]
    steps = hidden // columns
    ins = moves(
        (
            (dy, dyv), (g, gv), (up, upv), (h2, h2v), (r2, r2v), (mixed, mixedv), (ra, rav),
            (qk, qkv), (pre.at[:, pl.ds(0, width)], qpv),
            (pre.at[:, pl.ds(2 * width, 2 * width)], vuv), (low, lowv), (cosine, cv), (sine, sv),
        ),
        isem,
    )
    for copy in ins:
        copy.start()
    for copy in ins[:3]:
        copy.wait()
    heldg[...] = jnp.zeros_like(heldg)
    heldu[...] = jnp.zeros_like(heldu)
    total[...] = jnp.zeros_like(total)

    def chunk_out(i):
        at = pl.ds(pl.multiple_of(i * columns, LANES), columns)
        return [
            pltpu.make_async_copy(source.at[:, at], target.at[:, at], csem.at[n, i])
            for n, (source, target) in enumerate(((dgv, dg), (dupv, dup)))
        ]

    def step(i, carry):
        at = pl.ds(pl.multiple_of(i * columns, LANES), columns)
        before = pl.multiple_of(jnp.maximum(i - 1, 0) * columns, LANES)
        total[...] += nt(heldg[...], wi[:, pl.ds(before, columns)]) + nt(
            heldu[...], wi[:, pl.ds(before + hidden, columns)]
        )
        product = nt(dyv[...], wd[at, :])
        left = (product * upv[:, at].astype(f32)).astype(bf16)
        right = (product * gv[:, at].astype(f32)).astype(bf16)
        dgv[:, at] = left
        dupv[:, at] = right
        heldg[...] = left
        heldu[...] = right
        for copy in chunk_out(i):
            copy.start()
        return carry

    lax.fori_loop(0, steps, step, 0)
    for copy in ins[3:]:
        copy.wait()
    dh2 = (
        total[...]
        + nt(heldg[...], wi[:, hidden - columns : hidden])
        + nt(heldu[...], wi[:, 2 * hidden - columns :])
    )
    middle = dyv[...].astype(f32) + norm_back(dh2, h2v[...].astype(f32), r2v[:, 0:1], width)
    dmidv[...] = middle
    dmv[...] = middle.astype(bf16)
    outs = moves(((dmidv, dmid), (dmv, dm)), osem)
    for copy in outs:
        copy.start()
    dgated = nt(dmv[...], wo[...])
    normed = mixedv[...].astype(f32)
    duv[...] = (dgated * normed).astype(bf16)
    back = norm_back(dgated * vuv[:, width:].astype(f32), normed, rav[:, 0:1], width)
    datt[...] = back.astype(bf16)
    ahead = row_index(rows, LANES)
    row = lax.broadcasted_iota(jnp.int32, (rows, rows), 0)
    column = lax.broadcasted_iota(jnp.int32, (rows, rows), 1)
    distance = (row - column).astype(f32)

    def some(i, carry):
        for m in range(2):
            n = i * 2 + m
            at = pl.multiple_of(n * LANES, LANES)
            lane = pl.ds(at, LANES)
            query, key = qkv[:, lane], qkv[:, pl.ds(at + width, LANES)]
            value, cot = vuv[:, lane], datt[:, lane]
            power = jnp.exp(jnp.abs(distance) * (-slope[n]))
            mask = jnp.where(distance >= 0.0, power, 0.0)
            flipped = jnp.where(distance <= 0.0, power, 0.0)
            weights_t = (flipped * nt(key, query)).astype(bf16)
            scores = (mask * nt(cot, value)).astype(bf16)
            scores_t = (flipped * nt(value, cot)).astype(bf16)
            scaled = (jnp.exp(ahead * (-slope[n])) * cot.astype(f32)).astype(bf16)
            statev[n] = tn(query, scaled).astype(bf16)
            dquery = nn(scores, key) + nt(scaled, lowv[n])
            turned = dquery * cv[...] + half_turn(dquery * sv[...])
            p = qpv[:, lane].astype(f32)
            s = sigmoid(p)
            dqv[:, lane] = (turned * (s * (1.0 + p * (1.0 - s)))).astype(bf16)
            dkv[:, lane] = nn(scores_t, query)
            dvv[:, lane] = nn(weights_t, cot)
        return carry

    lax.fori_loop(0, HEADS // 2, some, 0)
    last = moves(((statev, state), (dqv, dq), (duv, du), (dkv, dk), (dvv, dv)), osem, 2)
    for copy in last:
        copy.start()
    for copy in outs + last:
        copy.wait()

    def drain(i, carry):
        for copy in chunk_out(i):
            copy.wait()
        return carry

    lax.fori_loop(0, steps, drain, 0)


def back_channel(slopes, dy, r, cosine, sine, wo, wi, wd):
    rows, width = dy.shape
    hidden = wd.shape[0]
    columns = 256
    steps = hidden // columns
    states = (HEADS, LANES, LANES)
    act = hbm((rows, width), bf16)
    full = hbm((rows, width), f32)
    unit = hbm((rows, hidden), bf16)
    outs = [unit, unit, full, act, act, act, full, full, hbm(states, bf16)]
    wide = pltpu.VMEM((rows, width), bf16)
    thin = pltpu.VMEM((rows, LANES), f32)
    twice = pltpu.VMEM((rows, 2 * width), bf16)
    tall = pltpu.VMEM((rows, hidden), bf16)
    return pl.pallas_call(
        back_channel_body,
        in_specs=[SMEM] + [ANY] + [VMEM] * 3 + [ANY] * 11,
        out_specs=[ANY] * len(outs),
        out_shape=outs,
        scratch_shapes=[
            wide, tall, tall, wide, thin, wide, thin, twice, wide, twice,
            pltpu.VMEM(states, bf16), thin, thin,
        ]
        + [pltpu.VMEM(o.shape, o.dtype) for o in outs]
        + [
            pltpu.VMEM((rows, width), f32),
            wide,
            pltpu.VMEM((rows, columns), bf16),
            pltpu.VMEM((rows, columns), bf16),
            pltpu.SemaphoreType.DMA((13,)),
            pltpu.SemaphoreType.DMA((7,)),
            pltpu.SemaphoreType.DMA((2, steps)),
        ],
        compiler_params=params(22),
        cost_estimate=pl.CostEstimate(
            flops=2 * rows * width * (width + 3 * hidden),
            bytes_accessed=2 * width * (width + 3 * hidden),
            transcendentals=0,
        ),
        name="back_channel",
    )(
        slopes, *far_away(dy), *close_by(wo, wi, wd),
        *far_away(
            r["g"], r["up"], r["h2"], r["r2"], r["mixed"], r["ra"], r["qk"], r["pre"], r["low"],
            cosine, sine,
        ),
    )


def back_mixer_body(
    slope, factors, dq, du, dk, dv, qk, pre, far, near, cosine, sine, h1, r1, dmid, w,
    dkp, dvp, dx,
    dkin, dvin, kvv, kpv, vv, statev, cv, sv, h1v, r1v, dmidv, parts, dxv, isem, osem,
):
    rows, width = dq.shape
    ins = moves(
        (
            (dk, dkin), (dv, dvin), (qk.at[:, pl.ds(width, width)], kvv),
            (pre.at[:, pl.ds(width, width)], kpv), (pre.at[:, pl.ds(2 * width, width)], vv),
            (far, statev.at[pl.ds(0, HEADS)]), (near, statev.at[pl.ds(HEADS, HEADS)]),
            (cosine, cv), (sine, sv),
            (dq, parts.at[:, pl.ds(0, width)]), (du, parts.at[:, pl.ds(3 * width, width)]),
            (h1, h1v), (r1, r1v), (dmid, dmidv),
        ),
        isem,
    )
    for copy in ins:
        copy.start()
    for copy in ins[:9]:
        copy.wait()
    ahead = rows - row_index(rows, LANES)

    def some(i, carry):
        for m in range(4):
            n = i * 4 + m
            at = pl.multiple_of(n * LANES, LANES)
            lane = pl.ds(at, LANES)
            state = entering_state(factors, statev, n)
            decay = jnp.exp(ahead * (-slope[n]))
            keyed = (kvv[:, lane].astype(f32) * decay).astype(bf16)
            dkey = dkin[:, lane] + decay * nt(vv[:, lane], state)
            turned = dkey * cv[...] + half_turn(dkey * sv[...])
            p = kpv[:, lane].astype(f32)
            s = sigmoid(p)
            parts[:, pl.ds(at + width, LANES)] = (turned * (s * (1.0 + p * (1.0 - s)))).astype(bf16)
            parts[:, pl.ds(at + 2 * width, LANES)] = (dvin[:, lane] + nn(keyed, state)).astype(bf16)
        return carry

    lax.fori_loop(0, HEADS // 4, some, 0)
    outs = moves(
        ((parts.at[:, pl.ds(width, width)], dkp), (parts.at[:, pl.ds(2 * width, width)], dvp)), osem
    )
    for copy in outs:
        copy.start()
    for copy in ins[9:]:
        copy.wait()
    total = nt(parts[...], w[...])
    back = norm_back(total, h1v[...].astype(f32), r1v[:, 0:1], width)
    dxv[...] = (dmidv[...] + back).astype(bf16)
    last = moves(((dxv, dx),), osem, 2)
    for copy in last:
        copy.start()
    for copy in outs + last:
        copy.wait()


def back_mixer(slopes, factors, r, entering, cosine, sine, w):
    rows, width = r["dq"].shape
    act = hbm((rows, width), bf16)
    wide = pltpu.VMEM((rows, width), bf16)
    full = pltpu.VMEM((rows, width), f32)
    thin = pltpu.VMEM((rows, LANES), f32)
    return pl.pallas_call(
        back_mixer_body,
        in_specs=[SMEM] * 2 + [ANY] * 13 + [VMEM],
        out_specs=[ANY] * 3,
        out_shape=[act, act, act],
        scratch_shapes=[
            full, full, wide, wide, wide, pltpu.VMEM((2 * HEADS, LANES, LANES), bf16), thin, thin,
            wide, thin,
            full,
            pltpu.VMEM((rows, w.shape[1]), bf16), wide,
            pltpu.SemaphoreType.DMA((14,)),
            pltpu.SemaphoreType.DMA((3,)),
        ],
        compiler_params=params(14),
        cost_estimate=pl.CostEstimate(
            flops=2 * rows * width * w.shape[1],
            bytes_accessed=2 * width * w.shape[1],
            transcendentals=0,
        ),
        name="back_mixer",
    )(
        slopes, factors,
        *far_away(
            r["dq"], r["du"], r["dk"], r["dv"], r["qk"], r["pre"], *entering, cosine, sine,
            r["h1"], r["r1"], r["dmid"],
        ),
        *close_by(w),
    )


def weight_body(*refs, batch, sides, groups):
    place = refs[0]
    lefts = refs[1 : 1 + 2 * batch]
    rights = refs[1 + 2 * batch : 1 + 2 * batch + 2 * batch * sides]
    outs = refs[1 + 2 * batch + 2 * batch * sides : -7]
    x, xt, ys, stage, xsem, ysem, osem = refs[-7:]
    rows = lefts[0].shape[0]
    columns = x.shape[1]
    quarter = columns // 4
    blocks = groups[0][2]

    def left_copies(section):
        return [
            pltpu.make_async_copy(
                lefts[section * batch + b], x.at[pl.ds(b * rows, rows)], xsem.at[b]
            )
            for b in range(batch)
        ]

    def right_copies(section, s):
        return [
            pltpu.make_async_copy(
                rights[(section * sides + s) * batch + b],
                ys.at[s, pl.ds(b * rows, rows)],
                ysem.at[s, b],
            )
            for b in range(batch)
        ]

    for section in range(2):

        @pl.when(place[4] == section)
        def _():
            for copy in left_copies(section):
                copy.start()
            for s in range(sides):
                for copy in right_copies(section, s):
                    copy.start()

    for copy in left_copies(0):
        copy.wait()
    for piece in range(columns // LANES):
        xt[piece * LANES : (piece + 1) * LANES, :] = x[:, piece * LANES : (piece + 1) * LANES].T

    def move(number, role, out):
        slot = number * 4 + role
        return pltpu.make_async_copy(
            stage.at[slot], out.at[pl.ds((role % 2) * blocks, blocks)], osem.at[slot]
        )

    def one(role, number, side, start):
        left = xt[pl.ds(pl.multiple_of(place[role] * quarter, 16), quarter), :]
        tile = nn(left, ys[side, :, start * LANES : (start + blocks) * LANES]).astype(bf16)
        for n in range(blocks):
            stage[number * 4 + role, n] = tile[:, head(n)]

    for number, (side, start, _) in enumerate(groups):
        if all(side != done for done, _, _ in groups[:number]):
            for copy in right_copies(0, side):
                copy.wait()

        def step(role, carry, number=number, side=side, start=start):
            one(role, number, side, start)

            @pl.when(role < 2)
            def _():
                move(number, role, outs[2 * number]).start()

            @pl.when(role >= 2)
            def _():
                move(number, role, outs[2 * number + 1]).start()

            return carry

        lax.fori_loop(0, 4, step, 0)
    for number in range(len(groups)):
        for role in range(4):
            move(number, role, outs[2 * number + role // 2]).wait()


def weight_gradient(place, lefts, rights, groups):
    batch = len(lefts[0])
    sides = len(rights[0])
    rows, columns = lefts[0][0].shape
    span = rights[0][0][0].shape[1]
    quarter = columns // 4
    blocks = groups[0][2]
    flat_left = [a for section in lefts for a in section]
    flat_right = [a for section in rights for side in section for a in side]
    out = pl.pallas_call(
        functools.partial(weight_body, batch=batch, sides=sides, groups=groups),
        in_specs=[SMEM] + [ANY] * (len(flat_left) + len(flat_right)),
        out_specs=[ANY] * (2 * len(groups)),
        out_shape=[hbm((2 * blocks, quarter, LANES), bf16)] * (2 * len(groups)),
        scratch_shapes=[
            pltpu.VMEM((batch * rows, columns), bf16),
            pltpu.VMEM((columns, batch * rows), bf16),
            pltpu.VMEM((sides, batch * rows, span), bf16),
            pltpu.VMEM((4 * len(groups), blocks, quarter, LANES), bf16),
            pltpu.SemaphoreType.DMA((batch,)),
            pltpu.SemaphoreType.DMA((sides, batch)),
            pltpu.SemaphoreType.DMA((4 * len(groups),)),
        ],
        compiler_params=params(24),
        cost_estimate=pl.CostEstimate(
            flops=2 * batch * rows * columns * sides * span,
            bytes_accessed=2 * columns * sides * span,
            transcendentals=0,
        ),
        name="weight_gradient",
    )(place, *far_away(*flat_left, *flat_right))
    return [(out[2 * n], out[2 * n + 1]) for n in range(len(groups))]


def settle_body(edge, outer, inner, *rest):
    out = rest[-1]

    @pl.when(edge[0] == 1)
    def _():
        for n in range(outer.shape[0]):
            out[:, head(n)] = outer[n].astype(f32)

    @pl.when(edge[0] == 0)
    def _():
        for n in range(inner.shape[0]):
            out[:, head(n)] = inner[n].astype(f32)


def settle(edge, outer, inner, total, held, number):
    blocks, quarter, _ = outer.shape
    more = [] if held is None else [held]
    return pl.pallas_call(
        settle_body,
        grid=(1,),
        in_specs=[SMEM, whole(outer.shape), whole(inner.shape)] + [ANY] * len(more),
        out_specs=pl.BlockSpec((quarter, blocks * LANES), lambda j: (0, number)),
        out_shape=hbm((quarter, total), f32),
        input_output_aliases={3: 0} if more else {},
        compiler_params=params(8),
        name="settle",
    )(edge, outer, inner, *more)


def add(a, b):
    return (a.astype(f32) + b.astype(f32)).astype(bf16)


def state_factors(slopes, forward):
    if lax.axis_size("seq") != 4:
        return jnp.stack([jnp.ones_like(slopes), jnp.zeros_like(slopes)])
    place = lax.axis_index("seq")
    second = (place % 2 == 1) if forward else (place % 2 == 0)
    decay = jnp.exp(-slopes * BLK)
    one = jnp.ones_like(slopes)
    return jnp.stack([jnp.where(second, decay, one), jnp.where(second, one, 0.0 * one)])


def join_factors(slopes, forward):
    place = lax.axis_index("seq")
    second = (place % 2 == 1) if forward else (place % 2 == 0)
    decay = jnp.exp(-slopes * BLK)
    one = jnp.ones_like(slopes)
    return jnp.stack([jnp.where(second, one, decay), jnp.where(second, decay, one)])


def entering_parts(own, slopes, factors, forward):
    count = lax.axis_size("seq")
    if count != 4:
        place = lax.axis_index("seq")
        gathered = lax.all_gather(own, "seq").astype(f32)
        device = jnp.arange(count)
        distance = place - 1 - device if forward else device - place - 1
        power = jnp.maximum(distance, 0).astype(f32) * BLK
        weight = jnp.where(distance[:, None] >= 0, jnp.exp(-slopes[None] * power[:, None]), 0.0)
        state = jnp.sum(weight[:, :, None, None] * gathered, axis=0).astype(bf16)
        return (state, state), state
    near = lax.ppermute(own, "seq", [(0, 1), (1, 0), (2, 3), (3, 2)])
    mine, other = factors[0][:, None, None], factors[1][:, None, None]
    joined = (mine * own.astype(f32) + other * near.astype(f32)).astype(bf16)
    far = lax.ppermute(joined, "seq", [(0, 2), (1, 3)] if forward else [(2, 0), (3, 1)])
    return (far, near), joined


class Sums:
    def __init__(self, edge, settled):
        self.edge = edge
        self.settled = settled
        self.waiting, self.parts, self.partial, self.across = [], [], [], []
        self.previous = None
        self.step = 0
        self.marks = []
        self.written = None

    def load(self, chunks):
        for given, kept in chunks:
            blocks = given.shape[0] // 2
            taken = lax.ppermute(given, "seq", [(0, 1), (1, 0), (2, 3), (3, 2)])
            self.waiting.append(
                (add(kept[:blocks], taken[:blocks]), add(kept[blocks:], taken[blocks:]))
            )

    def over_y(self):
        if not self.waiting:
            return
        far, own = self.waiting.pop(0)
        if self.previous is not None:
            far, _ = lax.optimization_barrier((far, self.previous))
        self.marks.append(far)
        self.previous = lax.ppermute(far, "seq", [(0, 2), (2, 0), (1, 3), (3, 1)])
        self.parts.append(add(own, self.previous))

    def over_z(self, last=False):
        step, count = self.step, len(self.parts)
        if step >= count + 2 or (step >= count and not last):
            return False
        part = self.parts[step] if step < count else None
        done = None
        if step >= 2:
            done = self.partial[step - 2].astype(f32) + self.across[step - 2].astype(f32)
        if part is not None and self.written is not None:
            part, _ = lax.optimization_barrier((part, self.written))
            self.written = None
        if 1 <= step <= count:
            self.marks.append(self.partial[step - 1])
            self.across.append(lax.ppermute(self.partial[step - 1], "dp", [(1, 2), (2, 1)]))
        if part is not None and done is not None and part.shape == done.shape:
            sent = jnp.where(self.edge, part.astype(f32), done).astype(bf16)
            self.marks.append(sent)
            got = lax.ppermute(sent, "dp", [(0, 1), (1, 0), (2, 3), (3, 2)])
            self.partial.append(add(part, got))
            self.written = self.settled(got, sent)
        else:
            if part is not None:
                self.marks.append(part)
                self.partial.append(add(part, lax.ppermute(part, "dp", [(0, 1), (3, 2)])))
            if done is not None:
                done = done.astype(bf16)
                self.marks.append(done)
                self.written = self.settled(lax.ppermute(done, "dp", [(1, 0), (2, 3)]), done)
        self.step += 1
        return True

    def started(self):
        marks, self.marks = self.marks, []
        return marks


def angle_tables(position_row, half_size):
    frequency = jnp.exp(
        jnp.arange(half_size, dtype=jnp.float32) * (-math.log(theta_base) / half_size)
    )
    angles = position_row.astype(jnp.float32)[..., None] * frequency
    cosine = jnp.cos(angles)
    sine_rows = jnp.sin(angles)
    return (
        jnp.concatenate([cosine, cosine], axis=-1),
        jnp.concatenate([-sine_rows, sine_rows], axis=-1),
    )


class Order:
    def __init__(self):
        self.last = []

    def after(self, value):
        if self.last:
            value = lax.optimization_barrier((value, *self.last))[0]
        return value

    def at(self, *values):
        self.last = list(values)


def first_half(order, x, shared, cosine, sine, w):
    h1, r1, pre, qk, state = project(order.after(shared[0]), x, cosine, sine, w)
    entering, joined = entering_parts(state, shared[0], shared[3], True)
    order.at(r1, joined)
    return dict(x=x, h1=h1, r1=r1, pre=pre, qk=qk), entering


def second_half(order, record, entering, shared, wo, wi, wd):
    mixed, gated, ra, h2, r2, low, g, up, product, y = finish(
        order.after(shared[0]), shared[1], record["x"], record["qk"], record["pre"], entering,
        wo, wi, wd,
    )
    order.at(ra)
    record.update(
        mixed=mixed, gated=gated, ra=ra, h2=h2, r2=r2, low=low, g=g, up=up, product=product
    )
    return y


def back_first(order, dy, record, shared, cosine, sine, wo, wi, wd):
    dg, dup, dmid, dm, dq, du, dk, dv, state = back_channel(
        order.after(shared[0]), dy, record, cosine, sine, wo, wi, wd
    )
    entering, joined = entering_parts(state, shared[0], shared[4], False)
    order.at(dm, joined)
    record.update(dy=dy, dg=dg, dup=dup, dmid=dmid, dm=dm, dq=dq, du=du, dk=dk, dv=dv)
    return entering


def back_second(order, record, entering, shared, cosine, sine, w):
    dkp, dvp, dx = back_mixer(
        order.after(shared[0]), shared[2], record, entering, cosine, sine, w
    )
    order.at(dkp)
    record.update(dkp=dkp, dvp=dvp)
    return dx


def per_device(boundary, positions, decay_exp, mixer_in, mixer_out, channel_in, channel_out):
    section = lax.axis_index("section")
    is_first = section == 0
    own = boundary[0]
    batch, rows, width = own.shape
    assert rows == BLK
    slopes = jnp.exp2(-0.5 * decay_exp[0].astype(jnp.float32))
    w, wo, wi, wd = mixer_in[0], mixer_out[0], channel_in[0], channel_out[0]
    hidden = wd.shape[0]
    half_size = width // HEADS // 2
    cosine, sine = angle_tables(positions, half_size)
    every = range(batch)
    usual = lax.axis_size("seq") == 4 and lax.axis_size("dp") == 4

    place, line = lax.axis_index("seq"), lax.axis_index("dp")
    core, y_place = place % 2, place // 2
    roles = [
        2 * (1 - y_place) + 1 - core,
        2 * y_place + 1 - core,
        2 * (1 - y_place) + core,
        2 * y_place + core,
    ]
    if not usual:
        roles = [0, 1, 2, 3]
    roles = jnp.stack([jnp.asarray(r, jnp.int32) for r in (*roles, section)])
    edge = (line == 0) | (line == lax.axis_size("dp") - 1)
    flag = edge.astype(jnp.int32)[None]
    shared = [
        slopes, state_factors(slopes, True), state_factors(slopes, False),
        join_factors(slopes, True), join_factors(slopes, False),
    ]
    own, roles, flag, *shared = lax.optimization_barrier((own, roles, flag, *shared))
    edge = flag[0] == 1
    order = Order()

    early, states = [None] * batch, [None] * batch
    for b in every:
        early[b], states[b] = first_half(order, own[b], shared, cosine[b], sine[b], w)
    arrived = []
    for b in every:
        y = second_half(order, early[b], states[b], shared, wo, wi, wd)
        arrived.append(lax.ppermute(y, "section", [(0, 1)]))
    late = [None] * batch
    for b in every:
        late[b], states[b] = first_half(order, arrived[b], shared, cosine[b], sine[b], w)
    outputs, later = [None] * batch, [None] * batch
    for b in every:
        outputs[b] = second_half(order, late[b], states[b], shared, wo, wi, wd)
        later[b] = back_first(order, own[b], late[b], shared, cosine[b], sine[b], wo, wi, wd)
    returned = []
    for b in every:
        dx = back_second(order, late[b], later[b], shared, cosine[b], sine[b], w)
        returned.append(lax.ppermute(dx, "section", [(1, 0)]))

    def operands(*names):
        return [[[r[name] for r in records] for name in names] for records in (early, late)]

    chunks = []
    spans = [(3, width), (3, width)] + [(2, 2 * hidden)] * 4 + [(1, width)] + [(0, 4 * width)] * 4
    numbers = [0, 1, 0, 1, 2, 3, 0, 0, 1, 2, 3]
    held = [None] * 4
    finished = []

    def settled(outer, inner):
        number = len(finished)
        index, total = spans[number]
        blocks, quarter = chunks[number][0].shape[0] // 2, chunks[number][0].shape[1]
        shape = (blocks, quarter, LANES)
        finished.append(number)
        held[index] = settle(
            flag, outer.reshape(shape), inner.reshape(shape), total, held[index], numbers[number]
        )
        return held[index]

    sums = Sums(edge, settled)

    def even(array):
        return array.reshape(array.shape[0] * array.shape[1] // 256, 256, LANES)

    def gradient(name, names, groups):
        left = [side[0] for side in operands(name)]
        found = weight_gradient(order.after(roles), left, operands(*names), groups)
        order.at(found[-1][1])
        chunks.extend(found)
        if usual:
            sums.load([(even(given), even(kept)) for given, kept in found])

    def move(*what):
        if not usual:
            return
        for way in what:
            way()
        order.at(*order.last, *sums.started())

    def first(b):
        return back_first(order, returned[b], early[b], shared, cosine[b], sine[b], wo, wi, wd)

    def second(b):
        return back_second(order, early[b], later[b], shared, cosine[b], sine[b], w)

    later = [first(b) for b in every[:-1]]
    for b in every:
        early[b]["dy"] = returned[b]
    gradient("product", ("dy",), [(0, 0, 4), (0, 4, 4)])
    move(sums.over_y)
    later.append(first(batch - 1))
    move(sums.over_y, sums.over_z)
    half = hidden // LANES // 2
    gradient("h2", ("dg", "dup"), [(0, 0, half), (0, half, half), (1, 0, half), (1, half, half)])
    move(sums.over_y, sums.over_z)
    dx = [second(b) for b in every]
    move(sums.over_y, sums.over_z)
    eight = width // LANES
    gradient("gated", ("dm",), [(0, 0, eight)])
    gradient("h1", ("dq", "dkp", "dvp", "du"), [(s, 0, eight) for s in range(4)])
    joined = jnp.where(is_first, jnp.stack(dx), jnp.stack(outputs))[None]
    if usual:
        while sums.waiting:
            move(sums.over_y, sums.over_z)
        while sums.over_z(last=True):
            pass
        return (joined, *(h[None] for h in held))
    found = [[], [], [], []]
    for (index, total), chunk in zip(spans, chunks):
        chunk = jnp.concatenate(chunk)
        blocks, quarter = chunk.shape[0] // 4, chunk.shape[1]
        rows_first = chunk.reshape(4, blocks, quarter, LANES).transpose(0, 2, 1, 3)
        found[index].append(rows_first.reshape(4 * quarter, blocks * LANES))
    summed = []
    for pieces in found:
        part = lax.psum_scatter(
            jnp.concatenate(pieces, axis=1), "seq", scatter_dimension=0, tiled=True
        )
        summed.append(lax.psum(part, "dp").astype(f32)[None])
    return (joined, *summed)


def solution(mesh):
    in_specs = (
        P("section", "dp", "seq", None),
        P("dp", "seq"),
        P("section", None),
        P("section", None, None),
        P("section", None, None),
        P("section", None, None),
        P("section", None, None),
    )
    out_specs = (
        P("section", "dp", "seq", None),
        P("section", "seq", None),
        P("section", "seq", None),
        P("section", "seq", None),
        P("section", "seq", None),
    )
    return jax.shard_map(
        per_device, mesh=mesh, in_specs=in_specs, out_specs=out_specs, check_vma=False
    )
```

time: 688 us -> 545 us (0.79)
  Pallas kernels: 327 us -> 233 us
  other arithmetic: 40 us -> 24.1 us
  local copies, waits for them, and re-layouts: 34.1 us -> 19.9 us
  starting transfers between devices: 129 us -> 120 us
  waiting for transfers between devices: 142 us -> 135 us
    pallas_call x16, Pallas kernels: 267 us -> 181 us  [the longest x4 65.7 us: back_channel(): pl.pallas_call(back_channel_body, in_specs=[SMEM] + [ANY] + [VMEM] * 3 +...]
    slice x13 -> x2, local copies, waits for them, and re-layouts: 19.1 us -> 1.63 us  [load(): kept[blocks:]]
    ppermute x64, starting transfers between devices: 119 us -> 104 us  [the longest x7 29.6 us: over_z(): got = lax.ppermute(sent, 'dp', [(0, 1), (1, 0), (2, 3), (3, 2)])]
    pallas_call x11, Pallas kernels: 26.8 us -> 13.1 us  [settle(): pl.pallas_call(settle_body, grid=(1,), in_specs=[SMEM, whole(outer.shape)...]
    convert_element_type x26 -> x32, other arithmetic: 19.5 us -> 7.48 us  [add(): return (a.astype(f32) + b.astype(f32)).astype(bf16)]
    ppermute x2, starting transfers between devices: 2.73 us -> 11.2 us  [per_device(): returned.append(lax.ppermute(dx, 'section', [(1, 0)]))]
    unnamed x112 -> x90, local copies, waits for them, and re-layouts: 11 us -> 15.9 us
  transfers between devices with their start and end apart: 68 -> 68, of which waited for: 23 -> 27; matrix products, arithmetic and copies ran while one was open for 8% -> 4% of each run, Pallas kernels for 44% -> 22%
where the time goes in v2:
time: 545 us; the launch traced here: 535 us
  Pallas kernels  233 us (43%)
  waiting for transfers between devices  135 us (25%)
  starting transfers between devices  120 us (22%)
  other arithmetic  24.1 us (4%)
  local copies, waits for them, and re-layouts  19.9 us (4%)
    pallas_call x4, Pallas kernels, back_channel(): pl.pallas_call(back_channel_body, in_specs=[SMEM] + [ANY] + [VMEM] * 3 +...  65.7 us
    pallas_call x4, Pallas kernels, finish(): pl.pallas_call(finish_body, in_specs=[SMEM] * 2 + [ANY] * 5 + [VMEM] * 3,...  51.6 us
    pallas_call x4, Pallas kernels, weight_gradient(): pl.pallas_call(functools.partial(weight_body, batch=batch, sides=sides, g...  39.3 us
    ppermute x7, waiting for transfers between devices, over_z(): got = lax.ppermute(sent, 'dp', [(0, 1), (1, 0), (2, 3), (3, 2)])  37.3 us
    pallas_call x4, Pallas kernels, project(): pl.pallas_call(project_body, in_specs=[SMEM] + [ANY] * 3 + [VMEM], out_sp...  33.5 us
    pallas_call x4, Pallas kernels, back_mixer(): pl.pallas_call(back_mixer_body, in_specs=[SMEM] * 2 + [ANY] * 13 + [VMEM]...  30.3 us
    ppermute x8, waiting for transfers between devices, entering_parts(): lax.ppermute(joined, 'seq', [(0, 2), (1, 3)] if forward else [(2, 0), (3,...  29.7 us
    ppermute x7, starting transfers between devices, over_z(): got = lax.ppermute(sent, 'dp', [(0, 1), (1, 0), (2, 3), (3, 2)])  29.6 us
  transfers between devices with their start and end apart: 68, of which 27 were waited for; matrix products, arithmetic and copies ran while one was open for 4% of the time, Pallas kernels for 22%

profile of v2, /device:TPU:0, one launch (start us, length us, event | category | flops | bytes accessed | tf_op | source)
XLA Modules:
  0.0 535.3 jit_solution(9173012226454494289)
XLA Ops:
  9.6 8.5 %project.4 = (bf16[256,1024]{1,0:T(8,128)(2,1)}, f32[256,128]{1,0:T(8,128)}, bf16[256,4096]{1,0:T(8,128)(2,1)}, bf16[256,2048]{1,0:T(8,128)(2,1)}, bf16[8,128,128]{2,1,0:T(8,128)(2,1)}) custom-call(f32[8]{0:T(128)S(1)} %get-tuple-element.302.slope, bf16[256,1024]{1,0:T(8,128)(2,1)} %get-tuple-element.362.x.dy.refs_7_, f32[256,128]{1,0:T(8,128)} %get-tuple-element.384.cosine, ...), custom_call_target="tpu_custom_call" | custom-call | flops 2147483648 | bytes 8388608 | tf_op jit(solution)/shard_map/project/pallas_call | solution.py:169
  24.6 8.5 %project.5 = (bf16[256,1024]{1,0:T(8,128)(2,1)}, f32[256,128]{1,0:T(8,128)}, bf16[256,4096]{1,0:T(8,128)(2,1)}, bf16[256,2048]{1,0:T(8,128)(2,1)}, bf16[8,128,128]{2,1,0:T(8,128)(2,1)}) custom-call(f32[8]{0:T(128)S(1)} %get-tuple-element.302.slope, bf16[256,1024]{1,0:T(8,128)(2,1)} %get-tuple-element.361.x.dy.refs_8_, f32[256,128]{1,0:T(8,128)} %get-tuple-element.385.cosine, ...), custom_call_target="tpu_custom_call" | custom-call | flops 2147483648 | bytes 8388608 | tf_op jit(solution)/shard_map/project/pallas_call | solution.py:169
  45.4 13.1 %finish.4 = (bf16[256,1024]{1,0:T(8,128)(2,1)}, bf16[256,1024]{1,0:T(8,128)(2,1)}, f32[256,128]{1,0:T(8,128)}, bf16[256,1024]{1,0:T(8,128)(2,1)}, f32[256,128]{1...) custom-call(f32[8]{0:T(128)S(1)} %get-tuple-element.302.slope, ...), custom_call_target="tpu_custom_call" | custom-call | flops 4966055936 | bytes 19398656 | tf_op jit(solution)/shard_map/finish/pallas_call | solution.py:323
  62.7 12.9 %finish.5 = (bf16[256,1024]{1,0:T(8,128)(2,1)}, bf16[256,1024]{1,0:T(8,128)(2,1)}, f32[256,128]{1,0:T(8,128)}, bf16[256,1024]{1,0:T(8,128)(2,1)}, f32[256,128]{1...) custom-call(f32[8]{0:T(128)S(1)} %get-tuple-element.302.slope, ...), custom_call_target="tpu_custom_call" | custom-call | flops 4966055936 | bytes 19398656 | tf_op jit(solution)/shard_map/finish/pallas_call | solution.py:323
  77.7 8.2 %project.6 = (bf16[256,1024]{1,0:T(8,128)(2,1)}, f32[256,128]{1,0:T(8,128)}, bf16[256,4096]{1,0:T(8,128)(2,1)}, bf16[256,2048]{1,0:T(8,128)(2,1)}, bf16[8,128,128]{2,1,0:T(8,128)(2,1)}) custom-call(f32[8]{0:T(128)S(1)} %get-tuple-element.302.slope, bf16[256,1024]{1,0:T(8,128)(2,1)} %copy-done.6, f32[256,128]{1,0:T(8,128)} %get-tuple-element.384.cosine, ...), custom_call_target="tpu_custom_call" | custom-call | flops 2147483648 | bytes 8388608 | tf_op jit(solution)/shard_map/project/pallas_call | solution.py:169
  89.8 8.2 %project.7 = (bf16[256,1024]{1,0:T(8,128)(2,1)}, f32[256,128]{1,0:T(8,128)}, bf16[256,4096]{1,0:T(8,128)(2,1)}, bf16[256,2048]{1,0:T(8,128)(2,1)}, bf16[8,128,128]{2,1,0:T(8,128)(2,1)}) custom-call(f32[8]{0:T(128)S(1)} %get-tuple-element.302.slope, bf16[256,1024]{1,0:T(8,128)(2,1)} %copy-done.5, f32[256,128]{1,0:T(8,128)} %get-tuple-element.385.cosine, ...), custom_call_target="tpu_custom_call" | custom-call | flops 2147483648 | bytes 8388608 | tf_op jit(solution)/shard_map/project/pallas_call | solution.py:169
  109.5 12.8 %finish.6 = (bf16[256,1024]{1,0:T(8,128)(2,1)}, bf16[256,1024]{1,0:T(8,128)(2,1)}, f32[256,128]{1,0:T(8,128)}, bf16[256,1024]{1,0:T(8,128)(2,1)}, f32[256,128]{1...) custom-call(f32[8]{0:T(128)S(1)} %get-tuple-element.302.slope, ...), custom_call_target="tpu_custom_call" | custom-call | flops 4966055936 | bytes 19398656 | tf_op jit(solution)/shard_map/finish/pallas_call | solution.py:323
  122.3 16.4 %back_channel.4 = (bf16[256,2816]{1,0:T(8,128)(2,1)}, bf16[256,2816]{1,0:T(8,128)(2,1)}, f32[256,1024]{1,0:T(8,128)}, bf16[256,1024]{1,0:T(8,128)(2,1)}, bf16[25...) custom-call(f32[8]{0:T(128)S(1)} %get-tuple-element.302.slope, ...), custom_call_target="tpu_custom_call" | custom-call | flops 4966055936 | bytes 19398656 | tf_op jit(solution)/shard_map/back_channel/pallas_call | solution.py:481
  150.1 12.8 %finish.7 = (bf16[256,1024]{1,0:T(8,128)(2,1)}, bf16[256,1024]{1,0:T(8,128)(2,1)}, f32[256,128]{1,0:T(8,128)}, bf16[256,1024]{1,0:T(8,128)(2,1)}, f32[256,128]{1...) custom-call(f32[8]{0:T(128)S(1)} %get-tuple-element.302.slope, ...), custom_call_target="tpu_custom_call" | custom-call | flops 4966055936 | bytes 19398656 | tf_op jit(solution)/shard_map/finish/pallas_call | solution.py:323
  162.9 16.4 %back_channel.5 = (bf16[256,2816]{1,0:T(8,128)(2,1)}, bf16[256,2816]{1,0:T(8,128)(2,1)}, f32[256,1024]{1,0:T(8,128)}, bf16[256,1024]{1,0:T(8,128)(2,1)}, bf16[25...) custom-call(f32[8]{0:T(128)S(1)} %get-tuple-element.302.slope, ...), custom_call_target="tpu_custom_call" | custom-call | flops 4966055936 | bytes 19398656 | tf_op jit(solution)/shard_map/back_channel/pallas_call | solution.py:481
  182.4 7.8 %collective-permute-done.12.far = bf16[8,128,128]{2,1,0:T(8,128)(2,1)S(1)} collective-permute-done((bf16[8,128,128]{2,1,0:T(8,128)(2,1)S(1)}, bf16[8,128,128]{2,1,0:T(8,128)(2,1)S(1)}, u32[]{:S(2)}, u32[]{:S(2)}) %collective-permute-start.12) | collective-permute-done | bytes 262176 | tf_op jit(solution)/shard_map/ppermute | solution.py:788
  190.8 7.6 %back_mixer.4 = (bf16[256,1024]{1,0:T(8,128)(2,1)}, bf16[256,1024]{1,0:T(8,128)(2,1)}, bf16[256,1024]{1,0:T(8,128)(2,1)}) custom-call(f32[8]{0:T(128)S(1)} %get-tuple-element.302.slope, f32[2,8]{1,0:T(2,128)S(1)} %get-tuple-element.234.factors, bf16[256,1024]{1,0:T(8,128)(2,1)} %get-tuple-element.235.dq.refs_13_, ...), custom_call_target="tpu_custom_call" | custom-call | flops 2147483648 | bytes 8388608 | tf_op jit(solution)/shard_map/back_mixer/pallas_call | solution.py:579
  201.0 8.6 %collective-permute-done.13.far = bf16[8,128,128]{2,1,0:T(8,128)(2,1)S(1)} collective-permute-done((bf16[8,128,128]{2,1,0:T(8,128)(2,1)S(1)}, bf16[8,128,128]{2,1,0:T(8,128)(2,1)S(1)}, u32[]{:S(2)}, u32[]{:S(2)}) %collective-permute-start.13) | collective-permute-done | bytes 262176 | tf_op jit(solution)/shard_map/ppermute | solution.py:788
  210.4 7.6 %back_mixer.5 = (bf16[256,1024]{1,0:T(8,128)(2,1)}, bf16[256,1024]{1,0:T(8,128)(2,1)}, bf16[256,1024]{1,0:T(8,128)(2,1)}) custom-call(f32[8]{0:T(128)S(1)} %get-tuple-element.302.slope, f32[2,8]{1,0:T(2,128)S(1)} %get-tuple-element.234.factors, bf16[256,1024]{1,0:T(8,128)(2,1)} %get-tuple-element.243.dq.refs_14_, ...), custom_call_target="tpu_custom_call" | custom-call | flops 2147483648 | bytes 8388608 | tf_op jit(solution)/shard_map/back_mixer/pallas_call | solution.py:579
  217.9 9.9 %collective-permute-start.16 = (bf16[256,1024]{1,0:T(8,128)(2,1)}, bf16[256,1024]{1,0:T(8,128)(2,1)S(1)}, u32[]{:S(2)}, u32[]{:S(2)}) collective-permute-start(bf16[256,1024]{1,0:T(8,128)(2,1)} %get-tuple-element.265), channel_id=1, source_target_pairs={{16,0},{17,1},{18,2},{19,3},{20,4},{21,5},{22,6},{23,7},{24,8},{25... | collective-permute-start | bytes 1572872 | tf_op jit(solution)/shard_map/ppermute | solution.py:972
  228.6 16.4 %back_channel.6 = (bf16[256,2816]{1,0:T(8,128)(2,1)}, bf16[256,2816]{1,0:T(8,128)(2,1)}, f32[256,1024]{1,0:T(8,128)}, bf16[256,1024]{1,0:T(8,128)(2,1)}, bf16[25...) custom-call(f32[8]{0:T(128)S(1)} %get-tuple-element.302.slope, ...), custom_call_target="tpu_custom_call" | custom-call | flops 4966055936 | bytes 19398656 | tf_op jit(solution)/shard_map/back_channel/pallas_call | solution.py:481
  248.9 8.6 %weight_gradient.4 = (bf16[8,704,128]{2,1,0:T(8,128)(2,1)}, bf16[8,704,128]{2,1,0:T(8,128)(2,1)}, bf16[8,704,128]{2,1,0:T(8,128)(2,1)}, bf16[8,704,128]{2,1,0:T(8,128)(2,1)}) custom-call(s32[5]{0:T(128)S(1)} %stack.61.refs_0_, bf16[256,2816]{1,0:T(8,128)(2,1)} %get-tuple-element.261.refs_1_, bf16[256,2816]{1,0:T(8,128)(2,1)} %get-tuple-element.262.refs_2_, ...), custom_call_target="tpu_custom_call" | custom-call | flops 2952790016 | bytes 5767168 | tf_op jit(solution)/shard_map/weight_gradient/pallas_call | solution.py:698
  261.2 16.5 %back_channel.7 = (bf16[256,2816]{1,0:T(8,128)(2,1)}, bf16[256,2816]{1,0:T(8,128)(2,1)}, f32[256,1024]{1,0:T(8,128)}, bf16[256,1024]{1,0:T(8,128)(2,1)}, bf16[25...) custom-call(f32[8]{0:T(128)S(1)} %get-tuple-element.302.slope, ...), custom_call_target="tpu_custom_call" | custom-call | flops 4966055936 | bytes 19398656 | tf_op jit(solution)/shard_map/back_channel/pallas_call | solution.py:481
  280.3 14.1 %weight_gradient.5 = (bf16[22,256,128]{2,1,0:T(8,128)(2,1)}, bf16[22,256,128]{2,1,0:T(8,128)(2,1)}, bf16[22,256,128]{2,1,0:T(8,128)(2,1)}, bf16[22,256,128]{2,1,...) custom-call(s32[5]{0:T(128)S(1)} %stack.61.refs_0_, ...), custom_call_target="tpu_custom_call" | custom-call | flops 5905580032 | bytes 11534336 | tf_op jit(solution)/shard_map/weight_gradient/pallas_call | solution.py:698
  302.0 11.4 %collective-permute-done.22 = bf16[11,256,128]{2,1,0:T(8,128)(2,1)S(1)} collective-permute-done((bf16[11,256,128]{2,1,0:T(8,128)(2,1)S(1)}, bf16[11,256,128]{2,1,0:T(8,128)(2,1)S(1)}, u32[]{:S(2)}, u32[]{:S(2)}) %collective-permute-start.22) | collective-permute-done | bytes 720928 | tf_op jit(solution)/shard_map/ppermute | solution.py:817
  317.1 7.5 %collective-permute-start.28 = (bf16[11,256,128]{2,1,0:T(8,128)(2,1)S(1)}, bf16[11,256,128]{2,1,0:T(8,128)(2,1)S(1)}, u32[]{:S(2)}, u32[]{:S(2)}) collective-permute-start(bf16[11,256,128]{2,1,0:T(8,128)(2,1)S(1)} %add_convert_fusion.14), channel_id=1, source_target_pairs={{0,1},{3,2},{4,5},{7,6},{8,9},{11,10},{12,13},{15,14},{16,17},{19,... | collective-permute-start | bytes 2162696 | tf_op jit(solution)/shard_map/ppermute | solution.py:843
  333.1 7.5 %collective-permute-done.28 = bf16[11,256,128]{2,1,0:T(8,128)(2,1)S(1)} collective-permute-done((bf16[11,256,128]{2,1,0:T(8,128)(2,1)S(1)}, bf16[11,256,128]{2,1,0:T(8,128)(2,1)S(1)}, u32[]{:S(2)}, u32[]{:S(2)}) %collective-permute-start.28) | collective-permute-done | bytes 720928 | tf_op jit(solution)/shard_map/ppermute | solution.py:843
  344.0 7.6 %back_mixer.6 = (bf16[256,1024]{1,0:T(8,128)(2,1)}, bf16[256,1024]{1,0:T(8,128)(2,1)}, bf16[256,1024]{1,0:T(8,128)(2,1)}) custom-call(f32[8]{0:T(128)S(1)} %get-tuple-element.302.slope, f32[2,8]{1,0:T(2,128)S(1)} %get-tuple-element.234.factors, bf16[256,1024]{1,0:T(8,128)(2,1)} %get-tuple-element.294.dq.refs_5_, ...), custom_call_target="tpu_custom_call" | custom-call | flops 2147483648 | bytes 8388608 | tf_op jit(solution)/shard_map/back_mixer/pallas_call | solution.py:579
  365.1 7.6 %back_mixer.7 = (bf16[256,1024]{1,0:T(8,128)(2,1)}, bf16[256,1024]{1,0:T(8,128)(2,1)}, bf16[256,1024]{1,0:T(8,128)(2,1)}) custom-call(f32[8]{0:T(128)S(1)} %get-tuple-element.302.slope, f32[2,8]{1,0:T(2,128)S(1)} %get-tuple-element.234.factors, bf16[256,1024]{1,0:T(8,128)(2,1)} %get-tuple-element.303.dq.refs_6_, ...), custom_call_target="tpu_custom_call" | custom-call | flops 2147483648 | bytes 8388608 | tf_op jit(solution)/shard_map/back_mixer/pallas_call | solution.py:579
  382.8 11.7 %weight_gradient.7 = (bf16[16,256,128]{2,1,0:T(8,128)(2,1)}, bf16[16,256,128]{2,1,0:T(8,128)(2,1)}, bf16[16,256,128]{2,1,0:T(8,128)(2,1)}, bf16[16,256,128]{2,1,...) custom-call(s32[5]{0:T(128)S(1)} %stack.61.refs_0_, ...), custom_call_target="tpu_custom_call" | custom-call | flops 4294967296 | bytes 8388608 | tf_op jit(solution)/shard_map/weight_gradient/pallas_call | solution.py:698
  403.3 15.4 %collective-permute-start.51 = (bf16[11,256,128]{2,1,0:T(8,128)(2,1)S(1)}, bf16[11,256,128]{2,1,0:T(8,128)(2,1)S(1)}, u32[]{:S(2)}, u32[]{:S(2)}) collective-permute-start(bf16[11,256,128]{2,1,0:T(8,128)(2,1)S(1)} %fusion.6.inner), channel_id=1, source_target_pairs={{0,1},{1,0},{2,3},{3,2},{4,5},{5,4},{6,7},{7,6},{8,9},{9,8},{10,11... | collective-permute-start | bytes 2162696 | tf_op jit(solution)/shard_map/ppermute | solution.py:837
  422.5 11.6 %collective-permute-done.51.outer = bf16[11,256,128]{2,1,0:T(8,128)(2,1)S(1)} collective-permute-done((bf16[11,256,128]{2,1,0:T(8,128)(2,1)S(1)}, bf16[11,256,128]{2,1,0:T(8,128)(2,1)S(1)}, u32[]{:S(2)}, u32[]{:S(2)}) %collective-permute-start.51) | collective-permute-done | bytes 720928 | tf_op jit(solution)/shard_map/ppermute | solution.py:837
  436.6 6.4 %collective-permute-start.56 = (bf16[8,256,128]{2,1,0:T(8,128)(2,1)S(1)}, bf16[8,256,128]{2,1,0:T(8,128)(2,1)S(1)}, u32[]{:S(2)}, u32[]{:S(2)}) collective-permute-start(bf16[8,256,128]{2,1,0:T(8,128)(2,1)S(1)} %add_convert_fusion.24), channel_id=1, source_target_pairs={{0,1},{3,2},{4,5},{7,6},{8,9},{11,10},{12,13},{15,14},{16,17},{19,... | collective-permute-start | bytes 1572872 | tf_op jit(solution)/shard_map/ppermute | solution.py:843
  476.3 6.7 %collective-permute-done.58.outer = bf16[8,256,128]{2,1,0:T(8,128)(2,1)S(1)} collective-permute-done((bf16[8,256,128]{2,1,0:T(8,128)(2,1)S(1)}, bf16[8,256,128]{2,1,0:T(8,128)(2,1)S(1)}, u32[]{:S(2)}, u32[]{:S(2)}) %collective-permute-start.58) | collective-permute-done | bytes 524320 | tf_op jit(solution)/shard_map/ppermute | solution.py:837
  487.4 7.4 %collective-permute-done.61.outer = bf16[8,256,128]{2,1,0:T(8,128)(2,1)S(1)} collective-permute-done((bf16[8,256,128]{2,1,0:T(8,128)(2,1)S(1)}, bf16[8,256,128]{2,1,0:T(8,128)(2,1)S(1)}, u32[]{:S(2)}, u32[]{:S(2)}) %collective-permute-start.61) | collective-permute-done | bytes 524320 | tf_op jit(solution)/shard_map/ppermute | solution.py:837
  513.3 12.3 %collective-permute-done.67.outer = bf16[8,256,128]{2,1,0:T(8,128)(2,1)S(1)} collective-permute-done((bf16[8,256,128]{2,1,0:T(8,128)(2,1)S(1)}, bf16[8,256,128]{2,1,0:T(8,128)(2,1)S(1)}, u32[]{:S(2)}, u32[]{:S(2)}) %collective-permute-start.67) | collective-permute-done | bytes 524320 | tf_op jit(solution)/shard_map/ppermute | solution.py:847
  526.7 7.1 %collective-permute-done.65.outer = bf16[8,256,128]{2,1,0:T(8,128)(2,1)S(1)} collective-permute-done((bf16[8,256,128]{2,1,0:T(8,128)(2,1)S(1)}, bf16[8,256,128]{2,1,0:T(8,128)(2,1)S(1)}, u32[]{:S(2)}, u32[]{:S(2)}) %collective-permute-start.65) | collective-permute-done | bytes 524320 | tf_op jit(solution)/shard_map/ppermute | solution.py:847
  (292 shorter events, 198.0 us)
Async XLA Ops:
  39.3 22.7 %collective-permute-start.3 = (bf16[8,128,128]{2,1,0:T(8,128)(2,1)S(1)}, bf16[8,128,128]{2,1,0:T(8,128)(2,1)S(1)}, u32[]{:S(2)}, u32[]{:S(2)}) collective-permute-start(bf16[8,128,128]{2,1,0:T(8,128)(2,1)S(1)} %add_convert_fusion.43), channel_id=1, source_target_pairs={{0,8},{4,12},{1,9},{5,13},{2,10},{6,14},{3,11},{7,15},{16,24},{20,... | collective-permute-start | bytes 786440 | tf_op jit(solution)/shard_map/ppermute | solution.py:788
  58.6 18.4 %collective-permute-start.4 = (bf16[256,1024]{1,0:T(8,128)(2,1)}, bf16[256,1024]{1,0:T(8,128)(2,1)S(1)}, u32[]{:S(2)}, u32[]{:S(2)}) collective-permute-start(bf16[256,1024]{1,0:T(8,128)(2,1)} %get-tuple-element.199), channel_id=1, source_target_pairs={{0,16},{1,17},{2,18},{3,19},{4,20},{5,21},{6,22},{7,23},{8,24},{9,... | collective-permute-start | bytes 1572872 | tf_op jit(solution)/shard_map/ppermute | solution.py:961
  198.4 29.4 %collective-permute-start.14 = (bf16[256,1024]{1,0:T(8,128)(2,1)}, bf16[256,1024]{1,0:T(8,128)(2,1)S(1)}, u32[]{:S(2)}, u32[]{:S(2)}) collective-permute-start(bf16[256,1024]{1,0:T(8,128)(2,1)} %get-tuple-element.251), channel_id=1, source_target_pairs={{16,0},{17,1},{18,2},{19,3},{20,4},{21,5},{22,6},{23,7},{24,8},{25... | collective-permute-start | bytes 1572872 | tf_op jit(solution)/shard_map/ppermute | solution.py:972
  217.9 30.1 %collective-permute-start.16 = (bf16[256,1024]{1,0:T(8,128)(2,1)}, bf16[256,1024]{1,0:T(8,128)(2,1)S(1)}, u32[]{:S(2)}, u32[]{:S(2)}) collective-permute-start(bf16[256,1024]{1,0:T(8,128)(2,1)} %get-tuple-element.265), channel_id=1, source_target_pairs={{16,0},{17,1},{18,2},{19,3},{20,4},{21,5},{22,6},{23,7},{24,8},{25... | collective-permute-start | bytes 1572872 | tf_op jit(solution)/shard_map/ppermute | solution.py:972
  257.7 20.3 %collective-permute-start.19 = (bf16[22,256,128]{2,1,0:T(8,128)(2,1)}, bf16[22,256,128]{2,1,0:T(8,128)(2,1)S(1)}, u32[]{:S(2)}, u32[]{:S(2)}) collective-permute-start(bf16[22,256,128]{2,1,0:T(8,128)(2,1)} %bitcast.109), channel_id=1, source_target_pairs={{0,4},{4,0},{8,12},{12,8},{1,5},{5,1},{9,13},{13,9},{2,6},{6,2},{1... | collective-permute-start | bytes 4325384 | tf_op jit(solution)/shard_map/ppermute | solution.py:805
  261.2 18.6 %collective-permute-start.20 = (bf16[11,256,128]{2,1,0:T(8,128)(2,1)S(1)}, bf16[11,256,128]{2,1,0:T(8,128)(2,1)S(1)}, u32[]{:S(2)}, u32[]{:S(2)}) collective-permute-start(bf16[11,256,128]{2,1,0:T(8,128)(2,1)S(1)} %fusion.11), channel_id=1, source_target_pairs={{0,8},{8,0},{4,12},{12,4},{1,9},{9,1},{5,13},{13,5},{2,10},{10,2},... | collective-permute-start | bytes 2162696 | tf_op jit(solution)/shard_map/ppermute | solution.py:817
  294.6 30.1 %collective-permute-start.26 = (bf16[22,256,128]{2,1,0:T(8,128)(2,1)}, bf16[22,256,128]{2,1,0:T(8,128)(2,1)S(1)}, u32[]{:S(2)}, u32[]{:S(2)}) collective-permute-start(bf16[22,256,128]{2,1,0:T(8,128)(2,1)} %get-tuple-element.315), channel_id=1, source_target_pairs={{0,4},{4,0},{8,12},{12,8},{1,5},{5,1},{9,13},{13,9},{2,6},{6,2},{1... | collective-permute-start | bytes 4325384 | tf_op jit(solution)/shard_map/ppermute | solution.py:805
  295.0 18.4 %collective-permute-start.22 = (bf16[11,256,128]{2,1,0:T(8,128)(2,1)S(1)}, bf16[11,256,128]{2,1,0:T(8,128)(2,1)S(1)}, u32[]{:S(2)}, u32[]{:S(2)}) collective-permute-start(bf16[11,256,128]{2,1,0:T(8,128)(2,1)S(1)} %fusion.10), channel_id=1, source_target_pairs={{0,8},{8,0},{4,12},{12,4},{1,9},{9,1},{5,13},{13,5},{2,10},{10,2},... | collective-permute-start | bytes 2162696 | tf_op jit(solution)/shard_map/ppermute | solution.py:817
  296.9 18.9 %collective-permute-start.23 = (bf16[11,256,128]{2,1,0:T(8,128)(2,1)S(1)}, bf16[11,256,128]{2,1,0:T(8,128)(2,1)S(1)}, u32[]{:S(2)}, u32[]{:S(2)}) collective-permute-start(bf16[11,256,128]{2,1,0:T(8,128)(2,1)S(1)} %add_convert_fusion.17), channel_id=1, source_target_pairs={{0,1},{3,2},{4,5},{7,6},{8,9},{11,10},{12,13},{15,14},{16,17},{19,... | collective-permute-start | bytes 2162696 | tf_op jit(solution)/shard_map/ppermute | solution.py:843
  313.4 19.1 %collective-permute-start.27 = (bf16[11,256,128]{2,1,0:T(8,128)(2,1)S(1)}, bf16[11,256,128]{2,1,0:T(8,128)(2,1)S(1)}, u32[]{:S(2)}, u32[]{:S(2)}) collective-permute-start(bf16[11,256,128]{2,1,0:T(8,128)(2,1)S(1)} %add_convert_fusion.16), channel_id=1, source_target_pairs={{0,8},{8,0},{4,12},{12,4},{1,9},{9,1},{5,13},{13,5},{2,10},{10,2},... | collective-permute-start | bytes 2162696 | tf_op jit(solution)/shard_map/ppermute | solution.py:817
  316.7 34.9 %collective-permute-start.36 = (bf16[22,256,128]{2,1,0:T(8,128)(2,1)S(1)}, bf16[22,256,128]{2,1,0:T(8,128)(2,1)S(1)}, u32[]{:S(2)}, u32[]{:S(2)}) collective-permute-start(bf16[22,256,128]{2,1,0:T(8,128)(2,1)S(1)} %copy-done.37), channel_id=1, source_target_pairs={{0,4},{4,0},{8,12},{12,8},{1,5},{5,1},{9,13},{13,9},{2,6},{6,2},{1... | collective-permute-start | bytes 4325384 | tf_op jit(solution)/shard_map/ppermute | solution.py:805
  317.1 23.5 %collective-permute-start.28 = (bf16[11,256,128]{2,1,0:T(8,128)(2,1)S(1)}, bf16[11,256,128]{2,1,0:T(8,128)(2,1)S(1)}, u32[]{:S(2)}, u32[]{:S(2)}) collective-permute-start(bf16[11,256,128]{2,1,0:T(8,128)(2,1)S(1)} %add_convert_fusion.14), channel_id=1, source_target_pairs={{0,1},{3,2},{4,5},{7,6},{8,9},{11,10},{12,13},{15,14},{16,17},{19,... | collective-permute-start | bytes 2162696 | tf_op jit(solution)/shard_map/ppermute | solution.py:843
  324.6 18.6 %collective-permute-start.24 = (bf16[8,128,128]{2,1,0:T(8,128)(2,1)S(1)}, bf16[8,128,128]{2,1,0:T(8,128)(2,1)S(1)}, u32[]{:S(2)}, u32[]{:S(2)}) collective-permute-start(bf16[8,128,128]{2,1,0:T(8,128)(2,1)S(1)} %add_convert_fusion.38), channel_id=1, source_target_pairs={{8,0},{12,4},{9,1},{13,5},{10,2},{14,6},{11,3},{15,7},{24,16},{28,... | collective-permute-start | bytes 786440 | tf_op jit(solution)/shard_map/ppermute | solution.py:788
  332.4 40.2 %collective-permute-start.35 = (bf16[22,256,128]{2,1,0:T(8,128)(2,1)S(1)}, bf16[22,256,128]{2,1,0:T(8,128)(2,1)S(1)}, u32[]{:S(2)}, u32[]{:S(2)}) collective-permute-start(bf16[22,256,128]{2,1,0:T(8,128)(2,1)S(1)} %copy-done.36), channel_id=1, source_target_pairs={{0,4},{4,0},{8,12},{12,8},{1,5},{5,1},{9,13},{13,9},{2,6},{6,2},{1... | collective-permute-start | bytes 4325384 | tf_op jit(solution)/shard_map/ppermute | solution.py:805
  332.5 20.7 %collective-permute-start.37 = (bf16[11,256,128]{2,1,0:T(8,128)(2,1)S(1)}, bf16[11,256,128]{2,1,0:T(8,128)(2,1)S(1)}, u32[]{:S(2)}, u32[]{:S(2)}) collective-permute-start(bf16[11,256,128]{2,1,0:T(8,128)(2,1)S(1)} %add_convert_fusion.13), channel_id=1, source_target_pairs={{0,8},{8,0},{4,12},{12,4},{1,9},{9,1},{5,13},{13,5},{2,10},{10,2},... | collective-permute-start | bytes 2162696 | tf_op jit(solution)/shard_map/ppermute | solution.py:817
  340.6 18.5 %collective-permute-start.45 = (bf16[11,256,128]{2,1,0:T(8,128)(2,1)S(1)}, bf16[11,256,128]{2,1,0:T(8,128)(2,1)S(1)}, u32[]{:S(2)}, u32[]{:S(2)}) collective-permute-start(bf16[11,256,128]{2,1,0:T(8,128)(2,1)S(1)} %fusion), channel_id=1, source_target_pairs={{0,1},{1,0},{2,3},{3,2},{4,5},{5,4},{6,7},{7,6},{8,9},{9,8},{10,11... | collective-permute-start | bytes 2162696 | tf_op jit(solution)/shard_map/ppermute | solution.py:837
  353.2 24.8 %collective-permute-start.38 = (bf16[11,256,128]{2,1,0:T(8,128)(2,1)S(1)}, bf16[11,256,128]{2,1,0:T(8,128)(2,1)S(1)}, u32[]{:S(2)}, u32[]{:S(2)}) collective-permute-start(bf16[11,256,128]{2,1,0:T(8,128)(2,1)S(1)} %add_convert_fusion.8), channel_id=1, source_target_pairs={{0,8},{8,0},{4,12},{12,4},{1,9},{9,1},{5,13},{13,5},{2,10},{10,2},... | collective-permute-start | bytes 2162696 | tf_op jit(solution)/shard_map/ppermute | solution.py:817
  377.9 18.5 %collective-permute-start.39 = (bf16[11,256,128]{2,1,0:T(8,128)(2,1)S(1)}, bf16[11,256,128]{2,1,0:T(8,128)(2,1)S(1)}, u32[]{:S(2)}, u32[]{:S(2)}) collective-permute-start(bf16[11,256,128]{2,1,0:T(8,128)(2,1)S(1)} %add_convert_fusion.9), channel_id=1, source_target_pairs={{0,8},{8,0},{4,12},{12,4},{1,9},{9,1},{5,13},{13,5},{2,10},{10,2},... | collective-permute-start | bytes 2162696 | tf_op jit(solution)/shard_map/ppermute | solution.py:817
  380.4 18.3 %collective-permute-start.49 = (bf16[11,256,128]{2,1,0:T(8,128)(2,1)S(1)}, bf16[11,256,128]{2,1,0:T(8,128)(2,1)S(1)}, u32[]{:S(2)}, u32[]{:S(2)}) collective-permute-start(bf16[11,256,128]{2,1,0:T(8,128)(2,1)S(1)} %fusion.4.inner), channel_id=1, source_target_pairs={{0,1},{1,0},{2,3},{3,2},{4,5},{5,4},{6,7},{7,6},{8,9},{9,8},{10,11... | collective-permute-start | bytes 2162696 | tf_op jit(solution)/shard_map/ppermute | solution.py:837
  394.6 40.4 %collective-permute-start.32 = (bf16[16,256,128]{2,1,0:T(8,128)(2,1)}, bf16[16,256,128]{2,1,0:T(8,128)(2,1)S(1)}, u32[]{:S(2)}, u32[]{:S(2)}) collective-permute-start(bf16[16,256,128]{2,1,0:T(8,128)(2,1)} %get-tuple-element.333), channel_id=1, source_target_pairs={{0,4},{4,0},{8,12},{12,8},{1,5},{5,1},{9,13},{13,9},{2,6},{6,2},{1... | collective-permute-start | bytes 3145736 | tf_op jit(solution)/shard_map/ppermute | solution.py:805
  396.5 22.3 %collective-permute-start.33 = (bf16[16,256,128]{2,1,0:T(8,128)(2,1)S(1)}, bf16[16,256,128]{2,1,0:T(8,128)(2,1)S(1)}, u32[]{:S(2)}, u32[]{:S(2)}) collective-permute-start(bf16[16,256,128]{2,1,0:T(8,128)(2,1)S(1)} %copy-done.39), channel_id=1, source_target_pairs={{0,4},{4,0},{8,12},{12,8},{1,5},{5,1},{9,13},{13,9},{2,6},{6,2},{1... | collective-permute-start | bytes 3145736 | tf_op jit(solution)/shard_map/ppermute | solution.py:805
  398.7 20.4 %collective-permute-start.40 = (bf16[8,256,128]{2,1,0:T(8,128)(2,1)S(1)}, bf16[8,256,128]{2,1,0:T(8,128)(2,1)S(1)}, u32[]{:S(2)}, u32[]{:S(2)}) collective-permute-start(bf16[8,256,128]{2,1,0:T(8,128)(2,1)S(1)} %add_convert_fusion.31), channel_id=1, source_target_pairs={{0,8},{8,0},{4,12},{12,4},{1,9},{9,1},{5,13},{13,5},{2,10},{10,2},... | collective-permute-start | bytes 1572872 | tf_op jit(solution)/shard_map/ppermute | solution.py:817
  402.1 18.7 %collective-permute-start.54 = (bf16[11,256,128]{2,1,0:T(8,128)(2,1)S(1)}, bf16[11,256,128]{2,1,0:T(8,128)(2,1)S(1)}, u32[]{:S(2)}, u32[]{:S(2)}) collective-permute-start(bf16[11,256,128]{2,1,0:T(8,128)(2,1)S(1)} %fusion.5), channel_id=1, source_target_pairs={{1,2},{2,1},{5,6},{6,5},{9,10},{10,9},{13,14},{14,13},{17,18},{18,... | collective-permute-start | bytes 2162696 | tf_op jit(solution)/shard_map/ppermute | solution.py:833
  403.3 30.8 %collective-permute-start.51 = (bf16[11,256,128]{2,1,0:T(8,128)(2,1)S(1)}, bf16[11,256,128]{2,1,0:T(8,128)(2,1)S(1)}, u32[]{:S(2)}, u32[]{:S(2)}) collective-permute-start(bf16[11,256,128]{2,1,0:T(8,128)(2,1)S(1)} %fusion.6.inner), channel_id=1, source_target_pairs={{0,1},{1,0},{2,3},{3,2},{4,5},{5,4},{6,7},{7,6},{8,9},{9,8},{10,11... | collective-permute-start | bytes 2162696 | tf_op jit(solution)/shard_map/ppermute | solution.py:837
  418.8 55.4 %collective-permute-start.30 = (bf16[16,256,128]{2,1,0:T(8,128)(2,1)S(1)}, bf16[16,256,128]{2,1,0:T(8,128)(2,1)S(1)}, u32[]{:S(2)}, u32[]{:S(2)}) collective-permute-start(bf16[16,256,128]{2,1,0:T(8,128)(2,1)S(1)} %copy-done.38), channel_id=1, source_target_pairs={{0,4},{4,0},{8,12},{12,8},{1,5},{5,1},{9,13},{13,9},{2,6},{6,2},{1... | collective-permute-start | bytes 3145736 | tf_op jit(solution)/shard_map/ppermute | solution.py:805
  419.1 23.9 %collective-permute-start.41 = (bf16[8,256,128]{2,1,0:T(8,128)(2,1)S(1)}, bf16[8,256,128]{2,1,0:T(8,128)(2,1)S(1)}, u32[]{:S(2)}, u32[]{:S(2)}) collective-permute-start(bf16[8,256,128]{2,1,0:T(8,128)(2,1)S(1)} %add_convert_fusion.32), channel_id=1, source_target_pairs={{0,8},{8,0},{4,12},{12,4},{1,9},{9,1},{5,13},{13,5},{2,10},{10,2},... | collective-permute-start | bytes 1572872 | tf_op jit(solution)/shard_map/ppermute | solution.py:817
  421.1 30.1 %collective-permute-start.55 = (bf16[11,256,128]{2,1,0:T(8,128)(2,1)S(1)}, bf16[11,256,128]{2,1,0:T(8,128)(2,1)S(1)}, u32[]{:S(2)}, u32[]{:S(2)}) collective-permute-start(bf16[11,256,128]{2,1,0:T(8,128)(2,1)S(1)} %add_convert_fusion.inner), channel_id=1, source_target_pairs={{1,0},{2,3},{5,4},{6,7},{9,8},{10,11},{13,12},{14,15},{17,16},{18,... | collective-permute-start | bytes 2162696 | tf_op jit(solution)/shard_map/ppermute | solution.py:847
  434.3 18.1 %collective-permute-start.52 = (bf16[11,256,128]{2,1,0:T(8,128)(2,1)S(1)}, bf16[11,256,128]{2,1,0:T(8,128)(2,1)S(1)}, u32[]{:S(2)}, u32[]{:S(2)}) collective-permute-start(bf16[11,256,128]{2,1,0:T(8,128)(2,1)S(1)} %fusion.7), channel_id=1, source_target_pairs={{1,2},{2,1},{5,6},{6,5},{9,10},{10,9},{13,14},{14,13},{17,18},{18,... | collective-permute-start | bytes 2162696 | tf_op jit(solution)/shard_map/ppermute | solution.py:833
  436.6 22.0 %collective-permute-start.56 = (bf16[8,256,128]{2,1,0:T(8,128)(2,1)S(1)}, bf16[8,256,128]{2,1,0:T(8,128)(2,1)S(1)}, u32[]{:S(2)}, u32[]{:S(2)}) collective-permute-start(bf16[8,256,128]{2,1,0:T(8,128)(2,1)S(1)} %add_convert_fusion.24), channel_id=1, source_target_pairs={{0,1},{3,2},{4,5},{7,6},{8,9},{11,10},{12,13},{15,14},{16,17},{19,... | collective-permute-start | bytes 1572872 | tf_op jit(solution)/shard_map/ppermute | solution.py:843
  452.6 17.8 %collective-permute-start.53 = (bf16[11,256,128]{2,1,0:T(8,128)(2,1)S(1)}, bf16[11,256,128]{2,1,0:T(8,128)(2,1)S(1)}, u32[]{:S(2)}, u32[]{:S(2)}) collective-permute-start(bf16[11,256,128]{2,1,0:T(8,128)(2,1)S(1)} %add_convert_fusion.1.inner), channel_id=1, source_target_pairs={{1,0},{2,3},{5,4},{6,7},{9,8},{10,11},{13,12},{14,15},{17,16},{18,... | collective-permute-start | bytes 2162696 | tf_op jit(solution)/shard_map/ppermute | solution.py:847
  506.8 18.8 %collective-permute-start.67 = (bf16[8,256,128]{2,1,0:T(8,128)(2,1)S(1)}, bf16[8,256,128]{2,1,0:T(8,128)(2,1)S(1)}, u32[]{:S(2)}, u32[]{:S(2)}) collective-permute-start(bf16[8,256,128]{2,1,0:T(8,128)(2,1)S(1)} %add_convert_fusion.18.inner), channel_id=1, source_target_pairs={{1,0},{2,3},{5,4},{6,7},{9,8},{10,11},{13,12},{14,15},{17,16},{18,... | collective-permute-start | bytes 1572872 | tf_op jit(solution)/shard_map/ppermute | solution.py:847
  508.3 25.5 %collective-permute-start.65 = (bf16[8,256,128]{2,1,0:T(8,128)(2,1)S(1)}, bf16[8,256,128]{2,1,0:T(8,128)(2,1)S(1)}, u32[]{:S(2)}, u32[]{:S(2)}) collective-permute-start(bf16[8,256,128]{2,1,0:T(8,128)(2,1)S(1)} %add_convert_fusion.19.inner), channel_id=1, source_target_pairs={{1,0},{2,3},{5,4},{6,7},{9,8},{10,11},{13,12},{14,15},{17,16},{18,... | collective-permute-start | bytes 1572872 | tf_op jit(solution)/shard_map/ppermute | solution.py:847
  (81 other events, 827.0 us)

commit v3 on v2

--- a/solution.py
+++ b/solution.py
@@ -97,15 +97,20 @@
     return jnp.cos(angle), jnp.where(lane < half, -jnp.sin(angle), jnp.sin(angle))
 
 
-def project_body(slope, x, cosine, sine, w, h1, r1, pre, qk, state,
-                 xv, cv, sv, hv, rv, prev, qkv, stv, isem, osem):
+def join(slope, before, own):
+    decay = jnp.exp(jnp.full((LANES, LANES), -BLK, f32) * slope)
+    return (decay * before.astype(f32) + own).astype(bf16)
+
+
+def project_body(slope, x, cosine, sine, before, w, h1, r1, pre, qk, state, joined,
+                 xv, cv, sv, bv, hv, rv, prev, qkv, stv, jv, isem, osem):
     rows, width = x.shape
     steps = STEPS
     columns = w.shape[1] // steps
     heads = columns // LANES
     first = [
         pltpu.make_async_copy(source, target, isem.at[n])
-        for n, (source, target) in enumerate(((x, xv), (cosine, cv), (sine, sv)))
+        for n, (source, target) in enumerate(((x, xv), (cosine, cv), (sine, sv), (before, bv)))
     ]
     for copy in first:
         copy.start()
@@ -115,8 +120,8 @@
     factor = norm_factor(v, width)
     hv[...] = (v * factor).astype(bf16)
     rv[...] = jnp.broadcast_to(factor, rv.shape)
-    first[1].wait()
-    first[2].wait()
+    for copy in first[1:]:
+        copy.wait()
     outs = [pltpu.make_async_copy(hv, h1, osem.at[0]), pltpu.make_async_copy(rv, r1, osem.at[1])]
     for copy in outs:
         copy.start()
@@ -148,12 +153,18 @@
                 decay = jnp.exp(ahead * (-slope[number]))
                 key = qkv[:, pl.ds(at - width + n * LANES, LANES)]
                 keyed = (key.astype(f32) * decay).astype(bf16)
-                stv[number] = tn(keyed, values[:, head(n)]).astype(bf16)
+                own = tn(keyed, values[:, head(n)])
+                stv[number] = own.astype(bf16)
+                jv[number] = join(slope[number], bv[number], own)
 
         return carry
 
     lax.fori_loop(0, steps, step, 0)
-    last = [pltpu.make_async_copy(qkv, qk, osem.at[2]), pltpu.make_async_copy(stv, state, osem.at[11])]
+    last = [
+        pltpu.make_async_copy(qkv, qk, osem.at[2]),
+        pltpu.make_async_copy(stv, state, osem.at[11]),
+        pltpu.make_async_copy(jv, joined, osem.at[12]),
+    ]
     for copy in last:
         copy.start()
     for copy in outs + last:
@@ -162,39 +173,42 @@
         pre_out(j).wait()
 
 
-def project(slopes, x, cosine, sine, w):
+def project(slopes, x, cosine, sine, before, w):
     rows, width = x.shape
     total = w.shape[1]
     states = (HEADS, LANES, LANES)
     return pl.pallas_call(
         project_body,
-        in_specs=[SMEM] + [ANY] * 3 + [VMEM],
-        out_specs=[ANY] * 5,
+        in_specs=[SMEM] + [ANY] * 4 + [VMEM],
+        out_specs=[ANY] * 6,
         out_shape=[
             hbm((rows, width), bf16),
             hbm((rows, LANES), f32),
             hbm((rows, total), bf16),
             hbm((rows, total // 2), bf16),
             hbm(states, bf16),
+            hbm(states, bf16),
         ],
         scratch_shapes=[
             pltpu.VMEM((rows, width), bf16),
             pltpu.VMEM((rows, LANES), f32),
             pltpu.VMEM((rows, LANES), f32),
+            pltpu.VMEM(states, bf16),
             pltpu.VMEM((rows, width), bf16),
             pltpu.VMEM((rows, LANES), f32),
             pltpu.VMEM((rows, total), bf16),
             pltpu.VMEM((rows, total // 2), bf16),
             pltpu.VMEM(states, bf16),
-            pltpu.SemaphoreType.DMA((3,)),
-            pltpu.SemaphoreType.DMA((12,)),
+            pltpu.VMEM(states, bf16),
+            pltpu.SemaphoreType.DMA((4,)),
+            pltpu.SemaphoreType.DMA((13,)),
         ],
         compiler_params=params(8),
         cost_estimate=pl.CostEstimate(
             flops=2 * rows * width * total, bytes_accessed=2 * width * total, transcendentals=0
         ),
         name="project",
-    )(slopes, *far_away(x, cosine, sine), *close_by(w))
+    )(slopes, *far_away(x, cosine, sine, before), *close_by(w))
 
 
 def moves(pairs, sem, start=0):
@@ -351,10 +365,10 @@
 
 
 def back_channel_body(
-    slope, dy, wo, wi, wd, g, up, h2, r2, mixed, ra, qk, pre, low, cosine, sine,
-    dg, dup, dmid, dm, dq, du, dk, dv, state,
-    dyv, gv, upv, h2v, r2v, mixedv, rav, qkv, qpv, vuv, lowv, cv, sv,
-    dgv, dupv, dmidv, dmv, dqv, duv, dkv, dvv, statev,
+    slope, dy, wo, wi, wd, g, up, h2, r2, mixed, ra, qk, pre, low, cosine, sine, behind,
+    dg, dup, dmid, dm, dq, du, dk, dv, state, joined,
+    dyv, gv, upv, h2v, r2v, mixedv, rav, qkv, qpv, vuv, lowv, cv, sv, bv,
+    dgv, dupv, dmidv, dmv, dqv, duv, dkv, dvv, statev, jv,
     total, datt, heldg, heldu, isem, osem, csem,
 ):
     rows, width = dy.shape
@@ -366,6 +380,7 @@
             (dy, dyv), (g, gv), (up, upv), (h2, h2v), (r2, r2v), (mixed, mixedv), (ra, rav),
             (qk, qkv), (pre.at[:, pl.ds(0, width)], qpv),
             (pre.at[:, pl.ds(2 * width, 2 * width)], vuv), (low, lowv), (cosine, cv), (sine, sv),
+            (behind, bv),
         ),
         isem,
     )
@@ -439,7 +454,9 @@
             scores = (mask * nt(cot, value)).astype(bf16)
             scores_t = (flipped * nt(value, cot)).astype(bf16)
             scaled = (jnp.exp(ahead * (-slope[n])) * cot.astype(f32)).astype(bf16)
-            statev[n] = tn(query, scaled).astype(bf16)
+            own = tn(query, scaled)
+            statev[n] = own.astype(bf16)
+            jv[n] = join(slope[n], bv[n], own)
             dquery = nn(scores, key) + nt(scaled, lowv[n])
             turned = dquery * cv[...] + half_turn(dquery * sv[...])
             p = qpv[:, lane].astype(f32)
@@ -450,7 +467,9 @@
         return carry
 
     lax.fori_loop(0, HEADS // 2, some, 0)
-    last = moves(((statev, state), (dqv, dq), (duv, du), (dkv, dk), (dvv, dv)), osem, 2)
+    last = moves(
+        ((statev, state), (jv, joined), (dqv, dq), (duv, du), (dkv, dk), (dvv, dv)), osem, 2
+    )
     for copy in last:
         copy.start()
     for copy in outs + last:
@@ -464,7 +483,7 @@
     lax.fori_loop(0, steps, drain, 0)
 
 
-def back_channel(slopes, dy, r, cosine, sine, wo, wi, wd):
+def back_channel(slopes, dy, r, cosine, sine, behind, wo, wi, wd):
     rows, width = dy.shape
     hidden = wd.shape[0]
     columns = 256
@@ -473,19 +492,20 @@
     act = hbm((rows, width), bf16)
     full = hbm((rows, width), f32)
     unit = hbm((rows, hidden), bf16)
-    outs = [unit, unit, full, act, act, act, full, full, hbm(states, bf16)]
+    state = hbm(states, bf16)
+    outs = [unit, unit, full, act, act, act, full, full, state, state]
     wide = pltpu.VMEM((rows, width), bf16)
     thin = pltpu.VMEM((rows, LANES), f32)
     twice = pltpu.VMEM((rows, 2 * width), bf16)
     tall = pltpu.VMEM((rows, hidden), bf16)
     return pl.pallas_call(
         back_channel_body,
-        in_specs=[SMEM] + [ANY] + [VMEM] * 3 + [ANY] * 11,
+        in_specs=[SMEM] + [ANY] + [VMEM] * 3 + [ANY] * 12,
         out_specs=[ANY] * len(outs),
         out_shape=outs,
         scratch_shapes=[
             wide, tall, tall, wide, thin, wide, thin, twice, wide, twice,
-            pltpu.VMEM(states, bf16), thin, thin,
+            pltpu.VMEM(states, bf16), thin, thin, pltpu.VMEM(states, bf16),
         ]
         + [pltpu.VMEM(o.shape, o.dtype) for o in outs]
         + [
@@ -493,8 +513,8 @@
             wide,
             pltpu.VMEM((rows, columns), bf16),
             pltpu.VMEM((rows, columns), bf16),
-            pltpu.SemaphoreType.DMA((13,)),
-            pltpu.SemaphoreType.DMA((7,)),
+            pltpu.SemaphoreType.DMA((14,)),
+            pltpu.SemaphoreType.DMA((8,)),
             pltpu.SemaphoreType.DMA((2, steps)),
         ],
         compiler_params=params(22),
@@ -508,7 +528,7 @@
         slopes, *far_away(dy), *close_by(wo, wi, wd),
         *far_away(
             r["g"], r["up"], r["h2"], r["r2"], r["mixed"], r["ra"], r["qk"], r["pre"], r["low"],
-            cosine, sine,
+            cosine, sine, behind,
         ),
     )
 
@@ -753,40 +773,36 @@
     return (a.astype(f32) + b.astype(f32)).astype(bf16)
 
 
-def state_factors(slopes, forward):
-    if lax.axis_size("seq") != 4:
-        return jnp.stack([jnp.ones_like(slopes), jnp.zeros_like(slopes)])
+def gathered_state(own, slopes, forward):
+    count = lax.axis_size("seq")
     place = lax.axis_index("seq")
-    second = (place % 2 == 1) if forward else (place % 2 == 0)
-    decay = jnp.exp(-slopes * BLK)
-    one = jnp.ones_like(slopes)
-    return jnp.stack([jnp.where(second, decay, one), jnp.where(second, one, 0.0 * one)])
-
-
-def join_factors(slopes, forward):
+    gathered = lax.all_gather(own, "seq").astype(f32)
+    device = jnp.arange(count)
+    distance = place - 1 - device if forward else device - place - 1
+    power = jnp.maximum(distance, 0).astype(f32) * BLK
+    weight = jnp.where(distance[:, None] >= 0, jnp.exp(-slopes[None] * power[:, None]), 0.0)
+    return jnp.sum(weight[:, :, None, None] * gathered, axis=0).astype(bf16)
+
+
+def halves(first, second):
     place = lax.axis_index("seq")
-    second = (place % 2 == 1) if forward else (place % 2 == 0)
-    decay = jnp.exp(-slopes * BLK)
-    one = jnp.ones_like(slopes)
-    return jnp.stack([jnp.where(second, one, decay), jnp.where(second, decay, one)])
-
-
-def entering_parts(own, slopes, factors, forward):
-    count = lax.axis_size("seq")
-    if count != 4:
-        place = lax.axis_index("seq")
-        gathered = lax.all_gather(own, "seq").astype(f32)
-        device = jnp.arange(count)
-        distance = place - 1 - device if forward else device - place - 1
-        power = jnp.maximum(distance, 0).astype(f32) * BLK
-        weight = jnp.where(distance[:, None] >= 0, jnp.exp(-slopes[None] * power[:, None]), 0.0)
-        state = jnp.sum(weight[:, :, None, None] * gathered, axis=0).astype(bf16)
-        return (state, state), state
-    near = lax.ppermute(own, "seq", [(0, 1), (1, 0), (2, 3), (3, 2)])
-    mine, other = factors[0][:, None, None], factors[1][:, None, None]
-    joined = (mine * own.astype(f32) + other * near.astype(f32)).astype(bf16)
-    far = lax.ppermute(joined, "seq", [(0, 2), (1, 3)] if forward else [(2, 0), (3, 1)])
-    return (far, near), joined
+    sent = jnp.where(place % 2 == 1, first, second)
+    one = lax.ppermute(sent, "seq", [(1, 0), (2, 3), (0, 2), (3, 1)])
+    two = lax.ppermute(jnp.where(place == 1, second, first), "seq", [(2, 1), (1, 2)])
+    return (
+        jnp.where(place == 0, first, jnp.where(place == 1, two, one)),
+        jnp.where(place == 3, second, jnp.where(place == 2, two, one)),
+    )
+
+
+def quarters(low, high):
+    place = lax.axis_index("seq")
+    one = lax.ppermute(jnp.where(place < 2, high, low), "seq", [(0, 1), (3, 2), (2, 0), (1, 3)])
+    two = lax.ppermute(jnp.where(place == 1, low, high), "seq", [(1, 2), (2, 1)])
+    return (
+        jnp.where(place == 0, low, jnp.where(place == 2, two, one)),
+        jnp.where(place == 3, high, jnp.where(place == 1, two, one)),
+    )
 
 
 class Sums:
@@ -879,60 +895,90 @@
         self.last = list(values)
 
 
-def first_half(order, x, shared, cosine, sine, w):
-    h1, r1, pre, qk, state = project(order.after(shared[0]), x, cosine, sine, w)
-    entering, joined = entering_parts(state, shared[0], shared[3], True)
-    order.at(r1, joined)
-    return dict(x=x, h1=h1, r1=r1, pre=pre, qk=qk), entering
-
-
-def second_half(order, record, entering, shared, wo, wi, wd):
-    mixed, gated, ra, h2, r2, low, g, up, product, y = finish(
-        order.after(shared[0]), shared[1], record["x"], record["qk"], record["pre"], entering,
-        wo, wi, wd,
-    )
-    order.at(ra)
-    record.update(
-        mixed=mixed, gated=gated, ra=ra, h2=h2, r2=r2, low=low, g=g, up=up, product=product
-    )
-    return y
-
-
-def back_first(order, dy, record, shared, cosine, sine, wo, wi, wd):
-    dg, dup, dmid, dm, dq, du, dk, dv, state = back_channel(
-        order.after(shared[0]), dy, record, cosine, sine, wo, wi, wd
-    )
-    entering, joined = entering_parts(state, shared[0], shared[4], False)
-    order.at(dm, joined)
-    record.update(dy=dy, dg=dg, dup=dup, dmid=dmid, dm=dm, dq=dq, du=du, dk=dk, dv=dv)
-    return entering
-
-
-def back_second(order, record, entering, shared, cosine, sine, w):
-    dkp, dvp, dx = back_mixer(
-        order.after(shared[0]), shared[2], record, entering, cosine, sine, w
-    )
-    order.at(dkp)
-    record.update(dkp=dkp, dvp=dvp)
-    return dx
+class Layer:
+    def __init__(self, order, slopes, factors, chained, cosine, sine, weights):
+        self.order, self.slopes, self.factors, self.chained = order, slopes, factors, chained
+        self.cosine, self.sine = cosine, sine
+        self.w, self.wo, self.wi, self.wd = weights
+        self.blocks = [None, None]
+        self.entering = [None, None]
+        self.later = [None, None]
+        self.zero = jnp.zeros((HEADS, LANES, LANES), bf16)
+
+    def first(self, b, x):
+        before = self.blocks[0]["state"] if b == 1 else self.zero
+        h1, r1, pre, qk, state, joined = project(
+            self.order.after(self.slopes), x, self.cosine[b], self.sine[b], before, self.w
+        )
+        self.order.at(r1)
+        self.blocks[b] = dict(x=x, h1=h1, r1=r1, pre=pre, qk=qk, state=state)
+        if not self.chained:
+            self.entering[b] = gathered_state(state, self.slopes, True)
+        elif b == 1:
+            near = lax.ppermute(joined, "seq", [(0, 1), (2, 3)])
+            self.entering = [near, near]
+
+    def second(self, b):
+        r = self.blocks[b]
+        near = self.blocks[0]["state"] if b == 1 else self.entering[b]
+        mixed, gated, ra, h2, r2, low, g, up, product, y = finish(
+            self.order.after(self.slopes), self.factors[b], r["x"], r["qk"], r["pre"],
+            (self.entering[b], near), self.wo, self.wi, self.wd,
+        )
+        self.order.at(ra)
+        r.update(
+            mixed=mixed, gated=gated, ra=ra, h2=h2, r2=r2, low=low, g=g, up=up, product=product
+        )
+        return y
+
+    def back_first(self, b, dy):
+        r = self.blocks[b]
+        behind = self.blocks[1]["dstate"] if b == 0 else self.zero
+        dg, dup, dmid, dm, dq, du, dk, dv, state, joined = back_channel(
+            self.order.after(self.slopes), dy, r, self.cosine[b], self.sine[b], behind,
+            self.wo, self.wi, self.wd,
+        )
+        self.order.at(dm)
+        r.update(dy=dy, dg=dg, dup=dup, dmid=dmid, dm=dm, dq=dq, du=du, dk=dk, dv=dv, dstate=state)
+        if not self.chained:
+            self.later[b] = gathered_state(state, self.slopes, False)
+        elif b == 0:
+            near = lax.ppermute(joined, "seq", [(1, 0), (3, 2)])
+            self.later = [near, near]
+
+    def back_second(self, b):
+        r = self.blocks[b]
+        near = self.blocks[1]["dstate"] if b == 0 else self.later[b]
+        dkp, dvp, dx = back_mixer(
+            self.order.after(self.slopes), self.factors[1 - b], r, (self.later[b], near),
+            self.cosine[b], self.sine[b], self.w,
+        )
+        self.order.at(dkp)
+        r.update(dkp=dkp, dvp=dvp)
+        return dx
 
 
 def per_device(boundary, positions, decay_exp, mixer_in, mixer_out, channel_in, channel_out):
     section = lax.axis_index("section")
     is_first = section == 0
-    own = boundary[0]
-    batch, rows, width = own.shape
-    assert rows == BLK
+    batch, rows, width = boundary.shape[1:]
+    assert rows == BLK and batch == 2
     slopes = jnp.exp2(-0.5 * decay_exp[0].astype(jnp.float32))
-    w, wo, wi, wd = mixer_in[0], mixer_out[0], channel_in[0], channel_out[0]
+    w, wo, wi, wd = weights = mixer_in[0], mixer_out[0], channel_in[0], channel_out[0]
     hidden = wd.shape[0]
     half_size = width // HEADS // 2
-    cosine, sine = angle_tables(positions, half_size)
-    every = range(batch)
     usual = lax.axis_size("seq") == 4 and lax.axis_size("dp") == 4
-
     place, line = lax.axis_index("seq"), lax.axis_index("dp")
     core, y_place = place % 2, place // 2
+
+    own = (boundary[0, 0], boundary[0, 1])
+    if usual:
+        own = halves(*own)
+        every = lax.all_gather(positions, "seq")
+        chosen = lax.dynamic_index_in_dim(every, y_place, 1, keepdims=False)
+        positions = lax.dynamic_slice_in_dim(chosen, 2 * core, 2, 0)
+    cosine, sine = angle_tables(positions, half_size)
+
     roles = [
         2 * (1 - y_place) + 1 - core,
         2 * y_place + 1 - core,
@@ -944,35 +990,33 @@
     roles = jnp.stack([jnp.asarray(r, jnp.int32) for r in (*roles, section)])
     edge = (line == 0) | (line == lax.axis_size("dp") - 1)
     flag = edge.astype(jnp.int32)[None]
-    shared = [
-        slopes, state_factors(slopes, True), state_factors(slopes, False),
-        join_factors(slopes, True), join_factors(slopes, False),
-    ]
-    own, roles, flag, *shared = lax.optimization_barrier((own, roles, flag, *shared))
+    one = jnp.ones_like(slopes)
+    factors = [jnp.stack([one, 0.0 * one])] * 2
+    if usual:
+        factors[1] = jnp.stack([jnp.exp(-slopes * BLK), one])
+    roles, flag, slopes, *factors = lax.optimization_barrier((roles, flag, slopes, *factors))
     edge = flag[0] == 1
     order = Order()
-
-    early, states = [None] * batch, [None] * batch
-    for b in every:
-        early[b], states[b] = first_half(order, own[b], shared, cosine[b], sine[b], w)
-    arrived = []
-    for b in every:
-        y = second_half(order, early[b], states[b], shared, wo, wi, wd)
-        arrived.append(lax.ppermute(y, "section", [(0, 1)]))
-    late = [None] * batch
-    for b in every:
-        late[b], states[b] = first_half(order, arrived[b], shared, cosine[b], sine[b], w)
-    outputs, later = [None] * batch, [None] * batch
-    for b in every:
-        outputs[b] = second_half(order, late[b], states[b], shared, wo, wi, wd)
-        later[b] = back_first(order, own[b], late[b], shared, cosine[b], sine[b], wo, wi, wd)
-    returned = []
-    for b in every:
-        dx = back_second(order, late[b], later[b], shared, cosine[b], sine[b], w)
-        returned.append(lax.ppermute(dx, "section", [(1, 0)]))
+    order.at(roles, flag)
+    layers = [
+        Layer(order, slopes, factors, usual, cosine, sine, weights) for section_of_it in range(2)
+    ]
+    early, late = layers
+
+    for b in range(2):
+        early.first(b, own[b])
+    arrived = [lax.ppermute(early.second(b), "section", [(0, 1)]) for b in range(2)]
+    for b in range(2):
+        late.first(b, arrived[b])
+    outputs = [late.second(b) for b in range(2)]
+    for b in (1, 0):
+        late.back_first(b, own[b])
+    returned = [None, None]
+    for b in (1, 0):
+        returned[b] = lax.ppermute(late.back_second(b), "section", [(1, 0)])
 
     def operands(*names):
-        return [[[r[name] for r in records] for name in names] for records in (early, late)]
+        return [[[r[name] for r in layer.blocks] for name in names] for layer in layers]
 
     chunks = []
     spans = [(3, width), (3, width)] + [(2, 2 * hidden)] * 4 + [(1, width)] + [(0, 4 * width)] * 4
@@ -1011,28 +1055,24 @@
             way()
         order.at(*order.last, *sums.started())
 
-    def first(b):
-        return back_first(order, returned[b], early[b], shared, cosine[b], sine[b], wo, wi, wd)
-
-    def second(b):
-        return back_second(order, early[b], later[b], shared, cosine[b], sine[b], w)
-
-    later = [first(b) for b in every[:-1]]
-    for b in every:
-        early[b]["dy"] = returned[b]
+    early.back_first(1, returned[1])
+    early.blocks[0]["dy"] = returned[0]
     gradient("product", ("dy",), [(0, 0, 4), (0, 4, 4)])
     move(sums.over_y)
-    later.append(first(batch - 1))
+    early.back_first(0, returned[0])
     move(sums.over_y, sums.over_z)
     half = hidden // LANES // 2
     gradient("h2", ("dg", "dup"), [(0, 0, half), (0, half, half), (1, 0, half), (1, half, half)])
     move(sums.over_y, sums.over_z)
-    dx = [second(b) for b in every]
+    dx = [None, None]
+    for b in (1, 0):
+        dx[b] = early.back_second(b)
     move(sums.over_y, sums.over_z)
     eight = width // LANES
     gradient("gated", ("dm",), [(0, 0, eight)])
     gradient("h1", ("dq", "dkp", "dvp", "du"), [(s, 0, eight) for s in range(4)])
-    joined = jnp.where(is_first, jnp.stack(dx), jnp.stack(outputs))[None]
+    ends = [jnp.where(is_first, dx[b], outputs[b]) for b in range(2)]
+    joined = jnp.stack(quarters(*ends) if usual else ends)[None]
     if usual:
         while sums.waiting:
             move(sums.over_y, sums.over_z)

time: 545 us -> 517 us (0.949)
  waiting for transfers between devices: 135 us -> 109 us
  blocking collectives: 0 us -> 13.5 us
  local copies, waits for them, and re-layouts: 19.9 us -> 11.6 us
  starting transfers between devices: 120 us -> 113 us
    ppermute x20 -> x12, waiting for transfers between devices: 36.4 us -> 17.3 us  [the longest x1 9.71 us: quarters(): lax.ppermute(jnp.where(place < 2, high, low), 'seq', [(0, 1), (3, 2), (2,...]
    all_gather x0 -> x1, blocking collectives: none -> 13.5 us  [per_device(): every = lax.all_gather(positions, 'seq')]
    convert_element_type x8 -> x0, other arithmetic: 8.65 us -> none  [entering_parts(): joined = (mine * own.astype(f32) + other * near.astype(f32)).astype(bf16)]
    ppermute x20 -> x12, starting transfers between devices: 37.9 us -> 30.4 us  [the longest x2 11.3 us: per_device(): returned[b] = lax.ppermute(late.back_second(b), 'section', [(1, 0)])]
    unnamed x90 -> x87, local copies, waits for them, and re-layouts: 15.9 us -> 9.09 us
    ppermute x4, waiting for transfers between devices: 27.7 us -> 22.1 us  [over_z(): lax.ppermute(done, 'dp', [(1, 0), (2, 3)])]
  transfers between devices with their start and end apart: 68 -> 60, of which waited for: 27 -> 22; matrix products, arithmetic and copies ran while one was open for 4% -> 3% of each run, Pallas kernels for 22% -> 21%
where the time goes in v3:
time: 517 us; the launch traced here: 508 us
  Pallas kernels  236 us (46%)
  starting transfers between devices  113 us (22%)
  waiting for transfers between devices  109 us (21%)
  other arithmetic  21.6 us (4%)
  blocking collectives  13.5 us (3%)
  local copies, waits for them, and re-layouts  11.6 us (2%)
    pallas_call x4, Pallas kernels, back_channel(): pl.pallas_call(back_channel_body, in_specs=[SMEM] + [ANY] + [VMEM] * 3 +...  66.3 us
    pallas_call x4, Pallas kernels, finish(): pl.pallas_call(finish_body, in_specs=[SMEM] * 2 + [ANY] * 5 + [VMEM] * 3,...  52 us
    pallas_call x4, Pallas kernels, weight_gradient(): pl.pallas_call(functools.partial(weight_body, batch=batch, sides=sides, g...  39.1 us
    ppermute x7, waiting for transfers between devices, over_z(): got = lax.ppermute(sent, 'dp', [(0, 1), (1, 0), (2, 3), (3, 2)])  37.4 us
    pallas_call x4, Pallas kernels, project(): pl.pallas_call(project_body, in_specs=[SMEM] + [ANY] * 4 + [VMEM], out_sp...  34 us
    pallas_call x4, Pallas kernels, back_mixer(): pl.pallas_call(back_mixer_body, in_specs=[SMEM] * 2 + [ANY] * 13 + [VMEM]...  31.8 us
    ppermute x7, starting transfers between devices, over_z(): got = lax.ppermute(sent, 'dp', [(0, 1), (1, 0), (2, 3), (3, 2)])  29.5 us
    ppermute x4, waiting for transfers between devices, over_z(): lax.ppermute(done, 'dp', [(1, 0), (2, 3)])  22.1 us
  transfers between devices with their start and end apart: 60, of which 22 were waited for; matrix products, arithmetic and copies ran while one was open for 3% of the time, Pallas kernels for 21%

profile of v3, /device:TPU:0, one launch (start us, length us, event | category | flops | bytes accessed | tf_op | source)
XLA Modules:
  0.0 507.9 jit_solution(731893846100886805)
XLA Ops:
  8.1 13.5 %all-gather.1 = s32[4,2,256]{2,1,0:T(2,128)S(1)} all-gather(s32[1,2,256]{2,1,0:T(2,128)S(1)} %bitcast.110), channel_id=2, replica_groups=mesh['section'=2,'seq'=4,'dp'=4] {'seq'}, dimensions={0}, use_global_device_ids=true | all-gather | bytes 10240 | tf_op jit(solution)/shard_map/all_gather | solution.py:977
  30.2 8.6 %project.4 = (bf16[256,1024]{1,0:T(8,128)(2,1)}, f32[256,128]{1,0:T(8,128)}, bf16[256,4096]{1,0:T(8,128)(2,1)}, bf16[256,2048]{1,0:T(8,128)(2,1)}, bf16[8,128,12...) custom-call(f32[8]{0:T(128)S(1)} %get-tuple-element.298.slope, bf16[256,1024]{1,0:T(8,128)(2,1)} %get-tuple-element.355.x.dy.refs_7_, ...), custom_call_target="tpu_custom_call" | custom-call | flops 2147483648 | bytes 8388608 | tf_op jit(solution)/shard_map/project/pallas_call | solution.py:180
  38.9 8.6 %project.5 = (bf16[256,1024]{1,0:T(8,128)(2,1)}, f32[256,128]{1,0:T(8,128)}, bf16[256,4096]{1,0:T(8,128)(2,1)}, bf16[256,2048]{1,0:T(8,128)(2,1)}, bf16[8,128,12...) custom-call(f32[8]{0:T(128)S(1)} %get-tuple-element.298.slope, bf16[256,1024]{1,0:T(8,128)(2,1)} %get-tuple-element.354.x.dy.refs_8_, ...), custom_call_target="tpu_custom_call" | custom-call | flops 2147483648 | bytes 8388608 | tf_op jit(solution)/shard_map/project/pallas_call | solution.py:180
  51.7 13.2 %finish.4 = (bf16[256,1024]{1,0:T(8,128)(2,1)}, bf16[256,1024]{1,0:T(8,128)(2,1)}, f32[256,128]{1,0:T(8,128)}, bf16[256,1024]{1,0:T(8,128)(2,1)}, f32[256,128]{1...) custom-call(f32[8]{0:T(128)S(1)} %get-tuple-element.298.slope, ...), custom_call_target="tpu_custom_call" | custom-call | flops 4966055936 | bytes 19398656 | tf_op jit(solution)/shard_map/finish/pallas_call | solution.py:337
  68.5 13.1 %finish.5 = (bf16[256,1024]{1,0:T(8,128)(2,1)}, bf16[256,1024]{1,0:T(8,128)(2,1)}, f32[256,128]{1,0:T(8,128)}, bf16[256,1024]{1,0:T(8,128)(2,1)}, f32[256,128]{1...) custom-call(f32[8]{0:T(128)S(1)} %get-tuple-element.298.slope, ...), custom_call_target="tpu_custom_call" | custom-call | flops 4966055936 | bytes 19398656 | tf_op jit(solution)/shard_map/finish/pallas_call | solution.py:337
  83.8 8.3 %project.6 = (bf16[256,1024]{1,0:T(8,128)(2,1)}, f32[256,128]{1,0:T(8,128)}, bf16[256,4096]{1,0:T(8,128)(2,1)}, bf16[256,2048]{1,0:T(8,128)(2,1)}, bf16[8,128,12...) custom-call(f32[8]{0:T(128)S(1)} %get-tuple-element.298.slope, bf16[256,1024]{1,0:T(8,128)(2,1)} %copy-done.9, ...), custom_call_target="tpu_custom_call" | custom-call | flops 2147483648 | bytes 8388608 | tf_op jit(solution)/shard_map/project/pallas_call | solution.py:180
  95.7 8.4 %project.7 = (bf16[256,1024]{1,0:T(8,128)(2,1)}, f32[256,128]{1,0:T(8,128)}, bf16[256,4096]{1,0:T(8,128)(2,1)}, bf16[256,2048]{1,0:T(8,128)(2,1)}, bf16[8,128,12...) custom-call(f32[8]{0:T(128)S(1)} %get-tuple-element.298.slope, bf16[256,1024]{1,0:T(8,128)(2,1)} %copy-done.10, ...), custom_call_target="tpu_custom_call" | custom-call | flops 2147483648 | bytes 8388608 | tf_op jit(solution)/shard_map/project/pallas_call | solution.py:180
  107.7 12.9 %finish.6 = (bf16[256,1024]{1,0:T(8,128)(2,1)}, bf16[256,1024]{1,0:T(8,128)(2,1)}, f32[256,128]{1,0:T(8,128)}, bf16[256,1024]{1,0:T(8,128)(2,1)}, f32[256,128]{1...) custom-call(f32[8]{0:T(128)S(1)} %get-tuple-element.298.slope, ...), custom_call_target="tpu_custom_call" | custom-call | flops 4966055936 | bytes 19398656 | tf_op jit(solution)/shard_map/finish/pallas_call | solution.py:337
  120.6 12.8 %finish.7 = (bf16[256,1024]{1,0:T(8,128)(2,1)}, bf16[256,1024]{1,0:T(8,128)(2,1)}, f32[256,128]{1,0:T(8,128)}, bf16[256,1024]{1,0:T(8,128)(2,1)}, f32[256,128]{1...) custom-call(f32[8]{0:T(128)S(1)} %get-tuple-element.298.slope, ...), custom_call_target="tpu_custom_call" | custom-call | flops 4966055936 | bytes 19398656 | tf_op jit(solution)/shard_map/finish/pallas_call | solution.py:337
  133.4 16.6 %back_channel.4 = (bf16[256,2816]{1,0:T(8,128)(2,1)}, bf16[256,2816]{1,0:T(8,128)(2,1)}, f32[256,1024]{1,0:T(8,128)}, bf16[256,1024]{1,0:T(8,128)(2,1)}, bf16[25...) custom-call(f32[8]{0:T(128)S(1)} %get-tuple-element.298.slope, ...), custom_call_target="tpu_custom_call" | custom-call | flops 4966055936 | bytes 19398656 | tf_op jit(solution)/shard_map/back_channel/pallas_call | solution.py:501
  149.9 16.5 %back_channel.5 = (bf16[256,2816]{1,0:T(8,128)(2,1)}, bf16[256,2816]{1,0:T(8,128)(2,1)}, f32[256,1024]{1,0:T(8,128)}, bf16[256,1024]{1,0:T(8,128)(2,1)}, bf16[25...) custom-call(f32[8]{0:T(128)S(1)} %get-tuple-element.298.slope, ...), custom_call_target="tpu_custom_call" | custom-call | flops 4966055936 | bytes 19398656 | tf_op jit(solution)/shard_map/back_channel/pallas_call | solution.py:501
  170.8 8.3 %back_mixer.4 = (bf16[256,1024]{1,0:T(8,128)(2,1)}, bf16[256,1024]{1,0:T(8,128)(2,1)}, bf16[256,1024]{1,0:T(8,128)(2,1)}) custom-call(f32[8]{0:T(128)S(1)} %get-tuple-element.298.slope, f32[2,8]{1,0:T(2,128)S(1)} %copy-done.2, bf16[256,1024]{1,0:T(8,128)(2,1)} %get-tuple-element.231.dq.refs_14_, bf16[256,1024]{1,0:T(8,128)(2,1)} %get-tuple-element.232.du.refs_20_, ...), custom_call_target="tpu_custom_call" | custom-call | flops 2147483648 | bytes 8388608 | tf_op jit(solution)/shard_map/back_mixer/pallas_call | solution.py:599
  180.4 7.6 %back_mixer.5 = (bf16[256,1024]{1,0:T(8,128)(2,1)}, bf16[256,1024]{1,0:T(8,128)(2,1)}, bf16[256,1024]{1,0:T(8,128)(2,1)}) custom-call(f32[8]{0:T(128)S(1)} %get-tuple-element.298.slope, f32[2,8]{1,0:T(2,128)S(1)} %stack.37.factors, bf16[256,1024]{1,0:T(8,128)(2,1)} %get-tuple-element.240.dq.refs_13_, bf16[256,1024]{1,0:T(8,128)(2,1)} %get-tuple-element.241.du.refs_19_, ...), custom_call_target="tpu_custom_call" | custom-call | flops 2147483648 | bytes 8388608 | tf_op jit(solution)/shard_map/back_mixer/pallas_call | solution.py:599
  188.0 10.0 %collective-permute-start.8 = (bf16[256,1024]{1,0:T(8,128)(2,1)}, bf16[256,1024]{1,0:T(8,128)(2,1)S(1)}, u32[]{:S(2)}, u32[]{:S(2)}) collective-permute-start(bf16[256,1024]{1,0:T(8,128)(2,1)} %get-tuple-element.261), channel_id=1, source_target_pairs={{16,0},{17,1},{18,2},{19,3},{20,4},{21,5},{22,6},{23,7},{24,8},{25... | collective-permute-start | bytes 1572872 | tf_op jit(solution)/shard_map/ppermute | solution.py:1016
  198.9 16.6 %back_channel.6 = (bf16[256,2816]{1,0:T(8,128)(2,1)}, bf16[256,2816]{1,0:T(8,128)(2,1)}, f32[256,1024]{1,0:T(8,128)}, bf16[256,1024]{1,0:T(8,128)(2,1)}, bf16[25...) custom-call(f32[8]{0:T(128)S(1)} %get-tuple-element.298.slope, ...), custom_call_target="tpu_custom_call" | custom-call | flops 4966055936 | bytes 19398656 | tf_op jit(solution)/shard_map/back_channel/pallas_call | solution.py:501
  216.3 8.6 %weight_gradient.4 = (bf16[8,704,128]{2,1,0:T(8,128)(2,1)}, bf16[8,704,128]{2,1,0:T(8,128)(2,1)}, bf16[8,704,128]{2,1,0:T(8,128)(2,1)}, bf16[8,704,128]{2,1,0:T(8,128)(2,1)}) custom-call(s32[5]{0:T(128)S(1)} %stack.36.refs_0_, bf16[256,2816]{1,0:T(8,128)(2,1)} %get-tuple-element.257.refs_1_, bf16[256,2816]{1,0:T(8,128)(2,1)} %get-tuple-element.258.refs_2_, ...), custom_call_target="tpu_custom_call" | custom-call | flops 2952790016 | bytes 5767168 | tf_op jit(solution)/shard_map/weight_gradient/pallas_call | solution.py:718
  230.8 16.6 %back_channel.7 = (bf16[256,2816]{1,0:T(8,128)(2,1)}, bf16[256,2816]{1,0:T(8,128)(2,1)}, f32[256,1024]{1,0:T(8,128)}, bf16[256,1024]{1,0:T(8,128)(2,1)}, bf16[25...) custom-call(f32[8]{0:T(128)S(1)} %get-tuple-element.298.slope, ...), custom_call_target="tpu_custom_call" | custom-call | flops 4966055936 | bytes 19398656 | tf_op jit(solution)/shard_map/back_channel/pallas_call | solution.py:501
  247.7 14.1 %weight_gradient.5 = (bf16[22,256,128]{2,1,0:T(8,128)(2,1)}, bf16[22,256,128]{2,1,0:T(8,128)(2,1)}, bf16[22,256,128]{2,1,0:T(8,128)(2,1)}, bf16[22,256,128]{2,1,...) custom-call(s32[5]{0:T(128)S(1)} %stack.36.refs_0_, ...), custom_call_target="tpu_custom_call" | custom-call | flops 5905580032 | bytes 11534336 | tf_op jit(solution)/shard_map/weight_gradient/pallas_call | solution.py:718
  269.1 11.6 %collective-permute-done.13 = bf16[11,256,128]{2,1,0:T(8,128)(2,1)S(1)} collective-permute-done((bf16[11,256,128]{2,1,0:T(8,128)(2,1)S(1)}, bf16[11,256,128]{2,1,0:T(8,128)(2,1)S(1)}, u32[]{:S(2)}, u32[]{:S(2)}) %collective-permute-start.13) | collective-permute-done | bytes 720928 | tf_op jit(solution)/shard_map/ppermute | solution.py:833
  284.6 7.5 %collective-permute-start.20 = (bf16[11,256,128]{2,1,0:T(8,128)(2,1)S(1)}, bf16[11,256,128]{2,1,0:T(8,128)(2,1)S(1)}, u32[]{:S(2)}, u32[]{:S(2)}) collective-permute-start(bf16[11,256,128]{2,1,0:T(8,128)(2,1)S(1)} %add_convert_fusion.14), channel_id=1, source_target_pairs={{0,1},{3,2},{4,5},{7,6},{8,9},{11,10},{12,13},{15,14},{16,17},{19,... | collective-permute-start | bytes 2162696 | tf_op jit(solution)/shard_map/ppermute | solution.py:859
  300.4 7.7 %collective-permute-done.20 = bf16[11,256,128]{2,1,0:T(8,128)(2,1)S(1)} collective-permute-done((bf16[11,256,128]{2,1,0:T(8,128)(2,1)S(1)}, bf16[11,256,128]{2,1,0:T(8,128)(2,1)S(1)}, u32[]{:S(2)}, u32[]{:S(2)}) %collective-permute-start.20) | collective-permute-done | bytes 720928 | tf_op jit(solution)/shard_map/ppermute | solution.py:859
  311.5 8.4 %back_mixer.6 = (bf16[256,1024]{1,0:T(8,128)(2,1)}, bf16[256,1024]{1,0:T(8,128)(2,1)}, bf16[256,1024]{1,0:T(8,128)(2,1)}) custom-call(f32[8]{0:T(128)S(1)} %get-tuple-element.298.slope, f32[2,8]{1,0:T(2,128)S(1)} %copy-done.2, bf16[256,1024]{1,0:T(8,128)(2,1)} %get-tuple-element.290.dq.refs_6_, bf16[256,1024]{1,0:T(8,128)(2,1)} %get-tuple-element.291.du.refs_12_, ...), custom_call_target="tpu_custom_call" | custom-call | flops 2147483648 | bytes 8388608 | tf_op jit(solution)/shard_map/back_mixer/pallas_call | solution.py:599
  331.9 7.6 %back_mixer.7 = (bf16[256,1024]{1,0:T(8,128)(2,1)}, bf16[256,1024]{1,0:T(8,128)(2,1)}, bf16[256,1024]{1,0:T(8,128)(2,1)}) custom-call(f32[8]{0:T(128)S(1)} %get-tuple-element.298.slope, f32[2,8]{1,0:T(2,128)S(1)} %stack.37.factors, bf16[256,1024]{1,0:T(8,128)(2,1)} %get-tuple-element.299.dq.refs_5_, bf16[256,1024]{1,0:T(8,128)(2,1)} %get-tuple-element.300.du.refs_11_, ...), custom_call_target="tpu_custom_call" | custom-call | flops 2147483648 | bytes 8388608 | tf_op jit(solution)/shard_map/back_mixer/pallas_call | solution.py:599
  350.3 11.5 %weight_gradient.7 = (bf16[16,256,128]{2,1,0:T(8,128)(2,1)}, bf16[16,256,128]{2,1,0:T(8,128)(2,1)}, bf16[16,256,128]{2,1,0:T(8,128)(2,1)}, bf16[16,256,128]{2,1,...) custom-call(s32[5]{0:T(128)S(1)} %stack.36.refs_0_, ...), custom_call_target="tpu_custom_call" | custom-call | flops 4294967296 | bytes 8388608 | tf_op jit(solution)/shard_map/weight_gradient/pallas_call | solution.py:718
  370.0 15.4 %collective-permute-start.43 = (bf16[11,256,128]{2,1,0:T(8,128)(2,1)S(1)}, bf16[11,256,128]{2,1,0:T(8,128)(2,1)S(1)}, u32[]{:S(2)}, u32[]{:S(2)}) collective-permute-start(bf16[11,256,128]{2,1,0:T(8,128)(2,1)S(1)} %fusion.6.inner), channel_id=1, source_target_pairs={{0,1},{1,0},{2,3},{3,2},{4,5},{5,4},{6,7},{7,6},{8,9},{9,8},{10,11... | collective-permute-start | bytes 2162696 | tf_op jit(solution)/shard_map/ppermute | solution.py:853
  389.0 11.9 %collective-permute-done.43.outer = bf16[11,256,128]{2,1,0:T(8,128)(2,1)S(1)} collective-permute-done((bf16[11,256,128]{2,1,0:T(8,128)(2,1)S(1)}, bf16[11,256,128]{2,1,0:T(8,128)(2,1)S(1)}, u32[]{:S(2)}, u32[]{:S(2)}) %collective-permute-start.43) | collective-permute-done | bytes 720928 | tf_op jit(solution)/shard_map/ppermute | solution.py:853
  403.4 6.5 %collective-permute-start.48 = (bf16[8,256,128]{2,1,0:T(8,128)(2,1)S(1)}, bf16[8,256,128]{2,1,0:T(8,128)(2,1)S(1)}, u32[]{:S(2)}, u32[]{:S(2)}) collective-permute-start(bf16[8,256,128]{2,1,0:T(8,128)(2,1)S(1)} %add_convert_fusion.24), channel_id=1, source_target_pairs={{0,1},{3,2},{4,5},{7,6},{8,9},{11,10},{12,13},{15,14},{16,17},{19,... | collective-permute-start | bytes 1572872 | tf_op jit(solution)/shard_map/ppermute | solution.py:859
  411.5 7.0 %collective-permute-done.47.outer = bf16[11,256,128]{2,1,0:T(8,128)(2,1)S(1)} collective-permute-done((bf16[11,256,128]{2,1,0:T(8,128)(2,1)S(1)}, bf16[11,256,128]{2,1,0:T(8,128)(2,1)S(1)}, u32[]{:S(2)}, u32[]{:S(2)}) %collective-permute-start.47) | collective-permute-done | bytes 720928 | tf_op jit(solution)/shard_map/ppermute | solution.py:863
  427.7 7.0 %collective-permute-done.51 = bf16[8,256,128]{2,1,0:T(8,128)(2,1)S(1)} collective-permute-done((bf16[8,256,128]{2,1,0:T(8,128)(2,1)S(1)}, bf16[8,256,128]{2,1,0:T(8,128)(2,1)S(1)}, u32[]{:S(2)}, u32[]{:S(2)}) %collective-permute-start.51) | collective-permute-done | bytes 524320 | tf_op jit(solution)/shard_map/ppermute | solution.py:859
  443.7 6.2 %collective-permute-done.50.outer = bf16[8,256,128]{2,1,0:T(8,128)(2,1)S(1)} collective-permute-done((bf16[8,256,128]{2,1,0:T(8,128)(2,1)S(1)}, bf16[8,256,128]{2,1,0:T(8,128)(2,1)S(1)}, u32[]{:S(2)}, u32[]{:S(2)}) %collective-permute-start.50) | collective-permute-done | bytes 524320 | tf_op jit(solution)/shard_map/ppermute | solution.py:853
  480.2 9.7 %collective-permute-done.17 = bf16[256,1024]{1,0:T(8,128)(2,1)S(1)} collective-permute-done((bf16[256,1024]{1,0:T(8,128)(2,1)S(1)}, bf16[256,1024]{1,0:T(8,128)(2,1)S(1)}, u32[]{:S(2)}, u32[]{:S(2)}) %collective-permute-start.17) | collective-permute-done | bytes 524320 | tf_op jit(solution)/shard_map/ppermute | solution.py:800
  496.9 9.5 %collective-permute-done.57.outer = bf16[8,256,128]{2,1,0:T(8,128)(2,1)S(1)} collective-permute-done((bf16[8,256,128]{2,1,0:T(8,128)(2,1)S(1)}, bf16[8,256,128]{2,1,0:T(8,128)(2,1)S(1)}, u32[]{:S(2)}, u32[]{:S(2)}) %collective-permute-start.57) | collective-permute-done | bytes 524320 | tf_op jit(solution)/shard_map/ppermute | solution.py:863
  (270 shorter events, 163.7 us)
Async XLA Ops:
  3.0 20.7 %collective-permute-start = (bf16[256,1024]{1,0:T(8,128)(2,1)}, bf16[256,1024]{1,0:T(8,128)(2,1)S(1)}, u32[]{:S(2)}, u32[]{:S(2)}) collective-permute-start(bf16[256,1024]{1,0:T(8,128)(2,1)} %get-tuple-element.363), channel_id=1, source_target_pairs={{8,4},{4,8},{9,5},{5,9},{10,6},{6,10},{11,7},{7,11},{24,20},{20,24... | collective-permute-start | bytes 1572872 | tf_op jit(solution)/shard_map/ppermute | solution.py:791
  3.9 19.9 %collective-permute-start.1 = (bf16[256,1024]{1,0:T(8,128)(2,1)}, bf16[256,1024]{1,0:T(8,128)(2,1)}, u32[]{:S(2)}, u32[]{:S(2)}) collective-permute-start(bf16[256,1024]{1,0:T(8,128)(2,1)} %get-tuple-element.362), channel_id=1, source_target_pairs={{4,0},{8,12},{0,8},{12,4},{5,1},{9,13},{1,9},{13,5},{6,2},{10,14},... | collective-permute-start | bytes 1572872 | tf_op jit(solution)/shard_map/ppermute | solution.py:790
  65.0 18.0 %collective-permute-start.3 = (bf16[256,1024]{1,0:T(8,128)(2,1)}, bf16[256,1024]{1,0:T(8,128)(2,1)S(1)}, u32[]{:S(2)}, u32[]{:S(2)}) collective-permute-start(bf16[256,1024]{1,0:T(8,128)(2,1)} %get-tuple-element.198), channel_id=1, source_target_pairs={{0,16},{1,17},{2,18},{3,19},{4,20},{5,21},{6,22},{7,23},{8,24},{9,... | collective-permute-start | bytes 1572872 | tf_op jit(solution)/shard_map/ppermute | solution.py:1008
  179.1 18.9 %collective-permute-start.7 = (bf16[256,1024]{1,0:T(8,128)(2,1)}, bf16[256,1024]{1,0:T(8,128)(2,1)S(1)}, u32[]{:S(2)}, u32[]{:S(2)}) collective-permute-start(bf16[256,1024]{1,0:T(8,128)(2,1)} %get-tuple-element.248), channel_id=1, source_target_pairs={{16,0},{17,1},{18,2},{19,3},{20,4},{21,5},{22,6},{23,7},{24,8},{25... | collective-permute-start | bytes 1572872 | tf_op jit(solution)/shard_map/ppermute | solution.py:1016
  188.0 27.4 %collective-permute-start.8 = (bf16[256,1024]{1,0:T(8,128)(2,1)}, bf16[256,1024]{1,0:T(8,128)(2,1)S(1)}, u32[]{:S(2)}, u32[]{:S(2)}) collective-permute-start(bf16[256,1024]{1,0:T(8,128)(2,1)} %get-tuple-element.261), channel_id=1, source_target_pairs={{16,0},{17,1},{18,2},{19,3},{20,4},{21,5},{22,6},{23,7},{24,8},{25... | collective-permute-start | bytes 1572872 | tf_op jit(solution)/shard_map/ppermute | solution.py:1016
  228.5 18.9 %collective-permute-start.11 = (bf16[11,256,128]{2,1,0:T(8,128)(2,1)S(1)}, bf16[11,256,128]{2,1,0:T(8,128)(2,1)S(1)}, u32[]{:S(2)}, u32[]{:S(2)}) collective-permute-start(bf16[11,256,128]{2,1,0:T(8,128)(2,1)S(1)} %fusion.11), channel_id=1, source_target_pairs={{0,8},{8,0},{4,12},{12,4},{1,9},{9,1},{5,13},{13,5},{2,10},{10,2},... | collective-permute-start | bytes 2162696 | tf_op jit(solution)/shard_map/ppermute | solution.py:833
  261.9 30.2 %collective-permute-start.18 = (bf16[22,256,128]{2,1,0:T(8,128)(2,1)}, bf16[22,256,128]{2,1,0:T(8,128)(2,1)S(1)}, u32[]{:S(2)}, u32[]{:S(2)}) collective-permute-start(bf16[22,256,128]{2,1,0:T(8,128)(2,1)} %get-tuple-element.311), channel_id=1, source_target_pairs={{0,4},{4,0},{8,12},{12,8},{1,5},{5,1},{9,13},{13,9},{2,6},{6,2},{1... | collective-permute-start | bytes 4325384 | tf_op jit(solution)/shard_map/ppermute | solution.py:821
  262.4 18.2 %collective-permute-start.13 = (bf16[11,256,128]{2,1,0:T(8,128)(2,1)S(1)}, bf16[11,256,128]{2,1,0:T(8,128)(2,1)S(1)}, u32[]{:S(2)}, u32[]{:S(2)}) collective-permute-start(bf16[11,256,128]{2,1,0:T(8,128)(2,1)S(1)} %fusion.10), channel_id=1, source_target_pairs={{0,8},{8,0},{4,12},{12,4},{1,9},{9,1},{5,13},{13,5},{2,10},{10,2},... | collective-permute-start | bytes 2162696 | tf_op jit(solution)/shard_map/ppermute | solution.py:833
  264.2 18.9 %collective-permute-start.14 = (bf16[11,256,128]{2,1,0:T(8,128)(2,1)S(1)}, bf16[11,256,128]{2,1,0:T(8,128)(2,1)S(1)}, u32[]{:S(2)}, u32[]{:S(2)}) collective-permute-start(bf16[11,256,128]{2,1,0:T(8,128)(2,1)S(1)} %add_convert_fusion.17), channel_id=1, source_target_pairs={{0,1},{3,2},{4,5},{7,6},{8,9},{11,10},{12,13},{15,14},{16,17},{19,... | collective-permute-start | bytes 2162696 | tf_op jit(solution)/shard_map/ppermute | solution.py:859
  284.2 35.7 %collective-permute-start.28 = (bf16[22,256,128]{2,1,0:T(8,128)(2,1)S(1)}, bf16[22,256,128]{2,1,0:T(8,128)(2,1)S(1)}, u32[]{:S(2)}, u32[]{:S(2)}) collective-permute-start(bf16[22,256,128]{2,1,0:T(8,128)(2,1)S(1)} %copy-done.29), channel_id=1, source_target_pairs={{0,4},{4,0},{8,12},{12,8},{1,5},{5,1},{9,13},{13,9},{2,6},{6,2},{1... | collective-permute-start | bytes 4325384 | tf_op jit(solution)/shard_map/ppermute | solution.py:821
  284.6 23.5 %collective-permute-start.20 = (bf16[11,256,128]{2,1,0:T(8,128)(2,1)S(1)}, bf16[11,256,128]{2,1,0:T(8,128)(2,1)S(1)}, u32[]{:S(2)}, u32[]{:S(2)}) collective-permute-start(bf16[11,256,128]{2,1,0:T(8,128)(2,1)S(1)} %add_convert_fusion.14), channel_id=1, source_target_pairs={{0,1},{3,2},{4,5},{7,6},{8,9},{11,10},{12,13},{15,14},{16,17},{19,... | collective-permute-start | bytes 2162696 | tf_op jit(solution)/shard_map/ppermute | solution.py:859
  292.1 18.6 %collective-permute-start.15 = (bf16[8,128,128]{2,1,0:T(8,128)(2,1)S(1)}, bf16[8,128,128]{2,1,0:T(8,128)(2,1)S(1)}, u32[]{:S(2)}, u32[]{:S(2)}) collective-permute-start(bf16[8,128,128]{2,1,0:T(8,128)(2,1)S(1)} %copy-done.32), channel_id=1, source_target_pairs={{4,0},{12,8},{5,1},{13,9},{6,2},{14,10},{7,3},{15,11},{20,16},{28,... | collective-permute-start | bytes 786440 | tf_op jit(solution)/shard_map/ppermute | solution.py:946
  298.1 41.4 %collective-permute-start.27 = (bf16[22,256,128]{2,1,0:T(8,128)(2,1)S(1)}, bf16[22,256,128]{2,1,0:T(8,128)(2,1)S(1)}, u32[]{:S(2)}, u32[]{:S(2)}) collective-permute-start(bf16[22,256,128]{2,1,0:T(8,128)(2,1)S(1)} %copy-done.28), channel_id=1, source_target_pairs={{0,4},{4,0},{8,12},{12,8},{1,5},{5,1},{9,13},{13,9},{2,6},{6,2},{1... | collective-permute-start | bytes 4325384 | tf_op jit(solution)/shard_map/ppermute | solution.py:821
  298.1 22.0 %collective-permute-start.29 = (bf16[11,256,128]{2,1,0:T(8,128)(2,1)S(1)}, bf16[11,256,128]{2,1,0:T(8,128)(2,1)S(1)}, u32[]{:S(2)}, u32[]{:S(2)}) collective-permute-start(bf16[11,256,128]{2,1,0:T(8,128)(2,1)S(1)} %add_convert_fusion.13), channel_id=1, source_target_pairs={{0,8},{8,0},{4,12},{12,4},{1,9},{9,1},{5,13},{13,5},{2,10},{10,2},... | collective-permute-start | bytes 2162696 | tf_op jit(solution)/shard_map/ppermute | solution.py:833
  308.1 18.5 %collective-permute-start.37 = (bf16[11,256,128]{2,1,0:T(8,128)(2,1)S(1)}, bf16[11,256,128]{2,1,0:T(8,128)(2,1)S(1)}, u32[]{:S(2)}, u32[]{:S(2)}) collective-permute-start(bf16[11,256,128]{2,1,0:T(8,128)(2,1)S(1)} %fusion), channel_id=1, source_target_pairs={{0,1},{1,0},{2,3},{3,2},{4,5},{5,4},{6,7},{7,6},{8,9},{9,8},{10,11... | collective-permute-start | bytes 2162696 | tf_op jit(solution)/shard_map/ppermute | solution.py:853
  320.1 24.5 %collective-permute-start.30 = (bf16[11,256,128]{2,1,0:T(8,128)(2,1)S(1)}, bf16[11,256,128]{2,1,0:T(8,128)(2,1)S(1)}, u32[]{:S(2)}, u32[]{:S(2)}) collective-permute-start(bf16[11,256,128]{2,1,0:T(8,128)(2,1)S(1)} %add_convert_fusion.8), channel_id=1, source_target_pairs={{0,8},{8,0},{4,12},{12,4},{1,9},{9,1},{5,13},{13,5},{2,10},{10,2},... | collective-permute-start | bytes 2162696 | tf_op jit(solution)/shard_map/ppermute | solution.py:833
  344.6 18.0 %collective-permute-start.26 = (bf16[16,256,128]{2,1,0:T(8,128)(2,1)}, bf16[16,256,128]{2,1,0:T(8,128)(2,1)S(1)}, u32[]{:S(2)}, u32[]{:S(2)}) collective-permute-start(bf16[16,256,128]{2,1,0:T(8,128)(2,1)} %get-tuple-element.332), channel_id=1, source_target_pairs={{0,4},{4,0},{8,12},{12,8},{1,5},{5,1},{9,13},{13,9},{2,6},{6,2},{1... | collective-permute-start | bytes 3145736 | tf_op jit(solution)/shard_map/ppermute | solution.py:821
  344.7 18.8 %collective-permute-start.31 = (bf16[11,256,128]{2,1,0:T(8,128)(2,1)S(1)}, bf16[11,256,128]{2,1,0:T(8,128)(2,1)S(1)}, u32[]{:S(2)}, u32[]{:S(2)}) collective-permute-start(bf16[11,256,128]{2,1,0:T(8,128)(2,1)S(1)} %add_convert_fusion.9), channel_id=1, source_target_pairs={{0,8},{8,0},{4,12},{12,4},{1,9},{9,1},{5,13},{13,5},{2,10},{10,2},... | collective-permute-start | bytes 2162696 | tf_op jit(solution)/shard_map/ppermute | solution.py:833
  347.7 17.7 %collective-permute-start.41 = (bf16[11,256,128]{2,1,0:T(8,128)(2,1)S(1)}, bf16[11,256,128]{2,1,0:T(8,128)(2,1)S(1)}, u32[]{:S(2)}, u32[]{:S(2)}) collective-permute-start(bf16[11,256,128]{2,1,0:T(8,128)(2,1)S(1)} %fusion.4.inner), channel_id=1, source_target_pairs={{0,1},{1,0},{2,3},{3,2},{4,5},{5,4},{6,7},{7,6},{8,9},{9,8},{10,11... | collective-permute-start | bytes 2162696 | tf_op jit(solution)/shard_map/ppermute | solution.py:853
  361.9 40.0 %collective-permute-start.24 = (bf16[16,256,128]{2,1,0:T(8,128)(2,1)}, bf16[16,256,128]{2,1,0:T(8,128)(2,1)S(1)}, u32[]{:S(2)}, u32[]{:S(2)}) collective-permute-start(bf16[16,256,128]{2,1,0:T(8,128)(2,1)} %get-tuple-element.329), channel_id=1, source_target_pairs={{0,4},{4,0},{8,12},{12,8},{1,5},{5,1},{9,13},{13,9},{2,6},{6,2},{1... | collective-permute-start | bytes 3145736 | tf_op jit(solution)/shard_map/ppermute | solution.py:821
  363.4 22.2 %collective-permute-start.25 = (bf16[16,256,128]{2,1,0:T(8,128)(2,1)S(1)}, bf16[16,256,128]{2,1,0:T(8,128)(2,1)S(1)}, u32[]{:S(2)}, u32[]{:S(2)}) collective-permute-start(bf16[16,256,128]{2,1,0:T(8,128)(2,1)S(1)} %copy-done.31), channel_id=1, source_target_pairs={{0,4},{4,0},{8,12},{12,8},{1,5},{5,1},{9,13},{13,9},{2,6},{6,2},{1... | collective-permute-start | bytes 3145736 | tf_op jit(solution)/shard_map/ppermute | solution.py:821
  365.4 20.5 %collective-permute-start.32 = (bf16[8,256,128]{2,1,0:T(8,128)(2,1)S(1)}, bf16[8,256,128]{2,1,0:T(8,128)(2,1)S(1)}, u32[]{:S(2)}, u32[]{:S(2)}) collective-permute-start(bf16[8,256,128]{2,1,0:T(8,128)(2,1)S(1)} %add_convert_fusion.31), channel_id=1, source_target_pairs={{0,8},{8,0},{4,12},{12,4},{1,9},{9,1},{5,13},{13,5},{2,10},{10,2},... | collective-permute-start | bytes 1572872 | tf_op jit(solution)/shard_map/ppermute | solution.py:833
  368.9 18.5 %collective-permute-start.46 = (bf16[11,256,128]{2,1,0:T(8,128)(2,1)S(1)}, bf16[11,256,128]{2,1,0:T(8,128)(2,1)S(1)}, u32[]{:S(2)}, u32[]{:S(2)}) collective-permute-start(bf16[11,256,128]{2,1,0:T(8,128)(2,1)S(1)} %fusion.5), channel_id=1, source_target_pairs={{1,2},{2,1},{5,6},{6,5},{9,10},{10,9},{13,14},{14,13},{17,18},{18,... | collective-permute-start | bytes 2162696 | tf_op jit(solution)/shard_map/ppermute | solution.py:849
  370.0 30.9 %collective-permute-start.43 = (bf16[11,256,128]{2,1,0:T(8,128)(2,1)S(1)}, bf16[11,256,128]{2,1,0:T(8,128)(2,1)S(1)}, u32[]{:S(2)}, u32[]{:S(2)}) collective-permute-start(bf16[11,256,128]{2,1,0:T(8,128)(2,1)S(1)} %fusion.6.inner), channel_id=1, source_target_pairs={{0,1},{1,0},{2,3},{3,2},{4,5},{5,4},{6,7},{7,6},{8,9},{9,8},{10,11... | collective-permute-start | bytes 2162696 | tf_op jit(solution)/shard_map/ppermute | solution.py:853
  385.6 55.5 %collective-permute-start.22 = (bf16[16,256,128]{2,1,0:T(8,128)(2,1)S(1)}, bf16[16,256,128]{2,1,0:T(8,128)(2,1)S(1)}, u32[]{:S(2)}, u32[]{:S(2)}) collective-permute-start(bf16[16,256,128]{2,1,0:T(8,128)(2,1)S(1)} %copy-done.30), channel_id=1, source_target_pairs={{0,4},{4,0},{8,12},{12,8},{1,5},{5,1},{9,13},{13,9},{2,6},{6,2},{1... | collective-permute-start | bytes 3145736 | tf_op jit(solution)/shard_map/ppermute | solution.py:821
  385.9 24.0 %collective-permute-start.33 = (bf16[8,256,128]{2,1,0:T(8,128)(2,1)S(1)}, bf16[8,256,128]{2,1,0:T(8,128)(2,1)S(1)}, u32[]{:S(2)}, u32[]{:S(2)}) collective-permute-start(bf16[8,256,128]{2,1,0:T(8,128)(2,1)S(1)} %add_convert_fusion.32), channel_id=1, source_target_pairs={{0,8},{8,0},{4,12},{12,4},{1,9},{9,1},{5,13},{13,5},{2,10},{10,2},... | collective-permute-start | bytes 1572872 | tf_op jit(solution)/shard_map/ppermute | solution.py:833
  387.6 30.8 %collective-permute-start.47 = (bf16[11,256,128]{2,1,0:T(8,128)(2,1)S(1)}, bf16[11,256,128]{2,1,0:T(8,128)(2,1)S(1)}, u32[]{:S(2)}, u32[]{:S(2)}) collective-permute-start(bf16[11,256,128]{2,1,0:T(8,128)(2,1)S(1)} %add_convert_fusion.inner), channel_id=1, source_target_pairs={{1,0},{2,3},{5,4},{6,7},{9,8},{10,11},{13,12},{14,15},{17,16},{18,... | collective-permute-start | bytes 2162696 | tf_op jit(solution)/shard_map/ppermute | solution.py:863
  401.1 18.6 %collective-permute-start.44 = (bf16[11,256,128]{2,1,0:T(8,128)(2,1)S(1)}, bf16[11,256,128]{2,1,0:T(8,128)(2,1)S(1)}, u32[]{:S(2)}, u32[]{:S(2)}) collective-permute-start(bf16[11,256,128]{2,1,0:T(8,128)(2,1)S(1)} %fusion.7), channel_id=1, source_target_pairs={{1,2},{2,1},{5,6},{6,5},{9,10},{10,9},{13,14},{14,13},{17,18},{18,... | collective-permute-start | bytes 2162696 | tf_op jit(solution)/shard_map/ppermute | solution.py:849
  403.4 22.4 %collective-permute-start.48 = (bf16[8,256,128]{2,1,0:T(8,128)(2,1)S(1)}, bf16[8,256,128]{2,1,0:T(8,128)(2,1)S(1)}, u32[]{:S(2)}, u32[]{:S(2)}) collective-permute-start(bf16[8,256,128]{2,1,0:T(8,128)(2,1)S(1)} %add_convert_fusion.24), channel_id=1, source_target_pairs={{0,1},{3,2},{4,5},{7,6},{8,9},{11,10},{12,13},{15,14},{16,17},{19,... | collective-permute-start | bytes 1572872 | tf_op jit(solution)/shard_map/ppermute | solution.py:859
  419.9 17.8 %collective-permute-start.45 = (bf16[11,256,128]{2,1,0:T(8,128)(2,1)S(1)}, bf16[11,256,128]{2,1,0:T(8,128)(2,1)S(1)}, u32[]{:S(2)}, u32[]{:S(2)}) collective-permute-start(bf16[11,256,128]{2,1,0:T(8,128)(2,1)S(1)} %add_convert_fusion.1.inner), channel_id=1, source_target_pairs={{1,0},{2,3},{5,4},{6,7},{9,8},{10,11},{13,12},{14,15},{17,16},{18,... | collective-permute-start | bytes 2162696 | tf_op jit(solution)/shard_map/ppermute | solution.py:863
  477.4 18.3 %collective-permute-start.59 = (bf16[8,256,128]{2,1,0:T(8,128)(2,1)S(1)}, bf16[8,256,128]{2,1,0:T(8,128)(2,1)S(1)}, u32[]{:S(2)}, u32[]{:S(2)}) collective-permute-start(bf16[8,256,128]{2,1,0:T(8,128)(2,1)S(1)} %add_convert_fusion.18.inner), channel_id=1, source_target_pairs={{1,0},{2,3},{5,4},{6,7},{9,8},{10,11},{13,12},{14,15},{17,16},{18,... | collective-permute-start | bytes 1572872 | tf_op jit(solution)/shard_map/ppermute | solution.py:863
  478.9 27.5 %collective-permute-start.57 = (bf16[8,256,128]{2,1,0:T(8,128)(2,1)S(1)}, bf16[8,256,128]{2,1,0:T(8,128)(2,1)S(1)}, u32[]{:S(2)}, u32[]{:S(2)}) collective-permute-start(bf16[8,256,128]{2,1,0:T(8,128)(2,1)S(1)} %add_convert_fusion.19.inner), channel_id=1, source_target_pairs={{1,0},{2,3},{5,4},{6,7},{9,8},{10,11},{13,12},{14,15},{17,16},{18,... | collective-permute-start | bytes 1572872 | tf_op jit(solution)/shard_map/ppermute | solution.py:863
  (71 other events, 746.0 us)

commit v4 on v3

--- a/solution.py
+++ b/solution.py
@@ -103,7 +103,7 @@
 
 
 def project_body(slope, x, cosine, sine, before, w, h1, r1, pre, qk, state, joined,
-                 xv, cv, sv, bv, hv, rv, prev, qkv, stv, jv, isem, osem):
+                 xv, cv, sv, bv, hv, rv, prev, qkv, stv, jv, isem, osem, qsem):
     rows, width = x.shape
     steps = STEPS
     columns = w.shape[1] // steps
@@ -130,6 +130,10 @@
         at = pl.ds(pl.multiple_of(j * columns, LANES), columns)
         return pltpu.make_async_copy(prev.at[:, at], pre.at[:, at], osem.at[3 + j])
 
+    def qk_out(j):
+        at = pl.ds(pl.multiple_of(j * columns, LANES), columns)
+        return pltpu.make_async_copy(qkv.at[:, at], qk.at[:, at], qsem.at[j])
+
     def step(j, carry):
         at = pl.multiple_of(j * columns, LANES)
         p = nn(hv[...], w[:, pl.ds(at, columns)])
@@ -143,6 +147,7 @@
                 v = v * sigmoid(v)
                 turned = v * cv[...] + half_turn(v) * sv[...]
                 qkv[:, pl.ds(at + n * LANES, LANES)] = turned.astype(bf16)
+            qk_out(j).start()
 
         @pl.when((j >= steps // 2) & (j < 3 * steps // 4))
         def _():
@@ -161,7 +166,6 @@
 
     lax.fori_loop(0, steps, step, 0)
     last = [
-        pltpu.make_async_copy(qkv, qk, osem.at[2]),
         pltpu.make_async_copy(stv, state, osem.at[11]),
         pltpu.make_async_copy(jv, joined, osem.at[12]),
     ]
@@ -171,6 +175,8 @@
         copy.wait()
     for j in range(steps):
         pre_out(j).wait()
+    for j in range(steps // 2):
+        qk_out(j).wait()
 
 
 def project(slopes, x, cosine, sine, before, w):
@@ -202,6 +208,7 @@
             pltpu.VMEM(states, bf16),
             pltpu.SemaphoreType.DMA((4,)),
             pltpu.SemaphoreType.DMA((13,)),
+            pltpu.SemaphoreType.DMA((STEPS // 2,)),
         ],
         compiler_params=params(8),
         cost_estimate=pl.CostEstimate(
@@ -369,7 +376,7 @@
     dg, dup, dmid, dm, dq, du, dk, dv, state, joined,
     dyv, gv, upv, h2v, r2v, mixedv, rav, qkv, qpv, vuv, lowv, cv, sv, bv,
     dgv, dupv, dmidv, dmv, dqv, duv, dkv, dvv, statev, jv,
-    total, datt, heldg, heldu, isem, osem, csem,
+    total, datt, heldg, heldu, isem, osem, csem, psem,
 ):
     rows, width = dy.shape
     hidden = wd.shape[0]
@@ -384,10 +391,12 @@
         ),
         isem,
     )
-    for copy in ins:
+    for copy in ins[:3]:
         copy.start()
     for copy in ins[:3]:
         copy.wait()
+    for copy in ins[3:]:
+        copy.start()
     heldg[...] = jnp.zeros_like(heldg)
     heldu[...] = jnp.zeros_like(heldu)
     total[...] = jnp.zeros_like(total)
@@ -439,6 +448,17 @@
     row = lax.broadcasted_iota(jnp.int32, (rows, rows), 0)
     column = lax.broadcasted_iota(jnp.int32, (rows, rows), 1)
     distance = (row - column).astype(f32)
+
+    early = moves(((duv, du),), osem, 2)
+    for copy in early:
+        copy.start()
+
+    def pair_out(i):
+        at = pl.ds(pl.multiple_of(i * 2 * LANES, LANES), 2 * LANES)
+        return [
+            pltpu.make_async_copy(source.at[:, at], target.at[:, at], psem.at[n, i])
+            for n, (source, target) in enumerate(((dqv, dq), (dkv, dk), (dvv, dv)))
+        ]
 
     def some(i, carry):
         for m in range(2):
@@ -464,16 +484,19 @@
             dqv[:, lane] = (turned * (s * (1.0 + p * (1.0 - s)))).astype(bf16)
             dkv[:, lane] = nn(scores_t, query)
             dvv[:, lane] = nn(weights_t, cot)
+        for copy in pair_out(i):
+            copy.start()
         return carry
 
     lax.fori_loop(0, HEADS // 2, some, 0)
-    last = moves(
-        ((statev, state), (jv, joined), (dqv, dq), (duv, du), (dkv, dk), (dvv, dv)), osem, 2
-    )
+    last = moves(((statev, state), (jv, joined)), osem, 3)
     for copy in last:
         copy.start()
-    for copy in outs + last:
+    for copy in outs + early + last:
         copy.wait()
+    for i in range(HEADS // 2):
+        for copy in pair_out(i):
+            copy.wait()
 
     def drain(i, carry):
         for copy in chunk_out(i):
@@ -514,8 +537,9 @@
             pltpu.VMEM((rows, columns), bf16),
             pltpu.VMEM((rows, columns), bf16),
             pltpu.SemaphoreType.DMA((14,)),
-            pltpu.SemaphoreType.DMA((8,)),
+            pltpu.SemaphoreType.DMA((5,)),
             pltpu.SemaphoreType.DMA((2, steps)),
+            pltpu.SemaphoreType.DMA((3, HEADS // 2)),
         ],
         compiler_params=params(22),
         cost_estimate=pl.CostEstimate(
@@ -536,7 +560,7 @@
 def back_mixer_body(
     slope, factors, dq, du, dk, dv, qk, pre, far, near, cosine, sine, h1, r1, dmid, w,
     dkp, dvp, dx,
-    dkin, dvin, kvv, kpv, vv, statev, cv, sv, h1v, r1v, dmidv, parts, dxv, isem, osem,
+    dkin, dvin, kvv, kpv, vv, statev, cv, sv, h1v, r1v, dmidv, parts, dxv, total, isem, osem,
 ):
     rows, width = dq.shape
     ins = moves(
@@ -580,8 +604,15 @@
         copy.start()
     for copy in ins[9:]:
         copy.wait()
-    total = nt(parts[...], w[...])
-    back = norm_back(total, h1v[...].astype(f32), r1v[:, 0:1], width)
+    columns = 512
+
+    def step(j, carry):
+        at = pl.ds(pl.multiple_of(j * columns, LANES), columns)
+        total[:, at] = nt(parts[...], w[at, :])
+        return carry
+
+    lax.fori_loop(0, width // columns, step, 0)
+    back = norm_back(total[...], h1v[...].astype(f32), r1v[:, 0:1], width)
     dxv[...] = (dmidv[...] + back).astype(bf16)
     last = moves(((dxv, dx),), osem, 2)
     for copy in last:
@@ -605,7 +636,7 @@
             full, full, wide, wide, wide, pltpu.VMEM((2 * HEADS, LANES, LANES), bf16), thin, thin,
             wide, thin,
             full,
-            pltpu.VMEM((rows, w.shape[1]), bf16), wide,
+            pltpu.VMEM((rows, w.shape[1]), bf16), wide, full,
             pltpu.SemaphoreType.DMA((14,)),
             pltpu.SemaphoreType.DMA((3,)),
         ],
@@ -1055,22 +1086,22 @@
             way()
         order.at(*order.last, *sums.started())
 
+    half, eight = hidden // LANES // 2, width // LANES
     early.back_first(1, returned[1])
     early.blocks[0]["dy"] = returned[0]
     gradient("product", ("dy",), [(0, 0, 4), (0, 4, 4)])
     move(sums.over_y)
     early.back_first(0, returned[0])
-    move(sums.over_y, sums.over_z)
-    half = hidden // LANES // 2
+    pass
     gradient("h2", ("dg", "dup"), [(0, 0, half), (0, half, half), (1, 0, half), (1, half, half)])
-    move(sums.over_y, sums.over_z)
+    pass
     dx = [None, None]
     for b in (1, 0):
         dx[b] = early.back_second(b)
     move(sums.over_y, sums.over_z)
-    eight = width // LANES
     gradient("gated", ("dm",), [(0, 0, eight)])
     gradient("h1", ("dq", "dkp", "dvp", "du"), [(s, 0, eight) for s in range(4)])
+
     ends = [jnp.where(is_first, dx[b], outputs[b]) for b in range(2)]
     joined = jnp.stack(quarters(*ends) if usual else ends)[None]
     if usual:

time: 517 us -> 497 us (0.961)
  starting transfers between devices: 113 us -> 92.7 us
    ppermute x7, starting transfers between devices: 29.5 us -> 19.1 us  [over_z(): got = lax.ppermute(sent, 'dp', [(0, 1), (1, 0), (2, 3), (3, 2)])]
    ppermute x7, waiting for transfers between devices: 37.4 us -> 28.4 us  [over_z(): got = lax.ppermute(sent, 'dp', [(0, 1), (1, 0), (2, 3), (3, 2)])]
    ppermute x11, waiting for transfers between devices: 16.1 us -> 22.2 us  [over_y(): self.previous = lax.ppermute(far, 'seq', [(0, 2), (2, 0), (1, 3), (3, 1)])]
  transfers between devices with their start and end apart: 60 -> 60, of which waited for: 22 -> 22; matrix products, arithmetic and copies ran while one was open for 3% -> 3% of each run, Pallas kernels for 21% -> 25%
where the time goes in v4:
time: 497 us; the launch traced here: 488 us
  Pallas kernels  234 us (47%)
  waiting for transfers between devices  114 us (23%)
  starting transfers between devices  92.7 us (19%)
  other arithmetic  20.5 us (4%)
  local copies, waits for them, and re-layouts  12 us (2%)
  blocking collectives  11.6 us (2%)
    pallas_call x4, Pallas kernels, back_channel(): pl.pallas_call(back_channel_body, in_specs=[SMEM] + [ANY] + [VMEM] * 3 +...  64.2 us
    pallas_call x4, Pallas kernels, finish(): pl.pallas_call(finish_body, in_specs=[SMEM] * 2 + [ANY] * 5 + [VMEM] * 3,...  52 us
    pallas_call x4, Pallas kernels, weight_gradient(): pl.pallas_call(functools.partial(weight_body, batch=batch, sides=sides, g...  39.3 us
    pallas_call x4, Pallas kernels, back_mixer(): pl.pallas_call(back_mixer_body, in_specs=[SMEM] * 2 + [ANY] * 13 + [VMEM]...  33.3 us
    pallas_call x4, Pallas kernels, project(): pl.pallas_call(project_body, in_specs=[SMEM] + [ANY] * 4 + [VMEM], out_sp...  32.8 us
    ppermute x7, waiting for transfers between devices, over_z(): got = lax.ppermute(sent, 'dp', [(0, 1), (1, 0), (2, 3), (3, 2)])  28.4 us
    ppermute x4, waiting for transfers between devices, over_z(): lax.ppermute(done, 'dp', [(1, 0), (2, 3)])  24.3 us
    ppermute x11, waiting for transfers between devices, over_y(): self.previous = lax.ppermute(far, 'seq', [(0, 2), (2, 0), (1, 3), (3, 1)])  22.2 us
  transfers between devices with their start and end apart: 60, of which 22 were waited for; matrix products, arithmetic and copies ran while one was open for 3% of the time, Pallas kernels for 25%

profile of v4, /device:TPU:0, one launch (start us, length us, event | category | flops | bytes accessed | tf_op | source)
XLA Modules:
  0.0 487.7 jit_solution(1182545588578267029)
XLA Ops:
  7.5 11.6 %all-gather.1 = s32[4,2,256]{2,1,0:T(2,128)S(1)} all-gather(s32[1,2,256]{2,1,0:T(2,128)S(1)} %bitcast.110), channel_id=2, replica_groups=mesh['section'=2,'seq'=4,'dp'=4] {'seq'}, dimensions={0}, use_global_device_ids=true | all-gather | bytes 10240 | tf_op jit(solution)/shard_map/all_gather | solution.py:1008
  27.6 8.3 %project.4 = (bf16[256,1024]{1,0:T(8,128)(2,1)}, f32[256,128]{1,0:T(8,128)}, bf16[256,4096]{1,0:T(8,128)(2,1)}, bf16[256,2048]{1,0:T(8,128)(2,1)}, bf16[8,128,12...) custom-call(f32[8]{0:T(128)S(1)} %get-tuple-element.293.slope, bf16[256,1024]{1,0:T(8,128)(2,1)} %get-tuple-element.355.x.dy.refs_7_, ...), custom_call_target="tpu_custom_call" | custom-call | flops 2147483648 | bytes 8388608 | tf_op jit(solution)/shard_map/project/pallas_call | solution.py:186
  36.0 8.3 %project.5 = (bf16[256,1024]{1,0:T(8,128)(2,1)}, f32[256,128]{1,0:T(8,128)}, bf16[256,4096]{1,0:T(8,128)(2,1)}, bf16[256,2048]{1,0:T(8,128)(2,1)}, bf16[8,128,12...) custom-call(f32[8]{0:T(128)S(1)} %get-tuple-element.293.slope, bf16[256,1024]{1,0:T(8,128)(2,1)} %get-tuple-element.354.x.dy.refs_8_, ...), custom_call_target="tpu_custom_call" | custom-call | flops 2147483648 | bytes 8388608 | tf_op jit(solution)/shard_map/project/pallas_call | solution.py:186
  48.7 13.2 %finish.4 = (bf16[256,1024]{1,0:T(8,128)(2,1)}, bf16[256,1024]{1,0:T(8,128)(2,1)}, f32[256,128]{1,0:T(8,128)}, bf16[256,1024]{1,0:T(8,128)(2,1)}, f32[256,128]{1...) custom-call(f32[8]{0:T(128)S(1)} %get-tuple-element.293.slope, ...), custom_call_target="tpu_custom_call" | custom-call | flops 4966055936 | bytes 19398656 | tf_op jit(solution)/shard_map/finish/pallas_call | solution.py:344
  65.7 13.1 %finish.5 = (bf16[256,1024]{1,0:T(8,128)(2,1)}, bf16[256,1024]{1,0:T(8,128)(2,1)}, f32[256,128]{1,0:T(8,128)}, bf16[256,1024]{1,0:T(8,128)(2,1)}, f32[256,128]{1...) custom-call(f32[8]{0:T(128)S(1)} %get-tuple-element.293.slope, ...), custom_call_target="tpu_custom_call" | custom-call | flops 4966055936 | bytes 19398656 | tf_op jit(solution)/shard_map/finish/pallas_call | solution.py:344
  81.0 8.1 %project.6 = (bf16[256,1024]{1,0:T(8,128)(2,1)}, f32[256,128]{1,0:T(8,128)}, bf16[256,4096]{1,0:T(8,128)(2,1)}, bf16[256,2048]{1,0:T(8,128)(2,1)}, bf16[8,128,12...) custom-call(f32[8]{0:T(128)S(1)} %get-tuple-element.293.slope, bf16[256,1024]{1,0:T(8,128)(2,1)} %copy-done.9, ...), custom_call_target="tpu_custom_call" | custom-call | flops 2147483648 | bytes 8388608 | tf_op jit(solution)/shard_map/project/pallas_call | solution.py:186
  92.9 8.1 %project.7 = (bf16[256,1024]{1,0:T(8,128)(2,1)}, f32[256,128]{1,0:T(8,128)}, bf16[256,4096]{1,0:T(8,128)(2,1)}, bf16[256,2048]{1,0:T(8,128)(2,1)}, bf16[8,128,12...) custom-call(f32[8]{0:T(128)S(1)} %get-tuple-element.293.slope, bf16[256,1024]{1,0:T(8,128)(2,1)} %copy-done.10, ...), custom_call_target="tpu_custom_call" | custom-call | flops 2147483648 | bytes 8388608 | tf_op jit(solution)/shard_map/project/pallas_call | solution.py:186
  104.5 12.9 %finish.6 = (bf16[256,1024]{1,0:T(8,128)(2,1)}, bf16[256,1024]{1,0:T(8,128)(2,1)}, f32[256,128]{1,0:T(8,128)}, bf16[256,1024]{1,0:T(8,128)(2,1)}, f32[256,128]{1...) custom-call(f32[8]{0:T(128)S(1)} %get-tuple-element.293.slope, ...), custom_call_target="tpu_custom_call" | custom-call | flops 4966055936 | bytes 19398656 | tf_op jit(solution)/shard_map/finish/pallas_call | solution.py:344
  117.4 12.8 %finish.7 = (bf16[256,1024]{1,0:T(8,128)(2,1)}, bf16[256,1024]{1,0:T(8,128)(2,1)}, f32[256,128]{1,0:T(8,128)}, bf16[256,1024]{1,0:T(8,128)(2,1)}, f32[256,128]{1...) custom-call(f32[8]{0:T(128)S(1)} %get-tuple-element.293.slope, ...), custom_call_target="tpu_custom_call" | custom-call | flops 4966055936 | bytes 19398656 | tf_op jit(solution)/shard_map/finish/pallas_call | solution.py:344
  130.2 16.1 %back_channel.4 = (bf16[256,2816]{1,0:T(8,128)(2,1)}, bf16[256,2816]{1,0:T(8,128)(2,1)}, f32[256,1024]{1,0:T(8,128)}, bf16[256,1024]{1,0:T(8,128)(2,1)}, bf16[25...) custom-call(f32[8]{0:T(128)S(1)} %get-tuple-element.293.slope, ...), custom_call_target="tpu_custom_call" | custom-call | flops 4966055936 | bytes 19398656 | tf_op jit(solution)/shard_map/back_channel/pallas_call | solution.py:524
  146.3 16.0 %back_channel.5 = (bf16[256,2816]{1,0:T(8,128)(2,1)}, bf16[256,2816]{1,0:T(8,128)(2,1)}, f32[256,1024]{1,0:T(8,128)}, bf16[256,1024]{1,0:T(8,128)(2,1)}, bf16[25...) custom-call(f32[8]{0:T(128)S(1)} %get-tuple-element.293.slope, ...), custom_call_target="tpu_custom_call" | custom-call | flops 4966055936 | bytes 19398656 | tf_op jit(solution)/shard_map/back_channel/pallas_call | solution.py:524
  166.7 8.6 %back_mixer.4 = (bf16[256,1024]{1,0:T(8,128)(2,1)}, bf16[256,1024]{1,0:T(8,128)(2,1)}, bf16[256,1024]{1,0:T(8,128)(2,1)}) custom-call(f32[8]{0:T(128)S(1)} %get-tuple-element.293.slope, f32[2,8]{1,0:T(2,128)S(1)} %copy-done.2, bf16[256,1024]{1,0:T(8,128)(2,1)} %get-tuple-element.231.dq.refs_14_, bf16[256,1024]{1,0:T(8,128)(2,1)} %get-tuple-element.232.du.refs_20_, ...), custom_call_target="tpu_custom_call" | custom-call | flops 2147483648 | bytes 8388608 | tf_op jit(solution)/shard_map/back_mixer/pallas_call | solution.py:630
  176.6 7.9 %back_mixer.5 = (bf16[256,1024]{1,0:T(8,128)(2,1)}, bf16[256,1024]{1,0:T(8,128)(2,1)}, bf16[256,1024]{1,0:T(8,128)(2,1)}) custom-call(f32[8]{0:T(128)S(1)} %get-tuple-element.293.slope, f32[2,8]{1,0:T(2,128)S(1)} %stack.37.factors, bf16[256,1024]{1,0:T(8,128)(2,1)} %get-tuple-element.240.dq.refs_13_, bf16[256,1024]{1,0:T(8,128)(2,1)} %get-tuple-element.241.du.refs_19_, ...), custom_call_target="tpu_custom_call" | custom-call | flops 2147483648 | bytes 8388608 | tf_op jit(solution)/shard_map/back_mixer/pallas_call | solution.py:630
  184.6 10.0 %collective-permute-start.8 = (bf16[256,1024]{1,0:T(8,128)(2,1)}, bf16[256,1024]{1,0:T(8,128)(2,1)S(1)}, u32[]{:S(2)}, u32[]{:S(2)}) collective-permute-start(bf16[256,1024]{1,0:T(8,128)(2,1)} %get-tuple-element.261), channel_id=1, source_target_pairs={{16,0},{17,1},{18,2},{19,3},{20,4},{21,5},{22,6},{23,7},{24,8},{25... | collective-permute-start | bytes 1572872 | tf_op jit(solution)/shard_map/ppermute | solution.py:1047
  195.4 16.0 %back_channel.6 = (bf16[256,2816]{1,0:T(8,128)(2,1)}, bf16[256,2816]{1,0:T(8,128)(2,1)}, f32[256,1024]{1,0:T(8,128)}, bf16[256,1024]{1,0:T(8,128)(2,1)}, bf16[25...) custom-call(f32[8]{0:T(128)S(1)} %get-tuple-element.293.slope, ...), custom_call_target="tpu_custom_call" | custom-call | flops 4966055936 | bytes 19398656 | tf_op jit(solution)/shard_map/back_channel/pallas_call | solution.py:524
  212.2 8.6 %weight_gradient.4 = (bf16[8,704,128]{2,1,0:T(8,128)(2,1)}, bf16[8,704,128]{2,1,0:T(8,128)(2,1)}, bf16[8,704,128]{2,1,0:T(8,128)(2,1)}, bf16[8,704,128]{2,1,0:T(8,128)(2,1)}) custom-call(s32[5]{0:T(128)S(1)} %stack.36.refs_0_, bf16[256,2816]{1,0:T(8,128)(2,1)} %get-tuple-element.257.refs_1_, bf16[256,2816]{1,0:T(8,128)(2,1)} %get-tuple-element.258.refs_2_, ...), custom_call_target="tpu_custom_call" | custom-call | flops 2952790016 | bytes 5767168 | tf_op jit(solution)/shard_map/weight_gradient/pallas_call | solution.py:749
  227.0 16.0 %back_channel.7 = (bf16[256,2816]{1,0:T(8,128)(2,1)}, bf16[256,2816]{1,0:T(8,128)(2,1)}, f32[256,1024]{1,0:T(8,128)}, bf16[256,1024]{1,0:T(8,128)(2,1)}, bf16[25...) custom-call(f32[8]{0:T(128)S(1)} %get-tuple-element.293.slope, ...), custom_call_target="tpu_custom_call" | custom-call | flops 4966055936 | bytes 19398656 | tf_op jit(solution)/shard_map/back_channel/pallas_call | solution.py:524
  243.1 14.1 %weight_gradient.5 = (bf16[22,256,128]{2,1,0:T(8,128)(2,1)}, bf16[22,256,128]{2,1,0:T(8,128)(2,1)}, bf16[22,256,128]{2,1,0:T(8,128)(2,1)}, bf16[22,256,128]{2,1,...) custom-call(s32[5]{0:T(128)S(1)} %stack.36.refs_0_, ...), custom_call_target="tpu_custom_call" | custom-call | flops 5905580032 | bytes 11534336 | tf_op jit(solution)/shard_map/weight_gradient/pallas_call | solution.py:749
  263.6 13.6 %collective-permute-done.34 = bf16[11,256,128]{2,1,0:T(8,128)(2,1)S(1)} collective-permute-done((bf16[11,256,128]{2,1,0:T(8,128)(2,1)S(1)}, bf16[11,256,128]{2,1,0:T(8,128)(2,1)S(1)}, u32[]{:S(2)}, u32[]{:S(2)}) %collective-permute-start.34) | collective-permute-done | bytes 720928 | tf_op jit(solution)/shard_map/ppermute | solution.py:890
  286.3 8.7 %back_mixer.6 = (bf16[256,1024]{1,0:T(8,128)(2,1)}, bf16[256,1024]{1,0:T(8,128)(2,1)}, bf16[256,1024]{1,0:T(8,128)(2,1)}) custom-call(f32[8]{0:T(128)S(1)} %get-tuple-element.293.slope, f32[2,8]{1,0:T(2,128)S(1)} %copy-done.2, bf16[256,1024]{1,0:T(8,128)(2,1)} %get-tuple-element.285.dq.refs_6_, bf16[256,1024]{1,0:T(8,128)(2,1)} %get-tuple-element.286.du.refs_12_, ...), custom_call_target="tpu_custom_call" | custom-call | flops 2147483648 | bytes 8388608 | tf_op jit(solution)/shard_map/back_mixer/pallas_call | solution.py:630
  304.0 8.0 %back_mixer.7 = (bf16[256,1024]{1,0:T(8,128)(2,1)}, bf16[256,1024]{1,0:T(8,128)(2,1)}, bf16[256,1024]{1,0:T(8,128)(2,1)}) custom-call(f32[8]{0:T(128)S(1)} %get-tuple-element.293.slope, f32[2,8]{1,0:T(2,128)S(1)} %stack.37.factors, bf16[256,1024]{1,0:T(8,128)(2,1)} %get-tuple-element.294.dq.refs_5_, bf16[256,1024]{1,0:T(8,128)(2,1)} %get-tuple-element.295.du.refs_11_, ...), custom_call_target="tpu_custom_call" | custom-call | flops 2147483648 | bytes 8388608 | tf_op jit(solution)/shard_map/back_mixer/pallas_call | solution.py:630
  325.4 11.7 %weight_gradient.7 = (bf16[16,256,128]{2,1,0:T(8,128)(2,1)}, bf16[16,256,128]{2,1,0:T(8,128)(2,1)}, bf16[16,256,128]{2,1,0:T(8,128)(2,1)}, bf16[16,256,128]{2,1,...) custom-call(s32[5]{0:T(128)S(1)} %stack.36.refs_0_, ...), custom_call_target="tpu_custom_call" | custom-call | flops 4294967296 | bytes 8388608 | tf_op jit(solution)/shard_map/weight_gradient/pallas_call | solution.py:749
  345.7 11.3 %collective-permute-done.28 = bf16[11,256,128]{2,1,0:T(8,128)(2,1)S(1)} collective-permute-done((bf16[11,256,128]{2,1,0:T(8,128)(2,1)S(1)}, bf16[11,256,128]{2,1,0:T(8,128)(2,1)S(1)}, u32[]{:S(2)}, u32[]{:S(2)}) %collective-permute-start.28) | collective-permute-done | bytes 720928 | tf_op jit(solution)/shard_map/ppermute | solution.py:864
  366.1 6.7 %collective-permute-done.29 = bf16[8,256,128]{2,1,0:T(8,128)(2,1)S(1)} collective-permute-done((bf16[8,256,128]{2,1,0:T(8,128)(2,1)S(1)}, bf16[8,256,128]{2,1,0:T(8,128)(2,1)S(1)}, u32[]{:S(2)}, u32[]{:S(2)}) %collective-permute-start.29) | collective-permute-done | bytes 524320 | tf_op jit(solution)/shard_map/ppermute | solution.py:864
  374.3 5.8 %collective-permute-done.43.outer = bf16[11,256,128]{2,1,0:T(8,128)(2,1)S(1)} collective-permute-done((bf16[11,256,128]{2,1,0:T(8,128)(2,1)S(1)}, bf16[11,256,128]{2,1,0:T(8,128)(2,1)S(1)}, u32[]{:S(2)}, u32[]{:S(2)}) %collective-permute-start.43) | collective-permute-done | bytes 720928 | tf_op jit(solution)/shard_map/ppermute | solution.py:884
  383.9 6.6 %collective-permute-start.48 = (bf16[8,256,128]{2,1,0:T(8,128)(2,1)S(1)}, bf16[8,256,128]{2,1,0:T(8,128)(2,1)S(1)}, u32[]{:S(2)}, u32[]{:S(2)}) collective-permute-start(bf16[8,256,128]{2,1,0:T(8,128)(2,1)S(1)} %add_convert_fusion.24), channel_id=1, source_target_pairs={{0,1},{3,2},{4,5},{7,6},{8,9},{11,10},{12,13},{15,14},{16,17},{19,... | collective-permute-start | bytes 1572872 | tf_op jit(solution)/shard_map/ppermute | solution.py:890
  393.2 9.7 %collective-permute-done.47.outer = bf16[11,256,128]{2,1,0:T(8,128)(2,1)S(1)} collective-permute-done((bf16[11,256,128]{2,1,0:T(8,128)(2,1)S(1)}, bf16[11,256,128]{2,1,0:T(8,128)(2,1)S(1)}, u32[]{:S(2)}, u32[]{:S(2)}) %collective-permute-start.47) | collective-permute-done | bytes 720928 | tf_op jit(solution)/shard_map/ppermute | solution.py:894
  407.4 6.5 %collective-permute-done.51 = bf16[8,256,128]{2,1,0:T(8,128)(2,1)S(1)} collective-permute-done((bf16[8,256,128]{2,1,0:T(8,128)(2,1)S(1)}, bf16[8,256,128]{2,1,0:T(8,128)(2,1)S(1)}, u32[]{:S(2)}, u32[]{:S(2)}) %collective-permute-start.51) | collective-permute-done | bytes 524320 | tf_op jit(solution)/shard_map/ppermute | solution.py:890
  423.3 7.3 %collective-permute-done.50.outer = bf16[8,256,128]{2,1,0:T(8,128)(2,1)S(1)} collective-permute-done((bf16[8,256,128]{2,1,0:T(8,128)(2,1)S(1)}, bf16[8,256,128]{2,1,0:T(8,128)(2,1)S(1)}, u32[]{:S(2)}, u32[]{:S(2)}) %collective-permute-start.50) | collective-permute-done | bytes 524320 | tf_op jit(solution)/shard_map/ppermute | solution.py:884
  448.3 6.2 %collective-permute-done.55.outer = bf16[8,256,128]{2,1,0:T(8,128)(2,1)S(1)} collective-permute-done((bf16[8,256,128]{2,1,0:T(8,128)(2,1)S(1)}, bf16[8,256,128]{2,1,0:T(8,128)(2,1)S(1)}, u32[]{:S(2)}, u32[]{:S(2)}) %collective-permute-start.55) | collective-permute-done | bytes 524320 | tf_op jit(solution)/shard_map/ppermute | solution.py:884
  460.9 9.7 %collective-permute-done.12 = bf16[256,1024]{1,0:T(8,128)(2,1)S(1)} collective-permute-done((bf16[256,1024]{1,0:T(8,128)(2,1)S(1)}, bf16[256,1024]{1,0:T(8,128)(2,1)S(1)}, u32[]{:S(2)}, u32[]{:S(2)}) %collective-permute-start.12) | collective-permute-done | bytes 524320 | tf_op jit(solution)/shard_map/ppermute | solution.py:831
  477.7 8.5 %collective-permute-done.57.outer = bf16[8,256,128]{2,1,0:T(8,128)(2,1)S(1)} collective-permute-done((bf16[8,256,128]{2,1,0:T(8,128)(2,1)S(1)}, bf16[8,256,128]{2,1,0:T(8,128)(2,1)S(1)}, u32[]{:S(2)}, u32[]{:S(2)}) %collective-permute-start.57) | collective-permute-done | bytes 524320 | tf_op jit(solution)/shard_map/ppermute | solution.py:894
  (276 shorter events, 155.1 us)
Async XLA Ops:
  3.0 18.1 %collective-permute-start.1 = (bf16[256,1024]{1,0:T(8,128)(2,1)}, bf16[256,1024]{1,0:T(8,128)(2,1)S(1)}, u32[]{:S(2)}, u32[]{:S(2)}) collective-permute-start(bf16[256,1024]{1,0:T(8,128)(2,1)} %get-tuple-element.362), channel_id=1, source_target_pairs={{4,0},{8,12},{0,8},{12,4},{5,1},{9,13},{1,9},{13,5},{6,2},{10,14},... | collective-permute-start | bytes 1572872 | tf_op jit(solution)/shard_map/ppermute | solution.py:821
  62.0 18.2 %collective-permute-start.3 = (bf16[256,1024]{1,0:T(8,128)(2,1)}, bf16[256,1024]{1,0:T(8,128)(2,1)S(1)}, u32[]{:S(2)}, u32[]{:S(2)}) collective-permute-start(bf16[256,1024]{1,0:T(8,128)(2,1)} %get-tuple-element.198), channel_id=1, source_target_pairs={{0,16},{1,17},{2,18},{3,19},{4,20},{5,21},{6,22},{7,23},{8,24},{9,... | collective-permute-start | bytes 1572872 | tf_op jit(solution)/shard_map/ppermute | solution.py:1039
  175.3 19.2 %collective-permute-start.7 = (bf16[256,1024]{1,0:T(8,128)(2,1)}, bf16[256,1024]{1,0:T(8,128)(2,1)S(1)}, u32[]{:S(2)}, u32[]{:S(2)}) collective-permute-start(bf16[256,1024]{1,0:T(8,128)(2,1)} %get-tuple-element.248), channel_id=1, source_target_pairs={{16,0},{17,1},{18,2},{19,3},{20,4},{21,5},{22,6},{23,7},{24,8},{25... | collective-permute-start | bytes 1572872 | tf_op jit(solution)/shard_map/ppermute | solution.py:1047
  184.6 26.9 %collective-permute-start.8 = (bf16[256,1024]{1,0:T(8,128)(2,1)}, bf16[256,1024]{1,0:T(8,128)(2,1)S(1)}, u32[]{:S(2)}, u32[]{:S(2)}) collective-permute-start(bf16[256,1024]{1,0:T(8,128)(2,1)} %get-tuple-element.261), channel_id=1, source_target_pairs={{16,0},{17,1},{18,2},{19,3},{20,4},{21,5},{22,6},{23,7},{24,8},{25... | collective-permute-start | bytes 1572872 | tf_op jit(solution)/shard_map/ppermute | solution.py:1047
  221.0 40.6 %collective-permute-start.13 = (bf16[22,256,128]{2,1,0:T(8,128)(2,1)}, bf16[22,256,128]{2,1,0:T(8,128)(2,1)S(1)}, u32[]{:S(2)}, u32[]{:S(2)}) collective-permute-start(bf16[22,256,128]{2,1,0:T(8,128)(2,1)} %bitcast.111), channel_id=1, source_target_pairs={{0,4},{4,0},{8,12},{12,8},{1,5},{5,1},{9,13},{13,9},{2,6},{6,2},{1... | collective-permute-start | bytes 4325384 | tf_op jit(solution)/shard_map/ppermute | solution.py:852
  224.5 32.8 %collective-permute-start.14 = (bf16[11,256,128]{2,1,0:T(8,128)(2,1)S(1)}, bf16[11,256,128]{2,1,0:T(8,128)(2,1)S(1)}, u32[]{:S(2)}, u32[]{:S(2)}) collective-permute-start(bf16[11,256,128]{2,1,0:T(8,128)(2,1)S(1)} %fusion.11), channel_id=1, source_target_pairs={{0,8},{8,0},{4,12},{12,4},{1,9},{9,1},{5,13},{13,5},{2,10},{10,2},... | collective-permute-start | bytes 2162696 | tf_op jit(solution)/shard_map/ppermute | solution.py:864
  257.2 20.2 %collective-permute-start.23 = (bf16[22,256,128]{2,1,0:T(8,128)(2,1)}, bf16[22,256,128]{2,1,0:T(8,128)(2,1)S(1)}, u32[]{:S(2)}, u32[]{:S(2)}) collective-permute-start(bf16[22,256,128]{2,1,0:T(8,128)(2,1)} %get-tuple-element.333), channel_id=1, source_target_pairs={{0,4},{4,0},{8,12},{12,8},{1,5},{5,1},{9,13},{13,9},{2,6},{6,2},{1... | collective-permute-start | bytes 4325384 | tf_op jit(solution)/shard_map/ppermute | solution.py:852
  257.6 19.6 %collective-permute-start.34 = (bf16[11,256,128]{2,1,0:T(8,128)(2,1)S(1)}, bf16[11,256,128]{2,1,0:T(8,128)(2,1)S(1)}, u32[]{:S(2)}, u32[]{:S(2)}) collective-permute-start(bf16[11,256,128]{2,1,0:T(8,128)(2,1)S(1)} %add_convert_fusion.17), channel_id=1, source_target_pairs={{0,1},{3,2},{4,5},{7,6},{8,9},{11,10},{12,13},{15,14},{16,17},{19,... | collective-permute-start | bytes 2162696 | tf_op jit(solution)/shard_map/ppermute | solution.py:890
  261.4 33.6 %collective-permute-start.22 = (bf16[22,256,128]{2,1,0:T(8,128)(2,1)S(1)}, bf16[22,256,128]{2,1,0:T(8,128)(2,1)S(1)}, u32[]{:S(2)}, u32[]{:S(2)}) collective-permute-start(bf16[22,256,128]{2,1,0:T(8,128)(2,1)S(1)} %copy-done.30), channel_id=1, source_target_pairs={{0,4},{4,0},{8,12},{12,8},{1,5},{5,1},{9,13},{13,9},{2,6},{6,2},{1... | collective-permute-start | bytes 4325384 | tf_op jit(solution)/shard_map/ppermute | solution.py:852
  261.9 18.4 %collective-permute-start.24 = (bf16[11,256,128]{2,1,0:T(8,128)(2,1)S(1)}, bf16[11,256,128]{2,1,0:T(8,128)(2,1)S(1)}, u32[]{:S(2)}, u32[]{:S(2)}) collective-permute-start(bf16[11,256,128]{2,1,0:T(8,128)(2,1)S(1)} %fusion.10), channel_id=1, source_target_pairs={{0,8},{8,0},{4,12},{12,4},{1,9},{9,1},{5,13},{13,5},{2,10},{10,2},... | collective-permute-start | bytes 2162696 | tf_op jit(solution)/shard_map/ppermute | solution.py:864
  262.3 18.5 %collective-permute-start.10 = (bf16[8,128,128]{2,1,0:T(8,128)(2,1)S(1)}, bf16[8,128,128]{2,1,0:T(8,128)(2,1)S(1)}, u32[]{:S(2)}, u32[]{:S(2)}) collective-permute-start(bf16[8,128,128]{2,1,0:T(8,128)(2,1)S(1)} %copy-done.35), channel_id=1, source_target_pairs={{4,0},{12,8},{5,1},{13,9},{6,2},{14,10},{7,3},{15,11},{20,16},{28,... | collective-permute-start | bytes 786440 | tf_op jit(solution)/shard_map/ppermute | solution.py:977
  277.2 39.7 %collective-permute-start.21 = (bf16[22,256,128]{2,1,0:T(8,128)(2,1)S(1)}, bf16[22,256,128]{2,1,0:T(8,128)(2,1)S(1)}, u32[]{:S(2)}, u32[]{:S(2)}) collective-permute-start(bf16[22,256,128]{2,1,0:T(8,128)(2,1)S(1)} %copy-done.29), channel_id=1, source_target_pairs={{0,4},{4,0},{8,12},{12,8},{1,5},{5,1},{9,13},{13,9},{2,6},{6,2},{1... | collective-permute-start | bytes 4325384 | tf_op jit(solution)/shard_map/ppermute | solution.py:852
  277.4 21.0 %collective-permute-start.35 = (bf16[11,256,128]{2,1,0:T(8,128)(2,1)S(1)}, bf16[11,256,128]{2,1,0:T(8,128)(2,1)S(1)}, u32[]{:S(2)}, u32[]{:S(2)}) collective-permute-start(bf16[11,256,128]{2,1,0:T(8,128)(2,1)S(1)} %add_convert_fusion.4), channel_id=1, source_target_pairs={{1,2},{2,1},{5,6},{6,5},{9,10},{10,9},{13,14},{14,13},{17,18},{18,... | collective-permute-start | bytes 2162696 | tf_op jit(solution)/shard_map/ppermute | solution.py:880
  280.3 17.5 %collective-permute-start.25 = (bf16[11,256,128]{2,1,0:T(8,128)(2,1)S(1)}, bf16[11,256,128]{2,1,0:T(8,128)(2,1)S(1)}, u32[]{:S(2)}, u32[]{:S(2)}) collective-permute-start(bf16[11,256,128]{2,1,0:T(8,128)(2,1)S(1)} %add_convert_fusion.13), channel_id=1, source_target_pairs={{0,8},{8,0},{4,12},{12,4},{1,9},{9,1},{5,13},{13,5},{2,10},{10,2},... | collective-permute-start | bytes 2162696 | tf_op jit(solution)/shard_map/ppermute | solution.py:864
  280.9 22.2 %collective-permute-start.37 = (bf16[11,256,128]{2,1,0:T(8,128)(2,1)S(1)}, bf16[11,256,128]{2,1,0:T(8,128)(2,1)S(1)}, u32[]{:S(2)}, u32[]{:S(2)}) collective-permute-start(bf16[11,256,128]{2,1,0:T(8,128)(2,1)S(1)} %add_convert_fusion.3), channel_id=1, source_target_pairs={{0,1},{3,2},{4,5},{7,6},{8,9},{11,10},{12,13},{15,14},{16,17},{19,... | collective-permute-start | bytes 2162696 | tf_op jit(solution)/shard_map/ppermute | solution.py:890
  295.0 42.2 %collective-permute-start.20 = (bf16[22,256,128]{2,1,0:T(8,128)(2,1)S(1)}, bf16[22,256,128]{2,1,0:T(8,128)(2,1)S(1)}, u32[]{:S(2)}, u32[]{:S(2)}) collective-permute-start(bf16[22,256,128]{2,1,0:T(8,128)(2,1)S(1)} %copy-done.28), channel_id=1, source_target_pairs={{0,4},{4,0},{8,12},{12,8},{1,5},{5,1},{9,13},{13,9},{2,6},{6,2},{1... | collective-permute-start | bytes 4325384 | tf_op jit(solution)/shard_map/ppermute | solution.py:852
  297.8 19.3 %collective-permute-start.26 = (bf16[11,256,128]{2,1,0:T(8,128)(2,1)S(1)}, bf16[11,256,128]{2,1,0:T(8,128)(2,1)S(1)}, u32[]{:S(2)}, u32[]{:S(2)}) collective-permute-start(bf16[11,256,128]{2,1,0:T(8,128)(2,1)S(1)} %add_convert_fusion.14), channel_id=1, source_target_pairs={{0,8},{8,0},{4,12},{12,4},{1,9},{9,1},{5,13},{13,5},{2,10},{10,2},... | collective-permute-start | bytes 2162696 | tf_op jit(solution)/shard_map/ppermute | solution.py:864
  299.0 19.9 %collective-permute-start.36 = (bf16[11,256,128]{2,1,0:T(8,128)(2,1)S(1)}, bf16[11,256,128]{2,1,0:T(8,128)(2,1)S(1)}, u32[]{:S(2)}, u32[]{:S(2)}) collective-permute-start(bf16[11,256,128]{2,1,0:T(8,128)(2,1)S(1)} %fusion), channel_id=1, source_target_pairs={{0,1},{1,0},{2,3},{3,2},{4,5},{5,4},{6,7},{7,6},{8,9},{9,8},{10,11... | collective-permute-start | bytes 2162696 | tf_op jit(solution)/shard_map/ppermute | solution.py:884
  317.1 20.8 %collective-permute-start.27 = (bf16[11,256,128]{2,1,0:T(8,128)(2,1)S(1)}, bf16[11,256,128]{2,1,0:T(8,128)(2,1)S(1)}, u32[]{:S(2)}, u32[]{:S(2)}) collective-permute-start(bf16[11,256,128]{2,1,0:T(8,128)(2,1)S(1)} %add_convert_fusion.15), channel_id=1, source_target_pairs={{0,8},{8,0},{4,12},{12,4},{1,9},{9,1},{5,13},{13,5},{2,10},{10,2},... | collective-permute-start | bytes 2162696 | tf_op jit(solution)/shard_map/ppermute | solution.py:864
  320.8 18.3 %collective-permute-start.39 = (bf16[11,256,128]{2,1,0:T(8,128)(2,1)S(1)}, bf16[11,256,128]{2,1,0:T(8,128)(2,1)S(1)}, u32[]{:S(2)}, u32[]{:S(2)}) collective-permute-start(bf16[11,256,128]{2,1,0:T(8,128)(2,1)S(1)} %fusion.2), channel_id=1, source_target_pairs={{0,1},{1,0},{2,3},{3,2},{4,5},{5,4},{6,7},{7,6},{8,9},{9,8},{10,11... | collective-permute-start | bytes 2162696 | tf_op jit(solution)/shard_map/ppermute | solution.py:884
  337.1 84.6 %collective-permute-start.15 = (bf16[16,256,128]{2,1,0:T(8,128)(2,1)}, bf16[16,256,128]{2,1,0:T(8,128)(2,1)S(1)}, u32[]{:S(2)}, u32[]{:S(2)}) collective-permute-start(bf16[16,256,128]{2,1,0:T(8,128)(2,1)} %get-tuple-element.319), channel_id=1, source_target_pairs={{0,4},{4,0},{8,12},{12,8},{1,5},{5,1},{9,13},{13,9},{2,6},{6,2},{1... | collective-permute-start | bytes 3145736 | tf_op jit(solution)/shard_map/ppermute | solution.py:852
  339.1 17.8 %collective-permute-start.28 = (bf16[11,256,128]{2,1,0:T(8,128)(2,1)S(1)}, bf16[11,256,128]{2,1,0:T(8,128)(2,1)S(1)}, u32[]{:S(2)}, u32[]{:S(2)}) collective-permute-start(bf16[11,256,128]{2,1,0:T(8,128)(2,1)S(1)} %add_convert_fusion.16), channel_id=1, source_target_pairs={{0,8},{8,0},{4,12},{12,4},{1,9},{9,1},{5,13},{13,5},{2,10},{10,2},... | collective-permute-start | bytes 2162696 | tf_op jit(solution)/shard_map/ppermute | solution.py:864
  342.1 17.9 %collective-permute-start.41 = (bf16[11,256,128]{2,1,0:T(8,128)(2,1)S(1)}, bf16[11,256,128]{2,1,0:T(8,128)(2,1)S(1)}, u32[]{:S(2)}, u32[]{:S(2)}) collective-permute-start(bf16[11,256,128]{2,1,0:T(8,128)(2,1)S(1)} %fusion.4.inner), channel_id=1, source_target_pairs={{0,1},{1,0},{2,3},{3,2},{4,5},{5,4},{6,7},{7,6},{8,9},{9,8},{10,11... | collective-permute-start | bytes 2162696 | tf_op jit(solution)/shard_map/ppermute | solution.py:884
  344.1 18.6 %collective-permute-start.42 = (bf16[11,256,128]{2,1,0:T(8,128)(2,1)S(1)}, bf16[11,256,128]{2,1,0:T(8,128)(2,1)S(1)}, u32[]{:S(2)}, u32[]{:S(2)}) collective-permute-start(bf16[11,256,128]{2,1,0:T(8,128)(2,1)S(1)} %fusion.3), channel_id=1, source_target_pairs={{1,2},{2,1},{5,6},{6,5},{9,10},{10,9},{13,14},{14,13},{17,18},{18,... | collective-permute-start | bytes 2162696 | tf_op jit(solution)/shard_map/ppermute | solution.py:880
  345.4 19.6 %collective-permute-start.17 = (bf16[16,256,128]{2,1,0:T(8,128)(2,1)S(1)}, bf16[16,256,128]{2,1,0:T(8,128)(2,1)S(1)}, u32[]{:S(2)}, u32[]{:S(2)}) collective-permute-start(bf16[16,256,128]{2,1,0:T(8,128)(2,1)S(1)} %copy-done.33), channel_id=1, source_target_pairs={{0,4},{4,0},{8,12},{12,8},{1,5},{5,1},{9,13},{13,9},{2,6},{6,2},{1... | collective-permute-start | bytes 3145736 | tf_op jit(solution)/shard_map/ppermute | solution.py:852
  372.8 17.7 %collective-permute-start.30 = (bf16[8,256,128]{2,1,0:T(8,128)(2,1)S(1)}, bf16[8,256,128]{2,1,0:T(8,128)(2,1)S(1)}, u32[]{:S(2)}, u32[]{:S(2)}) collective-permute-start(bf16[8,256,128]{2,1,0:T(8,128)(2,1)S(1)} %add_convert_fusion.32), channel_id=1, source_target_pairs={{0,8},{8,0},{4,12},{12,4},{1,9},{9,1},{5,13},{13,5},{2,10},{10,2},... | collective-permute-start | bytes 1572872 | tf_op jit(solution)/shard_map/ppermute | solution.py:864
  381.2 21.7 %collective-permute-start.47 = (bf16[11,256,128]{2,1,0:T(8,128)(2,1)S(1)}, bf16[11,256,128]{2,1,0:T(8,128)(2,1)S(1)}, u32[]{:S(2)}, u32[]{:S(2)}) collective-permute-start(bf16[11,256,128]{2,1,0:T(8,128)(2,1)S(1)} %add_convert_fusion.inner), channel_id=1, source_target_pairs={{1,0},{2,3},{5,4},{6,7},{9,8},{10,11},{13,12},{14,15},{17,16},{18,... | collective-permute-start | bytes 2162696 | tf_op jit(solution)/shard_map/ppermute | solution.py:894
  383.9 21.6 %collective-permute-start.48 = (bf16[8,256,128]{2,1,0:T(8,128)(2,1)S(1)}, bf16[8,256,128]{2,1,0:T(8,128)(2,1)S(1)}, u32[]{:S(2)}, u32[]{:S(2)}) collective-permute-start(bf16[8,256,128]{2,1,0:T(8,128)(2,1)S(1)} %add_convert_fusion.24), channel_id=1, source_target_pairs={{0,1},{3,2},{4,5},{7,6},{8,9},{11,10},{12,13},{15,14},{16,17},{19,... | collective-permute-start | bytes 1572872 | tf_op jit(solution)/shard_map/ppermute | solution.py:890
  391.9 25.2 %collective-permute-start.45 = (bf16[11,256,128]{2,1,0:T(8,128)(2,1)S(1)}, bf16[11,256,128]{2,1,0:T(8,128)(2,1)S(1)}, u32[]{:S(2)}, u32[]{:S(2)}) collective-permute-start(bf16[11,256,128]{2,1,0:T(8,128)(2,1)S(1)} %add_convert_fusion.1.inner), channel_id=1, source_target_pairs={{1,0},{2,3},{5,4},{6,7},{9,8},{10,11},{13,12},{14,15},{17,16},{18,... | collective-permute-start | bytes 2162696 | tf_op jit(solution)/shard_map/ppermute | solution.py:894
  414.0 17.7 %collective-permute-start.52 = (bf16[8,256,128]{2,1,0:T(8,128)(2,1)S(1)}, bf16[8,256,128]{2,1,0:T(8,128)(2,1)S(1)}, u32[]{:S(2)}, u32[]{:S(2)}) collective-permute-start(bf16[8,256,128]{2,1,0:T(8,128)(2,1)S(1)} %add_convert_fusion.20), channel_id=1, source_target_pairs={{1,2},{2,1},{5,6},{6,5},{9,10},{10,9},{13,14},{14,13},{17,18},{18,... | collective-permute-start | bytes 1572872 | tf_op jit(solution)/shard_map/ppermute | solution.py:880
  458.1 18.5 %collective-permute-start.59 = (bf16[8,256,128]{2,1,0:T(8,128)(2,1)S(1)}, bf16[8,256,128]{2,1,0:T(8,128)(2,1)S(1)}, u32[]{:S(2)}, u32[]{:S(2)}) collective-permute-start(bf16[8,256,128]{2,1,0:T(8,128)(2,1)S(1)} %add_convert_fusion.18.inner), channel_id=1, source_target_pairs={{1,0},{2,3},{5,4},{6,7},{9,8},{10,11},{13,12},{14,15},{17,16},{18,... | collective-permute-start | bytes 1572872 | tf_op jit(solution)/shard_map/ppermute | solution.py:894
  459.5 26.6 %collective-permute-start.57 = (bf16[8,256,128]{2,1,0:T(8,128)(2,1)S(1)}, bf16[8,256,128]{2,1,0:T(8,128)(2,1)S(1)}, u32[]{:S(2)}, u32[]{:S(2)}) collective-permute-start(bf16[8,256,128]{2,1,0:T(8,128)(2,1)S(1)} %add_convert_fusion.19.inner), channel_id=1, source_target_pairs={{1,0},{2,3},{5,4},{6,7},{9,8},{10,11},{13,12},{14,15},{17,16},{18,... | collective-permute-start | bytes 1572872 | tf_op jit(solution)/shard_map/ppermute | solution.py:894
  (74 other events, 716.4 us)

commit v5 on v4

--- a/solution.py
+++ b/solution.py
@@ -86,6 +86,7 @@
 SMEM = pl.BlockSpec(memory_space=pltpu.SMEM)
 ANY = pl.BlockSpec(memory_space=pltpu.HBM)
 VMEM = pl.BlockSpec(memory_space=pltpu.VMEM)
+FREE = pl.BlockSpec(memory_space=pl.ANY)
 
 
 def tables(position, rows):
@@ -185,7 +186,7 @@
     states = (HEADS, LANES, LANES)
     return pl.pallas_call(
         project_body,
-        in_specs=[SMEM] + [ANY] * 4 + [VMEM],
+        in_specs=[SMEM, FREE] + [ANY] * 3 + [VMEM],
         out_specs=[ANY] * 6,
         out_shape=[
             hbm((rows, width), bf16),
@@ -215,7 +216,7 @@
             flops=2 * rows * width * total, bytes_accessed=2 * width * total, transcendentals=0
         ),
         name="project",
-    )(slopes, *far_away(x, cosine, sine, before), *close_by(w))
+    )(slopes, x, *far_away(cosine, sine, before), *close_by(w))
 
 
 def moves(pairs, sem, start=0):
@@ -255,8 +256,8 @@
     ahead = row_index(rows, LANES)
 
     def pair(i, carry):
-        for m in range(4):
-            n = i * 4 + m
+        for m in range(2):
+            n = i * 2 + m
             at = pl.multiple_of(n * LANES, LANES)
             lane = pl.ds(at, LANES)
             state = entering_state(factors, statev, n)
@@ -269,7 +270,7 @@
             attended[:, lane] = inner + jnp.exp(ahead * (-slope[n])) * carried
         return carry
 
-    lax.fori_loop(0, HEADS // 4, pair, 0)
+    lax.fori_loop(0, HEADS // 2, pair, 0)
     rows_out = attended[...]
     factor = norm_factor(rows_out, width)
     rav[...] = jnp.broadcast_to(factor, rav.shape)
@@ -343,7 +344,7 @@
     ]
     return pl.pallas_call(
         finish_body,
-        in_specs=[SMEM] * 2 + [ANY] * 5 + [VMEM] * 3,
+        in_specs=[SMEM] * 2 + [FREE] + [ANY] * 2 + [FREE] * 2 + [VMEM] * 3,
         out_specs=[ANY] * len(outs),
         out_shape=outs,
         scratch_shapes=[
@@ -368,7 +369,7 @@
             transcendentals=0,
         ),
         name="finish",
-    )(slopes, factors, *far_away(x, qk, pre, *entering), *close_by(wo, wi, wd))
+    )(slopes, factors, x, *far_away(qk, pre), *entering, *close_by(wo, wi, wd))
 
 
 def back_channel_body(
@@ -523,7 +524,7 @@
     tall = pltpu.VMEM((rows, hidden), bf16)
     return pl.pallas_call(
         back_channel_body,
-        in_specs=[SMEM] + [ANY] + [VMEM] * 3 + [ANY] * 12,
+        in_specs=[SMEM] + [FREE] + [VMEM] * 3 + [ANY] * 12,
         out_specs=[ANY] * len(outs),
         out_shape=outs,
         scratch_shapes=[
@@ -549,7 +550,7 @@
         ),
         name="back_channel",
     )(
-        slopes, *far_away(dy), *close_by(wo, wi, wd),
+        slopes, dy, *close_by(wo, wi, wd),
         *far_away(
             r["g"], r["up"], r["h2"], r["r2"], r["mixed"], r["ra"], r["qk"], r["pre"], r["low"],
             cosine, sine, behind,
@@ -604,7 +605,7 @@
         copy.start()
     for copy in ins[9:]:
         copy.wait()
-    columns = 512
+    columns = 256
 
     def step(j, carry):
         at = pl.ds(pl.multiple_of(j * columns, LANES), columns)
@@ -629,7 +630,7 @@
     thin = pltpu.VMEM((rows, LANES), f32)
     return pl.pallas_call(
         back_mixer_body,
-        in_specs=[SMEM] * 2 + [ANY] * 13 + [VMEM],
+        in_specs=[SMEM] * 2 + [ANY] * 6 + [FREE] * 2 + [ANY] * 5 + [VMEM],
         out_specs=[ANY] * 3,
         out_shape=[act, act, act],
         scratch_shapes=[
@@ -649,10 +650,9 @@
         name="back_mixer",
     )(
         slopes, factors,
-        *far_away(
-            r["dq"], r["du"], r["dk"], r["dv"], r["qk"], r["pre"], *entering, cosine, sine,
-            r["h1"], r["r1"], r["dmid"],
-        ),
+        *far_away(r["dq"], r["du"], r["dk"], r["dv"], r["qk"], r["pre"]),
+        *entering,
+        *far_away(cosine, sine, r["h1"], r["r1"], r["dmid"]),
         *close_by(w),
     )
 
@@ -698,8 +698,12 @@
 
     for copy in left_copies(0):
         copy.wait()
-    for piece in range(columns // LANES):
-        xt[piece * LANES : (piece + 1) * LANES, :] = x[:, piece * LANES : (piece + 1) * LANES].T
+    def turn(piece, carry):
+        at = pl.ds(pl.multiple_of(piece * 2 * LANES, LANES), 2 * LANES)
+        xt[at, :] = x[:, at].T
+        return carry
+
+    lax.fori_loop(0, columns // (2 * LANES), turn, 0)
 
     def move(number, role, out):
         slot = number * 4 + role
@@ -774,15 +778,20 @@
 def settle_body(edge, outer, inner, *rest):
     out = rest[-1]
 
+    def write(source):
+        def one(n, carry):
+            out[:, pl.ds(pl.multiple_of(n * LANES, LANES), LANES)] = source[n].astype(f32)
+            return carry
+
+        lax.fori_loop(0, source.shape[0], one, 0)
+
     @pl.when(edge[0] == 1)
     def _():
-        for n in range(outer.shape[0]):
-            out[:, head(n)] = outer[n].astype(f32)
+        write(outer)
 
     @pl.when(edge[0] == 0)
     def _():
-        for n in range(inner.shape[0]):
-            out[:, head(n)] = inner[n].astype(f32)
+        write(inner)
 
 
 def settle(edge, outer, inner, total, held, number):

time: 497 us -> 491 us (0.988)
  starting transfers between devices: 92.7 us -> 84.3 us
  waiting for transfers between devices: 114 us -> 120 us
    ppermute x2, starting transfers between devices: 11.3 us -> 2.76 us  [per_device(): returned[b] = lax.ppermute(late.back_second(b), 'section', [(1, 0)])]
    ppermute x2, waiting for transfers between devices: 0.01 us -> 5.83 us  [per_device(): returned[b] = lax.ppermute(late.back_second(b), 'section', [(1, 0)])]
  transfers between devices with their start and end apart: 60 -> 60, of which waited for: 22 -> 23; matrix products, arithmetic and copies ran while one was open for 3% -> 3% of each run, Pallas kernels for 25% -> 25%
where the time goes in v5:
time: 491 us; the launch traced here: 483 us
  Pallas kernels  235 us (48%)
  waiting for transfers between devices  120 us (24%)
  starting transfers between devices  84.3 us (17%)
  other arithmetic  17.1 us (3%)
  blocking collectives  12.1 us (2%)
  local copies, waits for them, and re-layouts  11.7 us (2%)
    pallas_call x4, Pallas kernels, back_channel(): pl.pallas_call(back_channel_body, in_specs=[SMEM] + [FREE] + [VMEM] * 3 +...  63.5 us
    pallas_call x4, Pallas kernels, finish(): pl.pallas_call(finish_body, in_specs=[SMEM] * 2 + [FREE] + [ANY] * 2 + [F...  52.6 us
    pallas_call x4, Pallas kernels, weight_gradient(): pl.pallas_call(functools.partial(weight_body, batch=batch, sides=sides, g...  40.3 us
    pallas_call x4, Pallas kernels, back_mixer(): pl.pallas_call(back_mixer_body, in_specs=[SMEM] * 2 + [ANY] * 6 + [FREE]...  33.2 us
    pallas_call x4, Pallas kernels, project(): pl.pallas_call(project_body, in_specs=[SMEM, FREE] + [ANY] * 3 + [VMEM],...  32.3 us
    ppermute x7, waiting for transfers between devices, over_z(): got = lax.ppermute(sent, 'dp', [(0, 1), (1, 0), (2, 3), (3, 2)])  27 us
    ppermute x4, waiting for transfers between devices, over_z(): lax.ppermute(done, 'dp', [(1, 0), (2, 3)])  23.8 us
    ppermute x11, waiting for transfers between devices, over_y(): self.previous = lax.ppermute(far, 'seq', [(0, 2), (2, 0), (1, 3), (3, 1)])  23.7 us
  transfers between devices with their start and end apart: 60, of which 23 were waited for; matrix products, arithmetic and copies ran while one was open for 3% of the time, Pallas kernels for 25%

profile of v5, /device:TPU:0, one launch (start us, length us, event | category | flops | bytes accessed | tf_op | source)
XLA Modules:
  0.0 482.6 jit_solution(6995075795218517498)
XLA Ops:
  5.7 12.1 %all-gather.1 = s32[4,2,256]{2,1,0:T(2,128)S(1)} all-gather(s32[1,2,256]{2,1,0:T(2,128)S(1)} %bitcast.106), channel_id=2, replica_groups=mesh['section'=2,'seq'=4,'dp'=4] {'seq'}, dimensions={0}, use_global_device_ids=true | all-gather | bytes 10240 | tf_op jit(solution)/shard_map/all_gather | solution.py:1017
  25.0 8.2 %project.4 = (bf16[256,1024]{1,0:T(8,128)(2,1)}, f32[256,128]{1,0:T(8,128)}, bf16[256,4096]{1,0:T(8,128)(2,1)}, bf16[256,2048]{1,0:T(8,128)(2,1)}, bf16[8,128,12...) custom-call(f32[8]{0:T(128)S(1)} %get-tuple-element.293.slope, bf16[256,1024]{1,0:T(8,128)(2,1)S(1)} %get-tuple-element.355.x.dy.refs_7_, ...), custom_call_target="tpu_custom_call" | custom-call | flops 2147483648 | bytes 8388608 | tf_op jit(solution)/shard_map/project/pallas_call | solution.py:187
  36.6 8.2 %project.5 = (bf16[256,1024]{1,0:T(8,128)(2,1)}, f32[256,128]{1,0:T(8,128)}, bf16[256,4096]{1,0:T(8,128)(2,1)}, bf16[256,2048]{1,0:T(8,128)(2,1)}, bf16[8,128,12...) custom-call(f32[8]{0:T(128)S(1)} %get-tuple-element.293.slope, bf16[256,1024]{1,0:T(8,128)(2,1)S(1)} %get-tuple-element.354.x.dy.refs_8_, ...), custom_call_target="tpu_custom_call" | custom-call | flops 2147483648 | bytes 8388608 | tf_op jit(solution)/shard_map/project/pallas_call | solution.py:187
  48.5 13.0 %finish.4 = (bf16[256,1024]{1,0:T(8,128)(2,1)}, bf16[256,1024]{1,0:T(8,128)(2,1)}, f32[256,128]{1,0:T(8,128)}, bf16[256,1024]{1,0:T(8,128)(2,1)}, f32[256,128]{1...) custom-call(f32[8]{0:T(128)S(1)} %get-tuple-element.293.slope, ...), custom_call_target="tpu_custom_call" | custom-call | flops 4966055936 | bytes 19398656 | tf_op jit(solution)/shard_map/finish/pallas_call | solution.py:345
  65.2 13.4 %finish.5 = (bf16[256,1024]{1,0:T(8,128)(2,1)}, bf16[256,1024]{1,0:T(8,128)(2,1)}, f32[256,128]{1,0:T(8,128)}, bf16[256,1024]{1,0:T(8,128)(2,1)}, f32[256,128]{1...) custom-call(f32[8]{0:T(128)S(1)} %get-tuple-element.293.slope, ...), custom_call_target="tpu_custom_call" | custom-call | flops 4966055936 | bytes 19398656 | tf_op jit(solution)/shard_map/finish/pallas_call | solution.py:345
  80.0 7.9 %project.6 = (bf16[256,1024]{1,0:T(8,128)(2,1)}, f32[256,128]{1,0:T(8,128)}, bf16[256,4096]{1,0:T(8,128)(2,1)}, bf16[256,2048]{1,0:T(8,128)(2,1)}, bf16[8,128,12...) custom-call(f32[8]{0:T(128)S(1)} %get-tuple-element.293.slope, bf16[256,1024]{1,0:T(8,128)(2,1)S(1)} %collective-permute-done.3.x, ...), custom_call_target="tpu_custom_call" | custom-call | flops 2147483648 | bytes 8388608 | tf_op jit(solution)/shard_map/project/pallas_call | solution.py:187
  91.9 8.0 %project.7 = (bf16[256,1024]{1,0:T(8,128)(2,1)}, f32[256,128]{1,0:T(8,128)}, bf16[256,4096]{1,0:T(8,128)(2,1)}, bf16[256,2048]{1,0:T(8,128)(2,1)}, bf16[8,128,12...) custom-call(f32[8]{0:T(128)S(1)} %get-tuple-element.293.slope, bf16[256,1024]{1,0:T(8,128)(2,1)S(1)} %collective-permute-done.4.x, ...), custom_call_target="tpu_custom_call" | custom-call | flops 2147483648 | bytes 8388608 | tf_op jit(solution)/shard_map/project/pallas_call | solution.py:187
  102.7 13.1 %finish.6 = (bf16[256,1024]{1,0:T(8,128)(2,1)}, bf16[256,1024]{1,0:T(8,128)(2,1)}, f32[256,128]{1,0:T(8,128)}, bf16[256,1024]{1,0:T(8,128)(2,1)}, f32[256,128]{1...) custom-call(f32[8]{0:T(128)S(1)} %get-tuple-element.293.slope, ...), custom_call_target="tpu_custom_call" | custom-call | flops 4966055936 | bytes 19398656 | tf_op jit(solution)/shard_map/finish/pallas_call | solution.py:345
  115.8 13.1 %finish.7 = (bf16[256,1024]{1,0:T(8,128)(2,1)}, bf16[256,1024]{1,0:T(8,128)(2,1)}, f32[256,128]{1,0:T(8,128)}, bf16[256,1024]{1,0:T(8,128)(2,1)}, f32[256,128]{1...) custom-call(f32[8]{0:T(128)S(1)} %get-tuple-element.293.slope, ...), custom_call_target="tpu_custom_call" | custom-call | flops 4966055936 | bytes 19398656 | tf_op jit(solution)/shard_map/finish/pallas_call | solution.py:345
  128.9 15.9 %back_channel.4 = (bf16[256,2816]{1,0:T(8,128)(2,1)}, bf16[256,2816]{1,0:T(8,128)(2,1)}, f32[256,1024]{1,0:T(8,128)}, bf16[256,1024]{1,0:T(8,128)(2,1)}, bf16[25...) custom-call(f32[8]{0:T(128)S(1)} %get-tuple-element.293.slope, ...), custom_call_target="tpu_custom_call" | custom-call | flops 4966055936 | bytes 19398656 | tf_op jit(solution)/shard_map/back_channel/pallas_call | solution.py:525
  144.8 15.9 %back_channel.5 = (bf16[256,2816]{1,0:T(8,128)(2,1)}, bf16[256,2816]{1,0:T(8,128)(2,1)}, f32[256,1024]{1,0:T(8,128)}, bf16[256,1024]{1,0:T(8,128)(2,1)}, bf16[25...) custom-call(f32[8]{0:T(128)S(1)} %get-tuple-element.293.slope, ...), custom_call_target="tpu_custom_call" | custom-call | flops 4966055936 | bytes 19398656 | tf_op jit(solution)/shard_map/back_channel/pallas_call | solution.py:525
  164.4 8.2 %back_mixer.4 = (bf16[256,1024]{1,0:T(8,128)(2,1)}, bf16[256,1024]{1,0:T(8,128)(2,1)}, bf16[256,1024]{1,0:T(8,128)(2,1)}) custom-call(f32[8]{0:T(128)S(1)} %get-tuple-element.293.slope, f32[2,8]{1,0:T(2,128)S(1)} %copy-done.13, bf16[256,1024]{1,0:T(8,128)(2,1)} %get-tuple-element.231.dq.refs_14_, bf16[256,1024]{1,0:T(8,128)(2,1)} %get-tuple-element.232.du.refs_20_, ...), custom_call_target="tpu_custom_call" | custom-call | flops 2147483648 | bytes 8388608 | tf_op jit(solution)/shard_map/back_mixer/pallas_call | solution.py:631
  174.1 8.3 %back_mixer.5 = (bf16[256,1024]{1,0:T(8,128)(2,1)}, bf16[256,1024]{1,0:T(8,128)(2,1)}, bf16[256,1024]{1,0:T(8,128)(2,1)}) custom-call(f32[8]{0:T(128)S(1)} %get-tuple-element.293.slope, f32[2,8]{1,0:T(2,128)S(1)} %stack.37.factors, bf16[256,1024]{1,0:T(8,128)(2,1)} %get-tuple-element.240.dq.refs_13_, bf16[256,1024]{1,0:T(8,128)(2,1)} %get-tuple-element.241.du.refs_19_, ...), custom_call_target="tpu_custom_call" | custom-call | flops 2147483648 | bytes 8388608 | tf_op jit(solution)/shard_map/back_mixer/pallas_call | solution.py:631
  183.6 5.8 %collective-permute-done.7.dy.refs_6_ = bf16[256,1024]{1,0:T(8,128)(2,1)S(1)} collective-permute-done((bf16[256,1024]{1,0:T(8,128)(2,1)}, bf16[256,1024]{1,0:T(8,128)(2,1)S(1)}, u32[]{:S(2)}, u32[]{:S(2)}) %collective-permute-start.7) | collective-permute-done | bytes 524320 | tf_op jit(solution)/shard_map/ppermute | solution.py:1056
  189.4 15.8 %back_channel.6 = (bf16[256,2816]{1,0:T(8,128)(2,1)}, bf16[256,2816]{1,0:T(8,128)(2,1)}, f32[256,1024]{1,0:T(8,128)}, bf16[256,1024]{1,0:T(8,128)(2,1)}, bf16[25...) custom-call(f32[8]{0:T(128)S(1)} %get-tuple-element.293.slope, ...), custom_call_target="tpu_custom_call" | custom-call | flops 4966055936 | bytes 19398656 | tf_op jit(solution)/shard_map/back_channel/pallas_call | solution.py:525
  206.1 9.1 %weight_gradient.4 = (bf16[8,704,128]{2,1,0:T(8,128)(2,1)}, bf16[8,704,128]{2,1,0:T(8,128)(2,1)}, bf16[8,704,128]{2,1,0:T(8,128)(2,1)}, bf16[8,704,128]{2,1,0:T(8,128)(2,1)}) custom-call(s32[5]{0:T(128)S(1)} %stack.36.refs_0_, bf16[256,2816]{1,0:T(8,128)(2,1)} %get-tuple-element.257.refs_1_, bf16[256,2816]{1,0:T(8,128)(2,1)} %get-tuple-element.258.refs_2_, ...), custom_call_target="tpu_custom_call" | custom-call | flops 2952790016 | bytes 5767168 | tf_op jit(solution)/shard_map/weight_gradient/pallas_call | solution.py:753
  221.3 15.9 %back_channel.7 = (bf16[256,2816]{1,0:T(8,128)(2,1)}, bf16[256,2816]{1,0:T(8,128)(2,1)}, f32[256,1024]{1,0:T(8,128)}, bf16[256,1024]{1,0:T(8,128)(2,1)}, bf16[25...) custom-call(f32[8]{0:T(128)S(1)} %get-tuple-element.293.slope, ...), custom_call_target="tpu_custom_call" | custom-call | flops 4966055936 | bytes 19398656 | tf_op jit(solution)/shard_map/back_channel/pallas_call | solution.py:525
  237.2 14.3 %weight_gradient.5 = (bf16[22,256,128]{2,1,0:T(8,128)(2,1)}, bf16[22,256,128]{2,1,0:T(8,128)(2,1)}, bf16[22,256,128]{2,1,0:T(8,128)(2,1)}, bf16[22,256,128]{2,1,...) custom-call(s32[5]{0:T(128)S(1)} %stack.36.refs_0_, ...), custom_call_target="tpu_custom_call" | custom-call | flops 5905580032 | bytes 11534336 | tf_op jit(solution)/shard_map/weight_gradient/pallas_call | solution.py:753
  258.2 13.4 %collective-permute-done.34 = bf16[11,256,128]{2,1,0:T(8,128)(2,1)S(1)} collective-permute-done((bf16[11,256,128]{2,1,0:T(8,128)(2,1)S(1)}, bf16[11,256,128]{2,1,0:T(8,128)(2,1)S(1)}, u32[]{:S(2)}, u32[]{:S(2)}) %collective-permute-start.34) | collective-permute-done | bytes 720928 | tf_op jit(solution)/shard_map/ppermute | solution.py:899
  280.4 8.5 %back_mixer.6 = (bf16[256,1024]{1,0:T(8,128)(2,1)}, bf16[256,1024]{1,0:T(8,128)(2,1)}, bf16[256,1024]{1,0:T(8,128)(2,1)}) custom-call(f32[8]{0:T(128)S(1)} %get-tuple-element.293.slope, f32[2,8]{1,0:T(2,128)S(1)} %copy-done.13, bf16[256,1024]{1,0:T(8,128)(2,1)} %get-tuple-element.285.dq.refs_6_, bf16[256,1024]{1,0:T(8,128)(2,1)} %get-tuple-element.286.du.refs_12_, ...), custom_call_target="tpu_custom_call" | custom-call | flops 2147483648 | bytes 8388608 | tf_op jit(solution)/shard_map/back_mixer/pallas_call | solution.py:631
  298.2 8.2 %back_mixer.7 = (bf16[256,1024]{1,0:T(8,128)(2,1)}, bf16[256,1024]{1,0:T(8,128)(2,1)}, bf16[256,1024]{1,0:T(8,128)(2,1)}) custom-call(f32[8]{0:T(128)S(1)} %get-tuple-element.293.slope, f32[2,8]{1,0:T(2,128)S(1)} %stack.37.factors, bf16[256,1024]{1,0:T(8,128)(2,1)} %get-tuple-element.294.dq.refs_5_, bf16[256,1024]{1,0:T(8,128)(2,1)} %get-tuple-element.295.du.refs_11_, ...), custom_call_target="tpu_custom_call" | custom-call | flops 2147483648 | bytes 8388608 | tf_op jit(solution)/shard_map/back_mixer/pallas_call | solution.py:631
  319.5 11.8 %weight_gradient.7 = (bf16[16,256,128]{2,1,0:T(8,128)(2,1)}, bf16[16,256,128]{2,1,0:T(8,128)(2,1)}, bf16[16,256,128]{2,1,0:T(8,128)(2,1)}, bf16[16,256,128]{2,1,...) custom-call(s32[5]{0:T(128)S(1)} %stack.36.refs_0_, ...), custom_call_target="tpu_custom_call" | custom-call | flops 4294967296 | bytes 8388608 | tf_op jit(solution)/shard_map/weight_gradient/pallas_call | solution.py:753
  339.5 11.6 %collective-permute-done.28 = bf16[11,256,128]{2,1,0:T(8,128)(2,1)S(1)} collective-permute-done((bf16[11,256,128]{2,1,0:T(8,128)(2,1)S(1)}, bf16[11,256,128]{2,1,0:T(8,128)(2,1)S(1)}, u32[]{:S(2)}, u32[]{:S(2)}) %collective-permute-start.28) | collective-permute-done | bytes 720928 | tf_op jit(solution)/shard_map/ppermute | solution.py:873
  361.1 6.7 %collective-permute-done.29 = bf16[8,256,128]{2,1,0:T(8,128)(2,1)S(1)} collective-permute-done((bf16[8,256,128]{2,1,0:T(8,128)(2,1)S(1)}, bf16[8,256,128]{2,1,0:T(8,128)(2,1)S(1)}, u32[]{:S(2)}, u32[]{:S(2)}) %collective-permute-start.29) | collective-permute-done | bytes 524320 | tf_op jit(solution)/shard_map/ppermute | solution.py:873
  369.5 6.1 %collective-permute-done.43.outer = bf16[11,256,128]{2,1,0:T(8,128)(2,1)S(1)} collective-permute-done((bf16[11,256,128]{2,1,0:T(8,128)(2,1)S(1)}, bf16[11,256,128]{2,1,0:T(8,128)(2,1)S(1)}, u32[]{:S(2)}, u32[]{:S(2)}) %collective-permute-start.43) | collective-permute-done | bytes 720928 | tf_op jit(solution)/shard_map/ppermute | solution.py:893
  379.5 5.3 %collective-permute-start.48 = (bf16[8,256,128]{2,1,0:T(8,128)(2,1)S(1)}, bf16[8,256,128]{2,1,0:T(8,128)(2,1)S(1)}, u32[]{:S(2)}, u32[]{:S(2)}) collective-permute-start(bf16[8,256,128]{2,1,0:T(8,128)(2,1)S(1)} %add_convert_fusion.24), channel_id=1, source_target_pairs={{0,1},{3,2},{4,5},{7,6},{8,9},{11,10},{12,13},{15,14},{16,17},{19,... | collective-permute-start | bytes 1572872 | tf_op jit(solution)/shard_map/ppermute | solution.py:899
  387.8 8.6 %collective-permute-done.47.outer = bf16[11,256,128]{2,1,0:T(8,128)(2,1)S(1)} collective-permute-done((bf16[11,256,128]{2,1,0:T(8,128)(2,1)S(1)}, bf16[11,256,128]{2,1,0:T(8,128)(2,1)S(1)}, u32[]{:S(2)}, u32[]{:S(2)}) %collective-permute-start.47) | collective-permute-done | bytes 720928 | tf_op jit(solution)/shard_map/ppermute | solution.py:903
  402.4 6.3 %collective-permute-done.51 = bf16[8,256,128]{2,1,0:T(8,128)(2,1)S(1)} collective-permute-done((bf16[8,256,128]{2,1,0:T(8,128)(2,1)S(1)}, bf16[8,256,128]{2,1,0:T(8,128)(2,1)S(1)}, u32[]{:S(2)}, u32[]{:S(2)}) %collective-permute-start.51) | collective-permute-done | bytes 524320 | tf_op jit(solution)/shard_map/ppermute | solution.py:899
  417.9 6.5 %collective-permute-done.50.outer = bf16[8,256,128]{2,1,0:T(8,128)(2,1)S(1)} collective-permute-done((bf16[8,256,128]{2,1,0:T(8,128)(2,1)S(1)}, bf16[8,256,128]{2,1,0:T(8,128)(2,1)S(1)}, u32[]{:S(2)}, u32[]{:S(2)}) %collective-permute-start.50) | collective-permute-done | bytes 524320 | tf_op jit(solution)/shard_map/ppermute | solution.py:893
  441.5 6.2 %collective-permute-done.55.outer = bf16[8,256,128]{2,1,0:T(8,128)(2,1)S(1)} collective-permute-done((bf16[8,256,128]{2,1,0:T(8,128)(2,1)S(1)}, bf16[8,256,128]{2,1,0:T(8,128)(2,1)S(1)}, u32[]{:S(2)}, u32[]{:S(2)}) %collective-permute-start.55) | collective-permute-done | bytes 524320 | tf_op jit(solution)/shard_map/ppermute | solution.py:893
  454.4 9.7 %collective-permute-done.12 = bf16[256,1024]{1,0:T(8,128)(2,1)S(1)} collective-permute-done((bf16[256,1024]{1,0:T(8,128)(2,1)S(1)}, bf16[256,1024]{1,0:T(8,128)(2,1)S(1)}, u32[]{:S(2)}, u32[]{:S(2)}) %collective-permute-start.12) | collective-permute-done | bytes 524320 | tf_op jit(solution)/shard_map/ppermute | solution.py:840
  472.0 9.1 %collective-permute-done.57.outer = bf16[8,256,128]{2,1,0:T(8,128)(2,1)S(1)} collective-permute-done((bf16[8,256,128]{2,1,0:T(8,128)(2,1)S(1)}, bf16[8,256,128]{2,1,0:T(8,128)(2,1)S(1)}, u32[]{:S(2)}, u32[]{:S(2)}) %collective-permute-start.57) | collective-permute-done | bytes 524320 | tf_op jit(solution)/shard_map/ppermute | solution.py:903
  (272 shorter events, 156.0 us)
Async XLA Ops:
  2.0 18.0 %collective-permute-start.1 = (bf16[256,1024]{1,0:T(8,128)(2,1)S(1)}, bf16[256,1024]{1,0:T(8,128)(2,1)S(1)}, u32[]{:S(2)}, u32[]{:S(2)}) collective-permute-start(bf16[256,1024]{1,0:T(8,128)(2,1)S(1)} %get-tuple-element.362), channel_id=1, source_target_pairs={{4,0},{8,12},{0,8},{12,4},{5,1},{9,13},{1,9},{13,5},{6,2},{10,14},... | collective-permute-start | bytes 1572872 | tf_op jit(solution)/shard_map/ppermute | solution.py:830
  61.5 18.4 %collective-permute-start.3 = (bf16[256,1024]{1,0:T(8,128)(2,1)}, bf16[256,1024]{1,0:T(8,128)(2,1)S(1)}, u32[]{:S(2)}, u32[]{:S(2)}) collective-permute-start(bf16[256,1024]{1,0:T(8,128)(2,1)} %get-tuple-element.198), channel_id=1, source_target_pairs={{0,16},{1,17},{2,18},{3,19},{4,20},{5,21},{6,22},{7,23},{8,24},{9,... | collective-permute-start | bytes 1572872 | tf_op jit(solution)/shard_map/ppermute | solution.py:1048
  182.3 23.0 %collective-permute-start.8 = (bf16[256,1024]{1,0:T(8,128)(2,1)}, bf16[256,1024]{1,0:T(8,128)(2,1)S(1)}, u32[]{:S(2)}, u32[]{:S(2)}) collective-permute-start(bf16[256,1024]{1,0:T(8,128)(2,1)} %get-tuple-element.261), channel_id=1, source_target_pairs={{16,0},{17,1},{18,2},{19,3},{20,4},{21,5},{22,6},{23,7},{24,8},{25... | collective-permute-start | bytes 1572872 | tf_op jit(solution)/shard_map/ppermute | solution.py:1056
  215.3 40.9 %collective-permute-start.13 = (bf16[22,256,128]{2,1,0:T(8,128)(2,1)}, bf16[22,256,128]{2,1,0:T(8,128)(2,1)S(1)}, u32[]{:S(2)}, u32[]{:S(2)}) collective-permute-start(bf16[22,256,128]{2,1,0:T(8,128)(2,1)} %bitcast.107), channel_id=1, source_target_pairs={{0,4},{4,0},{8,12},{12,8},{1,5},{5,1},{9,13},{13,9},{2,6},{6,2},{1... | collective-permute-start | bytes 4325384 | tf_op jit(solution)/shard_map/ppermute | solution.py:861
  218.9 32.7 %collective-permute-start.14 = (bf16[11,256,128]{2,1,0:T(8,128)(2,1)S(1)}, bf16[11,256,128]{2,1,0:T(8,128)(2,1)S(1)}, u32[]{:S(2)}, u32[]{:S(2)}) collective-permute-start(bf16[11,256,128]{2,1,0:T(8,128)(2,1)S(1)} %fusion.11), channel_id=1, source_target_pairs={{0,8},{8,0},{4,12},{12,4},{1,9},{9,1},{5,13},{13,5},{2,10},{10,2},... | collective-permute-start | bytes 2162696 | tf_op jit(solution)/shard_map/ppermute | solution.py:873
  251.6 20.2 %collective-permute-start.23 = (bf16[22,256,128]{2,1,0:T(8,128)(2,1)}, bf16[22,256,128]{2,1,0:T(8,128)(2,1)S(1)}, u32[]{:S(2)}, u32[]{:S(2)}) collective-permute-start(bf16[22,256,128]{2,1,0:T(8,128)(2,1)} %get-tuple-element.333), channel_id=1, source_target_pairs={{0,4},{4,0},{8,12},{12,8},{1,5},{5,1},{9,13},{13,9},{2,6},{6,2},{1... | collective-permute-start | bytes 4325384 | tf_op jit(solution)/shard_map/ppermute | solution.py:861
  252.0 19.6 %collective-permute-start.34 = (bf16[11,256,128]{2,1,0:T(8,128)(2,1)S(1)}, bf16[11,256,128]{2,1,0:T(8,128)(2,1)S(1)}, u32[]{:S(2)}, u32[]{:S(2)}) collective-permute-start(bf16[11,256,128]{2,1,0:T(8,128)(2,1)S(1)} %add_convert_fusion.17), channel_id=1, source_target_pairs={{0,1},{3,2},{4,5},{7,6},{8,9},{11,10},{12,13},{15,14},{16,17},{19,... | collective-permute-start | bytes 2162696 | tf_op jit(solution)/shard_map/ppermute | solution.py:899
  256.0 32.9 %collective-permute-start.22 = (bf16[22,256,128]{2,1,0:T(8,128)(2,1)S(1)}, bf16[22,256,128]{2,1,0:T(8,128)(2,1)S(1)}, u32[]{:S(2)}, u32[]{:S(2)}) collective-permute-start(bf16[22,256,128]{2,1,0:T(8,128)(2,1)S(1)} %copy-done.33), channel_id=1, source_target_pairs={{0,4},{4,0},{8,12},{12,8},{1,5},{5,1},{9,13},{13,9},{2,6},{6,2},{1... | collective-permute-start | bytes 4325384 | tf_op jit(solution)/shard_map/ppermute | solution.py:861
  256.4 18.4 %collective-permute-start.24 = (bf16[11,256,128]{2,1,0:T(8,128)(2,1)S(1)}, bf16[11,256,128]{2,1,0:T(8,128)(2,1)S(1)}, u32[]{:S(2)}, u32[]{:S(2)}) collective-permute-start(bf16[11,256,128]{2,1,0:T(8,128)(2,1)S(1)} %fusion.10), channel_id=1, source_target_pairs={{0,8},{8,0},{4,12},{12,4},{1,9},{9,1},{5,13},{13,5},{2,10},{10,2},... | collective-permute-start | bytes 2162696 | tf_op jit(solution)/shard_map/ppermute | solution.py:873
  256.9 18.5 %collective-permute-start.10 = (bf16[8,128,128]{2,1,0:T(8,128)(2,1)S(1)}, bf16[8,128,128]{2,1,0:T(8,128)(2,1)S(1)}, u32[]{:S(2)}, u32[]{:S(2)}) collective-permute-start(bf16[8,128,128]{2,1,0:T(8,128)(2,1)S(1)} %copy-done.38), channel_id=1, source_target_pairs={{4,0},{12,8},{5,1},{13,9},{6,2},{14,10},{7,3},{15,11},{20,16},{28,... | collective-permute-start | bytes 786440 | tf_op jit(solution)/shard_map/ppermute | solution.py:986
  271.6 39.9 %collective-permute-start.21 = (bf16[22,256,128]{2,1,0:T(8,128)(2,1)S(1)}, bf16[22,256,128]{2,1,0:T(8,128)(2,1)S(1)}, u32[]{:S(2)}, u32[]{:S(2)}) collective-permute-start(bf16[22,256,128]{2,1,0:T(8,128)(2,1)S(1)} %copy-done.32), channel_id=1, source_target_pairs={{0,4},{4,0},{8,12},{12,8},{1,5},{5,1},{9,13},{13,9},{2,6},{6,2},{1... | collective-permute-start | bytes 4325384 | tf_op jit(solution)/shard_map/ppermute | solution.py:861
  271.8 21.2 %collective-permute-start.35 = (bf16[11,256,128]{2,1,0:T(8,128)(2,1)S(1)}, bf16[11,256,128]{2,1,0:T(8,128)(2,1)S(1)}, u32[]{:S(2)}, u32[]{:S(2)}) collective-permute-start(bf16[11,256,128]{2,1,0:T(8,128)(2,1)S(1)} %add_convert_fusion.4), channel_id=1, source_target_pairs={{1,2},{2,1},{5,6},{6,5},{9,10},{10,9},{13,14},{14,13},{17,18},{18,... | collective-permute-start | bytes 2162696 | tf_op jit(solution)/shard_map/ppermute | solution.py:889
  274.9 17.5 %collective-permute-start.25 = (bf16[11,256,128]{2,1,0:T(8,128)(2,1)S(1)}, bf16[11,256,128]{2,1,0:T(8,128)(2,1)S(1)}, u32[]{:S(2)}, u32[]{:S(2)}) collective-permute-start(bf16[11,256,128]{2,1,0:T(8,128)(2,1)S(1)} %add_convert_fusion.13), channel_id=1, source_target_pairs={{0,8},{8,0},{4,12},{12,4},{1,9},{9,1},{5,13},{13,5},{2,10},{10,2},... | collective-permute-start | bytes 2162696 | tf_op jit(solution)/shard_map/ppermute | solution.py:873
  275.4 21.8 %collective-permute-start.37 = (bf16[11,256,128]{2,1,0:T(8,128)(2,1)S(1)}, bf16[11,256,128]{2,1,0:T(8,128)(2,1)S(1)}, u32[]{:S(2)}, u32[]{:S(2)}) collective-permute-start(bf16[11,256,128]{2,1,0:T(8,128)(2,1)S(1)} %add_convert_fusion.3), channel_id=1, source_target_pairs={{0,1},{3,2},{4,5},{7,6},{8,9},{11,10},{12,13},{15,14},{16,17},{19,... | collective-permute-start | bytes 2162696 | tf_op jit(solution)/shard_map/ppermute | solution.py:899
  288.9 42.6 %collective-permute-start.20 = (bf16[22,256,128]{2,1,0:T(8,128)(2,1)S(1)}, bf16[22,256,128]{2,1,0:T(8,128)(2,1)S(1)}, u32[]{:S(2)}, u32[]{:S(2)}) collective-permute-start(bf16[22,256,128]{2,1,0:T(8,128)(2,1)S(1)} %copy-done.31), channel_id=1, source_target_pairs={{0,4},{4,0},{8,12},{12,8},{1,5},{5,1},{9,13},{13,9},{2,6},{6,2},{1... | collective-permute-start | bytes 4325384 | tf_op jit(solution)/shard_map/ppermute | solution.py:861
  292.4 19.3 %collective-permute-start.26 = (bf16[11,256,128]{2,1,0:T(8,128)(2,1)S(1)}, bf16[11,256,128]{2,1,0:T(8,128)(2,1)S(1)}, u32[]{:S(2)}, u32[]{:S(2)}) collective-permute-start(bf16[11,256,128]{2,1,0:T(8,128)(2,1)S(1)} %add_convert_fusion.14), channel_id=1, source_target_pairs={{0,8},{8,0},{4,12},{12,4},{1,9},{9,1},{5,13},{13,5},{2,10},{10,2},... | collective-permute-start | bytes 2162696 | tf_op jit(solution)/shard_map/ppermute | solution.py:873
  293.5 20.0 %collective-permute-start.36 = (bf16[11,256,128]{2,1,0:T(8,128)(2,1)S(1)}, bf16[11,256,128]{2,1,0:T(8,128)(2,1)S(1)}, u32[]{:S(2)}, u32[]{:S(2)}) collective-permute-start(bf16[11,256,128]{2,1,0:T(8,128)(2,1)S(1)} %fusion), channel_id=1, source_target_pairs={{0,1},{1,0},{2,3},{3,2},{4,5},{5,4},{6,7},{7,6},{8,9},{9,8},{10,11... | collective-permute-start | bytes 2162696 | tf_op jit(solution)/shard_map/ppermute | solution.py:893
  297.4 17.7 %collective-permute-start.38 = (bf16[11,256,128]{2,1,0:T(8,128)(2,1)S(1)}, bf16[11,256,128]{2,1,0:T(8,128)(2,1)S(1)}, u32[]{:S(2)}, u32[]{:S(2)}) collective-permute-start(bf16[11,256,128]{2,1,0:T(8,128)(2,1)S(1)} %add_convert_fusion.2), channel_id=1, source_target_pairs={{1,2},{2,1},{5,6},{6,5},{9,10},{10,9},{13,14},{14,13},{17,18},{18,... | collective-permute-start | bytes 2162696 | tf_op jit(solution)/shard_map/ppermute | solution.py:889
  311.7 20.5 %collective-permute-start.27 = (bf16[11,256,128]{2,1,0:T(8,128)(2,1)S(1)}, bf16[11,256,128]{2,1,0:T(8,128)(2,1)S(1)}, u32[]{:S(2)}, u32[]{:S(2)}) collective-permute-start(bf16[11,256,128]{2,1,0:T(8,128)(2,1)S(1)} %add_convert_fusion.15), channel_id=1, source_target_pairs={{0,8},{8,0},{4,12},{12,4},{1,9},{9,1},{5,13},{13,5},{2,10},{10,2},... | collective-permute-start | bytes 2162696 | tf_op jit(solution)/shard_map/ppermute | solution.py:873
  315.4 17.8 %collective-permute-start.39 = (bf16[11,256,128]{2,1,0:T(8,128)(2,1)S(1)}, bf16[11,256,128]{2,1,0:T(8,128)(2,1)S(1)}, u32[]{:S(2)}, u32[]{:S(2)}) collective-permute-start(bf16[11,256,128]{2,1,0:T(8,128)(2,1)S(1)} %fusion.2), channel_id=1, source_target_pairs={{0,1},{1,0},{2,3},{3,2},{4,5},{5,4},{6,7},{7,6},{8,9},{9,8},{10,11... | collective-permute-start | bytes 2162696 | tf_op jit(solution)/shard_map/ppermute | solution.py:893
  318.8 17.1 %collective-permute-start.40 = (bf16[11,256,128]{2,1,0:T(8,128)(2,1)S(1)}, bf16[11,256,128]{2,1,0:T(8,128)(2,1)S(1)}, u32[]{:S(2)}, u32[]{:S(2)}) collective-permute-start(bf16[11,256,128]{2,1,0:T(8,128)(2,1)S(1)} %fusion.1), channel_id=1, source_target_pairs={{1,2},{2,1},{5,6},{6,5},{9,10},{10,9},{13,14},{14,13},{17,18},{18,... | collective-permute-start | bytes 2162696 | tf_op jit(solution)/shard_map/ppermute | solution.py:889
  331.4 84.4 %collective-permute-start.15 = (bf16[16,256,128]{2,1,0:T(8,128)(2,1)}, bf16[16,256,128]{2,1,0:T(8,128)(2,1)S(1)}, u32[]{:S(2)}, u32[]{:S(2)}) collective-permute-start(bf16[16,256,128]{2,1,0:T(8,128)(2,1)} %get-tuple-element.319), channel_id=1, source_target_pairs={{0,4},{4,0},{8,12},{12,8},{1,5},{5,1},{9,13},{13,9},{2,6},{6,2},{1... | collective-permute-start | bytes 3145736 | tf_op jit(solution)/shard_map/ppermute | solution.py:861
  333.2 17.9 %collective-permute-start.28 = (bf16[11,256,128]{2,1,0:T(8,128)(2,1)S(1)}, bf16[11,256,128]{2,1,0:T(8,128)(2,1)S(1)}, u32[]{:S(2)}, u32[]{:S(2)}) collective-permute-start(bf16[11,256,128]{2,1,0:T(8,128)(2,1)S(1)} %add_convert_fusion.16), channel_id=1, source_target_pairs={{0,8},{8,0},{4,12},{12,4},{1,9},{9,1},{5,13},{13,5},{2,10},{10,2},... | collective-permute-start | bytes 2162696 | tf_op jit(solution)/shard_map/ppermute | solution.py:873
  336.2 18.1 %collective-permute-start.41 = (bf16[11,256,128]{2,1,0:T(8,128)(2,1)S(1)}, bf16[11,256,128]{2,1,0:T(8,128)(2,1)S(1)}, u32[]{:S(2)}, u32[]{:S(2)}) collective-permute-start(bf16[11,256,128]{2,1,0:T(8,128)(2,1)S(1)} %fusion.4.inner), channel_id=1, source_target_pairs={{0,1},{1,0},{2,3},{3,2},{4,5},{5,4},{6,7},{7,6},{8,9},{9,8},{10,11... | collective-permute-start | bytes 2162696 | tf_op jit(solution)/shard_map/ppermute | solution.py:893
  338.3 19.4 %collective-permute-start.42 = (bf16[11,256,128]{2,1,0:T(8,128)(2,1)S(1)}, bf16[11,256,128]{2,1,0:T(8,128)(2,1)S(1)}, u32[]{:S(2)}, u32[]{:S(2)}) collective-permute-start(bf16[11,256,128]{2,1,0:T(8,128)(2,1)S(1)} %fusion.3), channel_id=1, source_target_pairs={{1,2},{2,1},{5,6},{6,5},{9,10},{10,9},{13,14},{14,13},{17,18},{18,... | collective-permute-start | bytes 2162696 | tf_op jit(solution)/shard_map/ppermute | solution.py:889
  339.3 20.7 %collective-permute-start.17 = (bf16[16,256,128]{2,1,0:T(8,128)(2,1)S(1)}, bf16[16,256,128]{2,1,0:T(8,128)(2,1)S(1)}, u32[]{:S(2)}, u32[]{:S(2)}) collective-permute-start(bf16[16,256,128]{2,1,0:T(8,128)(2,1)S(1)} %copy-done.36), channel_id=1, source_target_pairs={{0,4},{4,0},{8,12},{12,8},{1,5},{5,1},{9,13},{13,9},{2,6},{6,2},{1... | collective-permute-start | bytes 3145736 | tf_op jit(solution)/shard_map/ppermute | solution.py:861
  358.0 17.6 %collective-permute-start.43 = (bf16[11,256,128]{2,1,0:T(8,128)(2,1)S(1)}, bf16[11,256,128]{2,1,0:T(8,128)(2,1)S(1)}, u32[]{:S(2)}, u32[]{:S(2)}) collective-permute-start(bf16[11,256,128]{2,1,0:T(8,128)(2,1)S(1)} %fusion.6.inner), channel_id=1, source_target_pairs={{0,1},{1,0},{2,3},{3,2},{4,5},{5,4},{6,7},{7,6},{8,9},{9,8},{10,11... | collective-permute-start | bytes 2162696 | tf_op jit(solution)/shard_map/ppermute | solution.py:893
  376.7 19.6 %collective-permute-start.47 = (bf16[11,256,128]{2,1,0:T(8,128)(2,1)S(1)}, bf16[11,256,128]{2,1,0:T(8,128)(2,1)S(1)}, u32[]{:S(2)}, u32[]{:S(2)}) collective-permute-start(bf16[11,256,128]{2,1,0:T(8,128)(2,1)S(1)} %add_convert_fusion.inner), channel_id=1, source_target_pairs={{1,0},{2,3},{5,4},{6,7},{9,8},{10,11},{13,12},{14,15},{17,16},{18,... | collective-permute-start | bytes 2162696 | tf_op jit(solution)/shard_map/ppermute | solution.py:903
  379.5 20.6 %collective-permute-start.48 = (bf16[8,256,128]{2,1,0:T(8,128)(2,1)S(1)}, bf16[8,256,128]{2,1,0:T(8,128)(2,1)S(1)}, u32[]{:S(2)}, u32[]{:S(2)}) collective-permute-start(bf16[8,256,128]{2,1,0:T(8,128)(2,1)S(1)} %add_convert_fusion.24), channel_id=1, source_target_pairs={{0,1},{3,2},{4,5},{7,6},{8,9},{11,10},{12,13},{15,14},{16,17},{19,... | collective-permute-start | bytes 1572872 | tf_op jit(solution)/shard_map/ppermute | solution.py:899
  386.5 24.7 %collective-permute-start.45 = (bf16[11,256,128]{2,1,0:T(8,128)(2,1)S(1)}, bf16[11,256,128]{2,1,0:T(8,128)(2,1)S(1)}, u32[]{:S(2)}, u32[]{:S(2)}) collective-permute-start(bf16[11,256,128]{2,1,0:T(8,128)(2,1)S(1)} %add_convert_fusion.1.inner), channel_id=1, source_target_pairs={{1,0},{2,3},{5,4},{6,7},{9,8},{10,11},{13,12},{14,15},{17,16},{18,... | collective-permute-start | bytes 2162696 | tf_op jit(solution)/shard_map/ppermute | solution.py:903
  451.6 19.2 %collective-permute-start.59 = (bf16[8,256,128]{2,1,0:T(8,128)(2,1)S(1)}, bf16[8,256,128]{2,1,0:T(8,128)(2,1)S(1)}, u32[]{:S(2)}, u32[]{:S(2)}) collective-permute-start(bf16[8,256,128]{2,1,0:T(8,128)(2,1)S(1)} %add_convert_fusion.18.inner), channel_id=1, source_target_pairs={{1,0},{2,3},{5,4},{6,7},{9,8},{10,11},{13,12},{14,15},{17,16},{18,... | collective-permute-start | bytes 1572872 | tf_op jit(solution)/shard_map/ppermute | solution.py:903
  453.1 28.0 %collective-permute-start.57 = (bf16[8,256,128]{2,1,0:T(8,128)(2,1)S(1)}, bf16[8,256,128]{2,1,0:T(8,128)(2,1)S(1)}, u32[]{:S(2)}, u32[]{:S(2)}) collective-permute-start(bf16[8,256,128]{2,1,0:T(8,128)(2,1)S(1)} %add_convert_fusion.19.inner), channel_id=1, source_target_pairs={{1,0},{2,3},{5,4},{6,7},{9,8},{10,11},{13,12},{14,15},{17,16},{18,... | collective-permute-start | bytes 1572872 | tf_op jit(solution)/shard_map/ppermute | solution.py:903
  (73 other events, 912.9 us)

commit v6 on v5

--- a/solution.py
+++ b/solution.py
@@ -104,7 +104,7 @@
 
 
 def project_body(slope, x, cosine, sine, before, w, h1, r1, pre, qk, state, joined,
-                 xv, cv, sv, bv, hv, rv, prev, qkv, stv, jv, isem, osem, qsem):
+                 xv, cv, sv, bv, hv, rv, prev, qkv, stv, jv, isem, osem, qsem, *own):
     rows, width = x.shape
     steps = STEPS
     columns = w.shape[1] // steps
@@ -116,6 +116,13 @@
     for copy in first:
         copy.start()
 
+    def weight(j):
+        at = pl.ds(pl.multiple_of(j * columns, LANES), columns)
+        return pltpu.make_async_copy(w.at[:, at], own[0].at[j], own[1].at[j])
+
+    if own:
+        for j in range(steps):
+            weight(j).start()
     first[0].wait()
     v = xv[...].astype(f32)
     factor = norm_factor(v, width)
@@ -137,7 +144,11 @@
 
     def step(j, carry):
         at = pl.multiple_of(j * columns, LANES)
-        p = nn(hv[...], w[:, pl.ds(at, columns)])
+        if own:
+            weight(j).wait()
+            p = nn(hv[...], own[0][j])
+        else:
+            p = nn(hv[...], w[:, pl.ds(at, columns)])
         prev[:, pl.ds(at, columns)] = p.astype(bf16)
         pre_out(j).start()
 
@@ -180,13 +191,13 @@
         qk_out(j).wait()
 
 
-def project(slopes, x, cosine, sine, before, w):
+def project(slopes, x, cosine, sine, before, w, streamed):
     rows, width = x.shape
     total = w.shape[1]
     states = (HEADS, LANES, LANES)
     return pl.pallas_call(
         project_body,
-        in_specs=[SMEM, FREE] + [ANY] * 3 + [VMEM],
+        in_specs=[SMEM, FREE] + [ANY] * 3 + [ANY if streamed else VMEM],
         out_specs=[ANY] * 6,
         out_shape=[
             hbm((rows, width), bf16),
@@ -210,13 +221,18 @@
             pltpu.SemaphoreType.DMA((4,)),
             pltpu.SemaphoreType.DMA((13,)),
             pltpu.SemaphoreType.DMA((STEPS // 2,)),
-        ],
-        compiler_params=params(8),
+        ]
+        + [
+            pltpu.VMEM((STEPS, width, total // STEPS), bf16),
+            pltpu.SemaphoreType.DMA((STEPS,)),
+        ]
+        * streamed,
+        compiler_params=params(18 if streamed else 8),
         cost_estimate=pl.CostEstimate(
             flops=2 * rows * width * total, bytes_accessed=2 * width * total, transcendentals=0
         ),
         name="project",
-    )(slopes, x, *far_away(cosine, sine, before), *close_by(w))
+    )(slopes, x, *far_away(cosine, sine, before), *(far_away(w) if streamed else close_by(w)))
 
 
 def moves(pairs, sem, start=0):
@@ -859,19 +875,18 @@
         for given, kept in chunks:
             blocks = given.shape[0] // 2
             taken = lax.ppermute(given, "seq", [(0, 1), (1, 0), (2, 3), (3, 2)])
-            self.waiting.append(
-                (add(kept[:blocks], taken[:blocks]), add(kept[blocks:], taken[blocks:]))
-            )
+            self.waiting.append((add(kept[:blocks], taken[:blocks]), kept[blocks:], taken[blocks:]))
 
     def over_y(self):
         if not self.waiting:
             return
-        far, own = self.waiting.pop(0)
+        far, own, other = self.waiting.pop(0)
         if self.previous is not None:
             far, _ = lax.optimization_barrier((far, self.previous))
         self.marks.append(far)
         self.previous = lax.ppermute(far, "seq", [(0, 2), (2, 0), (1, 3), (3, 1)])
-        self.parts.append(add(own, self.previous))
+        total = own.astype(f32) + other.astype(f32) + self.previous.astype(f32)
+        self.parts.append(total.astype(bf16))
 
     def over_z(self, last=False):
         step, count = self.step, len(self.parts)
@@ -936,7 +951,8 @@
 
 
 class Layer:
-    def __init__(self, order, slopes, factors, chained, cosine, sine, weights):
+    def __init__(self, order, slopes, factors, chained, cosine, sine, weights, first_of_all):
+        self.first_of_all = first_of_all
         self.order, self.slopes, self.factors, self.chained = order, slopes, factors, chained
         self.cosine, self.sine = cosine, sine
         self.w, self.wo, self.wi, self.wd = weights
@@ -948,7 +964,8 @@
     def first(self, b, x):
         before = self.blocks[0]["state"] if b == 1 else self.zero
         h1, r1, pre, qk, state, joined = project(
-            self.order.after(self.slopes), x, self.cosine[b], self.sine[b], before, self.w
+            self.order.after(self.slopes), x, self.cosine[b], self.sine[b], before, self.w,
+            self.first_of_all and b == 0,
         )
         self.order.at(r1)
         self.blocks[b] = dict(x=x, h1=h1, r1=r1, pre=pre, qk=qk, state=state)
@@ -1039,7 +1056,8 @@
     order = Order()
     order.at(roles, flag)
     layers = [
-        Layer(order, slopes, factors, usual, cosine, sine, weights) for section_of_it in range(2)
+        Layer(order, slopes, factors, usual, cosine, sine, weights, number == 0)
+        for number in range(2)
     ]
     early, late = layers
 

time: 491 us -> 489 us (level)
  local copies, waits for them, and re-layouts: 11.7 us -> 6.76 us
    unnamed x91 -> x87, local copies, waits for them, and re-layouts: 9.31 us -> 4.39 us
where the time goes in v6:
time: 489 us; the launch traced here: 480 us
  Pallas kernels  238 us (49%)
  waiting for transfers between devices  119 us (24%)
  starting transfers between devices  84.8 us (17%)
  other arithmetic  17.2 us (4%)
  blocking collectives  12.1 us (2%)
  local copies, waits for them, and re-layouts  6.76 us (1%)
    pallas_call x4, Pallas kernels, back_channel(): pl.pallas_call(back_channel_body, in_specs=[SMEM] + [FREE] + [VMEM] * 3 +...  63.5 us
    pallas_call x4, Pallas kernels, finish(): pl.pallas_call(finish_body, in_specs=[SMEM] * 2 + [FREE] + [ANY] * 2 + [F...  52.5 us
    pallas_call x4, Pallas kernels, weight_gradient(): pl.pallas_call(functools.partial(weight_body, batch=batch, sides=sides, g...  40.3 us
    pallas_call x4, Pallas kernels, project(): pl.pallas_call(project_body, in_specs=[SMEM, FREE] + [ANY] * 3 + [ANY if...  34.9 us
    pallas_call x4, Pallas kernels, back_mixer(): pl.pallas_call(back_mixer_body, in_specs=[SMEM] * 2 + [ANY] * 6 + [FREE]...  33.2 us
    ppermute x7, waiting for transfers between devices, over_z(): got = lax.ppermute(sent, 'dp', [(0, 1), (1, 0), (2, 3), (3, 2)])  26.8 us
    ppermute x11, waiting for transfers between devices, over_y(): self.previous = lax.ppermute(far, 'seq', [(0, 2), (2, 0), (1, 3), (3, 1)])  23.7 us
    ppermute x4, waiting for transfers between devices, over_z(): lax.ppermute(done, 'dp', [(1, 0), (2, 3)])  23.5 us
  transfers between devices with their start and end apart: 60, of which 23 were waited for; matrix products, arithmetic and copies ran while one was open for 3% of the time, Pallas kernels for 25%

profile of v6, /device:TPU:0, one launch (start us, length us, event | category | flops | bytes accessed | tf_op | source)
XLA Modules:
  0.0 480.3 jit_solution(12976767762628015215)
XLA Ops:
  5.7 12.1 %all-gather.1 = s32[4,2,256]{2,1,0:T(2,128)S(1)} all-gather(s32[1,2,256]{2,1,0:T(2,128)S(1)} %bitcast.104), channel_id=2, replica_groups=mesh['section'=2,'seq'=4,'dp'=4] {'seq'}, dimensions={0}, use_global_device_ids=true | all-gather | bytes 10240 | tf_op jit(solution)/shard_map/all_gather | solution.py:1034
  20.9 10.9 %project.4 = (bf16[256,1024]{1,0:T(8,128)(2,1)}, f32[256,128]{1,0:T(8,128)}, bf16[256,4096]{1,0:T(8,128)(2,1)}, bf16[256,2048]{1,0:T(8,128)(2,1)}, bf16[8,128,12...) custom-call(f32[8]{0:T(128)S(1)} %get-tuple-element.293.slope, bf16[256,1024]{1,0:T(8,128)(2,1)S(1)} %get-tuple-element.355.x.dy.refs_7_, ...), custom_call_target="tpu_custom_call" | custom-call | flops 2147483648 | bytes 8388608 | tf_op jit(solution)/shard_map/project/pallas_call | solution.py:198
  31.8 8.2 %project.5 = (bf16[256,1024]{1,0:T(8,128)(2,1)}, f32[256,128]{1,0:T(8,128)}, bf16[256,4096]{1,0:T(8,128)(2,1)}, bf16[256,2048]{1,0:T(8,128)(2,1)}, bf16[8,128,12...) custom-call(f32[8]{0:T(128)S(1)} %get-tuple-element.293.slope, bf16[256,1024]{1,0:T(8,128)(2,1)S(1)} %get-tuple-element.354.x.dy.refs_8_, ...), custom_call_target="tpu_custom_call" | custom-call | flops 2147483648 | bytes 8388608 | tf_op jit(solution)/shard_map/project/pallas_call | solution.py:198
  46.3 13.3 %finish.4 = (bf16[256,1024]{1,0:T(8,128)(2,1)}, bf16[256,1024]{1,0:T(8,128)(2,1)}, f32[256,128]{1,0:T(8,128)}, bf16[256,1024]{1,0:T(8,128)(2,1)}, f32[256,128]{1...) custom-call(f32[8]{0:T(128)S(1)} %get-tuple-element.293.slope, ...), custom_call_target="tpu_custom_call" | custom-call | flops 4966055936 | bytes 19398656 | tf_op jit(solution)/shard_map/finish/pallas_call | solution.py:361
  63.3 13.1 %finish.5 = (bf16[256,1024]{1,0:T(8,128)(2,1)}, bf16[256,1024]{1,0:T(8,128)(2,1)}, f32[256,128]{1,0:T(8,128)}, bf16[256,1024]{1,0:T(8,128)(2,1)}, f32[256,128]{1...) custom-call(f32[8]{0:T(128)S(1)} %get-tuple-element.293.slope, ...), custom_call_target="tpu_custom_call" | custom-call | flops 4966055936 | bytes 19398656 | tf_op jit(solution)/shard_map/finish/pallas_call | solution.py:361
  77.7 7.9 %project.6 = (bf16[256,1024]{1,0:T(8,128)(2,1)}, f32[256,128]{1,0:T(8,128)}, bf16[256,4096]{1,0:T(8,128)(2,1)}, bf16[256,2048]{1,0:T(8,128)(2,1)}, bf16[8,128,12...) custom-call(f32[8]{0:T(128)S(1)} %get-tuple-element.293.slope, bf16[256,1024]{1,0:T(8,128)(2,1)S(1)} %collective-permute-done.3.x, ...), custom_call_target="tpu_custom_call" | custom-call | flops 2147483648 | bytes 8388608 | tf_op jit(solution)/shard_map/project/pallas_call | solution.py:198
  89.7 7.9 %project.7 = (bf16[256,1024]{1,0:T(8,128)(2,1)}, f32[256,128]{1,0:T(8,128)}, bf16[256,4096]{1,0:T(8,128)(2,1)}, bf16[256,2048]{1,0:T(8,128)(2,1)}, bf16[8,128,12...) custom-call(f32[8]{0:T(128)S(1)} %get-tuple-element.293.slope, bf16[256,1024]{1,0:T(8,128)(2,1)S(1)} %collective-permute-done.4.x, ...), custom_call_target="tpu_custom_call" | custom-call | flops 2147483648 | bytes 8388608 | tf_op jit(solution)/shard_map/project/pallas_call | solution.py:198
  100.4 13.1 %finish.6 = (bf16[256,1024]{1,0:T(8,128)(2,1)}, bf16[256,1024]{1,0:T(8,128)(2,1)}, f32[256,128]{1,0:T(8,128)}, bf16[256,1024]{1,0:T(8,128)(2,1)}, f32[256,128]{1...) custom-call(f32[8]{0:T(128)S(1)} %get-tuple-element.293.slope, ...), custom_call_target="tpu_custom_call" | custom-call | flops 4966055936 | bytes 19398656 | tf_op jit(solution)/shard_map/finish/pallas_call | solution.py:361
  113.5 13.1 %finish.7 = (bf16[256,1024]{1,0:T(8,128)(2,1)}, bf16[256,1024]{1,0:T(8,128)(2,1)}, f32[256,128]{1,0:T(8,128)}, bf16[256,1024]{1,0:T(8,128)(2,1)}, f32[256,128]{1...) custom-call(f32[8]{0:T(128)S(1)} %get-tuple-element.293.slope, ...), custom_call_target="tpu_custom_call" | custom-call | flops 4966055936 | bytes 19398656 | tf_op jit(solution)/shard_map/finish/pallas_call | solution.py:361
  126.6 15.8 %back_channel.4 = (bf16[256,2816]{1,0:T(8,128)(2,1)}, bf16[256,2816]{1,0:T(8,128)(2,1)}, f32[256,1024]{1,0:T(8,128)}, bf16[256,1024]{1,0:T(8,128)(2,1)}, bf16[25...) custom-call(f32[8]{0:T(128)S(1)} %get-tuple-element.293.slope, ...), custom_call_target="tpu_custom_call" | custom-call | flops 4966055936 | bytes 19398656 | tf_op jit(solution)/shard_map/back_channel/pallas_call | solution.py:541
  142.5 15.9 %back_channel.5 = (bf16[256,2816]{1,0:T(8,128)(2,1)}, bf16[256,2816]{1,0:T(8,128)(2,1)}, f32[256,1024]{1,0:T(8,128)}, bf16[256,1024]{1,0:T(8,128)(2,1)}, bf16[25...) custom-call(f32[8]{0:T(128)S(1)} %get-tuple-element.293.slope, ...), custom_call_target="tpu_custom_call" | custom-call | flops 4966055936 | bytes 19398656 | tf_op jit(solution)/shard_map/back_channel/pallas_call | solution.py:541
  162.0 8.2 %back_mixer.4 = (bf16[256,1024]{1,0:T(8,128)(2,1)}, bf16[256,1024]{1,0:T(8,128)(2,1)}, bf16[256,1024]{1,0:T(8,128)(2,1)}) custom-call(f32[8]{0:T(128)S(1)} %get-tuple-element.293.slope, f32[2,8]{1,0:T(2,128)S(1)} %copy-done.13, bf16[256,1024]{1,0:T(8,128)(2,1)} %get-tuple-element.231.dq.refs_14_, bf16[256,1024]{1,0:T(8,128)(2,1)} %get-tuple-element.232.du.refs_20_, ...), custom_call_target="tpu_custom_call" | custom-call | flops 2147483648 | bytes 8388608 | tf_op jit(solution)/shard_map/back_mixer/pallas_call | solution.py:647
  171.7 8.3 %back_mixer.5 = (bf16[256,1024]{1,0:T(8,128)(2,1)}, bf16[256,1024]{1,0:T(8,128)(2,1)}, bf16[256,1024]{1,0:T(8,128)(2,1)}) custom-call(f32[8]{0:T(128)S(1)} %get-tuple-element.293.slope, f32[2,8]{1,0:T(2,128)S(1)} %stack.37.factors, bf16[256,1024]{1,0:T(8,128)(2,1)} %get-tuple-element.240.dq.refs_13_, bf16[256,1024]{1,0:T(8,128)(2,1)} %get-tuple-element.241.du.refs_19_, ...), custom_call_target="tpu_custom_call" | custom-call | flops 2147483648 | bytes 8388608 | tf_op jit(solution)/shard_map/back_mixer/pallas_call | solution.py:647
  181.2 5.8 %collective-permute-done.7.dy.refs_6_ = bf16[256,1024]{1,0:T(8,128)(2,1)S(1)} collective-permute-done((bf16[256,1024]{1,0:T(8,128)(2,1)}, bf16[256,1024]{1,0:T(8,128)(2,1)S(1)}, u32[]{:S(2)}, u32[]{:S(2)}) %collective-permute-start.7) | collective-permute-done | bytes 524320 | tf_op jit(solution)/shard_map/ppermute | solution.py:1074
  187.1 15.9 %back_channel.6 = (bf16[256,2816]{1,0:T(8,128)(2,1)}, bf16[256,2816]{1,0:T(8,128)(2,1)}, f32[256,1024]{1,0:T(8,128)}, bf16[256,1024]{1,0:T(8,128)(2,1)}, bf16[25...) custom-call(f32[8]{0:T(128)S(1)} %get-tuple-element.293.slope, ...), custom_call_target="tpu_custom_call" | custom-call | flops 4966055936 | bytes 19398656 | tf_op jit(solution)/shard_map/back_channel/pallas_call | solution.py:541
  203.8 9.1 %weight_gradient.4 = (bf16[8,704,128]{2,1,0:T(8,128)(2,1)}, bf16[8,704,128]{2,1,0:T(8,128)(2,1)}, bf16[8,704,128]{2,1,0:T(8,128)(2,1)}, bf16[8,704,128]{2,1,0:T(8,128)(2,1)}) custom-call(s32[5]{0:T(128)S(1)} %stack.36.refs_0_, bf16[256,2816]{1,0:T(8,128)(2,1)} %get-tuple-element.257.refs_1_, bf16[256,2816]{1,0:T(8,128)(2,1)} %get-tuple-element.258.refs_2_, ...), custom_call_target="tpu_custom_call" | custom-call | flops 2952790016 | bytes 5767168 | tf_op jit(solution)/shard_map/weight_gradient/pallas_call | solution.py:769
  219.0 15.9 %back_channel.7 = (bf16[256,2816]{1,0:T(8,128)(2,1)}, bf16[256,2816]{1,0:T(8,128)(2,1)}, f32[256,1024]{1,0:T(8,128)}, bf16[256,1024]{1,0:T(8,128)(2,1)}, bf16[25...) custom-call(f32[8]{0:T(128)S(1)} %get-tuple-element.293.slope, ...), custom_call_target="tpu_custom_call" | custom-call | flops 4966055936 | bytes 19398656 | tf_op jit(solution)/shard_map/back_channel/pallas_call | solution.py:541
  234.9 14.3 %weight_gradient.5 = (bf16[22,256,128]{2,1,0:T(8,128)(2,1)}, bf16[22,256,128]{2,1,0:T(8,128)(2,1)}, bf16[22,256,128]{2,1,0:T(8,128)(2,1)}, bf16[22,256,128]{2,1,...) custom-call(s32[5]{0:T(128)S(1)} %stack.36.refs_0_, ...), custom_call_target="tpu_custom_call" | custom-call | flops 5905580032 | bytes 11534336 | tf_op jit(solution)/shard_map/weight_gradient/pallas_call | solution.py:769
  255.8 13.4 %collective-permute-done.34 = bf16[11,256,128]{2,1,0:T(8,128)(2,1)S(1)} collective-permute-done((bf16[11,256,128]{2,1,0:T(8,128)(2,1)S(1)}, bf16[11,256,128]{2,1,0:T(8,128)(2,1)S(1)}, u32[]{:S(2)}, u32[]{:S(2)}) %collective-permute-start.34) | collective-permute-done | bytes 720928 | tf_op jit(solution)/shard_map/ppermute | solution.py:914
  278.0 8.5 %back_mixer.6 = (bf16[256,1024]{1,0:T(8,128)(2,1)}, bf16[256,1024]{1,0:T(8,128)(2,1)}, bf16[256,1024]{1,0:T(8,128)(2,1)}) custom-call(f32[8]{0:T(128)S(1)} %get-tuple-element.293.slope, f32[2,8]{1,0:T(2,128)S(1)} %copy-done.13, bf16[256,1024]{1,0:T(8,128)(2,1)} %get-tuple-element.285.dq.refs_6_, bf16[256,1024]{1,0:T(8,128)(2,1)} %get-tuple-element.286.du.refs_12_, ...), custom_call_target="tpu_custom_call" | custom-call | flops 2147483648 | bytes 8388608 | tf_op jit(solution)/shard_map/back_mixer/pallas_call | solution.py:647
  295.8 8.2 %back_mixer.7 = (bf16[256,1024]{1,0:T(8,128)(2,1)}, bf16[256,1024]{1,0:T(8,128)(2,1)}, bf16[256,1024]{1,0:T(8,128)(2,1)}) custom-call(f32[8]{0:T(128)S(1)} %get-tuple-element.293.slope, f32[2,8]{1,0:T(2,128)S(1)} %stack.37.factors, bf16[256,1024]{1,0:T(8,128)(2,1)} %get-tuple-element.294.dq.refs_5_, bf16[256,1024]{1,0:T(8,128)(2,1)} %get-tuple-element.295.du.refs_11_, ...), custom_call_target="tpu_custom_call" | custom-call | flops 2147483648 | bytes 8388608 | tf_op jit(solution)/shard_map/back_mixer/pallas_call | solution.py:647
  317.2 11.8 %weight_gradient.7 = (bf16[16,256,128]{2,1,0:T(8,128)(2,1)}, bf16[16,256,128]{2,1,0:T(8,128)(2,1)}, bf16[16,256,128]{2,1,0:T(8,128)(2,1)}, bf16[16,256,128]{2,1,...) custom-call(s32[5]{0:T(128)S(1)} %stack.36.refs_0_, ...), custom_call_target="tpu_custom_call" | custom-call | flops 4294967296 | bytes 8388608 | tf_op jit(solution)/shard_map/weight_gradient/pallas_call | solution.py:769
  337.2 11.6 %collective-permute-done.28 = bf16[11,256,128]{2,1,0:T(8,128)(2,1)S(1)} collective-permute-done((bf16[11,256,128]{2,1,0:T(8,128)(2,1)S(1)}, bf16[11,256,128]{2,1,0:T(8,128)(2,1)S(1)}, u32[]{:S(2)}, u32[]{:S(2)}) %collective-permute-start.28) | collective-permute-done | bytes 720928 | tf_op jit(solution)/shard_map/ppermute | solution.py:887
  358.7 6.7 %collective-permute-done.29 = bf16[8,256,128]{2,1,0:T(8,128)(2,1)S(1)} collective-permute-done((bf16[8,256,128]{2,1,0:T(8,128)(2,1)S(1)}, bf16[8,256,128]{2,1,0:T(8,128)(2,1)S(1)}, u32[]{:S(2)}, u32[]{:S(2)}) %collective-permute-start.29) | collective-permute-done | bytes 524320 | tf_op jit(solution)/shard_map/ppermute | solution.py:887
  367.1 6.1 %collective-permute-done.43.outer = bf16[11,256,128]{2,1,0:T(8,128)(2,1)S(1)} collective-permute-done((bf16[11,256,128]{2,1,0:T(8,128)(2,1)S(1)}, bf16[11,256,128]{2,1,0:T(8,128)(2,1)S(1)}, u32[]{:S(2)}, u32[]{:S(2)}) %collective-permute-start.43) | collective-permute-done | bytes 720928 | tf_op jit(solution)/shard_map/ppermute | solution.py:908
  377.1 5.2 %collective-permute-start.48 = (bf16[8,256,128]{2,1,0:T(8,128)(2,1)S(1)}, bf16[8,256,128]{2,1,0:T(8,128)(2,1)S(1)}, u32[]{:S(2)}, u32[]{:S(2)}) collective-permute-start(bf16[8,256,128]{2,1,0:T(8,128)(2,1)S(1)} %add_convert_fusion.17), channel_id=1, source_target_pairs={{0,1},{3,2},{4,5},{7,6},{8,9},{11,10},{12,13},{15,14},{16,17},{19,... | collective-permute-start | bytes 1572872 | tf_op jit(solution)/shard_map/ppermute | solution.py:914
  385.4 8.4 %collective-permute-done.47.outer = bf16[11,256,128]{2,1,0:T(8,128)(2,1)S(1)} collective-permute-done((bf16[11,256,128]{2,1,0:T(8,128)(2,1)S(1)}, bf16[11,256,128]{2,1,0:T(8,128)(2,1)S(1)}, u32[]{:S(2)}, u32[]{:S(2)}) %collective-permute-start.47) | collective-permute-done | bytes 720928 | tf_op jit(solution)/shard_map/ppermute | solution.py:918
  400.0 6.3 %collective-permute-done.51 = bf16[8,256,128]{2,1,0:T(8,128)(2,1)S(1)} collective-permute-done((bf16[8,256,128]{2,1,0:T(8,128)(2,1)S(1)}, bf16[8,256,128]{2,1,0:T(8,128)(2,1)S(1)}, u32[]{:S(2)}, u32[]{:S(2)}) %collective-permute-start.51) | collective-permute-done | bytes 524320 | tf_op jit(solution)/shard_map/ppermute | solution.py:914
  415.5 6.4 %collective-permute-done.50.outer = bf16[8,256,128]{2,1,0:T(8,128)(2,1)S(1)} collective-permute-done((bf16[8,256,128]{2,1,0:T(8,128)(2,1)S(1)}, bf16[8,256,128]{2,1,0:T(8,128)(2,1)S(1)}, u32[]{:S(2)}, u32[]{:S(2)}) %collective-permute-start.50) | collective-permute-done | bytes 524320 | tf_op jit(solution)/shard_map/ppermute | solution.py:908
  439.0 6.2 %collective-permute-done.55.outer = bf16[8,256,128]{2,1,0:T(8,128)(2,1)S(1)} collective-permute-done((bf16[8,256,128]{2,1,0:T(8,128)(2,1)S(1)}, bf16[8,256,128]{2,1,0:T(8,128)(2,1)S(1)}, u32[]{:S(2)}, u32[]{:S(2)}) %collective-permute-start.55) | collective-permute-done | bytes 524320 | tf_op jit(solution)/shard_map/ppermute | solution.py:908
  452.0 9.7 %collective-permute-done.12 = bf16[256,1024]{1,0:T(8,128)(2,1)S(1)} collective-permute-done((bf16[256,1024]{1,0:T(8,128)(2,1)S(1)}, bf16[256,1024]{1,0:T(8,128)(2,1)S(1)}, u32[]{:S(2)}, u32[]{:S(2)}) %collective-permute-start.12) | collective-permute-done | bytes 524320 | tf_op jit(solution)/shard_map/ppermute | solution.py:856
  469.2 9.5 %collective-permute-done.57.outer = bf16[8,256,128]{2,1,0:T(8,128)(2,1)S(1)} collective-permute-done((bf16[8,256,128]{2,1,0:T(8,128)(2,1)S(1)}, bf16[8,256,128]{2,1,0:T(8,128)(2,1)S(1)}, u32[]{:S(2)}, u32[]{:S(2)}) %collective-permute-start.57) | collective-permute-done | bytes 524320 | tf_op jit(solution)/shard_map/ppermute | solution.py:918
  (267 shorter events, 151.1 us)
Async XLA Ops:
  2.0 18.0 %collective-permute-start.1 = (bf16[256,1024]{1,0:T(8,128)(2,1)S(1)}, bf16[256,1024]{1,0:T(8,128)(2,1)S(1)}, u32[]{:S(2)}, u32[]{:S(2)}) collective-permute-start(bf16[256,1024]{1,0:T(8,128)(2,1)S(1)} %get-tuple-element.362), channel_id=1, source_target_pairs={{4,0},{8,12},{0,8},{12,4},{5,1},{9,13},{1,9},{13,5},{6,2},{10,14},... | collective-permute-start | bytes 1572872 | tf_op jit(solution)/shard_map/ppermute | solution.py:846
  59.6 18.1 %collective-permute-start.3 = (bf16[256,1024]{1,0:T(8,128)(2,1)}, bf16[256,1024]{1,0:T(8,128)(2,1)S(1)}, u32[]{:S(2)}, u32[]{:S(2)}) collective-permute-start(bf16[256,1024]{1,0:T(8,128)(2,1)} %get-tuple-element.198), channel_id=1, source_target_pairs={{0,16},{1,17},{2,18},{3,19},{4,20},{5,21},{6,22},{7,23},{8,24},{9,... | collective-permute-start | bytes 1572872 | tf_op jit(solution)/shard_map/ppermute | solution.py:1066
  179.9 23.0 %collective-permute-start.8 = (bf16[256,1024]{1,0:T(8,128)(2,1)}, bf16[256,1024]{1,0:T(8,128)(2,1)S(1)}, u32[]{:S(2)}, u32[]{:S(2)}) collective-permute-start(bf16[256,1024]{1,0:T(8,128)(2,1)} %get-tuple-element.261), channel_id=1, source_target_pairs={{16,0},{17,1},{18,2},{19,3},{20,4},{21,5},{22,6},{23,7},{24,8},{25... | collective-permute-start | bytes 1572872 | tf_op jit(solution)/shard_map/ppermute | solution.py:1074
  213.0 40.9 %collective-permute-start.13 = (bf16[22,256,128]{2,1,0:T(8,128)(2,1)}, bf16[22,256,128]{2,1,0:T(8,128)(2,1)S(1)}, u32[]{:S(2)}, u32[]{:S(2)}) collective-permute-start(bf16[22,256,128]{2,1,0:T(8,128)(2,1)} %bitcast.105), channel_id=1, source_target_pairs={{0,4},{4,0},{8,12},{12,8},{1,5},{5,1},{9,13},{13,9},{2,6},{6,2},{1... | collective-permute-start | bytes 4325384 | tf_op jit(solution)/shard_map/ppermute | solution.py:877
  216.6 32.7 %collective-permute-start.14 = (bf16[11,256,128]{2,1,0:T(8,128)(2,1)S(1)}, bf16[11,256,128]{2,1,0:T(8,128)(2,1)S(1)}, u32[]{:S(2)}, u32[]{:S(2)}) collective-permute-start(bf16[11,256,128]{2,1,0:T(8,128)(2,1)S(1)} %fusion.13), channel_id=1, source_target_pairs={{0,8},{8,0},{4,12},{12,4},{1,9},{9,1},{5,13},{13,5},{2,10},{10,2},... | collective-permute-start | bytes 2162696 | tf_op jit(solution)/shard_map/ppermute | solution.py:887
  249.2 20.2 %collective-permute-start.23 = (bf16[22,256,128]{2,1,0:T(8,128)(2,1)}, bf16[22,256,128]{2,1,0:T(8,128)(2,1)S(1)}, u32[]{:S(2)}, u32[]{:S(2)}) collective-permute-start(bf16[22,256,128]{2,1,0:T(8,128)(2,1)} %get-tuple-element.333), channel_id=1, source_target_pairs={{0,4},{4,0},{8,12},{12,8},{1,5},{5,1},{9,13},{13,9},{2,6},{6,2},{1... | collective-permute-start | bytes 4325384 | tf_op jit(solution)/shard_map/ppermute | solution.py:877
  249.6 19.6 %collective-permute-start.34 = (bf16[11,256,128]{2,1,0:T(8,128)(2,1)S(1)}, bf16[11,256,128]{2,1,0:T(8,128)(2,1)S(1)}, u32[]{:S(2)}, u32[]{:S(2)}) collective-permute-start(bf16[11,256,128]{2,1,0:T(8,128)(2,1)S(1)} %fusion.11), channel_id=1, source_target_pairs={{0,1},{3,2},{4,5},{7,6},{8,9},{11,10},{12,13},{15,14},{16,17},{19,... | collective-permute-start | bytes 2162696 | tf_op jit(solution)/shard_map/ppermute | solution.py:914
  253.6 32.9 %collective-permute-start.22 = (bf16[22,256,128]{2,1,0:T(8,128)(2,1)S(1)}, bf16[22,256,128]{2,1,0:T(8,128)(2,1)S(1)}, u32[]{:S(2)}, u32[]{:S(2)}) collective-permute-start(bf16[22,256,128]{2,1,0:T(8,128)(2,1)S(1)} %copy-done.33), channel_id=1, source_target_pairs={{0,4},{4,0},{8,12},{12,8},{1,5},{5,1},{9,13},{13,9},{2,6},{6,2},{1... | collective-permute-start | bytes 4325384 | tf_op jit(solution)/shard_map/ppermute | solution.py:877
  254.1 18.4 %collective-permute-start.24 = (bf16[11,256,128]{2,1,0:T(8,128)(2,1)S(1)}, bf16[11,256,128]{2,1,0:T(8,128)(2,1)S(1)}, u32[]{:S(2)}, u32[]{:S(2)}) collective-permute-start(bf16[11,256,128]{2,1,0:T(8,128)(2,1)S(1)} %fusion.12), channel_id=1, source_target_pairs={{0,8},{8,0},{4,12},{12,4},{1,9},{9,1},{5,13},{13,5},{2,10},{10,2},... | collective-permute-start | bytes 2162696 | tf_op jit(solution)/shard_map/ppermute | solution.py:887
  254.5 18.5 %collective-permute-start.10 = (bf16[8,128,128]{2,1,0:T(8,128)(2,1)S(1)}, bf16[8,128,128]{2,1,0:T(8,128)(2,1)S(1)}, u32[]{:S(2)}, u32[]{:S(2)}) collective-permute-start(bf16[8,128,128]{2,1,0:T(8,128)(2,1)S(1)} %copy-done.38), channel_id=1, source_target_pairs={{4,0},{12,8},{5,1},{13,9},{6,2},{14,10},{7,3},{15,11},{20,16},{28,... | collective-permute-start | bytes 786440 | tf_op jit(solution)/shard_map/ppermute | solution.py:1003
  269.2 39.9 %collective-permute-start.21 = (bf16[22,256,128]{2,1,0:T(8,128)(2,1)S(1)}, bf16[22,256,128]{2,1,0:T(8,128)(2,1)S(1)}, u32[]{:S(2)}, u32[]{:S(2)}) collective-permute-start(bf16[22,256,128]{2,1,0:T(8,128)(2,1)S(1)} %copy-done.32), channel_id=1, source_target_pairs={{0,4},{4,0},{8,12},{12,8},{1,5},{5,1},{9,13},{13,9},{2,6},{6,2},{1... | collective-permute-start | bytes 4325384 | tf_op jit(solution)/shard_map/ppermute | solution.py:877
  269.4 21.2 %collective-permute-start.35 = (bf16[11,256,128]{2,1,0:T(8,128)(2,1)S(1)}, bf16[11,256,128]{2,1,0:T(8,128)(2,1)S(1)}, u32[]{:S(2)}, u32[]{:S(2)}) collective-permute-start(bf16[11,256,128]{2,1,0:T(8,128)(2,1)S(1)} %add_convert_fusion.3), channel_id=1, source_target_pairs={{1,2},{2,1},{5,6},{6,5},{9,10},{10,9},{13,14},{14,13},{17,18},{18,... | collective-permute-start | bytes 2162696 | tf_op jit(solution)/shard_map/ppermute | solution.py:904
  272.5 17.5 %collective-permute-start.25 = (bf16[11,256,128]{2,1,0:T(8,128)(2,1)S(1)}, bf16[11,256,128]{2,1,0:T(8,128)(2,1)S(1)}, u32[]{:S(2)}, u32[]{:S(2)}) collective-permute-start(bf16[11,256,128]{2,1,0:T(8,128)(2,1)S(1)} %add_convert_fusion.8), channel_id=1, source_target_pairs={{0,8},{8,0},{4,12},{12,4},{1,9},{9,1},{5,13},{13,5},{2,10},{10,2},... | collective-permute-start | bytes 2162696 | tf_op jit(solution)/shard_map/ppermute | solution.py:887
  273.1 21.8 %collective-permute-start.37 = (bf16[11,256,128]{2,1,0:T(8,128)(2,1)S(1)}, bf16[11,256,128]{2,1,0:T(8,128)(2,1)S(1)}, u32[]{:S(2)}, u32[]{:S(2)}) collective-permute-start(bf16[11,256,128]{2,1,0:T(8,128)(2,1)S(1)} %fusion.9), channel_id=1, source_target_pairs={{0,1},{3,2},{4,5},{7,6},{8,9},{11,10},{12,13},{15,14},{16,17},{19,... | collective-permute-start | bytes 2162696 | tf_op jit(solution)/shard_map/ppermute | solution.py:914
  286.5 42.6 %collective-permute-start.20 = (bf16[22,256,128]{2,1,0:T(8,128)(2,1)S(1)}, bf16[22,256,128]{2,1,0:T(8,128)(2,1)S(1)}, u32[]{:S(2)}, u32[]{:S(2)}) collective-permute-start(bf16[22,256,128]{2,1,0:T(8,128)(2,1)S(1)} %copy-done.31), channel_id=1, source_target_pairs={{0,4},{4,0},{8,12},{12,8},{1,5},{5,1},{9,13},{13,9},{2,6},{6,2},{1... | collective-permute-start | bytes 4325384 | tf_op jit(solution)/shard_map/ppermute | solution.py:877
  290.0 19.3 %collective-permute-start.26 = (bf16[11,256,128]{2,1,0:T(8,128)(2,1)S(1)}, bf16[11,256,128]{2,1,0:T(8,128)(2,1)S(1)}, u32[]{:S(2)}, u32[]{:S(2)}) collective-permute-start(bf16[11,256,128]{2,1,0:T(8,128)(2,1)S(1)} %add_convert_fusion.9), channel_id=1, source_target_pairs={{0,8},{8,0},{4,12},{12,4},{1,9},{9,1},{5,13},{13,5},{2,10},{10,2},... | collective-permute-start | bytes 2162696 | tf_op jit(solution)/shard_map/ppermute | solution.py:887
  291.2 20.0 %collective-permute-start.36 = (bf16[11,256,128]{2,1,0:T(8,128)(2,1)S(1)}, bf16[11,256,128]{2,1,0:T(8,128)(2,1)S(1)}, u32[]{:S(2)}, u32[]{:S(2)}) collective-permute-start(bf16[11,256,128]{2,1,0:T(8,128)(2,1)S(1)} %fusion), channel_id=1, source_target_pairs={{0,1},{1,0},{2,3},{3,2},{4,5},{5,4},{6,7},{7,6},{8,9},{9,8},{10,11... | collective-permute-start | bytes 2162696 | tf_op jit(solution)/shard_map/ppermute | solution.py:908
  295.1 17.6 %collective-permute-start.38 = (bf16[11,256,128]{2,1,0:T(8,128)(2,1)S(1)}, bf16[11,256,128]{2,1,0:T(8,128)(2,1)S(1)}, u32[]{:S(2)}, u32[]{:S(2)}) collective-permute-start(bf16[11,256,128]{2,1,0:T(8,128)(2,1)S(1)} %add_convert_fusion.2), channel_id=1, source_target_pairs={{1,2},{2,1},{5,6},{6,5},{9,10},{10,9},{13,14},{14,13},{17,18},{18,... | collective-permute-start | bytes 2162696 | tf_op jit(solution)/shard_map/ppermute | solution.py:904
  309.3 20.5 %collective-permute-start.27 = (bf16[11,256,128]{2,1,0:T(8,128)(2,1)S(1)}, bf16[11,256,128]{2,1,0:T(8,128)(2,1)S(1)}, u32[]{:S(2)}, u32[]{:S(2)}) collective-permute-start(bf16[11,256,128]{2,1,0:T(8,128)(2,1)S(1)} %add_convert_fusion.10), channel_id=1, source_target_pairs={{0,8},{8,0},{4,12},{12,4},{1,9},{9,1},{5,13},{13,5},{2,10},{10,2},... | collective-permute-start | bytes 2162696 | tf_op jit(solution)/shard_map/ppermute | solution.py:887
  313.0 17.8 %collective-permute-start.39 = (bf16[11,256,128]{2,1,0:T(8,128)(2,1)S(1)}, bf16[11,256,128]{2,1,0:T(8,128)(2,1)S(1)}, u32[]{:S(2)}, u32[]{:S(2)}) collective-permute-start(bf16[11,256,128]{2,1,0:T(8,128)(2,1)S(1)} %fusion.2), channel_id=1, source_target_pairs={{0,1},{1,0},{2,3},{3,2},{4,5},{5,4},{6,7},{7,6},{8,9},{9,8},{10,11... | collective-permute-start | bytes 2162696 | tf_op jit(solution)/shard_map/ppermute | solution.py:908
  316.5 17.1 %collective-permute-start.40 = (bf16[11,256,128]{2,1,0:T(8,128)(2,1)S(1)}, bf16[11,256,128]{2,1,0:T(8,128)(2,1)S(1)}, u32[]{:S(2)}, u32[]{:S(2)}) collective-permute-start(bf16[11,256,128]{2,1,0:T(8,128)(2,1)S(1)} %fusion.1), channel_id=1, source_target_pairs={{1,2},{2,1},{5,6},{6,5},{9,10},{10,9},{13,14},{14,13},{17,18},{18,... | collective-permute-start | bytes 2162696 | tf_op jit(solution)/shard_map/ppermute | solution.py:904
  329.0 84.2 %collective-permute-start.15 = (bf16[16,256,128]{2,1,0:T(8,128)(2,1)}, bf16[16,256,128]{2,1,0:T(8,128)(2,1)S(1)}, u32[]{:S(2)}, u32[]{:S(2)}) collective-permute-start(bf16[16,256,128]{2,1,0:T(8,128)(2,1)} %get-tuple-element.319), channel_id=1, source_target_pairs={{0,4},{4,0},{8,12},{12,8},{1,5},{5,1},{9,13},{13,9},{2,6},{6,2},{1... | collective-permute-start | bytes 3145736 | tf_op jit(solution)/shard_map/ppermute | solution.py:877
  330.9 17.9 %collective-permute-start.28 = (bf16[11,256,128]{2,1,0:T(8,128)(2,1)S(1)}, bf16[11,256,128]{2,1,0:T(8,128)(2,1)S(1)}, u32[]{:S(2)}, u32[]{:S(2)}) collective-permute-start(bf16[11,256,128]{2,1,0:T(8,128)(2,1)S(1)} %add_convert_fusion.11), channel_id=1, source_target_pairs={{0,8},{8,0},{4,12},{12,4},{1,9},{9,1},{5,13},{13,5},{2,10},{10,2},... | collective-permute-start | bytes 2162696 | tf_op jit(solution)/shard_map/ppermute | solution.py:887
  333.9 18.1 %collective-permute-start.41 = (bf16[11,256,128]{2,1,0:T(8,128)(2,1)S(1)}, bf16[11,256,128]{2,1,0:T(8,128)(2,1)S(1)}, u32[]{:S(2)}, u32[]{:S(2)}) collective-permute-start(bf16[11,256,128]{2,1,0:T(8,128)(2,1)S(1)} %fusion.4.inner), channel_id=1, source_target_pairs={{0,1},{1,0},{2,3},{3,2},{4,5},{5,4},{6,7},{7,6},{8,9},{9,8},{10,11... | collective-permute-start | bytes 2162696 | tf_op jit(solution)/shard_map/ppermute | solution.py:908
  335.9 19.4 %collective-permute-start.42 = (bf16[11,256,128]{2,1,0:T(8,128)(2,1)S(1)}, bf16[11,256,128]{2,1,0:T(8,128)(2,1)S(1)}, u32[]{:S(2)}, u32[]{:S(2)}) collective-permute-start(bf16[11,256,128]{2,1,0:T(8,128)(2,1)S(1)} %fusion.3), channel_id=1, source_target_pairs={{1,2},{2,1},{5,6},{6,5},{9,10},{10,9},{13,14},{14,13},{17,18},{18,... | collective-permute-start | bytes 2162696 | tf_op jit(solution)/shard_map/ppermute | solution.py:904
  336.9 20.7 %collective-permute-start.17 = (bf16[16,256,128]{2,1,0:T(8,128)(2,1)S(1)}, bf16[16,256,128]{2,1,0:T(8,128)(2,1)S(1)}, u32[]{:S(2)}, u32[]{:S(2)}) collective-permute-start(bf16[16,256,128]{2,1,0:T(8,128)(2,1)S(1)} %copy-done.36), channel_id=1, source_target_pairs={{0,4},{4,0},{8,12},{12,8},{1,5},{5,1},{9,13},{13,9},{2,6},{6,2},{1... | collective-permute-start | bytes 3145736 | tf_op jit(solution)/shard_map/ppermute | solution.py:877
  355.7 17.6 %collective-permute-start.43 = (bf16[11,256,128]{2,1,0:T(8,128)(2,1)S(1)}, bf16[11,256,128]{2,1,0:T(8,128)(2,1)S(1)}, u32[]{:S(2)}, u32[]{:S(2)}) collective-permute-start(bf16[11,256,128]{2,1,0:T(8,128)(2,1)S(1)} %fusion.6.inner), channel_id=1, source_target_pairs={{0,1},{1,0},{2,3},{3,2},{4,5},{5,4},{6,7},{7,6},{8,9},{9,8},{10,11... | collective-permute-start | bytes 2162696 | tf_op jit(solution)/shard_map/ppermute | solution.py:908
  374.3 19.4 %collective-permute-start.47 = (bf16[11,256,128]{2,1,0:T(8,128)(2,1)S(1)}, bf16[11,256,128]{2,1,0:T(8,128)(2,1)S(1)}, u32[]{:S(2)}, u32[]{:S(2)}) collective-permute-start(bf16[11,256,128]{2,1,0:T(8,128)(2,1)S(1)} %add_convert_fusion.inner), channel_id=1, source_target_pairs={{1,0},{2,3},{5,4},{6,7},{9,8},{10,11},{13,12},{14,15},{17,16},{18,... | collective-permute-start | bytes 2162696 | tf_op jit(solution)/shard_map/ppermute | solution.py:918
  377.1 20.6 %collective-permute-start.48 = (bf16[8,256,128]{2,1,0:T(8,128)(2,1)S(1)}, bf16[8,256,128]{2,1,0:T(8,128)(2,1)S(1)}, u32[]{:S(2)}, u32[]{:S(2)}) collective-permute-start(bf16[8,256,128]{2,1,0:T(8,128)(2,1)S(1)} %add_convert_fusion.17), channel_id=1, source_target_pairs={{0,1},{3,2},{4,5},{7,6},{8,9},{11,10},{12,13},{15,14},{16,17},{19,... | collective-permute-start | bytes 1572872 | tf_op jit(solution)/shard_map/ppermute | solution.py:914
  384.1 24.6 %collective-permute-start.45 = (bf16[11,256,128]{2,1,0:T(8,128)(2,1)S(1)}, bf16[11,256,128]{2,1,0:T(8,128)(2,1)S(1)}, u32[]{:S(2)}, u32[]{:S(2)}) collective-permute-start(bf16[11,256,128]{2,1,0:T(8,128)(2,1)S(1)} %add_convert_fusion.1.inner), channel_id=1, source_target_pairs={{1,0},{2,3},{5,4},{6,7},{9,8},{10,11},{13,12},{14,15},{17,16},{18,... | collective-permute-start | bytes 2162696 | tf_op jit(solution)/shard_map/ppermute | solution.py:918
  449.3 18.8 %collective-permute-start.59 = (bf16[8,256,128]{2,1,0:T(8,128)(2,1)S(1)}, bf16[8,256,128]{2,1,0:T(8,128)(2,1)S(1)}, u32[]{:S(2)}, u32[]{:S(2)}) collective-permute-start(bf16[8,256,128]{2,1,0:T(8,128)(2,1)S(1)} %add_convert_fusion.12.inner), channel_id=1, source_target_pairs={{1,0},{2,3},{5,4},{6,7},{9,8},{10,11},{13,12},{14,15},{17,16},{18,... | collective-permute-start | bytes 1572872 | tf_op jit(solution)/shard_map/ppermute | solution.py:918
  450.7 28.0 %collective-permute-start.57 = (bf16[8,256,128]{2,1,0:T(8,128)(2,1)S(1)}, bf16[8,256,128]{2,1,0:T(8,128)(2,1)S(1)}, u32[]{:S(2)}, u32[]{:S(2)}) collective-permute-start(bf16[8,256,128]{2,1,0:T(8,128)(2,1)S(1)} %add_convert_fusion.13.inner), channel_id=1, source_target_pairs={{1,0},{2,3},{5,4},{6,7},{9,8},{10,11},{13,12},{14,15},{17,16},{18,... | collective-permute-start | bytes 1572872 | tf_op jit(solution)/shard_map/ppermute | solution.py:918
  (71 other events, 874.4 us)

commit v7 on v6

--- a/solution.py
+++ b/solution.py
@@ -499,8 +499,8 @@
             p = qpv[:, lane].astype(f32)
             s = sigmoid(p)
             dqv[:, lane] = (turned * (s * (1.0 + p * (1.0 - s)))).astype(bf16)
-            dkv[:, lane] = nn(scores_t, query)
-            dvv[:, lane] = nn(weights_t, cot)
+            dkv[:, lane] = nn(scores_t, query).astype(bf16)
+            dvv[:, lane] = nn(weights_t, cot).astype(bf16)
         for copy in pair_out(i):
             copy.start()
         return carry
@@ -533,7 +533,7 @@
     full = hbm((rows, width), f32)
     unit = hbm((rows, hidden), bf16)
     state = hbm(states, bf16)
-    outs = [unit, unit, full, act, act, act, full, full, state, state]
+    outs = [unit, unit, full, act, act, act, act, act, state, state]
     wide = pltpu.VMEM((rows, width), bf16)
     thin = pltpu.VMEM((rows, LANES), f32)
     twice = pltpu.VMEM((rows, 2 * width), bf16)
@@ -605,12 +605,14 @@
             state = entering_state(factors, statev, n)
             decay = jnp.exp(ahead * (-slope[n]))
             keyed = (kvv[:, lane].astype(f32) * decay).astype(bf16)
-            dkey = dkin[:, lane] + decay * nt(vv[:, lane], state)
+            dkey = dkin[:, lane].astype(f32) + decay * nt(vv[:, lane], state)
             turned = dkey * cv[...] + half_turn(dkey * sv[...])
             p = kpv[:, lane].astype(f32)
             s = sigmoid(p)
             parts[:, pl.ds(at + width, LANES)] = (turned * (s * (1.0 + p * (1.0 - s)))).astype(bf16)
-            parts[:, pl.ds(at + 2 * width, LANES)] = (dvin[:, lane] + nn(keyed, state)).astype(bf16)
+            parts[:, pl.ds(at + 2 * width, LANES)] = (
+                dvin[:, lane].astype(f32) + nn(keyed, state)
+            ).astype(bf16)
         return carry
 
     lax.fori_loop(0, HEADS // 4, some, 0)
@@ -650,7 +652,7 @@
         out_specs=[ANY] * 3,
         out_shape=[act, act, act],
         scratch_shapes=[
-            full, full, wide, wide, wide, pltpu.VMEM((2 * HEADS, LANES, LANES), bf16), thin, thin,
+            wide, wide, wide, wide, wide, pltpu.VMEM((2 * HEADS, LANES, LANES), bf16), thin, thin,
             wide, thin,
             full,
             pltpu.VMEM((rows, w.shape[1]), bf16), wide, full,

time: 489 us -> 488 us (level)
  no operation moved by 1% of the time
where the time goes in v7:
time: 488 us; the launch traced here: 479 us
  Pallas kernels  236 us (48%)
  waiting for transfers between devices  122 us (25%)
  starting transfers between devices  82.3 us (17%)
  other arithmetic  17.1 us (4%)
  blocking collectives  12.1 us (2%)
  local copies, waits for them, and re-layouts  6.74 us (1%)
    pallas_call x4, Pallas kernels, back_channel(): pl.pallas_call(back_channel_body, in_specs=[SMEM] + [FREE] + [VMEM] * 3 +...  63 us
    pallas_call x4, Pallas kernels, finish(): pl.pallas_call(finish_body, in_specs=[SMEM] * 2 + [FREE] + [ANY] * 2 + [F...  52.4 us
    pallas_call x4, Pallas kernels, weight_gradient(): pl.pallas_call(functools.partial(weight_body, batch=batch, sides=sides, g...  40.3 us
    pallas_call x4, Pallas kernels, project(): pl.pallas_call(project_body, in_specs=[SMEM, FREE] + [ANY] * 3 + [ANY if...  34.9 us
    pallas_call x4, Pallas kernels, back_mixer(): pl.pallas_call(back_mixer_body, in_specs=[SMEM] * 2 + [ANY] * 6 + [FREE]...  32.2 us
    ppermute x7, waiting for transfers between devices, over_z(): got = lax.ppermute(sent, 'dp', [(0, 1), (1, 0), (2, 3), (3, 2)])  27.6 us
    ppermute x4, waiting for transfers between devices, over_z(): lax.ppermute(done, 'dp', [(1, 0), (2, 3)])  25.5 us
    ppermute x11, waiting for transfers between devices, over_y(): self.previous = lax.ppermute(far, 'seq', [(0, 2), (2, 0), (1, 3), (3, 1)])  23.9 us
  transfers between devices with their start and end apart: 60, of which 23 were waited for; matrix products, arithmetic and copies ran while one was open for 3% of the time, Pallas kernels for 25%

profile of v7, /device:TPU:0, one launch (start us, length us, event | category | flops | bytes accessed | tf_op | source)
XLA Modules:
  0.0 479.2 jit_solution(12058287067869609295)
XLA Ops:
  5.7 12.1 %all-gather.1 = s32[4,2,256]{2,1,0:T(2,128)S(1)} all-gather(s32[1,2,256]{2,1,0:T(2,128)S(1)} %bitcast.104), channel_id=2, replica_groups=mesh['section'=2,'seq'=4,'dp'=4] {'seq'}, dimensions={0}, use_global_device_ids=true | all-gather | bytes 10240 | tf_op jit(solution)/shard_map/all_gather | solution.py:1036
  20.8 10.9 %project.4 = (bf16[256,1024]{1,0:T(8,128)(2,1)}, f32[256,128]{1,0:T(8,128)}, bf16[256,4096]{1,0:T(8,128)(2,1)}, bf16[256,2048]{1,0:T(8,128)(2,1)}, bf16[8,128,12...) custom-call(f32[8]{0:T(128)S(1)} %get-tuple-element.293.slope, bf16[256,1024]{1,0:T(8,128)(2,1)S(1)} %get-tuple-element.355.x.dy.refs_7_, ...), custom_call_target="tpu_custom_call" | custom-call | flops 2147483648 | bytes 8388608 | tf_op jit(solution)/shard_map/project/pallas_call | solution.py:198
  31.8 8.2 %project.5 = (bf16[256,1024]{1,0:T(8,128)(2,1)}, f32[256,128]{1,0:T(8,128)}, bf16[256,4096]{1,0:T(8,128)(2,1)}, bf16[256,2048]{1,0:T(8,128)(2,1)}, bf16[8,128,12...) custom-call(f32[8]{0:T(128)S(1)} %get-tuple-element.293.slope, bf16[256,1024]{1,0:T(8,128)(2,1)S(1)} %get-tuple-element.354.x.dy.refs_8_, ...), custom_call_target="tpu_custom_call" | custom-call | flops 2147483648 | bytes 8388608 | tf_op jit(solution)/shard_map/project/pallas_call | solution.py:198
  46.3 13.3 %finish.4 = (bf16[256,1024]{1,0:T(8,128)(2,1)}, bf16[256,1024]{1,0:T(8,128)(2,1)}, f32[256,128]{1,0:T(8,128)}, bf16[256,1024]{1,0:T(8,128)(2,1)}, f32[256,128]{1...) custom-call(f32[8]{0:T(128)S(1)} %get-tuple-element.293.slope, ...), custom_call_target="tpu_custom_call" | custom-call | flops 4966055936 | bytes 19398656 | tf_op jit(solution)/shard_map/finish/pallas_call | solution.py:361
  63.2 13.1 %finish.5 = (bf16[256,1024]{1,0:T(8,128)(2,1)}, bf16[256,1024]{1,0:T(8,128)(2,1)}, f32[256,128]{1,0:T(8,128)}, bf16[256,1024]{1,0:T(8,128)(2,1)}, f32[256,128]{1...) custom-call(f32[8]{0:T(128)S(1)} %get-tuple-element.293.slope, ...), custom_call_target="tpu_custom_call" | custom-call | flops 4966055936 | bytes 19398656 | tf_op jit(solution)/shard_map/finish/pallas_call | solution.py:361
  77.6 7.9 %project.6 = (bf16[256,1024]{1,0:T(8,128)(2,1)}, f32[256,128]{1,0:T(8,128)}, bf16[256,4096]{1,0:T(8,128)(2,1)}, bf16[256,2048]{1,0:T(8,128)(2,1)}, bf16[8,128,12...) custom-call(f32[8]{0:T(128)S(1)} %get-tuple-element.293.slope, bf16[256,1024]{1,0:T(8,128)(2,1)S(1)} %collective-permute-done.3.x, ...), custom_call_target="tpu_custom_call" | custom-call | flops 2147483648 | bytes 8388608 | tf_op jit(solution)/shard_map/project/pallas_call | solution.py:198
  89.6 7.9 %project.7 = (bf16[256,1024]{1,0:T(8,128)(2,1)}, f32[256,128]{1,0:T(8,128)}, bf16[256,4096]{1,0:T(8,128)(2,1)}, bf16[256,2048]{1,0:T(8,128)(2,1)}, bf16[8,128,12...) custom-call(f32[8]{0:T(128)S(1)} %get-tuple-element.293.slope, bf16[256,1024]{1,0:T(8,128)(2,1)S(1)} %collective-permute-done.4.x, ...), custom_call_target="tpu_custom_call" | custom-call | flops 2147483648 | bytes 8388608 | tf_op jit(solution)/shard_map/project/pallas_call | solution.py:198
  100.4 13.0 %finish.6 = (bf16[256,1024]{1,0:T(8,128)(2,1)}, bf16[256,1024]{1,0:T(8,128)(2,1)}, f32[256,128]{1,0:T(8,128)}, bf16[256,1024]{1,0:T(8,128)(2,1)}, f32[256,128]{1...) custom-call(f32[8]{0:T(128)S(1)} %get-tuple-element.293.slope, ...), custom_call_target="tpu_custom_call" | custom-call | flops 4966055936 | bytes 19398656 | tf_op jit(solution)/shard_map/finish/pallas_call | solution.py:361
  113.4 13.1 %finish.7 = (bf16[256,1024]{1,0:T(8,128)(2,1)}, bf16[256,1024]{1,0:T(8,128)(2,1)}, f32[256,128]{1,0:T(8,128)}, bf16[256,1024]{1,0:T(8,128)(2,1)}, f32[256,128]{1...) custom-call(f32[8]{0:T(128)S(1)} %get-tuple-element.293.slope, ...), custom_call_target="tpu_custom_call" | custom-call | flops 4966055936 | bytes 19398656 | tf_op jit(solution)/shard_map/finish/pallas_call | solution.py:361
  126.5 15.8 %back_channel.4 = (bf16[256,2816]{1,0:T(8,128)(2,1)}, bf16[256,2816]{1,0:T(8,128)(2,1)}, f32[256,1024]{1,0:T(8,128)}, bf16[256,1024]{1,0:T(8,128)(2,1)}, bf16[25...) custom-call(f32[8]{0:T(128)S(1)} %get-tuple-element.293.slope, ...), custom_call_target="tpu_custom_call" | custom-call | flops 4966055936 | bytes 19398656 | tf_op jit(solution)/shard_map/back_channel/pallas_call | solution.py:541
  142.3 15.8 %back_channel.5 = (bf16[256,2816]{1,0:T(8,128)(2,1)}, bf16[256,2816]{1,0:T(8,128)(2,1)}, f32[256,1024]{1,0:T(8,128)}, bf16[256,1024]{1,0:T(8,128)(2,1)}, bf16[25...) custom-call(f32[8]{0:T(128)S(1)} %get-tuple-element.293.slope, ...), custom_call_target="tpu_custom_call" | custom-call | flops 4966055936 | bytes 19398656 | tf_op jit(solution)/shard_map/back_channel/pallas_call | solution.py:541
  161.7 8.0 %back_mixer.4 = (bf16[256,1024]{1,0:T(8,128)(2,1)}, bf16[256,1024]{1,0:T(8,128)(2,1)}, bf16[256,1024]{1,0:T(8,128)(2,1)}) custom-call(f32[8]{0:T(128)S(1)} %get-tuple-element.293.slope, f32[2,8]{1,0:T(2,128)S(1)} %copy-done.13, bf16[256,1024]{1,0:T(8,128)(2,1)} %get-tuple-element.231.dq.refs_14_, bf16[256,1024]{1,0:T(8,128)(2,1)} %get-tuple-element.232.du.refs_20_, ...), custom_call_target="tpu_custom_call" | custom-call | flops 2147483648 | bytes 8388608 | tf_op jit(solution)/shard_map/back_mixer/pallas_call | solution.py:649
  171.2 8.0 %back_mixer.5 = (bf16[256,1024]{1,0:T(8,128)(2,1)}, bf16[256,1024]{1,0:T(8,128)(2,1)}, bf16[256,1024]{1,0:T(8,128)(2,1)}) custom-call(f32[8]{0:T(128)S(1)} %get-tuple-element.293.slope, f32[2,8]{1,0:T(2,128)S(1)} %stack.37.factors, bf16[256,1024]{1,0:T(8,128)(2,1)} %get-tuple-element.240.dq.refs_13_, bf16[256,1024]{1,0:T(8,128)(2,1)} %get-tuple-element.241.du.refs_19_, ...), custom_call_target="tpu_custom_call" | custom-call | flops 2147483648 | bytes 8388608 | tf_op jit(solution)/shard_map/back_mixer/pallas_call | solution.py:649
  180.5 6.1 %collective-permute-done.7.dy.refs_6_ = bf16[256,1024]{1,0:T(8,128)(2,1)S(1)} collective-permute-done((bf16[256,1024]{1,0:T(8,128)(2,1)}, bf16[256,1024]{1,0:T(8,128)(2,1)S(1)}, u32[]{:S(2)}, u32[]{:S(2)}) %collective-permute-start.7) | collective-permute-done | bytes 524320 | tf_op jit(solution)/shard_map/ppermute | solution.py:1076
  186.6 15.7 %back_channel.6 = (bf16[256,2816]{1,0:T(8,128)(2,1)}, bf16[256,2816]{1,0:T(8,128)(2,1)}, f32[256,1024]{1,0:T(8,128)}, bf16[256,1024]{1,0:T(8,128)(2,1)}, bf16[25...) custom-call(f32[8]{0:T(128)S(1)} %get-tuple-element.293.slope, ...), custom_call_target="tpu_custom_call" | custom-call | flops 4966055936 | bytes 19398656 | tf_op jit(solution)/shard_map/back_channel/pallas_call | solution.py:541
  203.1 9.1 %weight_gradient.4 = (bf16[8,704,128]{2,1,0:T(8,128)(2,1)}, bf16[8,704,128]{2,1,0:T(8,128)(2,1)}, bf16[8,704,128]{2,1,0:T(8,128)(2,1)}, bf16[8,704,128]{2,1,0:T(8,128)(2,1)}) custom-call(s32[5]{0:T(128)S(1)} %stack.36.refs_0_, bf16[256,2816]{1,0:T(8,128)(2,1)} %get-tuple-element.257.refs_1_, bf16[256,2816]{1,0:T(8,128)(2,1)} %get-tuple-element.258.refs_2_, ...), custom_call_target="tpu_custom_call" | custom-call | flops 2952790016 | bytes 5767168 | tf_op jit(solution)/shard_map/weight_gradient/pallas_call | solution.py:771
  218.3 15.7 %back_channel.7 = (bf16[256,2816]{1,0:T(8,128)(2,1)}, bf16[256,2816]{1,0:T(8,128)(2,1)}, f32[256,1024]{1,0:T(8,128)}, bf16[256,1024]{1,0:T(8,128)(2,1)}, bf16[25...) custom-call(f32[8]{0:T(128)S(1)} %get-tuple-element.293.slope, ...), custom_call_target="tpu_custom_call" | custom-call | flops 4966055936 | bytes 19398656 | tf_op jit(solution)/shard_map/back_channel/pallas_call | solution.py:541
  234.1 14.3 %weight_gradient.5 = (bf16[22,256,128]{2,1,0:T(8,128)(2,1)}, bf16[22,256,128]{2,1,0:T(8,128)(2,1)}, bf16[22,256,128]{2,1,0:T(8,128)(2,1)}, bf16[22,256,128]{2,1,...) custom-call(s32[5]{0:T(128)S(1)} %stack.36.refs_0_, ...), custom_call_target="tpu_custom_call" | custom-call | flops 5905580032 | bytes 11534336 | tf_op jit(solution)/shard_map/weight_gradient/pallas_call | solution.py:771
  255.1 13.4 %collective-permute-done.34 = bf16[11,256,128]{2,1,0:T(8,128)(2,1)S(1)} collective-permute-done((bf16[11,256,128]{2,1,0:T(8,128)(2,1)S(1)}, bf16[11,256,128]{2,1,0:T(8,128)(2,1)S(1)}, u32[]{:S(2)}, u32[]{:S(2)}) %collective-permute-start.34) | collective-permute-done | bytes 720928 | tf_op jit(solution)/shard_map/ppermute | solution.py:916
  277.3 8.2 %back_mixer.6 = (bf16[256,1024]{1,0:T(8,128)(2,1)}, bf16[256,1024]{1,0:T(8,128)(2,1)}, bf16[256,1024]{1,0:T(8,128)(2,1)}) custom-call(f32[8]{0:T(128)S(1)} %get-tuple-element.293.slope, f32[2,8]{1,0:T(2,128)S(1)} %copy-done.13, bf16[256,1024]{1,0:T(8,128)(2,1)} %get-tuple-element.285.dq.refs_6_, bf16[256,1024]{1,0:T(8,128)(2,1)} %get-tuple-element.286.du.refs_12_, ...), custom_call_target="tpu_custom_call" | custom-call | flops 2147483648 | bytes 8388608 | tf_op jit(solution)/shard_map/back_mixer/pallas_call | solution.py:649
  295.1 8.0 %back_mixer.7 = (bf16[256,1024]{1,0:T(8,128)(2,1)}, bf16[256,1024]{1,0:T(8,128)(2,1)}, bf16[256,1024]{1,0:T(8,128)(2,1)}) custom-call(f32[8]{0:T(128)S(1)} %get-tuple-element.293.slope, f32[2,8]{1,0:T(2,128)S(1)} %stack.37.factors, bf16[256,1024]{1,0:T(8,128)(2,1)} %get-tuple-element.294.dq.refs_5_, bf16[256,1024]{1,0:T(8,128)(2,1)} %get-tuple-element.295.du.refs_11_, ...), custom_call_target="tpu_custom_call" | custom-call | flops 2147483648 | bytes 8388608 | tf_op jit(solution)/shard_map/back_mixer/pallas_call | solution.py:649
  316.4 11.8 %weight_gradient.7 = (bf16[16,256,128]{2,1,0:T(8,128)(2,1)}, bf16[16,256,128]{2,1,0:T(8,128)(2,1)}, bf16[16,256,128]{2,1,0:T(8,128)(2,1)}, bf16[16,256,128]{2,1,...) custom-call(s32[5]{0:T(128)S(1)} %stack.36.refs_0_, ...), custom_call_target="tpu_custom_call" | custom-call | flops 4294967296 | bytes 8388608 | tf_op jit(solution)/shard_map/weight_gradient/pallas_call | solution.py:771
  336.7 11.4 %collective-permute-done.28 = bf16[11,256,128]{2,1,0:T(8,128)(2,1)S(1)} collective-permute-done((bf16[11,256,128]{2,1,0:T(8,128)(2,1)S(1)}, bf16[11,256,128]{2,1,0:T(8,128)(2,1)S(1)}, u32[]{:S(2)}, u32[]{:S(2)}) %collective-permute-start.28) | collective-permute-done | bytes 720928 | tf_op jit(solution)/shard_map/ppermute | solution.py:889
  357.5 6.9 %collective-permute-done.29 = bf16[8,256,128]{2,1,0:T(8,128)(2,1)S(1)} collective-permute-done((bf16[8,256,128]{2,1,0:T(8,128)(2,1)S(1)}, bf16[8,256,128]{2,1,0:T(8,128)(2,1)S(1)}, u32[]{:S(2)}, u32[]{:S(2)}) %collective-permute-start.29) | collective-permute-done | bytes 524320 | tf_op jit(solution)/shard_map/ppermute | solution.py:889
  366.1 5.8 %collective-permute-done.43.outer = bf16[11,256,128]{2,1,0:T(8,128)(2,1)S(1)} collective-permute-done((bf16[11,256,128]{2,1,0:T(8,128)(2,1)S(1)}, bf16[11,256,128]{2,1,0:T(8,128)(2,1)S(1)}, u32[]{:S(2)}, u32[]{:S(2)}) %collective-permute-start.43) | collective-permute-done | bytes 720928 | tf_op jit(solution)/shard_map/ppermute | solution.py:910
  375.8 5.9 %collective-permute-start.48 = (bf16[8,256,128]{2,1,0:T(8,128)(2,1)S(1)}, bf16[8,256,128]{2,1,0:T(8,128)(2,1)S(1)}, u32[]{:S(2)}, u32[]{:S(2)}) collective-permute-start(bf16[8,256,128]{2,1,0:T(8,128)(2,1)S(1)} %add_convert_fusion.17), channel_id=1, source_target_pairs={{0,1},{3,2},{4,5},{7,6},{8,9},{11,10},{12,13},{15,14},{16,17},{19,... | collective-permute-start | bytes 1572872 | tf_op jit(solution)/shard_map/ppermute | solution.py:916
  384.4 9.7 %collective-permute-done.47.outer = bf16[11,256,128]{2,1,0:T(8,128)(2,1)S(1)} collective-permute-done((bf16[11,256,128]{2,1,0:T(8,128)(2,1)S(1)}, bf16[11,256,128]{2,1,0:T(8,128)(2,1)S(1)}, u32[]{:S(2)}, u32[]{:S(2)}) %collective-permute-start.47) | collective-permute-done | bytes 720928 | tf_op jit(solution)/shard_map/ppermute | solution.py:920
  399.0 6.1 %collective-permute-done.51 = bf16[8,256,128]{2,1,0:T(8,128)(2,1)S(1)} collective-permute-done((bf16[8,256,128]{2,1,0:T(8,128)(2,1)S(1)}, bf16[8,256,128]{2,1,0:T(8,128)(2,1)S(1)}, u32[]{:S(2)}, u32[]{:S(2)}) %collective-permute-start.51) | collective-permute-done | bytes 524320 | tf_op jit(solution)/shard_map/ppermute | solution.py:916
  414.6 7.1 %collective-permute-done.50.outer = bf16[8,256,128]{2,1,0:T(8,128)(2,1)S(1)} collective-permute-done((bf16[8,256,128]{2,1,0:T(8,128)(2,1)S(1)}, bf16[8,256,128]{2,1,0:T(8,128)(2,1)S(1)}, u32[]{:S(2)}, u32[]{:S(2)}) %collective-permute-start.50) | collective-permute-done | bytes 524320 | tf_op jit(solution)/shard_map/ppermute | solution.py:910
  439.0 6.2 %collective-permute-done.55.outer = bf16[8,256,128]{2,1,0:T(8,128)(2,1)S(1)} collective-permute-done((bf16[8,256,128]{2,1,0:T(8,128)(2,1)S(1)}, bf16[8,256,128]{2,1,0:T(8,128)(2,1)S(1)}, u32[]{:S(2)}, u32[]{:S(2)}) %collective-permute-start.55) | collective-permute-done | bytes 524320 | tf_op jit(solution)/shard_map/ppermute | solution.py:910
  451.1 9.7 %collective-permute-done.12 = bf16[256,1024]{1,0:T(8,128)(2,1)S(1)} collective-permute-done((bf16[256,1024]{1,0:T(8,128)(2,1)S(1)}, bf16[256,1024]{1,0:T(8,128)(2,1)S(1)}, u32[]{:S(2)}, u32[]{:S(2)}) %collective-permute-start.12) | collective-permute-done | bytes 524320 | tf_op jit(solution)/shard_map/ppermute | solution.py:858
  468.7 8.9 %collective-permute-done.57.outer = bf16[8,256,128]{2,1,0:T(8,128)(2,1)S(1)} collective-permute-done((bf16[8,256,128]{2,1,0:T(8,128)(2,1)S(1)}, bf16[8,256,128]{2,1,0:T(8,128)(2,1)S(1)}, u32[]{:S(2)}, u32[]{:S(2)}) %collective-permute-start.57) | collective-permute-done | bytes 524320 | tf_op jit(solution)/shard_map/ppermute | solution.py:920
  (267 shorter events, 149.5 us)
Async XLA Ops:
  2.0 17.9 %collective-permute-start.1 = (bf16[256,1024]{1,0:T(8,128)(2,1)S(1)}, bf16[256,1024]{1,0:T(8,128)(2,1)S(1)}, u32[]{:S(2)}, u32[]{:S(2)}) collective-permute-start(bf16[256,1024]{1,0:T(8,128)(2,1)S(1)} %get-tuple-element.362), channel_id=1, source_target_pairs={{4,0},{8,12},{0,8},{12,4},{5,1},{9,13},{1,9},{13,5},{6,2},{10,14},... | collective-permute-start | bytes 1572872 | tf_op jit(solution)/shard_map/ppermute | solution.py:848
  59.5 18.1 %collective-permute-start.3 = (bf16[256,1024]{1,0:T(8,128)(2,1)}, bf16[256,1024]{1,0:T(8,128)(2,1)S(1)}, u32[]{:S(2)}, u32[]{:S(2)}) collective-permute-start(bf16[256,1024]{1,0:T(8,128)(2,1)} %get-tuple-element.198), channel_id=1, source_target_pairs={{0,16},{1,17},{2,18},{3,19},{4,20},{5,21},{6,22},{7,23},{8,24},{9,... | collective-permute-start | bytes 1572872 | tf_op jit(solution)/shard_map/ppermute | solution.py:1068
  179.2 23.1 %collective-permute-start.8 = (bf16[256,1024]{1,0:T(8,128)(2,1)}, bf16[256,1024]{1,0:T(8,128)(2,1)S(1)}, u32[]{:S(2)}, u32[]{:S(2)}) collective-permute-start(bf16[256,1024]{1,0:T(8,128)(2,1)} %get-tuple-element.261), channel_id=1, source_target_pairs={{16,0},{17,1},{18,2},{19,3},{20,4},{21,5},{22,6},{23,7},{24,8},{25... | collective-permute-start | bytes 1572872 | tf_op jit(solution)/shard_map/ppermute | solution.py:1076
  212.3 40.8 %collective-permute-start.13 = (bf16[22,256,128]{2,1,0:T(8,128)(2,1)}, bf16[22,256,128]{2,1,0:T(8,128)(2,1)S(1)}, u32[]{:S(2)}, u32[]{:S(2)}) collective-permute-start(bf16[22,256,128]{2,1,0:T(8,128)(2,1)} %bitcast.105), channel_id=1, source_target_pairs={{0,4},{4,0},{8,12},{12,8},{1,5},{5,1},{9,13},{13,9},{2,6},{6,2},{1... | collective-permute-start | bytes 4325384 | tf_op jit(solution)/shard_map/ppermute | solution.py:879
  216.0 32.6 %collective-permute-start.14 = (bf16[11,256,128]{2,1,0:T(8,128)(2,1)S(1)}, bf16[11,256,128]{2,1,0:T(8,128)(2,1)S(1)}, u32[]{:S(2)}, u32[]{:S(2)}) collective-permute-start(bf16[11,256,128]{2,1,0:T(8,128)(2,1)S(1)} %fusion.13), channel_id=1, source_target_pairs={{0,8},{8,0},{4,12},{12,4},{1,9},{9,1},{5,13},{13,5},{2,10},{10,2},... | collective-permute-start | bytes 2162696 | tf_op jit(solution)/shard_map/ppermute | solution.py:889
  248.5 20.2 %collective-permute-start.23 = (bf16[22,256,128]{2,1,0:T(8,128)(2,1)}, bf16[22,256,128]{2,1,0:T(8,128)(2,1)S(1)}, u32[]{:S(2)}, u32[]{:S(2)}) collective-permute-start(bf16[22,256,128]{2,1,0:T(8,128)(2,1)} %get-tuple-element.333), channel_id=1, source_target_pairs={{0,4},{4,0},{8,12},{12,8},{1,5},{5,1},{9,13},{13,9},{2,6},{6,2},{1... | collective-permute-start | bytes 4325384 | tf_op jit(solution)/shard_map/ppermute | solution.py:879
  248.9 19.6 %collective-permute-start.34 = (bf16[11,256,128]{2,1,0:T(8,128)(2,1)S(1)}, bf16[11,256,128]{2,1,0:T(8,128)(2,1)S(1)}, u32[]{:S(2)}, u32[]{:S(2)}) collective-permute-start(bf16[11,256,128]{2,1,0:T(8,128)(2,1)S(1)} %fusion.11), channel_id=1, source_target_pairs={{0,1},{3,2},{4,5},{7,6},{8,9},{11,10},{12,13},{15,14},{16,17},{19,... | collective-permute-start | bytes 2162696 | tf_op jit(solution)/shard_map/ppermute | solution.py:916
  252.9 32.7 %collective-permute-start.22 = (bf16[22,256,128]{2,1,0:T(8,128)(2,1)S(1)}, bf16[22,256,128]{2,1,0:T(8,128)(2,1)S(1)}, u32[]{:S(2)}, u32[]{:S(2)}) collective-permute-start(bf16[22,256,128]{2,1,0:T(8,128)(2,1)S(1)} %copy-done.33), channel_id=1, source_target_pairs={{0,4},{4,0},{8,12},{12,8},{1,5},{5,1},{9,13},{13,9},{2,6},{6,2},{1... | collective-permute-start | bytes 4325384 | tf_op jit(solution)/shard_map/ppermute | solution.py:879
  253.3 18.4 %collective-permute-start.24 = (bf16[11,256,128]{2,1,0:T(8,128)(2,1)S(1)}, bf16[11,256,128]{2,1,0:T(8,128)(2,1)S(1)}, u32[]{:S(2)}, u32[]{:S(2)}) collective-permute-start(bf16[11,256,128]{2,1,0:T(8,128)(2,1)S(1)} %fusion.12), channel_id=1, source_target_pairs={{0,8},{8,0},{4,12},{12,4},{1,9},{9,1},{5,13},{13,5},{2,10},{10,2},... | collective-permute-start | bytes 2162696 | tf_op jit(solution)/shard_map/ppermute | solution.py:889
  253.8 18.5 %collective-permute-start.10 = (bf16[8,128,128]{2,1,0:T(8,128)(2,1)S(1)}, bf16[8,128,128]{2,1,0:T(8,128)(2,1)S(1)}, u32[]{:S(2)}, u32[]{:S(2)}) collective-permute-start(bf16[8,128,128]{2,1,0:T(8,128)(2,1)S(1)} %copy-done.38), channel_id=1, source_target_pairs={{4,0},{12,8},{5,1},{13,9},{6,2},{14,10},{7,3},{15,11},{20,16},{28,... | collective-permute-start | bytes 786440 | tf_op jit(solution)/shard_map/ppermute | solution.py:1005
  268.5 39.6 %collective-permute-start.21 = (bf16[22,256,128]{2,1,0:T(8,128)(2,1)S(1)}, bf16[22,256,128]{2,1,0:T(8,128)(2,1)S(1)}, u32[]{:S(2)}, u32[]{:S(2)}) collective-permute-start(bf16[22,256,128]{2,1,0:T(8,128)(2,1)S(1)} %copy-done.32), channel_id=1, source_target_pairs={{0,4},{4,0},{8,12},{12,8},{1,5},{5,1},{9,13},{13,9},{2,6},{6,2},{1... | collective-permute-start | bytes 4325384 | tf_op jit(solution)/shard_map/ppermute | solution.py:879
  268.7 21.2 %collective-permute-start.35 = (bf16[11,256,128]{2,1,0:T(8,128)(2,1)S(1)}, bf16[11,256,128]{2,1,0:T(8,128)(2,1)S(1)}, u32[]{:S(2)}, u32[]{:S(2)}) collective-permute-start(bf16[11,256,128]{2,1,0:T(8,128)(2,1)S(1)} %add_convert_fusion.3), channel_id=1, source_target_pairs={{1,2},{2,1},{5,6},{6,5},{9,10},{10,9},{13,14},{14,13},{17,18},{18,... | collective-permute-start | bytes 2162696 | tf_op jit(solution)/shard_map/ppermute | solution.py:906
  271.8 17.5 %collective-permute-start.25 = (bf16[11,256,128]{2,1,0:T(8,128)(2,1)S(1)}, bf16[11,256,128]{2,1,0:T(8,128)(2,1)S(1)}, u32[]{:S(2)}, u32[]{:S(2)}) collective-permute-start(bf16[11,256,128]{2,1,0:T(8,128)(2,1)S(1)} %add_convert_fusion.8), channel_id=1, source_target_pairs={{0,8},{8,0},{4,12},{12,4},{1,9},{9,1},{5,13},{13,5},{2,10},{10,2},... | collective-permute-start | bytes 2162696 | tf_op jit(solution)/shard_map/ppermute | solution.py:889
  272.4 21.8 %collective-permute-start.37 = (bf16[11,256,128]{2,1,0:T(8,128)(2,1)S(1)}, bf16[11,256,128]{2,1,0:T(8,128)(2,1)S(1)}, u32[]{:S(2)}, u32[]{:S(2)}) collective-permute-start(bf16[11,256,128]{2,1,0:T(8,128)(2,1)S(1)} %fusion.9), channel_id=1, source_target_pairs={{0,1},{3,2},{4,5},{7,6},{8,9},{11,10},{12,13},{15,14},{16,17},{19,... | collective-permute-start | bytes 2162696 | tf_op jit(solution)/shard_map/ppermute | solution.py:916
  285.6 42.8 %collective-permute-start.20 = (bf16[22,256,128]{2,1,0:T(8,128)(2,1)S(1)}, bf16[22,256,128]{2,1,0:T(8,128)(2,1)S(1)}, u32[]{:S(2)}, u32[]{:S(2)}) collective-permute-start(bf16[22,256,128]{2,1,0:T(8,128)(2,1)S(1)} %copy-done.31), channel_id=1, source_target_pairs={{0,4},{4,0},{8,12},{12,8},{1,5},{5,1},{9,13},{13,9},{2,6},{6,2},{1... | collective-permute-start | bytes 4325384 | tf_op jit(solution)/shard_map/ppermute | solution.py:879
  289.3 19.0 %collective-permute-start.26 = (bf16[11,256,128]{2,1,0:T(8,128)(2,1)S(1)}, bf16[11,256,128]{2,1,0:T(8,128)(2,1)S(1)}, u32[]{:S(2)}, u32[]{:S(2)}) collective-permute-start(bf16[11,256,128]{2,1,0:T(8,128)(2,1)S(1)} %add_convert_fusion.9), channel_id=1, source_target_pairs={{0,8},{8,0},{4,12},{12,4},{1,9},{9,1},{5,13},{13,5},{2,10},{10,2},... | collective-permute-start | bytes 2162696 | tf_op jit(solution)/shard_map/ppermute | solution.py:889
  290.4 19.7 %collective-permute-start.36 = (bf16[11,256,128]{2,1,0:T(8,128)(2,1)S(1)}, bf16[11,256,128]{2,1,0:T(8,128)(2,1)S(1)}, u32[]{:S(2)}, u32[]{:S(2)}) collective-permute-start(bf16[11,256,128]{2,1,0:T(8,128)(2,1)S(1)} %fusion), channel_id=1, source_target_pairs={{0,1},{1,0},{2,3},{3,2},{4,5},{5,4},{6,7},{7,6},{8,9},{9,8},{10,11... | collective-permute-start | bytes 2162696 | tf_op jit(solution)/shard_map/ppermute | solution.py:910
  294.3 17.4 %collective-permute-start.38 = (bf16[11,256,128]{2,1,0:T(8,128)(2,1)S(1)}, bf16[11,256,128]{2,1,0:T(8,128)(2,1)S(1)}, u32[]{:S(2)}, u32[]{:S(2)}) collective-permute-start(bf16[11,256,128]{2,1,0:T(8,128)(2,1)S(1)} %add_convert_fusion.2), channel_id=1, source_target_pairs={{1,2},{2,1},{5,6},{6,5},{9,10},{10,9},{13,14},{14,13},{17,18},{18,... | collective-permute-start | bytes 2162696 | tf_op jit(solution)/shard_map/ppermute | solution.py:906
  308.4 20.7 %collective-permute-start.27 = (bf16[11,256,128]{2,1,0:T(8,128)(2,1)S(1)}, bf16[11,256,128]{2,1,0:T(8,128)(2,1)S(1)}, u32[]{:S(2)}, u32[]{:S(2)}) collective-permute-start(bf16[11,256,128]{2,1,0:T(8,128)(2,1)S(1)} %add_convert_fusion.10), channel_id=1, source_target_pairs={{0,8},{8,0},{4,12},{12,4},{1,9},{9,1},{5,13},{13,5},{2,10},{10,2},... | collective-permute-start | bytes 2162696 | tf_op jit(solution)/shard_map/ppermute | solution.py:889
  312.1 18.0 %collective-permute-start.39 = (bf16[11,256,128]{2,1,0:T(8,128)(2,1)S(1)}, bf16[11,256,128]{2,1,0:T(8,128)(2,1)S(1)}, u32[]{:S(2)}, u32[]{:S(2)}) collective-permute-start(bf16[11,256,128]{2,1,0:T(8,128)(2,1)S(1)} %fusion.2), channel_id=1, source_target_pairs={{0,1},{1,0},{2,3},{3,2},{4,5},{5,4},{6,7},{7,6},{8,9},{9,8},{10,11... | collective-permute-start | bytes 2162696 | tf_op jit(solution)/shard_map/ppermute | solution.py:910
  328.3 84.7 %collective-permute-start.15 = (bf16[16,256,128]{2,1,0:T(8,128)(2,1)}, bf16[16,256,128]{2,1,0:T(8,128)(2,1)S(1)}, u32[]{:S(2)}, u32[]{:S(2)}) collective-permute-start(bf16[16,256,128]{2,1,0:T(8,128)(2,1)} %get-tuple-element.319), channel_id=1, source_target_pairs={{0,4},{4,0},{8,12},{12,8},{1,5},{5,1},{9,13},{13,9},{2,6},{6,2},{1... | collective-permute-start | bytes 3145736 | tf_op jit(solution)/shard_map/ppermute | solution.py:879
  330.1 18.0 %collective-permute-start.28 = (bf16[11,256,128]{2,1,0:T(8,128)(2,1)S(1)}, bf16[11,256,128]{2,1,0:T(8,128)(2,1)S(1)}, u32[]{:S(2)}, u32[]{:S(2)}) collective-permute-start(bf16[11,256,128]{2,1,0:T(8,128)(2,1)S(1)} %add_convert_fusion.11), channel_id=1, source_target_pairs={{0,8},{8,0},{4,12},{12,4},{1,9},{9,1},{5,13},{13,5},{2,10},{10,2},... | collective-permute-start | bytes 2162696 | tf_op jit(solution)/shard_map/ppermute | solution.py:889
  333.1 18.1 %collective-permute-start.41 = (bf16[11,256,128]{2,1,0:T(8,128)(2,1)S(1)}, bf16[11,256,128]{2,1,0:T(8,128)(2,1)S(1)}, u32[]{:S(2)}, u32[]{:S(2)}) collective-permute-start(bf16[11,256,128]{2,1,0:T(8,128)(2,1)S(1)} %fusion.4.inner), channel_id=1, source_target_pairs={{0,1},{1,0},{2,3},{3,2},{4,5},{5,4},{6,7},{7,6},{8,9},{9,8},{10,11... | collective-permute-start | bytes 2162696 | tf_op jit(solution)/shard_map/ppermute | solution.py:910
  335.2 19.0 %collective-permute-start.42 = (bf16[11,256,128]{2,1,0:T(8,128)(2,1)S(1)}, bf16[11,256,128]{2,1,0:T(8,128)(2,1)S(1)}, u32[]{:S(2)}, u32[]{:S(2)}) collective-permute-start(bf16[11,256,128]{2,1,0:T(8,128)(2,1)S(1)} %fusion.3), channel_id=1, source_target_pairs={{1,2},{2,1},{5,6},{6,5},{9,10},{10,9},{13,14},{14,13},{17,18},{18,... | collective-permute-start | bytes 2162696 | tf_op jit(solution)/shard_map/ppermute | solution.py:906
  336.4 20.0 %collective-permute-start.17 = (bf16[16,256,128]{2,1,0:T(8,128)(2,1)S(1)}, bf16[16,256,128]{2,1,0:T(8,128)(2,1)S(1)}, u32[]{:S(2)}, u32[]{:S(2)}) collective-permute-start(bf16[16,256,128]{2,1,0:T(8,128)(2,1)S(1)} %copy-done.36), channel_id=1, source_target_pairs={{0,4},{4,0},{8,12},{12,8},{1,5},{5,1},{9,13},{13,9},{2,6},{6,2},{1... | collective-permute-start | bytes 3145736 | tf_op jit(solution)/shard_map/ppermute | solution.py:879
  354.4 17.5 %collective-permute-start.43 = (bf16[11,256,128]{2,1,0:T(8,128)(2,1)S(1)}, bf16[11,256,128]{2,1,0:T(8,128)(2,1)S(1)}, u32[]{:S(2)}, u32[]{:S(2)}) collective-permute-start(bf16[11,256,128]{2,1,0:T(8,128)(2,1)S(1)} %fusion.6.inner), channel_id=1, source_target_pairs={{0,1},{1,0},{2,3},{3,2},{4,5},{5,4},{6,7},{7,6},{8,9},{9,8},{10,11... | collective-permute-start | bytes 2162696 | tf_op jit(solution)/shard_map/ppermute | solution.py:910
  373.1 21.1 %collective-permute-start.47 = (bf16[11,256,128]{2,1,0:T(8,128)(2,1)S(1)}, bf16[11,256,128]{2,1,0:T(8,128)(2,1)S(1)}, u32[]{:S(2)}, u32[]{:S(2)}) collective-permute-start(bf16[11,256,128]{2,1,0:T(8,128)(2,1)S(1)} %add_convert_fusion.inner), channel_id=1, source_target_pairs={{1,0},{2,3},{5,4},{6,7},{9,8},{10,11},{13,12},{14,15},{17,16},{18,... | collective-permute-start | bytes 2162696 | tf_op jit(solution)/shard_map/ppermute | solution.py:920
  375.8 21.0 %collective-permute-start.48 = (bf16[8,256,128]{2,1,0:T(8,128)(2,1)S(1)}, bf16[8,256,128]{2,1,0:T(8,128)(2,1)S(1)}, u32[]{:S(2)}, u32[]{:S(2)}) collective-permute-start(bf16[8,256,128]{2,1,0:T(8,128)(2,1)S(1)} %add_convert_fusion.17), channel_id=1, source_target_pairs={{0,1},{3,2},{4,5},{7,6},{8,9},{11,10},{12,13},{15,14},{16,17},{19,... | collective-permute-start | bytes 1572872 | tf_op jit(solution)/shard_map/ppermute | solution.py:916
  383.1 25.1 %collective-permute-start.45 = (bf16[11,256,128]{2,1,0:T(8,128)(2,1)S(1)}, bf16[11,256,128]{2,1,0:T(8,128)(2,1)S(1)}, u32[]{:S(2)}, u32[]{:S(2)}) collective-permute-start(bf16[11,256,128]{2,1,0:T(8,128)(2,1)S(1)} %add_convert_fusion.1.inner), channel_id=1, source_target_pairs={{1,0},{2,3},{5,4},{6,7},{9,8},{10,11},{13,12},{14,15},{17,16},{18,... | collective-permute-start | bytes 2162696 | tf_op jit(solution)/shard_map/ppermute | solution.py:920
  405.2 17.5 %collective-permute-start.52 = (bf16[8,256,128]{2,1,0:T(8,128)(2,1)S(1)}, bf16[8,256,128]{2,1,0:T(8,128)(2,1)S(1)}, u32[]{:S(2)}, u32[]{:S(2)}) collective-permute-start(bf16[8,256,128]{2,1,0:T(8,128)(2,1)S(1)} %add_convert_fusion.14), channel_id=1, source_target_pairs={{1,2},{2,1},{5,6},{6,5},{9,10},{10,9},{13,14},{14,13},{17,18},{18,... | collective-permute-start | bytes 1572872 | tf_op jit(solution)/shard_map/ppermute | solution.py:906
  448.3 19.3 %collective-permute-start.59 = (bf16[8,256,128]{2,1,0:T(8,128)(2,1)S(1)}, bf16[8,256,128]{2,1,0:T(8,128)(2,1)S(1)}, u32[]{:S(2)}, u32[]{:S(2)}) collective-permute-start(bf16[8,256,128]{2,1,0:T(8,128)(2,1)S(1)} %add_convert_fusion.12.inner), channel_id=1, source_target_pairs={{1,0},{2,3},{5,4},{6,7},{9,8},{10,11},{13,12},{14,15},{17,16},{18,... | collective-permute-start | bytes 1572872 | tf_op jit(solution)/shard_map/ppermute | solution.py:920
  449.7 27.9 %collective-permute-start.57 = (bf16[8,256,128]{2,1,0:T(8,128)(2,1)S(1)}, bf16[8,256,128]{2,1,0:T(8,128)(2,1)S(1)}, u32[]{:S(2)}, u32[]{:S(2)}) collective-permute-start(bf16[8,256,128]{2,1,0:T(8,128)(2,1)S(1)} %add_convert_fusion.13.inner), channel_id=1, source_target_pairs={{1,0},{2,3},{5,4},{6,7},{9,8},{10,11},{13,12},{14,15},{17,16},{18,... | collective-permute-start | bytes 1572872 | tf_op jit(solution)/shard_map/ppermute | solution.py:920
  (71 other events, 869.8 us)
